TPU v7x, 32 devices: a whole 2x2x4 slice. The times are simulated.
32 devices in a mesh: dp: 16 (over z, x, core), tensor: 2 (over y).
Axes of the slice: x: 2, y: 2, z: 4, core: 2. Of those that a mesh axis runs over, the one named last changes fastest.
Arguments:
- tokens: bfloat16 [4096, 2048], P(('dp', 'tensor')), may hold values from -6 to 6
- segments: int32 [4096], P('dp'), may hold values from -1 to 0, as said below
- cotangent: bfloat16 [4096, 2048], P(('dp', 'tensor')), may hold values from -6 to 6
- first_gain: bfloat16 [2048], P('dp'), may hold values from 0.5 to 1.5
- mixer_in: bfloat16 [2048, 2, 3072], P('dp', None, 'tensor'), may hold values from -0.125 to 0.125
- state_weight: bfloat16 [2048, 512], P('dp'), may hold values from -0.125 to 0.125
- step_weight: bfloat16 [2048, 24], P('dp', 'tensor'), may hold values from -0.125 to 0.125
- filter_taps: bfloat16 [5, 24, 128], P(None, 'tensor', 'dp'), may hold values from -3 to 3
- state_taps: bfloat16 [5, 512], P(None, 'dp'), may hold values from -3 to 3
- decay_log: float32 [24], P('tensor'), may hold values from -2 to 1.5
- step_bias: float32 [24], P('tensor'), may hold values from -6 to -2
- skip_gain: float32 [24], P('tensor'), may hold values from 0.5 to 1.5
- gate_gain: bfloat16 [24, 128], P('tensor', 'dp'), may hold values from 0.5 to 1.5
- mixer_out: bfloat16 [3072, 2048], P('tensor', 'dp'), may hold values from -0.109375 to 0.109375
- query_weight: bfloat16 [2048, 1024], P('dp', 'tensor'), may hold values from -1 to 1
- key_value_matrix: bfloat16 [2048, 2, 256], P('dp', None, 'tensor'), may hold values from -1 to 1
- attend_out: bfloat16 [1024, 2048], P('tensor', 'dp'), may hold values from -1.5 to 1.5
- second_gain: bfloat16 [2048], P('dp'), may hold values from 0.5 to 1.5
- gate_up: bfloat16 [2048, 2, 4096], P('dp', None, 'tensor'), may hold values from -0.125 to 0.125
- down_weight: bfloat16 [4096, 2048], P('tensor', 'dp'), may hold values from -0.09375 to 0.09375
Outputs:
- output: bfloat16 [4096, 2048], P(('dp', 'tensor'))
- tokens_grad: float32 [4096, 2048], P(('dp', 'tensor'))
- first_gain_grad: float32 [2048], P('dp')
- mixer_in_grad: float32 [2048, 2, 3072], P('dp', None, 'tensor')
- state_weight_grad: float32 [2048, 512], P('dp')
- step_weight_grad: float32 [2048, 24], P('dp', 'tensor')
- filter_taps_grad: float32 [5, 24, 128], P(None, 'tensor', 'dp')
- state_taps_grad: float32 [5, 512], P(None, 'dp')
- decay_log_grad: float32 [24], P('tensor')
- step_bias_grad: float32 [24], P('tensor')
- skip_gain_grad: float32 [24], P('tensor')
- gate_gain_grad: float32 [24, 128], P('tensor', 'dp')
- mixer_out_grad: float32 [3072, 2048], P('tensor', 'dp')
- query_weight_grad: float32 [2048, 1024], P('dp', 'tensor')
- keys_values_grad: float32 [2048, 2, 256], P('dp', None, 'tensor')
- attend_out_grad: float32 [1024, 2048], P('tensor', 'dp')
- second_gain_grad: float32 [2048], P('dp')
- gate_up_grad: float32 [2048, 2, 4096], P('dp', None, 'tensor')
- down_weight_grad: float32 [4096, 2048], P('tensor', 'dp')
Inputs may be any that keep to these rules, and one draw needn't show every extreme that they name: `segments`: in each group of 256 slots the live slots come first and hold one whole sequence numbered 0, then -1 in the empty slots; every group has at least 64 live slots, and in every draw some group is one sequence of 256 tokens.
All inputs are finite; a program needn't handle non-finite values.
Results may differ from a plain program's by a relative error of at most 0.015.
Values may be sent and summed in bfloat16 or wider, within the bound.
No kernel may reach another device: no remote copies, remote signals or barrier semaphores. Data moves between devices by JAX's collectives and lax.ppermute only.
A program may use at most 256 MiB of HBM per device.

v0:
```python
import jax
import jax.numpy as jnp
from jax import lax
from jax.sharding import PartitionSpec as P

MODEL_WIDTH = 2048
HM = 24
HEAD_DIMENSION = 128
NS = 256
CONV = 4


EPS = 1e-05
ROPE_BASE = 100000000000.0
HIGH = lax.Precision.HIGHEST


def matmul(left, right):
    return jnp.dot(left, right, preferred_element_type=jnp.float32)


def contract(form, left, right):
    return jnp.einsum(form, left, right, preferred_element_type=jnp.float32)


def norm_rows(values, gain):
    scale = lax.rsqrt(jnp.mean(values * values, axis=-1, keepdims=True) + EPS)
    return (values * scale * gain, scale)


def norm_rows_back(values, gain, scale, grad):
    normal = values * scale
    weighted = grad * gain
    back = scale * (weighted - normal * jnp.mean(weighted * normal, axis=-1, keepdims=True))
    return (back, jnp.sum(grad * normal, axis=0))


def silu_slope(values):
    sigma = jax.nn.sigmoid(values)
    return sigma * (1.0 + values * (1.0 - sigma))


def shift_down(values, offset):
    return jnp.concatenate(
        [jnp.zeros((offset,) + values.shape[1:], values.dtype), values[:-offset]], axis=0
    )


def shift_up(values, offset):
    return jnp.concatenate(
        [values[offset:], jnp.zeros((offset,) + values.shape[1:], values.dtype)], axis=0
    )


def tap_masks(segments, count):
    masks = [jnp.ones(segments.shape, jnp.float32)]
    for offset in range(1, count):
        earlier = jnp.concatenate([jnp.full((offset,), -2, jnp.int32), segments[:-offset]])
        masks.append((earlier == segments).astype(jnp.float32))
    return jnp.stack(masks)


def causal_filter(values, weights, masks):
    total = weights[-1] + weights[0] * values
    for offset in range(1, weights.shape[0] - 1):
        total = total + weights[offset] * shift_down(values, offset) * masks[offset][:, None]
    return total


def filter_back(values, weights, masks, grad):
    tap_grads = [jnp.sum(grad * values, axis=0)]
    back = weights[0] * grad
    for offset in range(1, weights.shape[0] - 1):
        masked = grad * masks[offset][:, None]
        tap_grads.append(jnp.sum(masked * shift_down(values, offset), axis=0))
        back = back + weights[offset] * shift_up(masked, offset)
    tap_grads.append(jnp.sum(grad, axis=0))
    return (back, jnp.stack(tap_grads))


def rotary_tables(position, head_size):
    half = head_size // 2
    frequency = ROPE_BASE ** (-2.0 * jnp.arange(half).astype(jnp.float32) / head_size)
    angle = position[:, None] * frequency[None, :]
    return (jnp.cos(angle)[:, None, :], jnp.sin(angle)[:, None, :])


def rotate_halves(values, cosine_table, sine_table):
    half = values.shape[-1] // 2
    first = values[..., :half]
    second = values[..., half:]
    return jnp.concatenate(
        [first * cosine_table - second * sine_table, second * cosine_table + first * sine_table],
        axis=-1,
    )


def send_feed(gate_up_grad, down_weight_grad):
    return (
        lax.psum_scatter(gate_up_grad, "dp", scatter_dimension=0, tiled=True),
        lax.psum_scatter(down_weight_grad, "dp", scatter_dimension=1, tiled=True),
    )


def on_device(
    tokens,
    segments,
    cotangent,
    first_gain,
    mixer_in,
    state_weight,
    step_weight,
    filter_taps,
    state_taps,
    decay_log,
    step_bias,
    skip_gain,
    gate_gain,
    mixer_out,
    query_weight,
    key_value_matrix,
    attend_out,
    second_gain,
    gate_up,
    down_weight,
):
    whole = (
        lax.all_gather(first_gain, "dp", axis=0, tiled=True),
        lax.all_gather(mixer_in, "dp", axis=0, tiled=True),
        lax.all_gather(state_weight, "dp", axis=0, tiled=True),
        lax.all_gather(step_weight, "dp", axis=0, tiled=True),
        lax.all_gather(filter_taps, "dp", axis=2, tiled=True),
        lax.all_gather(state_taps, "dp", axis=1, tiled=True),
        lax.all_gather(gate_gain, "dp", axis=1, tiled=True),
        lax.all_gather(mixer_out, "dp", axis=1, tiled=True),
        lax.all_gather(query_weight, "dp", axis=0, tiled=True),
        lax.all_gather(key_value_matrix, "dp", axis=0, tiled=True),
        lax.all_gather(attend_out, "dp", axis=1, tiled=True),
        lax.all_gather(second_gain, "dp", axis=0, tiled=True),
        lax.all_gather(gate_up, "dp", axis=0, tiled=True),
        lax.all_gather(down_weight, "dp", axis=1, tiled=True),
    )
    (
        first_full,
        mixer_full,
        state_full,
        step_full,
        taps_full,
        state_taps_full,
        gate_full,
        mixer_out_full,
        query_full,
        keys_full,
        attend_full,
        second_full,
        gate_up_full,
        down_full,
    ) = whole
    local_rows = tokens.shape[0]
    count_of_rows = segments.shape[0]
    part = lax.axis_index("tensor")
    heads = decay_log.shape[0]
    channels = heads * HEAD_DIMENSION
    query_heads = query_full.shape[1] // HEAD_DIMENSION
    value_heads = keys_full.shape[2] // HEAD_DIMENSION
    head_group = query_heads // value_heads
    ffn_width = gate_up_full.shape[2]
    scale = HEAD_DIMENSION ** (-0.5)
    order = jnp.arange(count_of_rows)
    live_all = (segments >= 0).astype(jnp.float32)[:, None]
    live_mine = lax.dynamic_slice_in_dim(live_all, part * local_rows, local_rows)
    causal = (segments[:, None] == segments[None, :]) & (order[None, :] <= order[:, None])
    position = jnp.sum(causal.astype(jnp.float32), axis=1) - 1.0
    masks = tap_masks(segments, CONV)
    cosine_table, sine_table = rotary_tables(position, HEAD_DIMENSION)
    resid = tokens.astype(jnp.float32)
    normed_input, scale_one = norm_rows(resid, first_full.astype(jnp.float32))
    normed_low = normed_input.astype(jnp.bfloat16)
    normed_all = lax.all_gather(normed_low, "tensor", axis=0, tiled=True)
    mix_proj = matmul(normed_all, mixer_full.reshape(MODEL_WIDTH, 2 * channels))
    gate_value = mix_proj[:, :channels]
    filter_input = mix_proj[:, channels:]
    state_raw = matmul(normed_all, state_full)
    step_raw = matmul(normed_all, step_full)
    taps_local = taps_full.reshape(CONV + 1, channels).astype(jnp.float32)
    state_taps_local = state_taps_full.astype(jnp.float32)
    filter_pre = causal_filter(filter_input, taps_local, masks)
    filtered = jax.nn.silu(filter_pre)
    state_pre = causal_filter(state_raw, state_taps_local, masks)
    state_act = jax.nn.silu(state_pre)
    state_write = state_act[:, :NS].astype(jnp.bfloat16)
    state_read = state_act[:, NS:].astype(jnp.bfloat16)
    step = jax.nn.softplus(step_raw + step_bias)
    decay_rate = -jnp.exp(decay_log)
    rate = decay_rate * step
    level = jnp.cumsum(rate, axis=0)
    affinity = contract("tn,sn->ts", state_read, state_write)
    spread = level.T[:, :, None] - level.T[:, None, :]
    decay = jnp.where(causal[None], jnp.exp(jnp.where(causal[None], spread, 0.0)), 0.0)
    mixing_full = affinity[None] * decay
    mixing = mixing_full.astype(jnp.bfloat16)
    filtered_heads = filtered.reshape(count_of_rows, heads, HEAD_DIMENSION)
    inner = (filtered_heads * step[:, :, None]).astype(jnp.bfloat16)
    scanned = contract("hts,shd->thd", mixing, inner)
    state_mix = (scanned + skip_gain[None, :, None] * filtered_heads).reshape(
        count_of_rows, channels
    )
    gate_act = jax.nn.silu(gate_value)
    gated = state_mix * gate_act
    squares = lax.psum(jnp.sum(gated * gated, axis=-1), "tensor")
    gate_scale = lax.rsqrt(squares / (HM * HEAD_DIMENSION) + EPS)[:, None]
    gate_normal = gated * gate_scale
    gate_gain_local = gate_full.reshape(channels).astype(jnp.float32)
    state_norm = (gate_normal * gate_gain_local).astype(jnp.bfloat16)
    query_unrotated = matmul(normed_all, query_full).reshape(
        count_of_rows, query_heads, HEAD_DIMENSION
    )
    key_unrotated = matmul(
        normed_all, keys_full.reshape(MODEL_WIDTH, 2 * value_heads * HEAD_DIMENSION)
    ).reshape(count_of_rows, 2, value_heads, HEAD_DIMENSION)
    query_rows = (
        rotate_halves(query_unrotated, cosine_table, sine_table)
        .astype(jnp.bfloat16)
        .reshape(count_of_rows, value_heads, head_group, HEAD_DIMENSION)
    )
    key_rows = rotate_halves(key_unrotated[:, 0], cosine_table, sine_table).astype(jnp.bfloat16)
    values = key_unrotated[:, 1].astype(jnp.bfloat16)
    scores = jnp.where(causal, contract("tkgd,skd->kgts", query_rows, key_rows) * scale, -1e30)
    top = jnp.max(scores, axis=-1, keepdims=True)
    raised = jnp.exp(scores - top)
    total = jnp.sum(raised, axis=-1, keepdims=True)
    log_total = top + jnp.log(total)
    shares_low = (raised / total).astype(jnp.bfloat16)
    attended = contract("kgts,skd->tkgd", shares_low, values).astype(jnp.bfloat16)
    attended = attended.reshape(count_of_rows, query_heads * HEAD_DIMENSION)
    rows_live = live_all
    mixed = lax.psum_scatter(
        rows_live * (matmul(state_norm, mixer_out_full) + matmul(attended, attend_full)),
        "tensor",
        scatter_dimension=0,
        tiled=True,
    )
    hidden = resid + mixed
    second, scale_two = norm_rows(hidden, second_full.astype(jnp.float32))
    second_low = second.astype(jnp.bfloat16)
    second_all = lax.all_gather(second_low, "tensor", axis=0, tiled=True)
    gate_up_out = matmul(second_all, gate_up_full.reshape(MODEL_WIDTH, 2 * ffn_width)).reshape(
        count_of_rows, 2, ffn_width
    )
    gate_part = gate_up_out[:, 0]
    up_part = gate_up_out[:, 1]
    activation = (jax.nn.silu(gate_part) * up_part).astype(jnp.bfloat16)
    rows_live = live_all
    feed_out = lax.psum_scatter(
        (rows_live * matmul(activation, down_full)).astype(jnp.bfloat16),
        "tensor",
        scatter_dimension=0,
        tiled=True,
    ).astype(jnp.float32)
    output = (hidden + feed_out).astype(jnp.bfloat16)
    grad_out = cotangent.astype(jnp.float32)
    feed_grad = (live_mine * grad_out).astype(jnp.bfloat16)
    feed_grad_all = lax.all_gather(feed_grad, "tensor", axis=0, tiled=True)
    down_weight_grad = contract("tf,td->fd", activation, feed_grad_all)
    act_grad = contract("td,fd->tf", feed_grad_all, down_full)
    gate_grad = act_grad * up_part * silu_slope(gate_part)
    up_grad = act_grad * jax.nn.silu(gate_part)
    gate_up_low = jnp.stack([gate_grad, up_grad], axis=1).astype(jnp.bfloat16)
    gate_up_grad = contract("tc,tkf->ckf", second_all, gate_up_low)
    gate_up_flat = gate_up_low.reshape(count_of_rows, 2 * ffn_width)
    gate_up_matrix = gate_up_full.reshape(MODEL_WIDTH, 2 * ffn_width)
    second_grad = lax.psum_scatter(
        contract("tk,ck->tc", gate_up_flat, gate_up_matrix),
        "tensor",
        scatter_dimension=0,
        tiled=True,
    )
    hidden_part, second_gain_grad = norm_rows_back(
        hidden, second_full.astype(jnp.float32), scale_two, second_grad
    )
    hidden_grad = grad_out + hidden_part
    mix_grad = (live_mine * hidden_grad).astype(jnp.bfloat16)
    mix_grad_all = lax.all_gather(mix_grad, "tensor", axis=0, tiled=True)
    mixer_out_grad = contract("tc,td->cd", state_norm, mix_grad_all)
    attend_out_grad = contract("tc,td->cd", attended, mix_grad_all)
    norm_grad = contract("td,cd->tc", mix_grad_all, mixer_out_full)
    attend_grad = contract("td,cd->tc", mix_grad_all, attend_full).astype(jnp.bfloat16)
    weighted = norm_grad * gate_gain_local
    inner_sum = lax.psum(jnp.sum(weighted * gate_normal, axis=-1), "tensor")
    gated_grad = gate_scale * (
        weighted - gate_normal * (inner_sum / (HM * HEAD_DIMENSION))[:, None]
    )
    gate_gain_grad = jnp.sum(norm_grad * gate_normal, axis=0).reshape(heads, HEAD_DIMENSION)
    mix_state_grad = gated_grad * gate_act
    gate_value_grad = gated_grad * state_mix * silu_slope(gate_value)
    mix_heads_grad = mix_state_grad.reshape(count_of_rows, heads, HEAD_DIMENSION)
    skip_gain_grad = jnp.sum(mix_heads_grad * filtered_heads, axis=(0, 2))
    scanned_low = mix_heads_grad.astype(jnp.bfloat16)
    mixing_grad = contract("thd,shd->hts", scanned_low, inner)
    inner_grad = contract("hts,thd->shd", mixing, scanned_low)
    flow = mixing_grad * mixing_full
    level_grad = (jnp.sum(flow, axis=2) - jnp.sum(flow, axis=1)).T
    rate_grad = jnp.cumsum(level_grad[::-1], axis=0)[::-1]
    decay_log_grad = jnp.sum(rate_grad * rate, axis=0)
    step_grad = rate_grad * decay_rate + jnp.sum(inner_grad * filtered_heads, axis=2)
    filtered_grad = (
        skip_gain[None, :, None] * mix_heads_grad + inner_grad * step[:, :, None]
    ).reshape(count_of_rows, channels)
    affinity_grad = jnp.sum(mixing_grad * decay, axis=0)
    read_grad = jnp.einsum(
        "ts,sn->tn", affinity_grad, state_write.astype(jnp.float32), precision=HIGH
    )
    write_grad = jnp.einsum(
        "ts,tn->sn", affinity_grad, state_read.astype(jnp.float32), precision=HIGH
    )
    state_act_grad = jnp.concatenate([write_grad, read_grad], axis=1) * silu_slope(state_pre)
    state_raw_grad, state_taps_grad = filter_back(
        state_raw, state_taps_local, masks, state_act_grad
    )
    step_pre_grad = step_grad * jax.nn.sigmoid(step_raw + step_bias)
    step_bias_grad = jnp.sum(step_pre_grad, axis=0)
    step_low = step_pre_grad.astype(jnp.bfloat16)
    filter_input_grad, filter_taps_grad = filter_back(
        filter_input, taps_local, masks, filtered_grad * silu_slope(filter_pre)
    )
    mix_proj_low = jnp.concatenate([gate_value_grad, filter_input_grad], axis=1).astype(
        jnp.bfloat16
    )
    scores = jnp.where(causal, contract("tkgd,skd->kgts", query_rows, key_rows) * scale, -1e30)
    shares = jnp.exp(scores - log_total)
    shares_low = shares.astype(jnp.bfloat16)
    attend_heads = attend_grad.reshape(count_of_rows, value_heads, head_group, HEAD_DIMENSION)
    values_grad = contract("kgts,tkgd->skd", shares_low, attend_heads)
    shares_grad = contract("tkgd,skd->kgts", attend_heads, values)
    scores_low = (
        shares * (shares_grad - jnp.sum(shares_grad * shares, axis=-1, keepdims=True))
    ).astype(jnp.bfloat16)
    query_grad = contract("kgts,skd->tkgd", scores_low, key_rows) * scale
    keys_grad = contract("kgts,tkgd->skd", scores_low, query_rows) * scale
    query_low = rotate_halves(
        query_grad.reshape(count_of_rows, query_heads, HEAD_DIMENSION), cosine_table, -sine_table
    ).astype(jnp.bfloat16)
    query_low = query_low.reshape(count_of_rows, query_heads * HEAD_DIMENSION)
    keys_low = jnp.stack(
        [rotate_halves(keys_grad, cosine_table, -sine_table), values_grad], axis=1
    ).astype(jnp.bfloat16)
    keys_low = keys_low.reshape(count_of_rows, 2 * value_heads * HEAD_DIMENSION)
    mixer_in_grad = contract("tc,tk->ck", normed_all, mix_proj_low).reshape(
        MODEL_WIDTH, 2, channels
    )
    step_weight_grad = contract("tc,th->ch", normed_all, step_low)
    query_weight_grad = contract("tc,tk->ck", normed_all, query_low)
    keys_values_grad = contract("tc,tk->ck", normed_all, keys_low).reshape(
        MODEL_WIDTH, 2, value_heads * HEAD_DIMENSION
    )
    mixer_matrix = mixer_full.reshape(MODEL_WIDTH, 2 * channels)
    keys_matrix = keys_full.reshape(MODEL_WIDTH, 2 * value_heads * HEAD_DIMENSION)
    partial_sum = contract("tk,ck->tc", mix_proj_low, mixer_matrix)
    partial_sum = partial_sum + contract("tk,ck->tc", step_low, step_full)
    partial_sum = partial_sum + contract("tk,ck->tc", query_low, query_full)
    partial_sum = partial_sum + contract("tk,ck->tc", keys_low, keys_matrix)
    summed = lax.psum_scatter(
        jnp.concatenate([partial_sum, state_raw_grad], axis=1).astype(jnp.bfloat16),
        "tensor",
        scatter_dimension=0,
        tiled=True,
    ).astype(jnp.float32)
    state_low = summed[:, MODEL_WIDTH:].astype(jnp.bfloat16)
    normed_grad = summed[:, :MODEL_WIDTH] + contract("tn,cn->tc", state_low, state_full)
    resid_part, first_gain_grad = norm_rows_back(
        resid, first_full.astype(jnp.float32), scale_one, normed_grad
    )
    tokens_grad = hidden_grad + resid_part
    state_weight_grad = contract("tc,tn->cn", normed_low, state_low)
    head_grads = jnp.stack([decay_log_grad, step_bias_grad, skip_gain_grad])
    head_full = lax.dynamic_update_slice_in_dim(
        jnp.zeros((3, HM), jnp.float32), head_grads, part * heads, 1
    )
    shared = lax.psum(
        (first_gain_grad, second_gain_grad, state_weight_grad, state_taps_grad, head_full),
        ("dp", "tensor"),
    )
    dp_size = lax.axis_size("dp")
    dp_index = lax.axis_index("dp")
    width_shard = MODEL_WIDTH // dp_size
    state_shard = 2 * NS // dp_size
    first_mine = lax.dynamic_slice_in_dim(shared[0], dp_index * width_shard, width_shard)
    second_mine = lax.dynamic_slice_in_dim(shared[1], dp_index * width_shard, width_shard)
    state_weight_mine = lax.dynamic_slice_in_dim(shared[2], dp_index * width_shard, width_shard)
    state_taps_mine = lax.dynamic_slice_in_dim(shared[3], dp_index * state_shard, state_shard, 1)
    head_mine = lax.dynamic_slice_in_dim(shared[4], part * heads, heads, 1)
    feed_done = send_feed(gate_up_grad, down_weight_grad)
    scattered = (
        lax.psum_scatter(mixer_in_grad, "dp", scatter_dimension=0, tiled=True),
        lax.psum_scatter(step_weight_grad, "dp", scatter_dimension=0, tiled=True),
        lax.psum_scatter(
            filter_taps_grad.reshape(CONV + 1, heads, HEAD_DIMENSION),
            "dp",
            scatter_dimension=2,
            tiled=True,
        ),
        lax.psum_scatter(gate_gain_grad, "dp", scatter_dimension=1, tiled=True),
        lax.psum_scatter(mixer_out_grad, "dp", scatter_dimension=1, tiled=True),
        lax.psum_scatter(query_weight_grad, "dp", scatter_dimension=0, tiled=True),
        lax.psum_scatter(keys_values_grad, "dp", scatter_dimension=0, tiled=True),
        lax.psum_scatter(attend_out_grad, "dp", scatter_dimension=1, tiled=True),
    )
    return (
        output,
        tokens_grad,
        first_mine,
        scattered[0],
        state_weight_mine,
        scattered[1],
        scattered[2],
        state_taps_mine,
        head_mine[0],
        head_mine[1],
        head_mine[2],
        scattered[3],
        scattered[4],
        scattered[5],
        scattered[6],
        scattered[7],
        second_mine,
        feed_done[0],
        feed_done[1],
    )


def solution(mesh):
    placed = (
        P(("dp", "tensor"), None),
        P("dp"),
        P(("dp", "tensor"), None),
        P("dp"),
        P("dp", None, "tensor"),
        P("dp", None),
        P("dp", "tensor"),
        P(None, "tensor", "dp"),
        P(None, "dp"),
        P("tensor"),
        P("tensor"),
        P("tensor"),
        P("tensor", "dp"),
        P("tensor", "dp"),
        P("dp", "tensor"),
        P("dp", None, "tensor"),
        P("tensor", "dp"),
        P("dp"),
        P("dp", None, "tensor"),
        P("tensor", "dp"),
    )
    return jax.shard_map(
        on_device,
        mesh=mesh,
        in_specs=placed,
        out_specs=(
            P(("dp", "tensor"), None),
            P(("dp", "tensor"), None),
            P("dp"),
            P("dp", None, "tensor"),
            P("dp", None),
            P("dp", "tensor"),
            P(None, "tensor", "dp"),
            P(None, "dp"),
            P("tensor"),
            P("tensor"),
            P("tensor"),
            P("tensor", "dp"),
            P("tensor", "dp"),
            P("dp", "tensor"),
            P("dp", None, "tensor"),
            P("tensor", "dp"),
            P("dp"),
            P("dp", None, "tensor"),
            P("tensor", "dp"),
        ),
        check_vma=False,
    )
```

profile of v0, /device:TPU:17, one launch (start us, length us, event | category | flops | bytes accessed | tf_op | source)
XLA Modules:
  0.0 2469.1 jit_solution(1119581908046733454)
XLA Ops:
  8.5 16.5 all-gather
  31.5 17.5 all-gather.1
  49.7 19.9 all_gather.58
  70.4 18.1 all_gather.54
  89.3 18.7 all_gather.61
  118.8 13.6 all-gather.26.cloned.1.call-done
  135.5 39.2 %all-gather.20.cloned.1.call-done = bf16[2048,512]{1,0:T(8,128)(2,1)} async-done(((bf16[128,512]{1,0:T(8,128)(2,1)}), bf16[2048,512]{1,0:T(8,128)(2,1)}) %all-gather.20.cloned.1.call-update) | async-done | bytes 2097168 | tf_op jit(solution)/shard_map/all_gather | solution.py:130
  180.0 97.1 %all-gather.18.cloned.1.call-done = bf16[2048,2,1536]{2,1,0:T(2,128)(2,1)} async-done(((bf16[128,2,1536]{2,1,0:T(2,128)(2,1)}), bf16[2048,2,1536]{2,1,0:T(2,128)(2,1)}) %all-gather.18.cloned.1.call-update) | async-done | bytes 12582928 | tf_op jit(solution)/shard_map/all_gather | solution.py:129
  277.1 8.8 copy.253
  285.9 4.6 copy-done.11
  290.5 3.5 fusion.119
  296.7 3.0 fusion.15
  299.7 3.2 copy.191
  302.9 4.0 bitcast_add_fusion
  306.9 3.0 copy.196
  309.9 3.8 multiply_reduce_fusion.8
  313.7 4.6 psum.49
  318.3 24.7 %all-gather.22.cloned.1.call-done = bf16[1536,2048]{1,0:T(8,128)(2,1)} async-done(((bf16[1536,128]{1,0:T(8,128)(2,1)}), bf16[1536,2048]{1,0:T(8,128)(2,1)}) %all-gather.22.cloned.1.call-update) | async-done | bytes 6291472 | tf_op jit(solution)/shard_map/all_gather | solution.py:135
  343.0 6.4 fusion.110
  349.5 34.9 %all-gather.28.cloned.1.call-done = bf16[512,2048]{1,0:T(8,128)(2,1)} async-done(((bf16[512,128]{1,0:T(8,128)(2,1)}), bf16[512,2048]{1,0:T(8,128)(2,1)}) %all-gather.28.cloned.1.call-update) | async-done | bytes 2097168 | tf_op jit(solution)/shard_map/all_gather | solution.py:138
  384.4 4.3 fusion.6
  391.3 15.6 all-gather.2
  406.9 13.4 reduce-scatter.14.cloned.1.call-done
  426.1 123.6 %all-gather.32.cloned.1.call-done = bf16[2048,2,2048]{2,0,1:T(8,128)(2,1)} async-done(((bf16[128,2,2048]{2,0,1:T(8,128)(2,1)}), bf16[2048,2,2048]{2,0,1:T(8,128)(2,1)}) %all-gather.32.cloned.1.call-update) | async-done | bytes 16777232 | tf_op jit(solution)/shard_map/all_gather | solution.py:140
  549.8 22.6 copy.204
  572.3 12.6 fusion
  584.9 10.4 all-gather.36.cloned.1.call-done
  595.3 79.9 %all-gather.34.cloned.1.call-done = bf16[2048,2048]{1,0:T(8,128)(2,1)} async-done(((bf16[2048,128]{1,0:T(8,128)(2,1)}), bf16[2048,2048]{1,0:T(8,128)(2,1)}) %all-gather.34.cloned.1.call-update) | async-done | bytes 8388624 | tf_op jit(solution)/shard_map/all_gather | solution.py:141
  675.2 9.6 fusion.43
  684.8 12.3 convolution_bitcast_fusion
  697.3 30.4 %reduce-scatter.18.cloned.1.call-done = f32[128,2048]{1,0:T(8,128)} async-done(((f32[256,2048]{1,0:T(8,128)}), f32[128,2048]{1,0:T(8,128)}) %reduce-scatter.18.cloned.1.call-update) | async-done | bytes 1048592 | tf_op jit(solution)/shard_map/reduce_scatter | solution.py:272
  733.0 20.1 all-gather.38.cloned.1.call-done
  753.1 7.3 multiply_reduce_fusion.1
  760.4 4.5 psum.50
  765.5 6.7 multiply_reduce_fusion.2
  772.3 3.1 copy.206
  775.4 4.5 fusion.10
  787.7 5.0 fusion.13
  802.0 3.1 copy.207
  805.1 3.9 multiply_reduce_fusion.3
  820.1 3.7 add_convert_fusion
  823.8 6.8 fusion.45
  837.5 7.0 fusion.7
  846.5 14.2 reduce-scatter.20.cloned.1.call-done
  860.7 3.6 fusion.60
  864.4 11.7 fusion.44
  876.1 32.3 %reshape.555 = f32[2048,2,1536]{2,1,0:T(2,128)} reshape(f32[2048,3072]{1,0:T(8,128)} %fusion.44) | data formatting | bytes 50331648 | tf_op jit(solution)/shard_map/reshape | solution.py:348
  908.7 17.5 fusion.24
  927.2 2.8 fusion.122
  934.7 7.9 fusion.109
  943.8 9.5 fusion.124
  955.9 22.9 all-reduce.15
  981.4 3.7 fusion.35
  985.0 49.4 %all-reduce.16 = (f32[2048]{0:T(1024)S(1)}, f32[5,512]{1,0:T(8,128)S(1)}, f32[3,24]{1,0:T(4,128)S(1)}, f32[2048]{0:T(1024)S(1)}) all-reduce(f32[2048]{0:T(1024)S(1)} %get-tuple-element.121, f32[5,512]{1,0:T(8,128)S(1)} %stack.86, f32[3,24]{1,0:T(4,128)S(1)} %dynamic_update_slice.3, ...), channel_id=1, replica_groups=mesh['dp'=16,'tensor'=2] {'dp','tensor'}, use_global_device_ids=true, to_apply=%region_25.26 | all-reduce | flops 6728 | bytes 53824 | tf_op jit(solution)/shard_map/psum | solution.py:379
  1036.9 3.0 fusion.34
  1041.5 110.6 %all-reduce.20.cloned.1.call-done = f32[2048,512]{1,0:T(8,128)} async-done(((f32[2048,512]{1,0:T(8,128)}), f32[2048,512]{1,0:T(8,128)}) %all-reduce.20.cloned.1.call-update) | async-done | bytes 4194320 | tf_op jit(solution)/shard_map/psum | solution.py:379
  1153.8 443.1 %all-reduce.22.cloned.1.call-done = f32[2048,2,1536]{2,1,0:T(2,128)} async-done(((f32[2048,2,1536]{2,1,0:T(2,128)}), f32[2048,2,1536]{2,1,0:T(2,128)}) %all-reduce.22.cloned.1.call-update) | async-done | bytes 25165840
  1599.5 333.3 %reduce-scatter.34.cloned.1.call-done = f32[128,2,2048]{2,0,1:T(8,128)} async-done(((f32[2048,2,2048]{2,0,1:T(8,128)}), f32[128,2,2048]{2,0,1:T(8,128)}) %reduce-scatter.34.cloned.1.call-update) | async-done | bytes 2097168 | tf_op jit(solution)/shard_map/reduce_scatter | solution.py:100
  1932.8 4.5 copy.229
  1937.3 48.7 %reduce-scatter.22.cloned.1.call-done = f32[128,12]{0,1:T(8,128)} async-done(((f32[2048,12]{0,1:T(8,128)}), f32[128,12]{0,1:T(8,128)}) %reduce-scatter.22.cloned.1.call-update) | async-done | bytes 6160 | tf_op jit(solution)/shard_map/reduce_scatter | solution.py:395
  1986.0 77.2 %reduce-scatter.28.cloned.1.call-done = f32[128,512]{1,0:T(8,128)} async-done(((f32[2048,512]{1,0:T(8,128)}), f32[128,512]{1,0:T(8,128)}) %reduce-scatter.28.cloned.1.call-update) | async-done | bytes 262160 | tf_op jit(solution)/shard_map/reduce_scatter | solution.py:404
  2063.2 75.8 %reduce-scatter.32.cloned.1.call-done = f32[512,128]{1,0:T(8,128)} async-done(((f32[512,2048]{1,0:T(8,128)}), f32[512,128]{1,0:T(8,128)}) %reduce-scatter.32.cloned.1.call-update) | async-done | bytes 262160 | tf_op jit(solution)/shard_map/reduce_scatter | solution.py:406
  2139.0 140.8 %reduce-scatter.26.cloned.1.call-done = f32[1536,128]{1,0:T(8,128)} async-done(((f32[1536,2048]{1,0:T(8,128)}), f32[1536,128]{1,0:T(8,128)}) %reduce-scatter.26.cloned.1.call-update) | async-done | bytes 786448 | tf_op jit(solution)/shard_map/reduce_scatter | solution.py:403
  2279.8 182.6 %reduce-scatter.36.cloned.1.call-done = f32[2048,128]{1,0:T(8,128)} async-done(((f32[2048,2048]{1,0:T(8,128)}), f32[2048,128]{1,0:T(8,128)}) %reduce-scatter.36.cloned.1.call-update) | async-done | bytes 1048592 | tf_op jit(solution)/shard_map/reduce_scatter | solution.py:101
  (486 shorter events, 101.0 us)
Async XLA Ops:
  7.2 102.8 %all-gather.16.cloned.1.call-start = ((), (), s32[]{:S(2)}) async-start(), calls=%async_computation.12 | async-start | bytes 1572864 | tf_op jit(solution)/shard_map/all_gather | solution.py:179
  8.5 22.6 copy-start.132
  25.0 24.7 copy-start.131
  25.0 44.6 %copy-start.144 = (f32[12]{0:T(128)S(1)}, f32[12]{0:T(128)}, u32[]{:S(2)}) copy-start(f32[12]{0:T(128)} %param.29) | copy-start | bytes 148
  27.1 43.3 %copy-start.117 = (bf16[5,12,8]{1,2,0:T(8,128)(2,1)S(1)}, bf16[5,12,8]{1,2,0:T(8,128)(2,1)}, u32[]{:S(2)}) copy-start(bf16[5,12,8]{1,2,0:T(8,128)(2,1)} %param.27) | copy-start | bytes 2884
  27.1 62.2 %copy-start.141 = (bf16[12,8]{0,1:T(8,128)(2,1)S(1)}, bf16[12,8]{0,1:T(8,128)(2,1)}, u32[]{:S(2)}) copy-start(bf16[12,8]{0,1:T(8,128)(2,1)} %param.32) | copy-start | bytes 580
  27.1 82.9 %copy-start.142 = (f32[12]{0:T(128)S(1)}, f32[12]{0:T(128)}, u32[]{:S(2)}) copy-start(f32[12]{0:T(128)} %param.30) | copy-start | bytes 148
  27.1 86.9 %all-gather.24.cloned.1.call-start = ((), (), s32[]{:S(2)}) async-start(), calls=%async_computation.16 | async-start | bytes 1114112 | tf_op jit(solution)/shard_map/all_gather | solution.py:137
  27.9 104.5 %all-gather.26.cloned.1.call-start = ((), (), s32[]{:S(2)}) async-start(), calls=%async_computation.17 | async-start | bytes 2228224 | tf_op jit(solution)/shard_map/all_gather | solution.py:136
  28.6 146.0 %all-gather.20.cloned.1.call-start = ((), (), s32[]{:S(2)}) async-start(), calls=%async_computation.14 | async-start | bytes 2228224 | tf_op jit(solution)/shard_map/all_gather | solution.py:130
  29.2 247.9 %all-gather.18.cloned.1.call-start = ((), (), s32[]{:S(2)}) async-start(), calls=%async_computation.13 | async-start | bytes 13369344 | tf_op jit(solution)/shard_map/all_gather | solution.py:129
  29.8 313.2 %all-gather.22.cloned.1.call-start = ((), (), s32[]{:S(2)}) async-start(), calls=%async_computation.15 | async-start | bytes 6684672 | tf_op jit(solution)/shard_map/all_gather | solution.py:135
  30.4 354.0 %all-gather.28.cloned.1.call-start = ((), (), s32[]{:S(2)}) async-start(), calls=%async_computation.18 | async-start | bytes 2228224 | tf_op jit(solution)/shard_map/all_gather | solution.py:138
  31.1 389.2 %reduce-scatter.14.cloned.1.call-start = ((), (), s32[]{:S(2)}) async-start(), calls=%async_computation.19 | async-start | bytes 3145728 | tf_op jit(solution)/shard_map/reduce_scatter | solution.py:237
  31.2 78.8 %copy-start.128 = (f32[64]{0:T(128)}, f32[64]{0:T(128)S(1)}, u32[]{:S(2)}) copy-start(f32[64]{0:T(128)S(1)} %multiply_power_fusion) | copy-start | bytes 772
  31.3 38.3 %copy-start.52 = (pred[256,256]{0,1:T(8,128)(4,1)}, pred[256,256]{0,1:T(8,128)(4,1)S(1)}, u32[]{:S(2)}) copy-start(pred[256,256]{0,1:T(8,128)(4,1)S(1)} %fusion.57) | copy-start | bytes 196612
  69.6 44.4 %copy-start.46 = (bf16[2048,12]{0,1:T(8,128)(2,1)}, bf16[2048,12]{0,1:T(8,128)(2,1)S(1)}, u32[]{:S(2)}) copy-start(bf16[2048,12]{0,1:T(8,128)(2,1)S(1)} %all_gather.58) | copy-start | bytes 147460
  69.6 42.7 %copy-start.136 = (f32[12]{0:T(128)}, f32[12]{0:T(128)S(1)}, u32[]{:S(2)}) copy-start(f32[12]{0:T(128)S(1)} %exponential_negate_fusion) | copy-start | bytes 148
  89.3 205.3 %copy-start.62 = (f32[1536]{0:T(1024)}, f32[1536]{0:T(1024)S(1)}, u32[]{:S(2)}) copy-start(f32[1536]{0:T(1024)S(1)} %get-tuple-element.184) | copy-start | bytes 18436
  135.4 42.9 %copy-start.27 = (bf16[256,4,64]{2,0,1:T(8,128)(2,1)}, bf16[256,4,64]{2,0,1:T(8,128)(2,1)S(1)}, u32[]{:S(2)}) copy-start(bf16[256,4,64]{2,0,1:T(8,128)(2,1)S(1)} %get-tuple-element.167) | copy-start | bytes 393220
  135.4 42.9 %copy-start.29 = (bf16[256,4,64]{2,0,1:T(8,128)(2,1)}, bf16[256,4,64]{2,0,1:T(8,128)(2,1)S(1)}, u32[]{:S(2)}) copy-start(bf16[256,4,64]{2,0,1:T(8,128)(2,1)S(1)} %get-tuple-element.168) | copy-start | bytes 393220
  135.4 41.6 %copy-start.82 = (f32[256]{0:T(256)S(1)}, f32[256]{0:T(256)}, u32[]{:S(2)}) copy-start(f32[256]{0:T(256)} %get-tuple-element.203) | copy-start | bytes 3076
  135.4 41.6 %copy-start.88 = (f32[256]{0:T(256)S(1)}, f32[256]{0:T(256)}, u32[]{:S(2)}) copy-start(f32[256]{0:T(256)} %get-tuple-element.201) | copy-start | bytes 3076
  135.4 41.6 %copy-start.92 = (f32[256]{0:T(256)S(1)}, f32[256]{0:T(256)}, u32[]{:S(2)}) copy-start(f32[256]{0:T(256)} %get-tuple-element.202) | copy-start | bytes 3076
  135.4 41.6 %copy-start.96 = (f32[1,512]{1,0:T(1,128)S(1)}, f32[1,512]{1,0:T(1,128)}, u32[]{:S(2)}) copy-start(f32[1,512]{1,0:T(1,128)} %get-tuple-element.190) | copy-start | bytes 6148
  135.4 41.6 %copy-start.98 = (f32[1,512]{1,0:T(1,128)S(1)}, f32[1,512]{1,0:T(1,128)}, u32[]{:S(2)}) copy-start(f32[1,512]{1,0:T(1,128)} %get-tuple-element.191) | copy-start | bytes 6148
  135.4 41.6 %copy-start.100 = (f32[1,512]{1,0:T(1,128)S(1)}, f32[1,512]{1,0:T(1,128)}, u32[]{:S(2)}) copy-start(f32[1,512]{1,0:T(1,128)} %get-tuple-element.192) | copy-start | bytes 6148
  135.4 41.6 %copy-start.102 = (f32[1,512]{1,0:T(1,128)S(1)}, f32[1,512]{1,0:T(1,128)}, u32[]{:S(2)}) copy-start(f32[1,512]{1,0:T(1,128)} %get-tuple-element.193) | copy-start | bytes 6148
  135.4 41.6 %copy-start.119 = (f32[1,512]{1,0:T(1,128)S(1)}, f32[1,512]{1,0:T(1,128)}, u32[]{:S(2)}) copy-start(f32[1,512]{1,0:T(1,128)} %get-tuple-element.189) | copy-start | bytes 6148
  179.7 123.2 %copy-start.58 = (f32[256,256]{1,0:T(8,128)}, f32[256,256]{1,0:T(8,128)S(1)}, u32[]{:S(2)}) copy-start(f32[256,256]{1,0:T(8,128)S(1)} %fusion.65) | copy-start | bytes 786436
  180.0 204.3 %copy-start.37 = (bf16[128,4,256]{2,0,1:T(8,128)(2,1)}, bf16[128,4,256]{2,0,1:T(8,128)(2,1)S(1)}, u32[]{:S(2)}) copy-start(bf16[128,4,256]{2,0,1:T(8,128)(2,1)S(1)} %convolution_convert_fusion.1) | copy-start | bytes 786436
  318.3 31.2 %copy-start.115 = (f32[256]{0:T(256)}, f32[256]{0:T(256)S(1)}, u32[]{:S(2)}) copy-start(f32[256]{0:T(256)S(1)} %add_rsqrt_fusion) | copy-start | bytes 3076
  343.0 41.3 %copy-start.86 = (f32[256]{0:T(256)S(1)}, f32[256]{0:T(256)}, u32[]{:S(2)}) copy-start(f32[256]{0:T(256)} %get-tuple-element.200) | copy-start | bytes 3076
  388.7 31.6 %copy-start.14 = (bf16[128,2048]{1,0:T(8,128)(2,1)S(1)}, bf16[128,2048]{1,0:T(8,128)(2,1)}, u32[]{:S(2)}) copy-start(bf16[128,2048]{1,0:T(8,128)(2,1)} %param.20) | copy-start | bytes 1572868
  388.7 161.1 %all-gather.32.cloned.1.call-start = ((), (), s32[]{:S(2)}) async-start(), calls=%async_computation.21 | async-start | bytes 17825792 | tf_op jit(solution)/shard_map/all_gather | solution.py:140
  391.2 181.1 %all-gather.30.cloned.1.call-start = ((), (), s32[]{:S(2)}) async-start(), calls=%async_computation.20 | async-start | bytes 1572864 | tf_op jit(solution)/shard_map/all_gather | solution.py:246
  423.3 172.1 %all-gather.36.cloned.1.call-start = ((), (), s32[]{:S(2)}) async-start(), calls=%async_computation.24 | async-start | bytes 1572864 | tf_op jit(solution)/shard_map/all_gather | solution.py:263
  425.5 249.7 %all-gather.34.cloned.1.call-start = ((), (), s32[]{:S(2)}) async-start(), calls=%async_computation.22 | async-start | bytes 8912896 | tf_op jit(solution)/shard_map/all_gather | solution.py:141
  426.1 301.6 %reduce-scatter.18.cloned.1.call-start = ((), (), s32[]{:S(2)}) async-start(), calls=%async_computation.25 | async-start | bytes 3145728 | tf_op jit(solution)/shard_map/reduce_scatter | solution.py:272
  697.1 56.1 %all-gather.38.cloned.1.call-start = ((), (), s32[]{:S(2)}) async-start(), calls=%async_computation.26 | async-start | bytes 1572864 | tf_op jit(solution)/shard_map/all_gather | solution.py:283
  731.7 129.0 %reduce-scatter.20.cloned.1.call-start = ((), (), s32[]{:S(2)}) async-start(), calls=%async_computation.27 | async-start | bytes 1966080 | tf_op jit(solution)/shard_map/reduce_scatter | solution.py:362
  836.2 143.7 %reduce-scatter.24.cloned.1.call-start = ((), (), s32[]{:S(2)}) async-start(), calls=%async_computation.30 | async-start | bytes 557056 | tf_op jit(solution)/shard_map/reduce_scatter | solution.py:396
  837.4 199.5 %reduce-scatter.16.cloned.1.call-start = ((), (), s32[]{:S(2)}) async-start(), calls=%async_computation.23 | async-start | bytes 1572864 | tf_op jit(solution)/shard_map/reduce_scatter | solution.py:254
  844.5 195.3 %reduce-scatter.30.cloned.1.call-start = ((), (), s32[]{:S(2)}) async-start(), calls=%async_computation.33 | async-start | bytes 2228224 | tf_op jit(solution)/shard_map/reduce_scatter | solution.py:405
  846.5 305.6 %all-reduce.20.cloned.1.call-start = ((), (), s32[]{:S(2)}) async-start(), calls=%async_computation.28 | async-start | bytes 8388608 | tf_op jit(solution)/shard_map/psum | solution.py:379
  864.3 732.5 %all-reduce.22.cloned.1.call-start = ((), (), s32[]{:S(2)}) async-start(), calls=%async_computation.37 | async-start | bytes 50331648
  908.5 1024.3 %reduce-scatter.34.cloned.1.call-start = ((), (), s32[]{:S(2)}) async-start(), calls=%async_computation.35 | async-start | bytes 35651584 | tf_op jit(solution)/shard_map/reduce_scatter | solution.py:100
  926.2 1059.7 %reduce-scatter.22.cloned.1.call-start = ((), (), s32[]{:S(2)}) async-start(), calls=%async_computation.29 | async-start | bytes 139264 | tf_op jit(solution)/shard_map/reduce_scatter | solution.py:395
  927.2 1136.0 %reduce-scatter.28.cloned.1.call-start = ((), (), s32[]{:S(2)}) async-start(), calls=%async_computation.32 | async-start | bytes 4456448 | tf_op jit(solution)/shard_map/reduce_scatter | solution.py:404
  930.1 1208.9 %reduce-scatter.32.cloned.1.call-start = ((), (), s32[]{:S(2)}) async-start(), calls=%async_computation.34 | async-start | bytes 4456448 | tf_op jit(solution)/shard_map/reduce_scatter | solution.py:406
  934.1 1345.7 %reduce-scatter.26.cloned.1.call-start = ((), (), s32[]{:S(2)}) async-start(), calls=%async_computation.31 | async-start | bytes 13369344 | tf_op jit(solution)/shard_map/reduce_scatter | solution.py:403
  942.6 1519.7 %reduce-scatter.36.cloned.1.call-start = ((), (), s32[]{:S(2)}) async-start(), calls=%async_computation.36 | async-start | bytes 17825792 | tf_op jit(solution)/shard_map/reduce_scatter | solution.py:101
  953.3 26.2 %copy-start.77 = (f32[1536]{0:T(1024)S(1)}, f32[1536]{0:T(1024)}, u32[]{:S(2)}) copy-start(f32[1536]{0:T(1024)} %get-tuple-element.140) | copy-start | bytes 18436
  953.3 26.5 %copy-start.120 = (f32[512]{0:T(512)S(1)}, f32[512]{0:T(512)}, u32[]{:S(2)}) copy-start(f32[512]{0:T(512)} %get-tuple-element.142) | copy-start | bytes 6148
  953.3 26.5 %copy-start.121 = (f32[512]{0:T(512)S(1)}, f32[512]{0:T(512)}, u32[]{:S(2)}) copy-start(f32[512]{0:T(512)} %get-tuple-element.125) | copy-start | bytes 6148
  953.3 26.5 %copy-start.122 = (f32[512]{0:T(512)S(1)}, f32[512]{0:T(512)}, u32[]{:S(2)}) copy-start(f32[512]{0:T(512)} %get-tuple-element.126) | copy-start | bytes 6148
  953.3 26.5 %copy-start.123 = (f32[512]{0:T(512)S(1)}, f32[512]{0:T(512)}, u32[]{:S(2)}) copy-start(f32[512]{0:T(512)} %get-tuple-element.173) | copy-start | bytes 6148
  953.3 26.5 %copy-start.124 = (f32[512]{0:T(512)S(1)}, f32[512]{0:T(512)}, u32[]{:S(2)}) copy-start(f32[512]{0:T(512)} %get-tuple-element.175) | copy-start | bytes 6148
  953.4 28.0 %copy-start.15 = (bf16[128,2048]{1,0:T(8,128)(2,1)S(1)}, bf16[128,2048]{1,0:T(8,128)(2,1)}, u32[]{:S(2)}) copy-start(bf16[128,2048]{1,0:T(8,128)(2,1)} %param.20) | copy-start | bytes 1572868
  953.4 28.0 %copy-start.67 = (f32[16,1,128]{2,1,0:T(1,128)S(1)}, f32[16,1,128]{2,1,0:T(1,128)}, u32[]{:S(2)}) copy-start(f32[16,1,128]{2,1,0:T(1,128)} %copy-done.66) | copy-start | bytes 24580
  953.4 27.9 %copy-start.133 = (f32[128]{0:T(128)S(1)}, f32[128]{0:T(128)}, u32[]{:S(2)}) copy-start(f32[128]{0:T(128)} %copy-done.132) | copy-start | bytes 1540
  981.3 55.5 %copy-start.13 = (f32[128,2048]{1,0:T(8,128)S(1)}, f32[128,2048]{1,0:T(8,128)}, u32[]{:S(2)}) copy-start(f32[128,2048]{1,0:T(8,128)} %reduce-scatter.18.cloned.1.call-done) | copy-start | bytes 3145732
  981.3 55.5 %copy-start.127 = (f32[128]{0:T(128)S(1)}, f32[128]{0:T(128)}, u32[]{:S(2)}) copy-start(f32[128]{0:T(128)} %copy-done.125) | copy-start | bytes 1540
  981.4 55.5 %copy-start.135 = (f32[128]{0:T(128)S(1)}, f32[128]{0:T(128)}, u32[]{:S(2)}) copy-start(f32[128]{0:T(128)} %copy-done.134) | copy-start | bytes 1540
  (110 other events, 307.8 us)
Sparse Core Ops, SparseCore 0:
  27.2 23.5 all-gather.15
  53.0 37.0 all-gather.23
  92.3 40.0 all-gather.25
  134.4 40.1 all-gather.19
  176.7 100.3 all-gather.17
  279.1 63.8 all-gather.21
  345.2 39.1 all-gather.27
  388.8 31.4 reduce-scatter.13
  423.3 126.4 all-gather.31
  551.8 19.9 all-gather.29
  574.0 21.2 all-gather.35
  597.6 77.6 all-gather.33
  697.2 30.4 reduce-scatter.17
  731.8 21.2 all-gather.37
  836.3 24.3 reduce-scatter.19
  864.5 52.8 reduce-scatter.23
  919.5 22.1 reduce-scatter.15
  946.4 59.3 reduce-scatter.29
  1011.3 140.7 all-reduce.19
  1156.1 440.7 all-reduce.21
  1601.1 331.6 reduce-scatter.33
  1936.7 49.2 reduce-scatter.21
  1990.9 72.2 reduce-scatter.27
  2067.5 71.4 reduce-scatter.31
  2144.2 135.5 reduce-scatter.25
  2284.9 177.4 reduce-scatter.35
where the time goes:
time: 2480 us; the launch traced here: 2470 us
  waiting for transfers between devices  1920 us (77%)
  blocking collectives  188 us (8%)
  matrix products  165 us (7%)
  local copies, waits for them, and re-layouts  130 us (5%)
  other arithmetic  49.3 us (2%)
    unnamed x27, waiting for transfers between devices  448 us
    reduce_scatter x1, waiting for transfers between devices, send_feed(): lax.psum_scatter(gate_up_grad, 'dp', scatter_dimension=0, tiled=True)  333 us
    reduce_scatter x1, waiting for transfers between devices, send_feed(): lax.psum_scatter(down_weight_grad, 'dp', scatter_dimension=1, tiled=True)  183 us
    reduce_scatter x1, waiting for transfers between devices, on_device(): lax.psum_scatter(mixer_out_grad, 'dp', scatter_dimension=1, tiled=True)  141 us
    all_gather x1, waiting for transfers between devices, on_device(): lax.all_gather(gate_up, 'dp', axis=0, tiled=True)  124 us
    dot_general x28, matrix products, contract(): return jnp.einsum(form, left, right, preferred_element_type=jnp.float32)  122 us
    psum x1, waiting for transfers between devices, on_device(): lax.psum((first_gain_grad, second_gain_grad, state_weight_grad, state_tap...  111 us
    all_gather x1, waiting for transfers between devices, on_device(): lax.all_gather(mixer_in, 'dp', axis=0, tiled=True)  97.1 us
  transfers between devices with their start and end apart: 26, of which 20 were waited for; matrix products, arithmetic and copies ran while one was open for 9% of the time, Pallas kernels for 0%

commit v1 on v0

v1 whole, which is shorter than its diff:
```python
import jax
import jax.numpy as jnp
from jax import lax
from jax.sharding import Mesh, PartitionSpec as P

HEAD = 128
NS = 256
CONV = 4
EPS = 1e-05
ROPE_BASE = 100000000000.0
BF = jnp.bfloat16
F32 = jnp.float32


def dot(left, right):
    return jnp.dot(left, right, preferred_element_type=F32)


def contract(form, left, right):
    return jnp.einsum(form, left, right, preferred_element_type=F32)


def silu_slope(values):
    sigma = jax.nn.sigmoid(values)
    return sigma * (1.0 + values * (1.0 - sigma))


def norm_rows(values, gain):
    scale = lax.rsqrt(jnp.mean(values * values, axis=-1, keepdims=True) + EPS)
    return values * scale * gain, scale


def norm_rows_back(values, gain, scale, grad):
    normal = values * scale
    weighted = grad * gain
    back = scale * (weighted - normal * jnp.mean(weighted * normal, axis=-1, keepdims=True))
    return back, jnp.sum(grad * normal, axis=0)


def swap_c(v):
    return lax.ppermute(v, "c", [(0, 1), (1, 0)])


def swap_x(v):
    return lax.ppermute(v, "x", [(0, 1), (1, 0)])


def swap_t(v):
    return lax.ppermute(v, "t", [(0, 1), (1, 0)])


def swap_xt(v):
    return lax.ppermute(v, ("x", "t"), [(0, 3), (1, 2), (2, 1), (3, 0)])


def swap_xc(v):
    return lax.ppermute(v, ("x", "c"), [(0, 3), (1, 2), (2, 1), (3, 0)])


def pick(rel, j, xi, ci):
    low = jnp.where(ci == 0, rel[j], rel[j ^ 1])
    high = jnp.where(ci == 0, rel[j ^ 2], rel[j ^ 3])
    return jnp.where(xi == 0, low, high)


def deal(blocks, axis, xi, ci):
    rel = [
        pick(blocks, 0, xi, ci),
        swap_c(pick(blocks, 1, xi, ci)),
        swap_x(pick(blocks, 2, xi, ci)),
        swap_xc(pick(blocks, 3, xi, ci)),
    ]
    return [pick(rel, j, xi, ci) for j in range(4)]


def order_t(mine, other, ti, axis=0):
    return jnp.where(
        ti == 0,
        jnp.concatenate([mine, other], axis=axis),
        jnp.concatenate([other, mine], axis=axis),
    )


def act_gather(v, ti):
    near = order_t(v, swap_t(v), ti)
    far = order_t(swap_x(v), swap_xt(v), ti)
    pair = jnp.stack([near, far])
    return jnp.concatenate([pair, swap_c(pair)])


def act_scatter(keep, send, ti):
    total = keep + swap_c(send.astype(BF)).astype(F32)
    rows = total.shape[1] // 2
    mine = lax.dynamic_slice_in_dim(total, ti * rows, rows, 1)
    other = lax.dynamic_slice_in_dim(total, (1 - ti) * rows, rows, 1)
    low = other.astype(BF)
    far = mine[1].astype(BF)
    got = (swap_t(low[0]), swap_x(far), swap_xt(low[1]))
    return mine[0] + got[0].astype(F32) + got[1].astype(F32) + got[2].astype(F32)


def z_gather(v, zi, depth):
    if depth != 4:
        whole = lax.all_gather(v, "z", axis=0, tiled=False)
        whole = jnp.roll(whole, -zi, axis=0)
        return [whole[k] for k in range(depth)]
    below = lax.ppermute(v, "z", [(0, 1), (1, 2), (2, 3)])
    above = lax.ppermute(v, "z", [(1, 0), (2, 1), (3, 2)])
    two = lax.ppermute(v, "z", [(0, 2), (1, 3), (2, 0), (3, 1)])
    last = lax.ppermute(two, "z", [(2, 3), (1, 0)])
    return [v, jnp.where(zi == 3, last, above), two, jnp.where(zi == 0, last, below)]


def z_scatter(parts, zi, depth):
    if depth != 4:
        whole = jnp.roll(jnp.stack([p.astype(BF) for p in parts]), zi, axis=0)
        return lax.psum_scatter(whole, "z", scatter_dimension=0, tiled=False).astype(F32)
    one, three = parts[1].astype(BF), parts[3].astype(BF)
    corner = lax.ppermute(jnp.where(zi == 3, one, three), "z", [(3, 2), (0, 1)])
    down = lax.ppermute(three, "z", [(1, 0), (2, 1), (3, 2)])
    up = lax.ppermute(one, "z", [(0, 1), (1, 2), (2, 3)])
    mid = (parts[2].astype(F32) + corner.astype(F32)).astype(BF)
    far = lax.ppermute(mid, "z", [(0, 2), (1, 3), (2, 0), (3, 1)])
    return parts[0].astype(F32) + down.astype(F32) + up.astype(F32) + far.astype(F32)


def sum_all(v, depth):
    v = v + swap_c(v)
    v = v + swap_x(v)
    v = v + swap_t(v)
    if depth != 4:
        return lax.psum(v, "z")
    v = v + lax.ppermute(v, "z", [(0, 1), (1, 0), (2, 3), (3, 2)])
    return v + lax.ppermute(v, "z", [(0, 2), (2, 0), (1, 3), (3, 1)])


def sum_group(v):
    v = v + jnp.roll(swap_c(v), 2, axis=0)
    got = swap_x(v)
    v = v + jnp.stack([got[1], got[0], got[3], got[2]])
    return v + swap_t(v)


def shift_down(values, offset):
    zero = jnp.zeros((values.shape[0], offset, values.shape[2]), values.dtype)
    return jnp.concatenate([zero, values[:, :-offset]], axis=1)


def shift_up(values, offset):
    zero = jnp.zeros((values.shape[0], offset, values.shape[2]), values.dtype)
    return jnp.concatenate([values[:, offset:], zero], axis=1)


def causal_filter(values, weights, masks):
    total = weights[CONV] + weights[0] * values
    for offset in range(1, CONV):
        total = total + weights[offset] * shift_down(values, offset) * masks[offset]
    return total


def filter_back(values, weights, masks, grad):
    taps = [jnp.sum(grad * values, axis=(0, 1))]
    back = weights[0] * grad
    for offset in range(1, CONV):
        masked = grad * masks[offset]
        taps.append(jnp.sum(masked * shift_down(values, offset), axis=(0, 1)))
        back = back + weights[offset] * shift_up(masked, offset)
    taps.append(jnp.sum(grad, axis=(0, 1)))
    return back, jnp.stack(taps)


def rotate_halves(values, cosine, sine):
    half = values.shape[-1] // 2
    first, second = values[..., :half], values[..., half:]
    return jnp.concatenate(
        [first * cosine - second * sine, second * cosine + first * sine], axis=-1
    )


def rotate_columns(v, start):
    width = v.shape[1]
    return lax.dynamic_slice_in_dim(jnp.concatenate([v, v], axis=1), start, width, 1)


def on_device(
    depth,
    tokens,
    segments,
    cotangent,
    first_gain,
    mixer_in,
    state_weight,
    step_weight,
    filter_taps,
    state_taps,
    decay_log,
    step_bias,
    skip_gain,
    gate_gain,
    mixer_out,
    query_weight,
    key_value_matrix,
    attend_out,
    second_gain,
    gate_up,
    down_weight,
):
    zi, xi = lax.axis_index("z"), lax.axis_index("x")
    ci, ti = lax.axis_index("c"), lax.axis_index("t")
    me = xi * 2 + ci
    rows, width = tokens.shape
    group = segments.shape[0]
    shard = mixer_in.shape[0]
    block = 4 * shard
    heads_in = decay_log.shape[0]
    heads = heads_in // 4
    chans = heads * HEAD
    total_chans = 2 * heads_in * HEAD
    ffn = gate_up.shape[2] // 4
    count = 4 * group
    scale = HEAD ** (-0.5)

    pieces = [first_gain, second_gain, filter_taps, state_taps, gate_gain, segments]
    sizes = [p.size for p in pieces]
    vec = jnp.concatenate([p.astype(BF).reshape(-1) for p in pieces])
    pad = -vec.size % 1024
    vec = jnp.pad(vec, (0, pad)).reshape(-1, 128)
    near = jnp.stack([vec, swap_x(vec)])
    quad = jnp.concatenate([near, swap_c(near)])
    by_offset = [quad[0], quad[2], quad[1], quad[3]]
    natural = jnp.stack([pick(by_offset, j, xi, ci) for j in range(4)])
    small = jnp.stack(z_gather(natural, zi, depth)).reshape(depth, 4, -1)
    segs = quad.reshape(4, -1)[:, sum(sizes[:5]) : sum(sizes)].astype(F32)
    offsets = [sum(sizes[:i]) for i in range(6)]
    cut = [small[:, :, offsets[i] : offsets[i] + sizes[i]] for i in range(5)]
    first_full = cut[0].reshape(-1).astype(F32)
    second_full = cut[1].reshape(-1).astype(F32)
    by_z = [jnp.roll(c, zi, axis=0) for c in cut[2:]]
    eighth = filter_taps.shape[2]
    taps_all = jnp.transpose(
        by_z[0].reshape(depth, 4, CONV + 1, heads_in, eighth), (2, 3, 0, 1, 4)
    ).reshape(CONV + 1, 4, chans)
    taps = lax.dynamic_index_in_dim(taps_all, me, 1, keepdims=False).astype(F32)
    staps = (
        jnp.transpose(by_z[1].reshape(depth, 4, CONV + 1, -1), (2, 0, 1, 3))
        .reshape(CONV + 1, 2 * NS)
        .astype(F32)
    )
    gate_all = jnp.transpose(
        by_z[2].reshape(depth, 4, heads_in, eighth), (2, 0, 1, 3)
    ).reshape(4, chans)
    gate_gain_mine = lax.dynamic_index_in_dim(gate_all, me, 0, keepdims=False).astype(F32)

    def quarters(v, axis):
        n = v.shape[axis] // 4
        return [lax.slice_in_dim(v, j * n, (j + 1) * n, axis=axis) for j in range(4)]

    state_half = lax.dynamic_slice_in_dim(state_weight, ti * NS, NS, 1)
    step_pad = jnp.pad(step_weight, ((0, 0), (0, 128 - heads_in)))
    row_pack = jnp.concatenate(
        [state_half, key_value_matrix.reshape(shard, -1), step_pad], axis=1
    )
    row_z = jnp.stack(z_gather(row_pack, zi, depth))
    state_other = swap_t(row_z[:, :, :NS])
    state_both = order_t(row_z[:, :, :NS], state_other, ti, axis=2)
    row_mine = jnp.concatenate([state_both, row_z[:, :, NS:]], axis=2)
    row_near = jnp.stack([row_mine, swap_x(row_mine)])
    row_quad = jnp.concatenate([row_near, swap_c(row_near)])
    row_by = [row_quad[0], row_quad[2], row_quad[1], row_quad[3]]
    row_full = jnp.stack([pick(row_by, j, xi, ci) for j in range(4)], axis=1).reshape(
        width, -1
    )
    state_full = row_full[:, : 2 * NS]
    kv_at, step_at = 2 * NS, 2 * NS + 2 * HEAD
    step_full = lax.dynamic_slice_in_dim(row_full[:, step_at:], me * heads, heads, 1)

    mix_q = [
        jnp.concatenate([a, b, q], axis=1)
        for a, b, q in zip(
            quarters(mixer_in[:, 0], 1), quarters(mixer_in[:, 1], 1), quarters(query_weight, 1)
        )
    ]
    mix_w = jnp.concatenate(
        z_gather(jnp.concatenate(deal(mix_q, 0, xi, ci), axis=0), zi, depth), axis=0
    )
    out_q = [
        jnp.concatenate([a, b], axis=0)
        for a, b in zip(quarters(mixer_out, 0), quarters(attend_out, 0))
    ]
    out_w = jnp.concatenate(
        z_gather(jnp.concatenate(deal(out_q, 1, xi, ci), axis=1), zi, depth), axis=1
    )
    gu_q = [
        jnp.concatenate([a, b], axis=1)
        for a, b in zip(quarters(gate_up[:, 0], 1), quarters(gate_up[:, 1], 1))
    ]
    gu_w = jnp.concatenate(
        z_gather(jnp.concatenate(deal(gu_q, 0, xi, ci), axis=0), zi, depth), axis=0
    )
    down_w = jnp.concatenate(
        z_gather(jnp.concatenate(deal(quarters(down_weight, 0), 1, xi, ci), axis=1), zi, depth),
        axis=1,
    )

    order = jnp.arange(group)
    live_all = (segs >= 0).astype(F32)
    causal = (segs[:, :, None] == segs[:, None, :]) & (order[None, None, :] <= order[None, :, None])
    position = jnp.sum(causal.astype(F32), axis=2) - 1.0
    masks = [None]
    for offset in range(1, CONV):
        earlier = jnp.concatenate(
            [jnp.full((4, offset), -2.0, F32), segs[:, :-offset]], axis=1
        )
        masks.append((earlier == segs).astype(F32)[:, :, None])
    half = HEAD // 2
    frequency = ROPE_BASE ** (-2.0 * jnp.arange(half).astype(F32) / HEAD)
    angle = position[:, :, None] * frequency[None, None, :]
    cosine, sine = jnp.cos(angle), jnp.sin(angle)
    live_mine = lax.dynamic_slice_in_dim(
        (segments >= 0).astype(F32), ti * rows, rows
    )[:, None]

    start = zi * block
    resid = rotate_columns(tokens, start).astype(F32)
    normed_input, scale_one = norm_rows(resid, first_full)
    normed_low = normed_input.astype(BF)
    normed = act_gather(normed_low, ti).reshape(count, width)
    row_out = dot(normed, row_full[:, :step_at])
    state_raw = row_out[:, : 2 * NS].reshape(4, group, 2 * NS)
    kv_raw = row_out[:, kv_at:].reshape(4, group, 2 * HEAD)
    step_raw = dot(normed, step_full).reshape(4, group, heads)
    mix_out = dot(normed, mix_w)
    gate_value = mix_out[:, :chans].reshape(4, group, chans)
    filter_input = mix_out[:, chans : 2 * chans].reshape(4, group, chans)
    query_raw = mix_out[:, 2 * chans :].reshape(4, group, HEAD)

    filter_pre = causal_filter(filter_input, taps, masks)
    filtered = jax.nn.silu(filter_pre)
    state_pre = causal_filter(state_raw, staps, masks)
    state_act = jax.nn.silu(state_pre)
    state_write = state_act[:, :, :NS].astype(BF)
    state_read = state_act[:, :, NS:].astype(BF)
    my_log = lax.dynamic_slice_in_dim(decay_log, me * heads, heads)
    my_bias = lax.dynamic_slice_in_dim(step_bias, me * heads, heads)
    my_skip = lax.dynamic_slice_in_dim(skip_gain, me * heads, heads)
    step = jax.nn.softplus(step_raw + my_bias)
    decay_rate = -jnp.exp(my_log)
    rate = decay_rate * step
    level = jnp.cumsum(rate, axis=1)
    level_t = jnp.transpose(level, (0, 2, 1))
    affinity = contract("gtn,gsn->gts", state_read, state_write)
    spread = level_t[:, :, :, None] - level_t[:, :, None, :]
    causal_h = causal[:, None]
    decay = jnp.where(causal_h, jnp.exp(jnp.where(causal_h, spread, 0.0)), 0.0)
    mixing_full = affinity[:, None] * decay
    mixing = mixing_full.astype(BF)
    step_wide = jnp.repeat(step, HEAD, axis=2)
    skip_wide = jnp.repeat(my_skip, HEAD)
    inner = (filtered * step_wide).astype(BF)

    def head(v, h):
        return v[:, :, h * HEAD : (h + 1) * HEAD]

    scanned = jnp.concatenate(
        [contract("gts,gsd->gtd", mixing[:, h], head(inner, h)) for h in range(heads)], axis=2
    )
    state_mix = scanned + skip_wide * filtered
    gate_act = jax.nn.silu(gate_value)
    gated = state_mix * gate_act
    squares = sum_group(jnp.sum(gated * gated, axis=-1))
    gate_scale = lax.rsqrt(squares / total_chans + EPS)[:, :, None]
    gate_normal = gated * gate_scale
    state_norm = (gate_normal * gate_gain_mine).astype(BF)

    query = rotate_halves(query_raw, cosine, sine).astype(BF)
    keys = rotate_halves(kv_raw[:, :, :HEAD], cosine, sine).astype(BF)
    values = kv_raw[:, :, HEAD:].astype(BF)
    scores = jnp.where(causal, contract("gtd,gsd->gts", query, keys) * scale, -1e30)
    top = jnp.max(scores, axis=-1, keepdims=True)
    raised = jnp.exp(scores - top)
    shares = raised / jnp.sum(raised, axis=-1, keepdims=True)
    shares_low = shares.astype(BF)
    attended = contract("gts,gsd->gtd", shares_low, values).astype(BF)

    branch = jnp.concatenate([state_norm, attended], axis=2)
    mixed = act_scatter(
        contract("gtk,kc->gtc", branch[:2], out_w) * live_all[:2, :, None],
        contract("gtk,kc->gtc", branch[2:], out_w) * live_all[2:, :, None],
        ti,
    )
    hidden = resid + mixed
    second, scale_two = norm_rows(hidden, second_full)
    second_all = act_gather(second.astype(BF), ti).reshape(count, width)
    gate_up_out = dot(second_all, gu_w)
    gate_part, up_part = gate_up_out[:, :ffn], gate_up_out[:, ffn:]
    activation = (jax.nn.silu(gate_part) * up_part).astype(BF)
    act_g = activation.reshape(4, group, ffn)
    feed_out = act_scatter(
        contract("gtk,kc->gtc", act_g[:2], down_w) * live_all[:2, :, None],
        contract("gtk,kc->gtc", act_g[2:], down_w) * live_all[2:, :, None],
        ti,
    )
    output = rotate_columns((hidden + feed_out).astype(BF), width - start)

    grad_out = rotate_columns(cotangent, start).astype(F32)
    feed_grad = act_gather((live_mine * grad_out).astype(BF), ti).reshape(count, width)
    act_grad = contract("td,fd->tf", feed_grad, down_w)
    gate_grad = act_grad * up_part * silu_slope(gate_part)
    up_grad = act_grad * jax.nn.silu(gate_part)
    gu_low = jnp.concatenate([gate_grad, up_grad], axis=1).astype(BF)
    gu_low_g = gu_low.reshape(4, group, 2 * ffn)
    second_grad = act_scatter(
        contract("gtk,ck->gtc", gu_low_g[:2], gu_w),
        contract("gtk,ck->gtc", gu_low_g[2:], gu_w),
        ti,
    )

    def column(v, k):
        return v[:, k * block : (k + 1) * block]

    down_sum = z_scatter(
        [contract("tf,td->fd", activation, column(feed_grad, k)) for k in range(depth)], zi, depth
    )
    gu_sum = z_scatter(
        [contract("tc,tk->ck", column(second_all, k), gu_low) for k in range(depth)], zi, depth
    )
    down_back = deal(quarters(down_sum.astype(BF), 1), 0, xi, ci)
    down_weight_grad = jnp.concatenate(down_back, axis=0).astype(F32)
    gu_back = deal(quarters(gu_sum.astype(BF), 0), 0, xi, ci)
    gate_up_grad = jnp.stack(
        [
            jnp.concatenate([b[:, :ffn] for b in gu_back], axis=1),
            jnp.concatenate([b[:, ffn:] for b in gu_back], axis=1),
        ],
        axis=1,
    ).astype(F32)

    hidden_part, second_gain_grad = norm_rows_back(hidden, second_full, scale_two, second_grad)
    hidden_grad = grad_out + hidden_part
    mix_grad = act_gather((live_mine * hidden_grad).astype(BF), ti).reshape(count, width)
    branch_flat = branch.reshape(count, chans + HEAD)
    branch_grad = contract("td,cd->tc", mix_grad, out_w)
    out_sum = z_scatter(
        [contract("tc,td->cd", branch_flat, column(mix_grad, k)) for k in range(depth)], zi, depth
    )
    out_back = deal(quarters(out_sum.astype(BF), 1), 0, xi, ci)
    mixer_out_grad = jnp.concatenate([b[:chans] for b in out_back], axis=0).astype(F32)
    attend_out_grad = jnp.concatenate([b[chans:] for b in out_back], axis=0).astype(F32)

    norm_grad = branch_grad[:, :chans].reshape(4, group, chans)
    attend_grad = branch_grad[:, chans:].astype(BF).reshape(4, group, HEAD)
    weighted = norm_grad * gate_gain_mine
    inner_sum = sum_group(jnp.sum(weighted * gate_normal, axis=-1))
    gated_grad = gate_scale * (weighted - gate_normal * (inner_sum / total_chans)[:, :, None])
    gate_gain_grad = jnp.sum(norm_grad * gate_normal, axis=(0, 1))
    mix_state_grad = gated_grad * gate_act
    gate_value_grad = gated_grad * state_mix * silu_slope(gate_value)
    skip_gain_grad = jnp.sum(
        (mix_state_grad * filtered).reshape(count, heads, HEAD), axis=(0, 2)
    )
    scanned_low = mix_state_grad.astype(BF)

    mixing_grad = jnp.stack(
        [contract("gtd,gsd->gts", head(scanned_low, h), head(inner, h)) for h in range(heads)],
        axis=1,
    )
    inner_grad = jnp.concatenate(
        [contract("gts,gtd->gsd", mixing[:, h], head(scanned_low, h)) for h in range(heads)],
        axis=2,
    )
    flow = mixing_grad * mixing_full
    level_grad = jnp.sum(flow, axis=3) - jnp.sum(flow, axis=2)
    rate_grad = jnp.transpose(
        lax.cumsum(level_grad, axis=2, reverse=True), (0, 2, 1)
    )
    decay_log_grad = jnp.sum(rate_grad * rate, axis=(0, 1))
    step_grad = rate_grad * decay_rate + jnp.sum(
        (inner_grad * filtered).reshape(4, group, heads, HEAD), axis=3
    )
    filtered_grad = skip_wide * mix_state_grad + inner_grad * step_wide
    affinity_grad = jnp.sum(mixing_grad * decay, axis=1).astype(BF)
    read_grad = contract("gts,gsn->gtn", affinity_grad, state_write)
    write_grad = contract("gts,gtn->gsn", affinity_grad, state_read)
    state_act_grad = jnp.concatenate([write_grad, read_grad], axis=2) * silu_slope(state_pre)
    state_raw_grad, state_taps_grad = filter_back(state_raw, staps, masks, state_act_grad)
    step_pre_grad = step_grad * jax.nn.sigmoid(step_raw + my_bias)
    step_bias_grad = jnp.sum(step_pre_grad, axis=(0, 1))
    step_low = step_pre_grad.astype(BF).reshape(count, heads)
    filter_input_grad, filter_taps_grad = filter_back(
        filter_input, taps, masks, filtered_grad * silu_slope(filter_pre)
    )

    values_grad = contract("gts,gtd->gsd", shares_low, attend_grad)
    shares_grad = contract("gtd,gsd->gts", attend_grad, values)
    scores_low = (
        shares * (shares_grad - jnp.sum(shares_grad * shares, axis=-1, keepdims=True))
    ).astype(BF)
    query_grad = contract("gts,gsd->gtd", scores_low, keys) * scale
    keys_grad = contract("gts,gtd->gsd", scores_low, query) * scale
    query_low = rotate_halves(query_grad, cosine, -sine)
    keys_low = jnp.concatenate([rotate_halves(keys_grad, cosine, -sine), values_grad], axis=2)
    mix_low = (
        jnp.concatenate([gate_value_grad, filter_input_grad, query_low], axis=2)
        .astype(BF)
        .reshape(count, 2 * chans + HEAD)
    )
    step_wide_low = lax.dynamic_update_slice_in_dim(
        jnp.zeros((count, 128), BF), step_low, me * heads, 1
    )
    kv_low = jnp.concatenate(
        [keys_low.astype(BF).reshape(count, 2 * HEAD), step_wide_low], axis=1
    )
    back_w = jnp.concatenate([mix_w, row_full[:, kv_at:]], axis=1)
    back_low = jnp.concatenate([mix_low, kv_low], axis=1).reshape(4, group, -1)
    summed = act_scatter(
        jnp.concatenate(
            [contract("gtk,ck->gtc", back_low[:2], back_w), state_raw_grad[:2]], axis=2
        ),
        jnp.concatenate(
            [contract("gtk,ck->gtc", back_low[2:], back_w), state_raw_grad[2:]], axis=2
        ),
        ti,
    )
    state_low = summed[:, width:].astype(BF)
    normed_grad = summed[:, :width] + contract("tn,cn->tc", state_low, state_full)
    resid_part, first_gain_grad = norm_rows_back(resid, first_full, scale_one, normed_grad)
    tokens_grad = rotate_columns(hidden_grad + resid_part, width - start)

    mix_sum = z_scatter(
        [contract("tc,tk->ck", column(normed, k), mix_low) for k in range(depth)], zi, depth
    )
    mix_back = deal(quarters(mix_sum.astype(BF), 0), 0, xi, ci)
    mixer_in_grad = jnp.stack(
        [
            jnp.concatenate([b[:, :chans] for b in mix_back], axis=1),
            jnp.concatenate([b[:, chans : 2 * chans] for b in mix_back], axis=1),
        ],
        axis=1,
    ).astype(F32)
    query_weight_grad = jnp.concatenate([b[:, 2 * chans :] for b in mix_back], axis=1).astype(F32)

    kv_part = contract("tc,tk->ck", normed, kv_low).reshape(depth, 2, 2, shard, 3 * HEAD)
    kv_mine = lax.dynamic_index_in_dim(kv_part, ci, 2, keepdims=False)
    kv_send = lax.dynamic_index_in_dim(kv_part, 1 - ci, 2, keepdims=False)
    kv_sum = kv_mine + swap_c(kv_send.astype(BF)).astype(F32)
    kv_mine = lax.dynamic_index_in_dim(kv_sum, xi, 1, keepdims=False)
    kv_send = lax.dynamic_index_in_dim(kv_sum, 1 - xi, 1, keepdims=False)
    kv_sum = kv_mine + swap_x(kv_send.astype(BF)).astype(F32)
    state_low_all = act_gather(state_low, ti).reshape(count, 2 * NS)
    state_cols = lax.dynamic_slice_in_dim(state_low_all, ti * NS, NS, 1)
    normed_mine = lax.dynamic_index_in_dim(
        normed.reshape(count, depth, 4, shard), me, 2, keepdims=False
    ).reshape(count, depth * shard)
    state_part = contract("tc,tk->ck", normed_mine, state_cols).reshape(depth, shard, NS)
    row_part = jnp.concatenate([kv_sum, state_part], axis=2)
    row_sum = z_scatter([row_part[k] for k in range(depth)], zi, depth)
    keys_values_grad = row_sum[:, : 2 * HEAD].reshape(shard, 2, HEAD)
    step_weight_grad = row_sum[:, 2 * HEAD : 2 * HEAD + heads_in]
    state_mine = row_sum[:, 3 * HEAD :]
    state_weight_grad = order_t(
        state_mine, swap_t(state_mine.astype(BF)).astype(F32), ti, axis=1
    )

    slot = ti * 4 + me

    def spread_out(v):
        wide = jnp.zeros((8,) + v.shape, F32)
        return lax.dynamic_update_index_in_dim(wide, v, slot, 0).reshape(-1)

    shapes = [
        second_gain_grad.shape,
        state_taps_grad.shape,
        (8, CONV + 1, chans),
        (8, chans),
        (8, heads),
        (8, heads),
        (8, heads),
        first_gain_grad.shape,
    ]

    def unrotate(v):
        return lax.dynamic_slice_in_dim(jnp.concatenate([v, v]), width - start, width)

    parts = [
        unrotate(second_gain_grad),
        state_taps_grad.reshape(-1),
        spread_out(filter_taps_grad),
        spread_out(gate_gain_grad),
        spread_out(decay_log_grad),
        spread_out(step_bias_grad),
        spread_out(skip_gain_grad),
        unrotate(first_gain_grad),
    ]
    lengths = [p.size for p in parts]
    packed = jnp.concatenate(parts)
    packed = jnp.pad(packed, (0, -packed.size % 1024)).reshape(-1, 128)
    packed = sum_all(packed, depth).reshape(-1)
    done, at = [], 0
    for shape, length in zip(shapes, lengths):
        done.append(packed[at : at + length].reshape(shape))
        at += length
    dp_at = zi * 4 + me
    second_mine = lax.dynamic_slice_in_dim(done[0], dp_at * shard, shard)
    first_mine = lax.dynamic_slice_in_dim(done[7], dp_at * shard, shard)
    state_shard = state_taps.shape[1]
    state_taps_mine = lax.dynamic_slice_in_dim(done[1], dp_at * state_shard, state_shard, 1)
    mine = [lax.dynamic_slice_in_dim(d, ti * 4, 4, 0) for d in done[2:7]]
    taps_out = jnp.transpose(mine[0], (1, 0, 2)).reshape(CONV + 1, heads_in, HEAD)
    taps_out = lax.dynamic_slice_in_dim(taps_out, dp_at * eighth, eighth, 2)
    gate_out = lax.dynamic_slice_in_dim(
        mine[1].reshape(heads_in, HEAD), dp_at * eighth, eighth, 1
    )
    return (
        output,
        tokens_grad,
        first_mine,
        mixer_in_grad,
        state_weight_grad,
        step_weight_grad,
        taps_out,
        state_taps_mine,
        mine[2].reshape(-1),
        mine[3].reshape(-1),
        mine[4].reshape(-1),
        gate_out,
        mixer_out_grad,
        query_weight_grad,
        keys_values_grad,
        attend_out_grad,
        second_mine,
        gate_up_grad,
        down_weight_grad,
    )


def solution(mesh):
    dp, tensor = mesh.shape["dp"], mesh.shape["tensor"]
    depth = dp // 4
    split = Mesh(mesh.devices.reshape(depth, 2, 2, tensor), ("z", "x", "c", "t"))
    D = ("z", "x", "c")
    T = "t"
    R = ("z", "x", "c", "t")
    weights = (
        P(D),
        P(D, None, T),
        P(D, None),
        P(D, T),
        P(None, T, D),
        P(None, D),
        P(T),
        P(T),
        P(T),
        P(T, D),
        P(T, D),
        P(D, T),
        P(D, None, T),
        P(T, D),
        P(D),
        P(D, None, T),
        P(T, D),
    )

    def run(*args):
        return on_device(depth, *args)

    return jax.shard_map(
        run,
        mesh=split,
        in_specs=(P(R, None), P(D), P(R, None)) + weights,
        out_specs=(P(R, None), P(R, None)) + weights,
        check_vma=False,
    )
```

time: 2480 us -> 1020 us (0.41)
  waiting for transfers between devices: 1920 us -> 401 us
  starting transfers between devices: 1.41 us -> 222 us
  blocking collectives: 188 us -> 0 us
  other arithmetic: 49.3 us -> 131 us
  matrix products: 165 us -> 98.7 us
    reduce_scatter x12 -> x0, waiting for transfers between devices: 916 us -> none  [the longest x1 333 us: send_feed(): lax.psum_scatter(gate_up_grad, 'dp', scatter_dimension=0, tiled=True)]
    unnamed x27 -> x0, waiting for transfers between devices: 448 us -> none
    all_gather x12 -> x0, waiting for transfers between devices: 444 us -> none  [the longest x1 124 us: on_device(): lax.all_gather(gate_up, 'dp', axis=0, tiled=True)]
    ppermute x0 -> x123, waiting for transfers between devices: none -> 401 us  [the longest x14 103 us: swap_t(): return lax.ppermute(v, 't', [(0, 1), (1, 0)])]
    ppermute x0 -> x123, starting transfers between devices: none -> 222 us  [the longest x23 36.7 us: swap_c(): return lax.ppermute(v, 'c', [(0, 1), (1, 0)])]
    psum x1 -> x0, waiting for transfers between devices: 111 us -> none  [on_device(): lax.psum((first_gain_grad, second_gain_grad, state_weight_grad, state_tap...]
    all_gather x6 -> x0, blocking collectives: 106 us -> none  [the longest x1 19.9 us: on_device(): lax.all_gather(step_weight, 'dp', axis=0, tiled=True)]
    dot_general x39 -> x50, matrix products: 165 us -> 95.9 us  [the longest x46 79.5 us: contract(): return jnp.einsum(form, left, right, preferred_element_type=F32)]
  transfers between devices with their start and end apart: 26 -> 123, of which waited for: 20 -> 48; matrix products, arithmetic and copies ran while one was open for 9% -> 32% of each run, Pallas kernels for 0% -> 0%
where the time goes in v1:
time: 1020 us; the launch traced here: 1000 us
  waiting for transfers between devices  401 us (39%)
  starting transfers between devices  222 us (22%)
  local copies, waits for them, and re-layouts  141 us (14%)
  other arithmetic  131 us (13%)
  matrix products  98.7 us (10%)
    ppermute x14, waiting for transfers between devices, swap_t(): return lax.ppermute(v, 't', [(0, 1), (1, 0)])  103 us
    dot_general x46, matrix products, contract(): return jnp.einsum(form, left, right, preferred_element_type=F32)  79.5 us
    ppermute x6, waiting for transfers between devices, z_gather(): below = lax.ppermute(v, 'z', [(0, 1), (1, 2), (2, 3)])  47 us
    ppermute x6, waiting for transfers between devices, z_gather(): two = lax.ppermute(v, 'z', [(0, 2), (1, 3), (2, 0), (3, 1)])  40.6 us
    ppermute x5, waiting for transfers between devices, z_scatter(): far = lax.ppermute(mid, 'z', [(0, 2), (1, 3), (2, 0), (3, 1)])  39.8 us
    unnamed x386, local copies, waits for them, and re-layouts  37.5 us
    ppermute x23, starting transfers between devices, swap_c(): return lax.ppermute(v, 'c', [(0, 1), (1, 0)])  36.7 us
    ppermute x23, waiting for transfers between devices, swap_x(): return lax.ppermute(v, 'x', [(0, 1), (1, 0)])  31.2 us
  transfers between devices with their start and end apart: 123, of which 48 were waited for; matrix products, arithmetic and copies ran while one was open for 32% of the time, Pallas kernels for 0%

profile of v1, /device:TPU:17, one launch (start us, length us, event | category | flops | bytes accessed | tf_op | source)
XLA Modules:
  0.0 999.7 jit_solution(14584148253273579905)
XLA Ops:
  3.1 4.4 collective-permute-start.12
  64.0 4.3 collective-permute-done.19
  77.7 4.2 collective-permute-start.30
  81.8 8.1 collective-permute-done.8
  90.4 6.9 collective-permute-done.6
  97.3 5.3 collective-permute-start.20
  102.9 5.2 collective-permute-start.32
  108.4 13.5 %collective-permute-done.30 = bf16[512,512]{1,0:T(8,128)(2,1)S(1)} collective-permute-done((bf16[512,512]{1,0:T(8,128)(2,1)S(1)}, bf16[512,512]{1,0:T(8,128)(2,1)S(1)}, u32[]{:S(2)}, u32[]{:S(2)}) %collective-permute-start.30) | collective-permute-done | bytes 524320 | tf_op jit(solution)/shard_map/ppermute | solution.py:109
  121.9 5.5 collective-permute-start.31
  130.5 4.2 collective-permute-done.51
  136.6 18.2 %collective-permute-done.32 = bf16[512,512]{1,0:T(8,128)(2,1)S(1)} collective-permute-done((bf16[512,512]{1,0:T(8,128)(2,1)S(1)}, bf16[512,512]{1,0:T(8,128)(2,1)S(1)}, u32[]{:S(2)}, u32[]{:S(2)}) %collective-permute-start.32) | collective-permute-done | bytes 524320 | tf_op jit(solution)/shard_map/ppermute | solution.py:108
  157.0 4.0 collective-permute-start.22
  165.9 4.1 collective-permute-start.23
  170.2 5.4 collective-permute-done.15
  180.5 5.0 collective-permute-done.21
  186.7 18.5 %collective-permute-done.23 = bf16[512,896]{1,0:T(8,128)(2,1)S(1)} collective-permute-done((bf16[512,896]{1,0:T(8,128)(2,1)S(1)}, bf16[512,896]{1,0:T(8,128)(2,1)S(1)}, u32[]{:S(2)}, u32[]{:S(2)}) %collective-permute-start.23) | collective-permute-done | bytes 917536 | tf_op jit(solution)/shard_map/ppermute | solution.py:107
  207.9 4.5 fusion.275
  224.6 7.2 copy.289
  231.8 7.1 reshape.973
  238.9 6.2 fusion.7
  256.9 9.5 fusion.11
  304.1 21.6 %collective-permute-done.60 = bf16[128,2048]{1,0:T(8,128)(2,1)S(1)} collective-permute-done((bf16[128,2048]{1,0:T(8,128)(2,1)}, bf16[128,2048]{1,0:T(8,128)(2,1)S(1)}, u32[]{:S(2)}, u32[]{:S(2)}) %collective-permute-start.60) | collective-permute-done | bytes 524320 | tf_op jit(solution)/shard_map/ppermute | solution.py:49
  328.3 8.6 collective-permute-done.35
  340.9 9.9 collective-permute-done.38
  352.4 4.1 collective-permute-start.55
  356.5 27.0 %collective-permute-done.45 = bf16[512,1024]{1,0:T(8,128)(2,1)S(1)} collective-permute-done((bf16[512,1024]{1,0:T(8,128)(2,1)S(1)}, bf16[512,1024]{1,0:T(8,128)(2,1)S(1)}, u32[]{:S(2)}, u32[]{:S(2)}) %collective-permute-start.45) | collective-permute-done | bytes 1048608 | tf_op jit(solution)/shard_map/ppermute | solution.py:109
  403.5 7.4 collective-permute-done.47
  410.9 12.5 %collective-permute-done.46 = bf16[512,1024]{1,0:T(8,128)(2,1)S(1)} collective-permute-done((bf16[512,1024]{1,0:T(8,128)(2,1)S(1)}, bf16[512,1024]{1,0:T(8,128)(2,1)S(1)}, u32[]{:S(2)}, u32[]{:S(2)}) %collective-permute-start.46) | collective-permute-done | bytes 1048608 | tf_op jit(solution)/shard_map/ppermute | solution.py:110
  424.0 22.0 %collective-permute-done.48 = bf16[512,1024]{1,0:T(8,128)(2,1)S(1)} collective-permute-done((bf16[512,1024]{1,0:T(8,128)(2,1)S(1)}, bf16[512,1024]{1,0:T(8,128)(2,1)S(1)}, u32[]{:S(2)}, u32[]{:S(2)}) %collective-permute-start.48) | collective-permute-done | bytes 1048608 | tf_op jit(solution)/shard_map/ppermute | solution.py:107
  450.4 7.7 reshape_reshape.3
  458.1 5.7 constant_dynamic-slice_fusion.8
  463.8 5.8 copy.380
  469.7 6.4 copy.344
  489.3 4.5 fusion.276
  507.1 4.0 collective-permute-start.117
  522.7 3.8 collective-permute-done.118
  528.6 20.5 %collective-permute-done.111 = bf16[512,1024]{1,0:T(8,128)(2,1)} collective-permute-done((bf16[512,1024]{1,0:T(8,128)(2,1)S(1)}, bf16[512,1024]{1,0:T(8,128)(2,1)}, u32[]{:S(2)}, u32[]{:S(2)}) %collective-permute-start.111) | collective-permute-done | bytes 1048608 | tf_op jit(solution)/shard_map/ppermute | solution.py:119
  549.1 4.0 collective-permute-start.64
  556.5 8.3 collective-permute-start.109
  578.8 17.6 %collective-permute-done.57 = bf16[128,2048]{1,0:T(8,128)(2,1)S(1)} collective-permute-done((bf16[128,2048]{1,0:T(8,128)(2,1)S(1)}, bf16[128,2048]{1,0:T(8,128)(2,1)S(1)}, u32[]{:S(2)}, u32[]{:S(2)}) %collective-permute-start.57) | collective-permute-done | bytes 524320 | tf_op jit(solution)/shard_map/ppermute | solution.py:49
  598.3 9.3 collective-permute-done.65
  609.7 11.4 %collective-permute-done.59 = bf16[128,2048]{1,0:T(8,128)(2,1)S(1)} collective-permute-done((bf16[128,2048]{1,0:T(8,128)(2,1)S(1)}, bf16[128,2048]{1,0:T(8,128)(2,1)S(1)}, u32[]{:S(2)}, u32[]{:S(2)}) %collective-permute-start.59) | collective-permute-done | bytes 524320 | tf_op jit(solution)/shard_map/ppermute | solution.py:53
  621.1 10.3 %collective-permute-done.58 = bf16[128,2048]{1,0:T(8,128)(2,1)S(1)} collective-permute-done((bf16[128,2048]{1,0:T(8,128)(2,1)S(1)}, bf16[128,2048]{1,0:T(8,128)(2,1)S(1)}, u32[]{:S(2)}, u32[]{:S(2)}) %collective-permute-start.58) | collective-permute-done | bytes 524320 | tf_op jit(solution)/shard_map/ppermute | solution.py:45
  635.9 16.4 %collective-permute-done.112 = bf16[512,1024]{1,0:T(8,128)(2,1)S(1)} collective-permute-done((bf16[512,1024]{1,0:T(8,128)(2,1)S(1)}, bf16[512,1024]{1,0:T(8,128)(2,1)S(1)}, u32[]{:S(2)}, u32[]{:S(2)}) %collective-permute-start.112) | collective-permute-done | bytes 1048608 | tf_op jit(solution)/shard_map/ppermute | solution.py:123
  656.2 7.5 collective-permute-start.71
  663.7 6.9 collective-permute-done.115
  681.4 14.2 %collective-permute-start.102 = (bf16[512,512]{1,0:T(8,128)(2,1)}, bf16[512,512]{1,0:T(8,128)(2,1)}, u32[]{:S(2)}, u32[]{:S(2)}) collective-permute-start(bf16[512,512]{1,0:T(8,128)(2,1)} %convolution_convert_fusion.7), channel_id=1, source_target_pairs={{8,0},{16,8},{24,16},{9,1},{17,9},{25,17},{10,2},{18,10},{26,18},{... | collective-permute-start | bytes 1572872 | tf_op jit(solution)/shard_map/ppermute | solution.py:120
  714.2 4.8 collective-permute-start.103
  720.2 5.0 fusion.136
  726.4 4.3 multiply_reduce_fusion.5
  741.0 3.8 convolution_convert_fusion.3
  744.8 4.1 broadcast_select_fusion.1
  766.0 15.1 %reduce-window.16 = f32[4,3,2,128]{3,2,1,0:T(2,128)S(1)} reduce-window(f32[4,3,2,128]{3,2,1,0:T(2,128)S(1)} %copy.331, f32[]{:T(128)} %constant.173.clone.1), window={size=1x1x1x128 pad=0_0x0_0x0_0x0_127}, to_apply=%region_13.14 | reduce-window | flops 390144 | bytes 24580 | tf_op jit(solution)/shard_map/reduce-window.2
  785.1 3.9 concatenate.639
  794.7 4.5 fusion.6
  803.4 4.8 fusion.103
  818.7 16.8 %collective-permute-done.105 = bf16[512,512]{1,0:T(8,128)(2,1)S(1)} collective-permute-done((bf16[512,512]{1,0:T(8,128)(2,1)S(1)}, bf16[512,512]{1,0:T(8,128)(2,1)S(1)}, u32[]{:S(2)}, u32[]{:S(2)}) %collective-permute-start.105) | collective-permute-done | bytes 524320 | tf_op jit(solution)/shard_map/ppermute | solution.py:123
  854.7 21.2 %collective-permute-done.85 = bf16[512,896]{1,0:T(8,128)(2,1)S(1)} collective-permute-done((bf16[512,896]{1,0:T(8,128)(2,1)S(1)}, bf16[512,896]{1,0:T(8,128)(2,1)S(1)}, u32[]{:S(2)}, u32[]{:S(2)}) %collective-permute-start.85) | collective-permute-done | bytes 917536 | tf_op jit(solution)/shard_map/ppermute | solution.py:121
  876.0 6.7 collective-permute-done.87
  886.8 5.4 collective-permute-done.89
  892.1 5.1 collective-permute-done.90
  904.8 24.2 %collective-permute-done.76 = bf16[128,2560]{1,0:T(8,128)(2,1)S(1)} collective-permute-done((bf16[128,2560]{1,0:T(8,128)(2,1)S(1)}, bf16[128,2560]{1,0:T(8,128)(2,1)S(1)}, u32[]{:S(2)}, u32[]{:S(2)}) %collective-permute-start.76) | collective-permute-done | bytes 655392 | tf_op jit(solution)/shard_map/ppermute | solution.py:49
  940.6 4.0 collective-permute-done.80
  948.3 14.3 %collective-permute-start.82 = (f32[200,128]{1,0:T(8,128)S(1)}, f32[200,128]{1,0:T(8,128)S(1)}, u32[]{:S(2)}, u32[]{:S(2)}) collective-permute-start(f32[200,128]{1,0:T(8,128)S(1)} %add.561), channel_id=1, source_target_pairs={{0,8},{8,0},{16,24},{24,16},{1,9},{9,1},{17,25},{25,17},{2,10},{10... | collective-permute-start | bytes 307208 | tf_op jit(solution)/shard_map/ppermute | solution.py:133
  (998 shorter events, 417.8 us)
Async XLA Ops:
  3.1 56.1 %collective-permute-start.10 = (bf16[128,640]{1,0:T(8,128)(2,1)}, bf16[128,640]{1,0:T(8,128)(2,1)S(1)}, u32[]{:S(2)}, u32[]{:S(2)}) collective-permute-start(bf16[128,640]{1,0:T(8,128)(2,1)} %get-tuple-element.342), channel_id=1, source_target_pairs={{0,16},{8,24},{16,0},{24,8},{1,17},{9,25},{17,1},{25,9},{2,18},{10... | collective-permute-start | bytes 491528 | tf_op jit(solution)/shard_map/ppermute | solution.py:109
  3.1 67.4 %collective-permute-start.12 = (bf16[128,640]{1,0:T(8,128)(2,1)}, bf16[128,640]{1,0:T(8,128)(2,1)}, u32[]{:S(2)}, u32[]{:S(2)}) collective-permute-start(bf16[128,640]{1,0:T(8,128)(2,1)} %get-tuple-element.342), channel_id=1, source_target_pairs={{8,0},{16,8},{24,16},{9,1},{17,9},{25,17},{10,2},{18,10},{26,18},{... | collective-permute-start | bytes 491528 | tf_op jit(solution)/shard_map/ppermute | solution.py:108
  62.3 27.6 %collective-permute-start.8 = (bf16[128,2048]{1,0:T(8,128)(2,1)S(1)}, bf16[128,2048]{1,0:T(8,128)(2,1)S(1)}, u32[]{:S(2)}, u32[]{:S(2)}) collective-permute-start(bf16[128,2048]{1,0:T(8,128)(2,1)S(1)} %copy-done.96), channel_id=1, source_target_pairs={{0,5},{1,4},{4,1},{5,0},{2,7},{3,6},{6,3},{7,2},{8,13},{9,12},{12,... | collective-permute-start | bytes 1572872 | tf_op jit(solution)/shard_map/ppermute | solution.py:53
  71.2 56.4 %collective-permute-start.49 = (bf16[512,128]{1,0:T(8,128)(2,1)S(1)}, bf16[512,128]{1,0:T(8,128)(2,1)S(1)}, u32[]{:S(2)}, u32[]{:S(2)}) collective-permute-start(bf16[512,128]{1,0:T(8,128)(2,1)S(1)} %copy-done.114), channel_id=1, source_target_pairs={{0,2},{2,0},{1,3},{3,1},{4,6},{6,4},{5,7},{7,5},{8,10},{10,8},{9,1... | collective-permute-start | bytes 393224 | tf_op jit(solution)/shard_map/ppermute | solution.py:41
  71.4 59.0 %collective-permute-start.50 = (bf16[512,128]{1,0:T(8,128)(2,1)S(1)}, bf16[512,128]{1,0:T(8,128)(2,1)S(1)}, u32[]{:S(2)}, u32[]{:S(2)}) collective-permute-start(bf16[512,128]{1,0:T(8,128)(2,1)S(1)} %copy-done.113), channel_id=1, source_target_pairs={{0,4},{4,0},{1,5},{5,1},{2,6},{6,2},{3,7},{7,3},{8,12},{12,8},{9,1... | collective-permute-start | bytes 393224 | tf_op jit(solution)/shard_map/ppermute | solution.py:45
  73.2 24.0 %collective-permute-start.6 = (bf16[128,2048]{1,0:T(8,128)(2,1)S(1)}, bf16[128,2048]{1,0:T(8,128)(2,1)S(1)}, u32[]{:S(2)}, u32[]{:S(2)}) collective-permute-start(bf16[128,2048]{1,0:T(8,128)(2,1)S(1)} %copy-done.96), channel_id=1, source_target_pairs={{0,1},{1,0},{2,3},{3,2},{4,5},{5,4},{6,7},{7,6},{8,9},{9,8},{10,11... | collective-permute-start | bytes 1572872 | tf_op jit(solution)/shard_map/ppermute | solution.py:49
  77.7 44.2 %collective-permute-start.30 = (bf16[512,512]{1,0:T(8,128)(2,1)S(1)}, bf16[512,512]{1,0:T(8,128)(2,1)S(1)}, u32[]{:S(2)}, u32[]{:S(2)}) collective-permute-start(bf16[512,512]{1,0:T(8,128)(2,1)S(1)} %pad_maximum_fusion.20), channel_id=1, source_target_pairs={{0,16},{8,24},{16,0},{24,8},{1,17},{9,25},{17,1},{25,9},{2,18},{10... | collective-permute-start | bytes 1572872 | tf_op jit(solution)/shard_map/ppermute | solution.py:109
  97.3 59.7 %collective-permute-start.20 = (bf16[512,896]{1,0:T(8,128)(2,1)S(1)}, bf16[512,896]{1,0:T(8,128)(2,1)S(1)}, u32[]{:S(2)}, u32[]{:S(2)}) collective-permute-start(bf16[512,896]{1,0:T(8,128)(2,1)S(1)} %pad_maximum_fusion.19), channel_id=1, source_target_pairs={{0,16},{8,24},{16,0},{24,8},{1,17},{9,25},{17,1},{25,9},{2,18},{10... | collective-permute-start | bytes 2752520 | tf_op jit(solution)/shard_map/ppermute | solution.py:109
  102.9 51.8 %collective-permute-start.32 = (bf16[512,512]{1,0:T(8,128)(2,1)S(1)}, bf16[512,512]{1,0:T(8,128)(2,1)S(1)}, u32[]{:S(2)}, u32[]{:S(2)}) collective-permute-start(bf16[512,512]{1,0:T(8,128)(2,1)S(1)} %pad_maximum_fusion.20), channel_id=1, source_target_pairs={{8,0},{16,8},{24,16},{9,1},{17,9},{25,17},{10,2},{18,10},{26,18},{... | collective-permute-start | bytes 1572872 | tf_op jit(solution)/shard_map/ppermute | solution.py:108
  121.9 39.2 %collective-permute-start.31 = (bf16[512,512]{1,0:T(8,128)(2,1)S(1)}, bf16[512,512]{1,0:T(8,128)(2,1)S(1)}, u32[]{:S(2)}, u32[]{:S(2)}) collective-permute-start(bf16[512,512]{1,0:T(8,128)(2,1)S(1)} %collective-permute-done.30), channel_id=1, source_target_pairs={{16,24},{8,0},{17,25},{9,1},{18,26},{10,2},{19,27},{11,3},{20,28},... | collective-permute-start | bytes 1572872 | tf_op jit(solution)/shard_map/ppermute | solution.py:110
  130.4 75.6 %collective-permute-start.9 = (bf16[2,256,2048]{2,1,0:T(8,128)(2,1)S(1)}, bf16[2,256,2048]{2,1,0:T(8,128)(2,1)S(1)}, u32[]{:S(2)}, u32[]{:S(2)}) collective-permute-start(bf16[2,256,2048]{2,1,0:T(8,128)(2,1)S(1)} %pad_maximum_fusion.8), channel_id=1, source_target_pairs={{0,2},{2,0},{1,3},{3,1},{4,6},{6,4},{5,7},{7,5},{8,10},{10,8},{9,1... | collective-permute-start | bytes 6291464 | tf_op jit(solution)/shard_map/ppermute | solution.py:41
  134.6 31.2 %collective-permute-start.33 = (bf16[512,512]{1,0:T(8,128)(2,1)S(1)}, bf16[512,512]{1,0:T(8,128)(2,1)S(1)}, u32[]{:S(2)}, u32[]{:S(2)}) collective-permute-start(bf16[512,512]{1,0:T(8,128)(2,1)S(1)} %pad_maximum_fusion.20), channel_id=1, source_target_pairs={{0,8},{8,16},{16,24},{1,9},{9,17},{17,25},{2,10},{10,18},{18,26},{... | collective-permute-start | bytes 1572872 | tf_op jit(solution)/shard_map/ppermute | solution.py:107
  157.0 23.2 %collective-permute-start.22 = (bf16[512,896]{1,0:T(8,128)(2,1)S(1)}, bf16[512,896]{1,0:T(8,128)(2,1)S(1)}, u32[]{:S(2)}, u32[]{:S(2)}) collective-permute-start(bf16[512,896]{1,0:T(8,128)(2,1)S(1)} %pad_maximum_fusion.19), channel_id=1, source_target_pairs={{8,0},{16,8},{24,16},{9,1},{17,9},{25,17},{10,2},{18,10},{26,18},{... | collective-permute-start | bytes 2752520 | tf_op jit(solution)/shard_map/ppermute | solution.py:108
  161.1 24.4 %collective-permute-start.21 = (bf16[512,896]{1,0:T(8,128)(2,1)S(1)}, bf16[512,896]{1,0:T(8,128)(2,1)S(1)}, u32[]{:S(2)}, u32[]{:S(2)}) collective-permute-start(bf16[512,896]{1,0:T(8,128)(2,1)S(1)} %collective-permute-done.20), channel_id=1, source_target_pairs={{16,24},{8,0},{17,25},{9,1},{18,26},{10,2},{19,27},{11,3},{20,28},... | collective-permute-start | bytes 2752520 | tf_op jit(solution)/shard_map/ppermute | solution.py:110
  165.9 39.3 %collective-permute-start.23 = (bf16[512,896]{1,0:T(8,128)(2,1)S(1)}, bf16[512,896]{1,0:T(8,128)(2,1)S(1)}, u32[]{:S(2)}, u32[]{:S(2)}) collective-permute-start(bf16[512,896]{1,0:T(8,128)(2,1)S(1)} %pad_maximum_fusion.19), channel_id=1, source_target_pairs={{0,8},{8,16},{16,24},{1,9},{9,17},{17,25},{2,10},{10,18},{18,26},{... | collective-permute-start | bytes 2752520 | tf_op jit(solution)/shard_map/ppermute | solution.py:107
  175.6 112.6 %collective-permute-start.42 = (bf16[128,1024]{1,0:T(8,128)(2,1)}, bf16[128,1024]{1,0:T(8,128)(2,1)}, u32[]{:S(2)}, u32[]{:S(2)}) collective-permute-start(bf16[128,1024]{1,0:T(8,128)(2,1)} %get-tuple-element.270), channel_id=1, source_target_pairs={{0,2},{2,0},{1,3},{3,1},{4,6},{6,4},{5,7},{7,5},{8,10},{10,8},{9,1... | collective-permute-start | bytes 786440 | tf_op jit(solution)/shard_map/ppermute | solution.py:41
  180.2 109.0 %collective-permute-start.43 = (bf16[128,1024]{1,0:T(8,128)(2,1)}, bf16[128,1024]{1,0:T(8,128)(2,1)}, u32[]{:S(2)}, u32[]{:S(2)}) collective-permute-start(bf16[128,1024]{1,0:T(8,128)(2,1)} %get-tuple-element.189), channel_id=1, source_target_pairs={{0,4},{4,0},{1,5},{5,1},{2,6},{6,2},{3,7},{7,3},{8,12},{12,8},{9,1... | collective-permute-start | bytes 786440 | tf_op jit(solution)/shard_map/ppermute | solution.py:45
  185.5 105.0 %collective-permute-start.44 = (bf16[128,1024]{1,0:T(8,128)(2,1)}, bf16[128,1024]{1,0:T(8,128)(2,1)}, u32[]{:S(2)}, u32[]{:S(2)}) collective-permute-start(bf16[128,1024]{1,0:T(8,128)(2,1)} %broadcast_select_fusion.36), channel_id=1, source_target_pairs={{0,6},{2,4},{4,2},{6,0},{1,7},{3,5},{5,3},{7,1},{8,14},{10,12},{12... | collective-permute-start | bytes 786440 | tf_op jit(solution)/shard_map/ppermute | solution.py:57
  206.0 93.3 %collective-permute-start.61 = (bf16[128,2048]{1,0:T(8,128)(2,1)}, bf16[128,2048]{1,0:T(8,128)(2,1)}, u32[]{:S(2)}, u32[]{:S(2)}) collective-permute-start(bf16[128,2048]{1,0:T(8,128)(2,1)} %fusion.56), channel_id=1, source_target_pairs={{0,4},{4,0},{1,5},{5,1},{2,6},{6,2},{3,7},{7,3},{8,12},{12,8},{9,1... | collective-permute-start | bytes 1572872 | tf_op jit(solution)/shard_map/ppermute | solution.py:45
  289.2 36.5 %collective-permute-start.60 = (bf16[128,2048]{1,0:T(8,128)(2,1)}, bf16[128,2048]{1,0:T(8,128)(2,1)S(1)}, u32[]{:S(2)}, u32[]{:S(2)}) collective-permute-start(bf16[128,2048]{1,0:T(8,128)(2,1)} %fusion.56), channel_id=1, source_target_pairs={{0,1},{1,0},{2,3},{3,2},{4,5},{5,4},{6,7},{7,6},{8,9},{9,8},{10,11... | collective-permute-start | bytes 1572872 | tf_op jit(solution)/shard_map/ppermute | solution.py:49
  297.6 39.4 %collective-permute-start.35 = (bf16[128,2048]{1,0:T(8,128)(2,1)S(1)}, bf16[128,2048]{1,0:T(8,128)(2,1)S(1)}, u32[]{:S(2)}, u32[]{:S(2)}) collective-permute-start(bf16[128,2048]{1,0:T(8,128)(2,1)S(1)} %get-tuple-element.273), channel_id=1, source_target_pairs={{0,1},{1,0},{2,3},{3,2},{4,5},{5,4},{6,7},{7,6},{8,9},{9,8},{10,11... | collective-permute-start | bytes 1572872 | tf_op jit(solution)/shard_map/ppermute | solution.py:49
  297.8 39.2 %collective-permute-start.37 = (bf16[128,2048]{1,0:T(8,128)(2,1)S(1)}, bf16[128,2048]{1,0:T(8,128)(2,1)S(1)}, u32[]{:S(2)}, u32[]{:S(2)}) collective-permute-start(bf16[128,2048]{1,0:T(8,128)(2,1)S(1)} %get-tuple-element.274), channel_id=1, source_target_pairs={{0,5},{1,4},{4,1},{5,0},{2,7},{3,6},{6,3},{7,2},{8,13},{9,12},{12,... | collective-permute-start | bytes 1572872 | tf_op jit(solution)/shard_map/ppermute | solution.py:53
  299.3 37.7 %collective-permute-start.36 = (bf16[128,2048]{1,0:T(8,128)(2,1)S(1)}, bf16[128,2048]{1,0:T(8,128)(2,1)S(1)}, u32[]{:S(2)}, u32[]{:S(2)}) collective-permute-start(bf16[128,2048]{1,0:T(8,128)(2,1)S(1)} %fusion.148), channel_id=1, source_target_pairs={{0,4},{4,0},{1,5},{5,1},{2,6},{6,2},{3,7},{7,3},{8,12},{12,8},{9,1... | collective-permute-start | bytes 1572872 | tf_op jit(solution)/shard_map/ppermute | solution.py:45
  302.5 36.8 %collective-permute-start.52 = (bf16[512,512]{1,0:T(8,128)(2,1)S(1)}, bf16[512,512]{1,0:T(8,128)(2,1)S(1)}, u32[]{:S(2)}, u32[]{:S(2)}) collective-permute-start(bf16[512,512]{1,0:T(8,128)(2,1)S(1)} %pad_maximum_fusion.21), channel_id=1, source_target_pairs={{0,16},{8,24},{16,0},{24,8},{1,17},{9,25},{17,1},{25,9},{2,18},{10... | collective-permute-start | bytes 1572872 | tf_op jit(solution)/shard_map/ppermute | solution.py:109
  325.7 26.7 %collective-permute-start.54 = (bf16[512,512]{1,0:T(8,128)(2,1)S(1)}, bf16[512,512]{1,0:T(8,128)(2,1)S(1)}, u32[]{:S(2)}, u32[]{:S(2)}) collective-permute-start(bf16[512,512]{1,0:T(8,128)(2,1)S(1)} %pad_maximum_fusion.21), channel_id=1, source_target_pairs={{8,0},{16,8},{24,16},{9,1},{17,9},{25,17},{10,2},{18,10},{26,18},{... | collective-permute-start | bytes 1572872 | tf_op jit(solution)/shard_map/ppermute | solution.py:108
  337.0 46.6 %collective-permute-start.45 = (bf16[512,1024]{1,0:T(8,128)(2,1)S(1)}, bf16[512,1024]{1,0:T(8,128)(2,1)S(1)}, u32[]{:S(2)}, u32[]{:S(2)}) collective-permute-start(bf16[512,1024]{1,0:T(8,128)(2,1)S(1)} %pad_maximum_fusion.17), channel_id=1, source_target_pairs={{0,16},{8,24},{16,0},{24,8},{1,17},{9,25},{17,1},{25,9},{2,18},{10... | collective-permute-start | bytes 3145736 | tf_op jit(solution)/shard_map/ppermute | solution.py:109
  338.1 48.5 %collective-permute-start.39 = (bf16[128,2048]{1,0:T(8,128)(2,1)S(1)}, bf16[128,2048]{1,0:T(8,128)(2,1)S(1)}, u32[]{:S(2)}, u32[]{:S(2)}) collective-permute-start(bf16[128,2048]{1,0:T(8,128)(2,1)S(1)} %multiply_convert_fusion.10), channel_id=1, source_target_pairs={{0,4},{4,0},{1,5},{5,1},{2,6},{6,2},{3,7},{7,3},{8,12},{12,8},{9,1... | collective-permute-start | bytes 1572872 | tf_op jit(solution)/shard_map/ppermute | solution.py:45
  339.2 50.7 %collective-permute-start.40 = (bf16[128,2048]{1,0:T(8,128)(2,1)S(1)}, bf16[128,2048]{1,0:T(8,128)(2,1)S(1)}, u32[]{:S(2)}, u32[]{:S(2)}) collective-permute-start(bf16[128,2048]{1,0:T(8,128)(2,1)S(1)} %multiply_convert_fusion.10), channel_id=1, source_target_pairs={{0,5},{1,4},{4,1},{5,0},{2,7},{3,6},{6,3},{7,2},{8,13},{9,12},{12,... | collective-permute-start | bytes 1572872 | tf_op jit(solution)/shard_map/ppermute | solution.py:53
  350.8 95.6 %collective-permute-start.63 = (bf16[2,256,2048]{2,1,0:T(8,128)(2,1)S(1)}, bf16[2,256,2048]{2,1,0:T(8,128)(2,1)S(1)}, u32[]{:S(2)}, u32[]{:S(2)}) collective-permute-start(bf16[2,256,2048]{2,1,0:T(8,128)(2,1)S(1)} %pad_maximum_fusion.10), channel_id=1, source_target_pairs={{0,2},{2,0},{1,3},{3,1},{4,6},{6,4},{5,7},{7,5},{8,10},{10,8},{9,1... | collective-permute-start | bytes 6291464 | tf_op jit(solution)/shard_map/ppermute | solution.py:41
  352.4 44.3 %collective-permute-start.55 = (bf16[512,512]{1,0:T(8,128)(2,1)S(1)}, bf16[512,512]{1,0:T(8,128)(2,1)S(1)}, u32[]{:S(2)}, u32[]{:S(2)}) collective-permute-start(bf16[512,512]{1,0:T(8,128)(2,1)S(1)} %pad_maximum_fusion.21), channel_id=1, source_target_pairs={{0,8},{8,16},{16,24},{1,9},{9,17},{17,25},{2,10},{10,18},{18,26},{... | collective-permute-start | bytes 1572872 | tf_op jit(solution)/shard_map/ppermute | solution.py:107
  383.6 27.4 %collective-permute-start.47 = (bf16[512,1024]{1,0:T(8,128)(2,1)S(1)}, bf16[512,1024]{1,0:T(8,128)(2,1)S(1)}, u32[]{:S(2)}, u32[]{:S(2)}) collective-permute-start(bf16[512,1024]{1,0:T(8,128)(2,1)S(1)} %pad_maximum_fusion.17), channel_id=1, source_target_pairs={{8,0},{16,8},{24,16},{9,1},{17,9},{25,17},{10,2},{18,10},{26,18},{... | collective-permute-start | bytes 3145736 | tf_op jit(solution)/shard_map/ppermute | solution.py:108
  390.0 33.5 %collective-permute-start.46 = (bf16[512,1024]{1,0:T(8,128)(2,1)S(1)}, bf16[512,1024]{1,0:T(8,128)(2,1)S(1)}, u32[]{:S(2)}, u32[]{:S(2)}) collective-permute-start(bf16[512,1024]{1,0:T(8,128)(2,1)S(1)} %collective-permute-done.45), channel_id=1, source_target_pairs={{16,24},{8,0},{17,25},{9,1},{18,26},{10,2},{19,27},{11,3},{20,28},... | collective-permute-start | bytes 3145736 | tf_op jit(solution)/shard_map/ppermute | solution.py:110
  396.7 49.2 %collective-permute-start.48 = (bf16[512,1024]{1,0:T(8,128)(2,1)S(1)}, bf16[512,1024]{1,0:T(8,128)(2,1)S(1)}, u32[]{:S(2)}, u32[]{:S(2)}) collective-permute-start(bf16[512,1024]{1,0:T(8,128)(2,1)S(1)} %pad_maximum_fusion.17), channel_id=1, source_target_pairs={{0,8},{8,16},{16,24},{1,9},{9,17},{17,25},{2,10},{10,18},{18,26},{... | collective-permute-start | bytes 3145736 | tf_op jit(solution)/shard_map/ppermute | solution.py:107
  401.0 84.8 %collective-permute-start.41 = (bf16[2,256,2048]{2,1,0:T(8,128)(2,1)}, bf16[2,256,2048]{2,1,0:T(8,128)(2,1)}, u32[]{:S(2)}, u32[]{:S(2)}) collective-permute-start(bf16[2,256,2048]{2,1,0:T(8,128)(2,1)} %pad_maximum_fusion.9), channel_id=1, source_target_pairs={{0,2},{2,0},{1,3},{3,1},{4,6},{6,4},{5,7},{7,5},{8,10},{10,8},{9,1... | collective-permute-start | bytes 6291464 | tf_op jit(solution)/shard_map/ppermute | solution.py:41
  501.0 63.9 %collective-permute-start.116 = (bf16[512,512]{1,0:T(8,128)(2,1)}, bf16[512,512]{1,0:T(8,128)(2,1)S(1)}, u32[]{:S(2)}, u32[]{:S(2)}) collective-permute-start(bf16[512,512]{1,0:T(8,128)(2,1)} %convolution_convert_fusion.5), channel_id=1, source_target_pairs={{8,0},{16,8},{24,16},{9,1},{17,9},{25,17},{10,2},{18,10},{26,18},{... | collective-permute-start | bytes 1572872 | tf_op jit(solution)/shard_map/ppermute | solution.py:120
  507.1 49.5 %collective-permute-start.117 = (bf16[512,512]{1,0:T(8,128)(2,1)}, bf16[512,512]{1,0:T(8,128)(2,1)}, u32[]{:S(2)}, u32[]{:S(2)}) collective-permute-start(bf16[512,512]{1,0:T(8,128)(2,1)} %get-tuple-element.402), channel_id=1, source_target_pairs={{0,8},{8,16},{16,24},{1,9},{9,17},{17,25},{2,10},{10,18},{18,26},{... | collective-permute-start | bytes 1572872 | tf_op jit(solution)/shard_map/ppermute | solution.py:121
  514.6 34.5 %collective-permute-start.111 = (bf16[512,1024]{1,0:T(8,128)(2,1)S(1)}, bf16[512,1024]{1,0:T(8,128)(2,1)}, u32[]{:S(2)}, u32[]{:S(2)}) collective-permute-start(bf16[512,1024]{1,0:T(8,128)(2,1)S(1)} %get-tuple-element.399), channel_id=1, source_target_pairs={{24,16},{0,8},{25,17},{1,9},{26,18},{2,10},{27,19},{3,11},{28,20},... | collective-permute-start | bytes 3145736 | tf_op jit(solution)/shard_map/ppermute | solution.py:119
  517.2 52.1 %collective-permute-start.56 = (bf16[2,256,2048]{2,1,0:T(8,128)(2,1)S(1)}, bf16[2,256,2048]{2,1,0:T(8,128)(2,1)S(1)}, u32[]{:S(2)}, u32[]{:S(2)}) collective-permute-start(bf16[2,256,2048]{2,1,0:T(8,128)(2,1)S(1)} %multiply_convert_fusion), channel_id=1, source_target_pairs={{0,2},{2,0},{1,3},{3,1},{4,6},{6,4},{5,7},{7,5},{8,10},{10,8},{9,1... | collective-permute-start | bytes 6291464 | tf_op jit(solution)/shard_map/ppermute | solution.py:41
  527.2 37.6 %collective-permute-start.119 = (bf16[512,512]{1,0:T(8,128)(2,1)S(1)}, bf16[512,512]{1,0:T(8,128)(2,1)S(1)}, u32[]{:S(2)}, u32[]{:S(2)}) collective-permute-start(bf16[512,512]{1,0:T(8,128)(2,1)S(1)} %fusion.52), channel_id=1, source_target_pairs={{0,16},{8,24},{16,0},{24,8},{1,17},{9,25},{17,1},{25,9},{2,18},{10... | collective-permute-start | bytes 1572872 | tf_op jit(solution)/shard_map/ppermute | solution.py:123
  549.1 22.6 %collective-permute-start.64 = (bf16[2,256,2048]{2,1,0:T(8,128)(2,1)S(1)}, bf16[2,256,2048]{2,1,0:T(8,128)(2,1)S(1)}, u32[]{:S(2)}, u32[]{:S(2)}) collective-permute-start(bf16[2,256,2048]{2,1,0:T(8,128)(2,1)S(1)} %fusion.15), channel_id=1, source_target_pairs={{0,2},{2,0},{1,3},{3,1},{4,6},{6,4},{5,7},{7,5},{8,10},{10,8},{9,1... | collective-permute-start | bytes 6291464 | tf_op jit(solution)/shard_map/ppermute | solution.py:41
  556.5 79.4 %collective-permute-start.109 = (bf16[512,1024]{1,0:T(8,128)(2,1)}, bf16[512,1024]{1,0:T(8,128)(2,1)S(1)}, u32[]{:S(2)}, u32[]{:S(2)}) collective-permute-start(bf16[512,1024]{1,0:T(8,128)(2,1)} %convolution_convert_fusion.1), channel_id=1, source_target_pairs={{8,0},{16,8},{24,16},{9,1},{17,9},{25,17},{10,2},{18,10},{26,18},{... | collective-permute-start | bytes 3145736 | tf_op jit(solution)/shard_map/ppermute | solution.py:120
  571.7 24.7 %collective-permute-start.57 = (bf16[128,2048]{1,0:T(8,128)(2,1)S(1)}, bf16[128,2048]{1,0:T(8,128)(2,1)S(1)}, u32[]{:S(2)}, u32[]{:S(2)}) collective-permute-start(bf16[128,2048]{1,0:T(8,128)(2,1)S(1)} %get-tuple-element.266), channel_id=1, source_target_pairs={{0,1},{1,0},{2,3},{3,2},{4,5},{5,4},{6,7},{7,6},{8,9},{9,8},{10,11... | collective-permute-start | bytes 1572872 | tf_op jit(solution)/shard_map/ppermute | solution.py:49
  574.8 32.9 %collective-permute-start.65 = (bf16[128,2048]{1,0:T(8,128)(2,1)S(1)}, bf16[128,2048]{1,0:T(8,128)(2,1)S(1)}, u32[]{:S(2)}, u32[]{:S(2)}) collective-permute-start(bf16[128,2048]{1,0:T(8,128)(2,1)S(1)} %get-tuple-element.264), channel_id=1, source_target_pairs={{0,1},{1,0},{2,3},{3,2},{4,5},{5,4},{6,7},{7,6},{8,9},{9,8},{10,11... | collective-permute-start | bytes 1572872 | tf_op jit(solution)/shard_map/ppermute | solution.py:49
  576.0 31.6 %collective-permute-start.67 = (bf16[128,2048]{1,0:T(8,128)(2,1)S(1)}, bf16[128,2048]{1,0:T(8,128)(2,1)S(1)}, u32[]{:S(2)}, u32[]{:S(2)}) collective-permute-start(bf16[128,2048]{1,0:T(8,128)(2,1)S(1)} %get-tuple-element.265), channel_id=1, source_target_pairs={{0,5},{1,4},{4,1},{5,0},{2,7},{3,6},{6,3},{7,2},{8,13},{9,12},{12,... | collective-permute-start | bytes 1572872 | tf_op jit(solution)/shard_map/ppermute | solution.py:53
  577.6 31.1 %collective-permute-start.66 = (bf16[128,2048]{1,0:T(8,128)(2,1)S(1)}, bf16[128,2048]{1,0:T(8,128)(2,1)S(1)}, u32[]{:S(2)}, u32[]{:S(2)}) collective-permute-start(bf16[128,2048]{1,0:T(8,128)(2,1)S(1)} %fusion.150), channel_id=1, source_target_pairs={{0,4},{4,0},{1,5},{5,1},{2,6},{6,2},{3,7},{7,3},{8,12},{12,8},{9,1... | collective-permute-start | bytes 1572872 | tf_op jit(solution)/shard_map/ppermute | solution.py:45
  596.4 38.1 %collective-permute-start.110 = (bf16[512,1024]{1,0:T(8,128)(2,1)S(1)}, bf16[512,1024]{1,0:T(8,128)(2,1)S(1)}, u32[]{:S(2)}, u32[]{:S(2)}) collective-permute-start(bf16[512,1024]{1,0:T(8,128)(2,1)S(1)} %copy-done.179), channel_id=1, source_target_pairs={{0,8},{8,16},{16,24},{1,9},{9,17},{17,25},{2,10},{10,18},{18,26},{... | collective-permute-start | bytes 3145736 | tf_op jit(solution)/shard_map/ppermute | solution.py:121
  607.6 44.7 %collective-permute-start.112 = (bf16[512,1024]{1,0:T(8,128)(2,1)S(1)}, bf16[512,1024]{1,0:T(8,128)(2,1)S(1)}, u32[]{:S(2)}, u32[]{:S(2)}) collective-permute-start(bf16[512,1024]{1,0:T(8,128)(2,1)S(1)} %copy-done.180), channel_id=1, source_target_pairs={{0,16},{8,24},{16,0},{24,8},{1,17},{9,25},{17,1},{25,9},{2,18},{10... | collective-permute-start | bytes 3145736 | tf_op jit(solution)/shard_map/ppermute | solution.py:123
  608.7 22.7 %collective-permute-start.58 = (bf16[128,2048]{1,0:T(8,128)(2,1)S(1)}, bf16[128,2048]{1,0:T(8,128)(2,1)S(1)}, u32[]{:S(2)}, u32[]{:S(2)}) collective-permute-start(bf16[128,2048]{1,0:T(8,128)(2,1)S(1)} %fusion.149), channel_id=1, source_target_pairs={{0,4},{4,0},{1,5},{5,1},{2,6},{6,2},{3,7},{7,3},{8,12},{12,8},{9,1... | collective-permute-start | bytes 1572872 | tf_op jit(solution)/shard_map/ppermute | solution.py:45
  681.4 136.3 %collective-permute-start.102 = (bf16[512,512]{1,0:T(8,128)(2,1)}, bf16[512,512]{1,0:T(8,128)(2,1)}, u32[]{:S(2)}, u32[]{:S(2)}) collective-permute-start(bf16[512,512]{1,0:T(8,128)(2,1)} %convolution_convert_fusion.7), channel_id=1, source_target_pairs={{8,0},{16,8},{24,16},{9,1},{17,9},{25,17},{10,2},{18,10},{26,18},{... | collective-permute-start | bytes 1572872 | tf_op jit(solution)/shard_map/ppermute | solution.py:120
  712.8 95.5 %collective-permute-start.104 = (bf16[512,512]{1,0:T(8,128)(2,1)}, bf16[512,512]{1,0:T(8,128)(2,1)}, u32[]{:S(2)}, u32[]{:S(2)}) collective-permute-start(bf16[512,512]{1,0:T(8,128)(2,1)} %get-tuple-element.397), channel_id=1, source_target_pairs={{24,16},{0,8},{25,17},{1,9},{26,18},{2,10},{27,19},{3,11},{28,20},... | collective-permute-start | bytes 1572872 | tf_op jit(solution)/shard_map/ppermute | solution.py:119
  714.2 100.2 %collective-permute-start.103 = (bf16[512,512]{1,0:T(8,128)(2,1)}, bf16[512,512]{1,0:T(8,128)(2,1)}, u32[]{:S(2)}, u32[]{:S(2)}) collective-permute-start(bf16[512,512]{1,0:T(8,128)(2,1)} %get-tuple-element.398), channel_id=1, source_target_pairs={{0,8},{8,16},{16,24},{1,9},{9,17},{17,25},{2,10},{10,18},{18,26},{... | collective-permute-start | bytes 1572872 | tf_op jit(solution)/shard_map/ppermute | solution.py:121
  748.9 127.0 %collective-permute-start.84 = (bf16[512,896]{1,0:T(8,128)(2,1)}, bf16[512,896]{1,0:T(8,128)(2,1)}, u32[]{:S(2)}, u32[]{:S(2)}) collective-permute-start(bf16[512,896]{1,0:T(8,128)(2,1)} %convolution_convert_fusion.3), channel_id=1, source_target_pairs={{8,0},{16,8},{24,16},{9,1},{17,9},{25,17},{10,2},{18,10},{26,18},{... | collective-permute-start | bytes 2752520 | tf_op jit(solution)/shard_map/ppermute | solution.py:120
  764.7 73.8 %collective-permute-start.86 = (bf16[512,896]{1,0:T(8,128)(2,1)}, bf16[512,896]{1,0:T(8,128)(2,1)}, u32[]{:S(2)}, u32[]{:S(2)}) collective-permute-start(bf16[512,896]{1,0:T(8,128)(2,1)} %get-tuple-element.395), channel_id=1, source_target_pairs={{24,16},{0,8},{25,17},{1,9},{26,18},{2,10},{27,19},{3,11},{28,20},... | collective-permute-start | bytes 2752520 | tf_op jit(solution)/shard_map/ppermute | solution.py:119
  810.3 25.2 %collective-permute-start.105 = (bf16[512,512]{1,0:T(8,128)(2,1)S(1)}, bf16[512,512]{1,0:T(8,128)(2,1)S(1)}, u32[]{:S(2)}, u32[]{:S(2)}) collective-permute-start(bf16[512,512]{1,0:T(8,128)(2,1)S(1)} %fusion.51), channel_id=1, source_target_pairs={{0,16},{8,24},{16,0},{24,8},{1,17},{9,25},{17,1},{25,9},{2,18},{10... | collective-permute-start | bytes 1572872 | tf_op jit(solution)/shard_map/ppermute | solution.py:123
  814.4 61.5 %collective-permute-start.85 = (bf16[512,896]{1,0:T(8,128)(2,1)S(1)}, bf16[512,896]{1,0:T(8,128)(2,1)S(1)}, u32[]{:S(2)}, u32[]{:S(2)}) collective-permute-start(bf16[512,896]{1,0:T(8,128)(2,1)S(1)} %copy-done.181), channel_id=1, source_target_pairs={{0,8},{8,16},{16,24},{1,9},{9,17},{17,25},{2,10},{10,18},{18,26},{... | collective-permute-start | bytes 2752520 | tf_op jit(solution)/shard_map/ppermute | solution.py:121
  817.7 26.5 %collective-permute-start.91 = (bf16[4,2,128,384]{3,2,1,0:T(8,128)(2,1)S(1)}, bf16[4,2,128,384]{3,2,1,0:T(8,128)(2,1)S(1)}, u32[]{:S(2)}, u32[]{:S(2)}) collective-permute-start(bf16[4,2,128,384]{3,2,1,0:T(8,128)(2,1)S(1)} %fusion.102), channel_id=1, source_target_pairs={{0,2},{2,0},{1,3},{3,1},{4,6},{6,4},{5,7},{7,5},{8,10},{10,8},{9,1... | collective-permute-start | bytes 2359304 | tf_op jit(solution)/shard_map/ppermute | solution.py:41
  841.0 41.6 %collective-permute-start.87 = (bf16[512,896]{1,0:T(8,128)(2,1)S(1)}, bf16[512,896]{1,0:T(8,128)(2,1)S(1)}, u32[]{:S(2)}, u32[]{:S(2)}) collective-permute-start(bf16[512,896]{1,0:T(8,128)(2,1)S(1)} %add_convert_fusion.3), channel_id=1, source_target_pairs={{0,16},{8,24},{16,0},{24,8},{1,17},{9,25},{17,1},{25,9},{2,18},{10... | collective-permute-start | bytes 2752520 | tf_op jit(solution)/shard_map/ppermute | solution.py:123
  848.9 48.5 %collective-permute-start.75 = (bf16[2,256,2560]{2,1,0:T(8,128)(2,1)}, bf16[2,256,2560]{2,1,0:T(8,128)(2,1)S(1)}, u32[]{:S(2)}, u32[]{:S(2)}) collective-permute-start(bf16[2,256,2560]{2,1,0:T(8,128)(2,1)} %pad_maximum_fusion.7), channel_id=1, source_target_pairs={{0,2},{2,0},{1,3},{3,1},{4,6},{6,4},{5,7},{7,5},{8,10},{10,8},{9,1... | collective-permute-start | bytes 7864328 | tf_op jit(solution)/shard_map/ppermute | solution.py:41
  852.5 34.2 %collective-permute-start.92 = (bf16[4,128,384]{2,1,0:T(8,128)(2,1)S(1)}, bf16[4,128,384]{2,1,0:T(8,128)(2,1)S(1)}, u32[]{:S(2)}, u32[]{:S(2)}) collective-permute-start(bf16[4,128,384]{2,1,0:T(8,128)(2,1)S(1)} %fusion.168), channel_id=1, source_target_pairs={{0,4},{4,0},{1,5},{5,1},{2,6},{6,2},{3,7},{7,3},{8,12},{12,8},{9,1... | collective-permute-start | bytes 1179656 | tf_op jit(solution)/shard_map/ppermute | solution.py:45
  898.7 30.2 %collective-permute-start.76 = (bf16[128,2560]{1,0:T(8,128)(2,1)S(1)}, bf16[128,2560]{1,0:T(8,128)(2,1)S(1)}, u32[]{:S(2)}, u32[]{:S(2)}) collective-permute-start(bf16[128,2560]{1,0:T(8,128)(2,1)S(1)} %get-tuple-element.253), channel_id=1, source_target_pairs={{0,1},{1,0},{2,3},{3,2},{4,5},{5,4},{6,7},{7,6},{8,9},{9,8},{10,11... | collective-permute-start | bytes 1966088 | tf_op jit(solution)/shard_map/ppermute | solution.py:49
  899.2 29.8 %collective-permute-start.78 = (bf16[128,2560]{1,0:T(8,128)(2,1)S(1)}, bf16[128,2560]{1,0:T(8,128)(2,1)S(1)}, u32[]{:S(2)}, u32[]{:S(2)}) collective-permute-start(bf16[128,2560]{1,0:T(8,128)(2,1)S(1)} %get-tuple-element.254), channel_id=1, source_target_pairs={{0,5},{1,4},{4,1},{5,0},{2,7},{3,6},{6,3},{7,2},{8,13},{9,12},{12,... | collective-permute-start | bytes 1966088 | tf_op jit(solution)/shard_map/ppermute | solution.py:53
  900.4 29.4 %collective-permute-start.77 = (bf16[128,2560]{1,0:T(8,128)(2,1)S(1)}, bf16[128,2560]{1,0:T(8,128)(2,1)S(1)}, u32[]{:S(2)}, u32[]{:S(2)}) collective-permute-start(bf16[128,2560]{1,0:T(8,128)(2,1)S(1)} %fusion.128), channel_id=1, source_target_pairs={{0,4},{4,0},{1,5},{5,1},{2,6},{6,2},{3,7},{7,3},{8,12},{12,8},{9,1... | collective-permute-start | bytes 1966088 | tf_op jit(solution)/shard_map/ppermute | solution.py:45
  930.6 31.9 %collective-permute-start.94 = (bf16[128,512]{1,0:T(8,128)(2,1)S(1)}, bf16[128,512]{1,0:T(8,128)(2,1)S(1)}, u32[]{:S(2)}, u32[]{:S(2)}) collective-permute-start(bf16[128,512]{1,0:T(8,128)(2,1)S(1)} %slice.1538), channel_id=1, source_target_pairs={{0,4},{4,0},{1,5},{5,1},{2,6},{6,2},{3,7},{7,3},{8,12},{12,8},{9,1... | collective-permute-start | bytes 393224 | tf_op jit(solution)/shard_map/ppermute | solution.py:45
  931.9 30.6 %collective-permute-start.95 = (bf16[128,512]{1,0:T(8,128)(2,1)S(1)}, bf16[128,512]{1,0:T(8,128)(2,1)S(1)}, u32[]{:S(2)}, u32[]{:S(2)}) collective-permute-start(bf16[128,512]{1,0:T(8,128)(2,1)S(1)} %slice.1538), channel_id=1, source_target_pairs={{0,5},{1,4},{4,1},{5,0},{2,7},{3,6},{6,3},{7,2},{8,13},{9,12},{12,... | collective-permute-start | bytes 393224 | tf_op jit(solution)/shard_map/ppermute | solution.py:53
  (246 other events, 3067.2 us)

commit v2 on v1

v2 whole, which is shorter than its diff:
```python
import functools

import jax
import jax.numpy as jnp
from jax import lax
from jax.experimental import pallas as pl
from jax.experimental.pallas import tpu as pltpu
from jax.sharding import Mesh, PartitionSpec as P

HEAD = 128
NS = 256
CONV = 4
EPS = 1e-05
ROPE_BASE = 100000000000.0
BF = jnp.bfloat16
F32 = jnp.float32
VMEM = pl.BlockSpec(memory_space=pltpu.VMEM)
SMEM = pl.BlockSpec(memory_space=pltpu.SMEM)


def grant(mebibytes):
    return pltpu.CompilerParams(vmem_limit_bytes=mebibytes << 20)


def dot(left, right):
    return jnp.dot(left, right, preferred_element_type=F32)


def contract(form, left, right):
    return jnp.einsum(form, left, right, preferred_element_type=F32)


def silu_slope(values):
    sigma = jax.nn.sigmoid(values)
    return sigma * (1.0 + values * (1.0 - sigma))


def after(v, *earlier):
    return lax.optimization_barrier((v, earlier))[0]


def norm_rows(values, gain):
    scale = lax.rsqrt(jnp.mean(values * values, axis=-1, keepdims=True) + EPS)
    return values * scale * gain, scale


def norm_rows_back(values, gain, scale, grad):
    normal = values * scale
    weighted = grad * gain
    back = scale * (weighted - normal * jnp.mean(weighted * normal, axis=-1, keepdims=True))
    return back, jnp.sum(grad * normal, axis=0)


def swap_c(v):
    return lax.ppermute(v, "c", [(0, 1), (1, 0)])


def swap_x(v):
    return lax.ppermute(v, "x", [(0, 1), (1, 0)])


def swap_t(v):
    return lax.ppermute(v, "t", [(0, 1), (1, 0)])


def swap_xt(v):
    return lax.ppermute(v, ("x", "t"), [(0, 3), (1, 2), (2, 1), (3, 0)])


def swap_xc(v):
    return lax.ppermute(v, ("x", "c"), [(0, 3), (1, 2), (2, 1), (3, 0)])


def pair(mine, other, index, axis):
    return jnp.where(
        index == 0, jnp.stack([mine, other], axis=axis), jnp.stack([other, mine], axis=axis)
    )


def spread_xc(v, xi, ci):
    v = pair(v, swap_x(v), xi, 0)
    return pair(v, swap_c(v), ci, 1)


def order_t(mine, other, ti, axis=0):
    return jnp.where(
        ti == 0,
        jnp.concatenate([mine, other], axis=axis),
        jnp.concatenate([other, mine], axis=axis),
    )


def act_gather(v, ti):
    rows, n = v.shape
    near = pl.pallas_call(
        place_pair,
        in_specs=[SMEM] + [VMEM] * 4,
        out_specs=VMEM,
        out_shape=jax.ShapeDtypeStruct((4 * rows, n), v.dtype),
        compiler_params=grant(8),
    )(ti.reshape(1), v, swap_t(v), swap_x(v), swap_xt(v))
    return near, swap_c(near)


def z_gather(v):
    return lax.all_gather(v, "z", axis=0, tiled=True)


def z_scatter(v):
    return lax.psum_scatter(v, "z", scatter_dimension=0, tiled=True)


def z_gather_first(v, depth):
    if depth != 4:
        return (lax.all_gather(v, "z", axis=0, tiled=False),)
    return (
        lax.ppermute(v, "z", [(0, 2), (1, 3), (2, 0), (3, 1)]),
        lax.ppermute(v, "z", [(0, 1), (1, 2), (2, 3)]),
        lax.ppermute(v, "z", [(1, 0), (2, 1), (3, 2)]),
    )


def z_gather_rel(v, got, zi, depth):
    if depth != 4:
        return jnp.roll(got[0], -zi, axis=0)
    two, below, above = got
    last = lax.ppermute(two, "z", [(2, 3), (1, 0)])
    return jnp.stack([v, jnp.where(zi == 3, last, above), two, jnp.where(zi == 0, last, below)])


def z_scatter_small(parts, zi, depth):
    if depth != 4:
        return lax.psum_scatter(parts.astype(BF), "z", scatter_dimension=0, tiled=False).astype(F32)

    def part(k):
        return lax.dynamic_index_in_dim(parts, (zi + k) % 4, 0, keepdims=False)

    one, two, three = part(1).astype(BF), part(2), part(3).astype(BF)
    corner = lax.ppermute(jnp.where(zi == 3, one, three), "z", [(3, 2), (0, 1)])
    down = lax.ppermute(three, "z", [(1, 0), (2, 1), (3, 2)])
    up = lax.ppermute(one, "z", [(0, 1), (1, 2), (2, 3)])
    mid = (two + corner.astype(F32)).astype(BF)
    far = lax.ppermute(mid, "z", [(0, 2), (1, 3), (2, 0), (3, 1)])
    return part(0) + down.astype(F32) + up.astype(F32) + far.astype(F32)


def sum_z(v, depth):
    if depth != 4:
        return lax.psum(v, "z")
    v = v + lax.ppermute(v, "z", [(0, 1), (1, 0), (2, 3), (3, 2)])
    return v + lax.ppermute(v, "z", [(0, 2), (2, 0), (1, 3), (3, 1)])


def sum_all(v, depth):
    v = v + swap_c(v)
    v = v + swap_x(v)
    v = v + swap_t(v)
    return sum_z(v, depth)


def sum_group(v):
    v = v + jnp.roll(swap_c(v), 2, axis=0)
    got = swap_x(v)
    v = v + jnp.stack([got[1], got[0], got[3], got[2]])
    return v + swap_t(v)


HIGH = lax.Precision.HIGHEST


def mm(left, right):
    return lax.dot_general(left, right, (((1,), (0,)), ((), ())), preferred_element_type=F32)


def mm_rt(left, right):
    return lax.dot_general(left, right, (((1,), (1,)), ((), ())), preferred_element_type=F32)


def mm_lt(left, right):
    return lax.dot_general(left, right, (((0,), (0,)), ((), ())), preferred_element_type=F32)


def mm_exact(left, right):
    return lax.dot_general(
        left, right, (((1,), (0,)), ((), ())), precision=HIGH, preferred_element_type=F32
    )


def sigmoid(v):
    return 1.0 / (1.0 + jnp.exp(-v))


def tap_masks(seg_col, rows):
    at = lax.broadcasted_iota(jnp.int32, (rows, HEAD), 0)
    masks = [None]
    for offset in range(1, CONV):
        same = (pltpu.roll(seg_col, offset, 0) == seg_col) & (at >= offset)
        masks.append(jnp.where(same, 1.0, 0.0)[:, :1])
    return masks


def filter_rows(values, taps, masks):
    total = taps[CONV : CONV + 1] + taps[0:1] * values
    for offset in range(1, CONV):
        total = total + taps[offset : offset + 1] * (pltpu.roll(values, offset, 0) * masks[offset])
    return total


def filter_rows_back(values, taps, masks, grad):
    rows = values.shape[0]
    tap_grads = [jnp.sum(grad * values, axis=0, keepdims=True)]
    back = taps[0:1] * grad
    for offset in range(1, CONV):
        masked = grad * masks[offset]
        tap_grads.append(
            jnp.sum(masked * pltpu.roll(values, offset, 0), axis=0, keepdims=True)
        )
        back = back + taps[offset : offset + 1] * pltpu.roll(masked, rows - offset, 0)
    tap_grads.append(jnp.sum(grad, axis=0, keepdims=True))
    return back, tap_grads


def causal_of(seg_col, seg_row, rows):
    down = lax.broadcasted_iota(jnp.int32, (rows, rows), 0)
    across = lax.broadcasted_iota(jnp.int32, (rows, rows), 1)
    wide = jnp.broadcast_to(seg_col[:, :1], (rows, rows))
    return (wide == seg_row[0:1]) & (across <= down)


def wide_steps(step_cols, pick_ref, head_ref, rows):
    raw = mm_exact(step_cols, pick_ref[...]) + head_ref[1:2]
    step = jnp.maximum(raw, 0.0) + jnp.log1p(jnp.exp(-jnp.abs(raw)))
    rate = head_ref[0:1] * step
    down = lax.broadcasted_iota(jnp.int32, (rows, rows), 0)
    across = lax.broadcasted_iota(jnp.int32, (rows, rows), 1)
    lower = jnp.where(across <= down, 1.0, 0.0)
    return raw, step, rate, mm_exact(lower, rate)


def decay_of(level, h, causal, rows):
    part = level[:, h * HEAD : (h + 1) * HEAD]
    across = jnp.transpose(part)[0:1]
    diff = jnp.broadcast_to(part[:, :1], (rows, rows)) - across
    return jnp.where(causal, jnp.exp(jnp.where(causal, diff, 0.0)), 0.0)


def rope(v, cosine, sine):
    return v * cosine + pltpu.roll(v, HEAD // 2, 1) * sine


def mixer_forward(heads, mix_ref, row_ref, seg_ref, seg_row_ref, taps_ref, staps_ref, pick_ref,
                  head_ref, cos_ref, sin_ref, gated_ref, square_ref, attended_ref):
    rows = mix_ref.shape[0]
    chans = heads * HEAD
    seg_col, seg_row = seg_ref[...], seg_row_ref[0]
    causal = causal_of(seg_col, seg_row, rows)
    masks = tap_masks(seg_col, rows)
    gate = mix_ref[:, :chans]
    pre = filter_rows(mix_ref[:, chans : 2 * chans], taps_ref[...], masks)
    filtered = pre * sigmoid(pre)
    spre = filter_rows(row_ref[:, : 2 * NS], staps_ref[...], masks)
    sact = (spre * sigmoid(spre)).astype(BF)
    affinity = mm_rt(sact[:, NS:], sact[:, :NS])
    _, step, _, level = wide_steps(row_ref[:, 2 * NS + 2 * HEAD :], pick_ref, head_ref, rows)
    inner = (filtered * step).astype(BF)
    gate_act = gate * sigmoid(gate)
    squares = jnp.zeros((rows, 1), F32)
    for h in range(heads):
        at = slice(h * HEAD, (h + 1) * HEAD)
        mixing = (affinity * decay_of(level, h, causal, rows)).astype(BF)
        scanned = mm(mixing, inner[:, at])
        gated = (scanned + head_ref[2:3, at] * filtered[:, at]) * gate_act[:, at]
        gated_ref[:, at] = gated
        squares = squares + jnp.sum(gated * gated, axis=1, keepdims=True)
    square_ref[0] = jnp.transpose(jnp.broadcast_to(squares, (rows, HEAD)))[:8]
    cosine, sine = cos_ref[...], sin_ref[...]
    query = rope(mix_ref[:, 2 * chans :], cosine, sine).astype(BF)
    keys = rope(row_ref[:, 2 * NS : 2 * NS + HEAD], cosine, sine).astype(BF)
    values = row_ref[:, 2 * NS + HEAD : 2 * NS + 2 * HEAD].astype(BF)
    scores = jnp.where(causal, mm_rt(query, keys) * (HEAD ** -0.5), -1e30)
    raised = jnp.exp(scores - jnp.max(scores, axis=1, keepdims=True))
    shares = (raised / jnp.sum(raised, axis=1, keepdims=True)).astype(BF)
    attended_ref[...] = mm(shares, values).astype(BF)


def mixer_backward(heads, total_chans, mix_ref, row_ref, seg_ref, seg_row_ref, taps_ref, staps_ref,
                   pick_ref, head_ref, cos_ref, sin_ref, slot_ref, grad_ref, gated_ref, scale_ref,
                   gain_ref, sum_ref, mix_low_ref, kv_low_ref, state_ref, small_ref, staps_out_ref):
    rows = mix_ref.shape[0]
    chans = heads * HEAD
    seg_col, seg_row = seg_ref[...], seg_row_ref[0]
    causal = causal_of(seg_col, seg_row, rows)
    masks = tap_masks(seg_col, rows)
    gate = mix_ref[:, :chans]
    filter_input = mix_ref[:, chans : 2 * chans]
    taps, staps = taps_ref[...], staps_ref[...]
    pre = filter_rows(filter_input, taps, masks)
    sig = sigmoid(pre)
    filtered = pre * sig
    state_raw = row_ref[:, : 2 * NS]
    spre = filter_rows(state_raw, staps, masks)
    ssig = sigmoid(spre)
    sact = (spre * ssig).astype(BF)
    affinity = mm_rt(sact[:, NS:], sact[:, :NS])
    raw, step, rate, level = wide_steps(row_ref[:, 2 * NS + 2 * HEAD :], pick_ref, head_ref, rows)
    inner = (filtered * step).astype(BF)
    gsig = sigmoid(gate)
    gate_act = gate * gsig
    norm_grad = grad_ref[:, :chans]
    scale = jnp.transpose(scale_ref[0])[:, :1]
    normal = gated_ref[...] * scale
    mean = jnp.transpose(sum_ref[0])[:, :1] * (1.0 / total_chans)
    gated_grad = scale * (norm_grad * gain_ref[0:1] - normal * mean)
    mix_state_grad = gated_grad * gate_act
    scanned_low = mix_state_grad.astype(BF)
    skip = head_ref[2:3]
    state_mix, inner_grads, level_grads, step_sums = [], [], [], []
    affinity_grad = jnp.zeros((rows, rows), F32)
    for h in range(heads):
        at = slice(h * HEAD, (h + 1) * HEAD)
        decay = decay_of(level, h, causal, rows)
        mixing_full = affinity * decay
        mixing = mixing_full.astype(BF)
        state_mix.append(mm(mixing, inner[:, at]) + skip[:, at] * filtered[:, at])
        mixing_grad = mm_rt(scanned_low[:, at], inner[:, at])
        inner_grad = mm_lt(mixing, scanned_low[:, at])
        flow = mixing_grad * mixing_full
        change = jnp.sum(flow - jnp.transpose(flow), axis=1, keepdims=True)
        level_grads.append(jnp.broadcast_to(change, (rows, HEAD)))
        affinity_grad = affinity_grad + mixing_grad * decay
        inner_grads.append(inner_grad)
        reach = jnp.sum(inner_grad * filtered[:, at], axis=1, keepdims=True)
        step_sums.append(jnp.broadcast_to(reach, (rows, HEAD)))
    state_mix = jnp.concatenate(state_mix, axis=1)
    inner_grad = jnp.concatenate(inner_grads, axis=1)
    mix_low_ref[:, :chans] = (
        gated_grad * state_mix * (gsig * (1.0 + gate * (1.0 - gsig)))
    ).astype(BF)
    down = lax.broadcasted_iota(jnp.int32, (rows, rows), 0)
    across = lax.broadcasted_iota(jnp.int32, (rows, rows), 1)
    upper = jnp.where(across >= down, 1.0, 0.0)
    rate_grad = mm_exact(upper, jnp.concatenate(level_grads, axis=1))
    step_grad = rate_grad * head_ref[0:1] + jnp.concatenate(step_sums, axis=1)
    step_pre_grad = step_grad * sigmoid(raw)
    filtered_grad = skip * mix_state_grad + inner_grad * step
    input_grad, tap_grads = filter_rows_back(
        filter_input, taps, masks, filtered_grad * (sig * (1.0 + pre * (1.0 - sig)))
    )
    mix_low_ref[:, chans : 2 * chans] = input_grad.astype(BF)
    extra = [
        jnp.sum(norm_grad * normal, axis=0, keepdims=True),
        jnp.sum(mix_state_grad * filtered, axis=0, keepdims=True),
        jnp.sum(rate_grad * rate, axis=0, keepdims=True),
        jnp.sum(step_pre_grad, axis=0, keepdims=True),
    ]
    small_ref[0] = jnp.zeros(small_ref.shape[1:], F32)
    for i, v in enumerate(tap_grads + extra):
        small_ref[0, i : i + 1] = v
    low = affinity_grad.astype(BF)
    read_grad = mm(low, sact[:, :NS])
    write_grad = mm_lt(low, sact[:, NS:])
    act_grad = jnp.concatenate([write_grad, read_grad], axis=1)
    state_grad, stap_grads = filter_rows_back(
        state_raw, staps, masks, act_grad * (ssig * (1.0 + spre * (1.0 - ssig)))
    )
    state_ref[...] = state_grad
    staps_out_ref[0] = jnp.zeros(staps_out_ref.shape[1:], F32)
    for i, v in enumerate(stap_grads):
        staps_out_ref[0, i : i + 1] = v
    cosine, sine = cos_ref[...], sin_ref[...]
    query = rope(mix_ref[:, 2 * chans :], cosine, sine).astype(BF)
    keys = rope(row_ref[:, 2 * NS : 2 * NS + HEAD], cosine, sine).astype(BF)
    values = row_ref[:, 2 * NS + HEAD : 2 * NS + 2 * HEAD].astype(BF)
    root = HEAD ** -0.5
    scores = jnp.where(causal, mm_rt(query, keys) * root, -1e30)
    raised = jnp.exp(scores - jnp.max(scores, axis=1, keepdims=True))
    shares = raised / jnp.sum(raised, axis=1, keepdims=True)
    attend_grad = grad_ref[:, chans:].astype(BF)
    values_grad = mm_lt(shares.astype(BF), attend_grad)
    shares_grad = mm_rt(attend_grad, values)
    scores_low = (
        shares * (shares_grad - jnp.sum(shares_grad * shares, axis=1, keepdims=True))
    ).astype(BF)
    query_grad = mm(scores_low, keys) * root
    keys_grad = mm_lt(scores_low, query) * root
    mix_low_ref[:, 2 * chans :] = rope(query_grad, cosine, -sine).astype(BF)
    kv_low_ref[:, :HEAD] = rope(keys_grad, cosine, -sine).astype(BF)
    kv_low_ref[:, HEAD : 2 * HEAD] = values_grad.astype(BF)
    kv_low_ref[:, 2 * HEAD :] = mm(step_pre_grad.astype(BF), slot_ref[...]).astype(BF)


def over_groups(kernel, groups, rows, args, whole, outs):
    def spec(shape):
        if len(shape) == 3:
            return pl.BlockSpec((1,) + shape[1:], lambda g: (g, 0, 0))
        return pl.BlockSpec((rows, shape[1]), lambda g: (g, 0))

    def fixed(shape):
        return pl.BlockSpec(shape, lambda g: (0, 0))

    specs = [
        fixed(v.shape) if w else spec(v.shape) for v, w in zip(args, whole)
    ]
    return pl.pallas_call(
        kernel,
        grid=(groups,),
        in_specs=specs,
        out_specs=[spec(o.shape) for o in outs],
        out_shape=outs,
        compiler_params=grant(24),
    )(*args)


def place_pair(ti_ref, own_ref, t_ref, x_ref, xt_ref, out_ref):
    rows = own_ref.shape[0]
    at = ti_ref[0]
    for i, ref in ((at, own_ref), (1 - at, t_ref), (2 + at, x_ref), (3 - at, xt_ref)):
        out_ref[pl.ds(pl.multiple_of(i * rows, rows), rows)] = ref[...]


def place_rows(at_ref, own_ref, x_ref, c_ref, xc_ref, out_ref, small_ref):
    z, me = at_ref[0], at_ref[1]
    depth, rows = out_ref.shape[0], out_ref.shape[2]
    for k in range(depth):
        to = lax.rem(z + k, depth)
        for offset, src in ((0, own_ref), (2, x_ref), (1, c_ref), (3, xc_ref)):
            out_ref[to, me ^ offset] = src[k, :rows]
            small_ref[to, me ^ offset] = src[k, rows:]


def times(rows, w):
    return tuple(dot(r, w) for r in rows)


def grads(left, right):
    near, far = (contract("tc,tk->ck", a, b) for a, b in zip(left, right))
    return (near + far).astype(BF)


def split_kernel(ti_ref, total_ref, got_ref, mine_ref, t_ref, x_ref, xt_ref):
    rows = mine_ref.shape[0]
    at = ti_ref[0]

    def part(i):
        where = pl.ds(pl.multiple_of(i * rows, rows), rows)
        return total_ref[where] + got_ref[where].astype(F32)

    mine_ref[...] = part(at)
    t_ref[...] = part(1 - at).astype(BF)
    x_ref[...] = part(2 + at).astype(BF)
    xt_ref[...] = part(3 - at).astype(BF)


def split_rows(keep, send, ti):
    got = swap_c(send.astype(BF))
    count, width = keep.shape
    rows, tile = count // 4, 512
    part = pl.BlockSpec((rows, tile), lambda j: (0, j))
    full = pl.BlockSpec((count, tile), lambda j: (0, j))
    return pl.pallas_call(
        split_kernel,
        grid=(width // tile,),
        in_specs=[SMEM, full, full],
        out_specs=[part] * 4,
        out_shape=[jax.ShapeDtypeStruct((rows, width), F32)]
        + [jax.ShapeDtypeStruct((rows, width), BF)] * 3,
        compiler_params=grant(8),
    )(ti.reshape(1), keep, got)


def join_rows(mine, to_t, to_x, to_xt):
    got = (swap_t(to_t), swap_x(to_x), swap_xt(to_xt))
    return mine + got[0].astype(F32) + got[1].astype(F32) + got[2].astype(F32)


def split_back(terms, ti):
    keep, send = (sum(contract("tk,ck->tc", a[i], w) for a, w in terms) for i in (0, 1))
    return split_rows(keep, send, ti)


def times_back(terms, ti):
    return join_rows(*split_back(terms, ti))


def turned(block):
    return jnp.transpose(block.astype(F32)).astype(BF)


def prepare_kernel(plan, xi_ref, *refs):
    sources, keep_ref, send_ref = refs[:-2], refs[-2], refs[-1]
    first = xi_ref[0] == 0
    for c in range(2):
        at = 0
        for ref, is_turned in zip(sources, plan):
            if is_turned:
                n = ref.shape[0] // 4
                low, high = (turned(ref[(x * 2 + c) * n : (x * 2 + c + 1) * n]) for x in range(2))
            else:
                n = ref.shape[1] // 4
                low, high = (ref[:, (x * 2 + c) * n : (x * 2 + c + 1) * n] for x in range(2))
            keep_ref[c, :, at : at + n] = jnp.where(first, low, high)
            send_ref[c, :, at : at + n] = jnp.where(first, high, low)
            at += n


def middle_kernel(ci_ref, keep_ref, got_ref, keep_out, send_out):
    c = ci_ref[0]
    for i, ref in enumerate((keep_ref, got_ref)):
        keep_out[i] = ref[c]
        send_out[i] = ref[1 - c]


def end_kernel(at_ref, keep_ref, got_ref, out_ref):
    x, c = at_ref[0], at_ref[1]
    for i, ref in enumerate((keep_ref, got_ref)):
        out_ref[x, c ^ i] = ref[0]
        out_ref[1 - x, c ^ i] = ref[1]


def simple(kernel, args, outs, scalars=1, grant_of=8):
    single = not isinstance(outs, list)
    return pl.pallas_call(
        kernel,
        in_specs=[SMEM] * scalars + [VMEM] * (len(args) - scalars),
        out_specs=VMEM if single else [VMEM] * len(outs),
        out_shape=outs,
        compiler_params=grant(grant_of),
    )(*args)


def middle(keep, send, xi, ci):
    shape = jax.ShapeDtypeStruct(keep.shape, BF)
    keep, send = simple(middle_kernel, (ci.reshape(1), keep, swap_x(send)), [shape, shape])
    return keep, swap_c(send)


def prepare(sources, plan, xi):
    rows = [s.shape[1] if t else s.shape[0] for s, t in zip(sources, plan)][0]
    wide = sum((s.shape[0] if t else s.shape[1]) // 4 for s, t in zip(sources, plan))
    shape = jax.ShapeDtypeStruct((2, rows, wide), BF)
    return simple(
        functools.partial(prepare_kernel, plan), (xi.reshape(1), *sources), [shape, shape]
    )


def deal_out(keep, send, xi, ci):
    keep, got = middle(keep, send, xi, ci)
    out = jax.ShapeDtypeStruct((2,) + keep.shape, BF)
    return simple(end_kernel, (jnp.stack([xi, ci]), keep, got), out).reshape(
        -1, keep.shape[-1]
    )


def start_kernel(xi_ref, blocks_ref, keep_ref, send_ref):
    keep_ref[...] = blocks_ref[xi_ref[0]]
    send_ref[...] = blocks_ref[1 - xi_ref[0]]


def finish_kernel(plan, at_ref, keep_ref, got_ref, *outs):
    x, c = at_ref[0], at_ref[1]
    for q in range(4):
        own = c == q % 2
        offset = x ^ (q // 2)
        at = 0
        for ref, kind in zip(outs, plan):
            n = (ref.shape[0] if kind == "turned" else ref.shape[-1]) // 4
            for i in range(2 if kind == "two" else 1):
                block = jnp.where(
                    own, keep_ref[offset, :, at : at + n], got_ref[offset, :, at : at + n]
                ).astype(F32)
                if kind == "turned":
                    ref[q * n : (q + 1) * n] = jnp.transpose(block)
                elif kind == "two":
                    ref[:, i, q * n : (q + 1) * n] = block
                else:
                    ref[:, q * n : (q + 1) * n] = block
                at += n


def deal_back(summed, plan, widths, xi, ci):
    shard = summed.shape[0] // 4
    blocks = summed.reshape(2, 2, shard, -1)
    shape = jax.ShapeDtypeStruct(blocks.shape[1:], BF)
    keep, send = simple(start_kernel, (xi.reshape(1), blocks), [shape, shape])
    keep, got = middle(keep, send, xi, ci)
    shapes = {"turned": lambda n: (4 * n, shard), "two": lambda n: (shard, 2, 4 * n)}
    outs = [
        jax.ShapeDtypeStruct(shapes.get(k, lambda n: (shard, 4 * n))(n), F32)
        for n, k in zip(widths, plan)
    ]
    return simple(
        functools.partial(finish_kernel, plan), (jnp.stack([xi, ci]), keep, got), outs
    )


def kv_first_kernel(ci_ref, part_ref, keep_ref, send_ref):
    c = ci_ref[0]
    for k in range(part_ref.shape[0]):
        for x in range(2):
            keep_ref[x, k] = part_ref[k, x, c]
            send_ref[x, k] = part_ref[k, x, 1 - c]


def kv_second_kernel(xi_ref, keep_ref, got_ref, keep_out, send_out):
    x = xi_ref[0]
    keep_out[...] = keep_ref[x].astype(F32) + got_ref[x].astype(F32)
    send_out[...] = (keep_ref[1 - x].astype(F32) + got_ref[1 - x].astype(F32)).astype(BF)


def on_device(
    depth,
    tokens,
    segments,
    cotangent,
    first_gain,
    mixer_in,
    state_weight,
    step_weight,
    filter_taps,
    state_taps,
    decay_log,
    step_bias,
    skip_gain,
    gate_gain,
    mixer_out,
    query_weight,
    key_value_matrix,
    attend_out,
    second_gain,
    gate_up,
    down_weight,
):
    zi, xi = lax.axis_index("z"), lax.axis_index("x")
    ci, ti = lax.axis_index("c"), lax.axis_index("t")
    me = xi * 2 + ci
    rows, width = tokens.shape
    group = segments.shape[0]
    shard = mixer_in.shape[0]
    block = 4 * shard
    heads_in = decay_log.shape[0]
    heads = heads_in // 4
    chans = heads * HEAD
    total_chans = 2 * heads_in * HEAD
    ffn = gate_up.shape[2] // 4
    count = 4 * group
    scale = HEAD ** (-0.5)

    pieces = [first_gain, second_gain, filter_taps, state_taps, gate_gain, segments]
    sizes = [p.size for p in pieces]
    step_pad = jnp.pad(step_weight, ((0, 0), (0, 128 - heads_in)))
    row_pack = jnp.concatenate(
        [state_weight, key_value_matrix.reshape(shard, -1), step_pad], axis=1
    )
    row_wide = row_pack.shape[1]
    vec = jnp.concatenate([p.astype(BF).reshape(-1) for p in pieces])
    vec = jnp.pad(vec, (0, 16 * row_wide - vec.size)).reshape(16, row_wide)
    row_own = jnp.concatenate([row_pack, vec])
    row_got = z_gather_first(row_own, depth)

    first_plan = (True, True, False, False, False)
    first_keep, first_send = prepare(
        (mixer_out, attend_out, mixer_in[:, 0], mixer_in[:, 1], query_weight), first_plan, xi
    )
    first_keep = after(first_keep, *row_got)
    first_mine = deal_out(first_keep, first_send, xi, ci)
    wide = chans + HEAD

    row_z = z_gather_rel(row_own, row_got, zi, depth)
    first_mine = after(first_mine, row_z)
    first_w = z_gather(first_mine)
    row_x = swap_x(row_z)
    row_full, small = simple(
        place_rows,
        (jnp.stack([zi, me]), row_z, row_x, swap_c(row_z), swap_c(row_x)),
        [
            jax.ShapeDtypeStruct((depth, 4, shard, row_wide), BF),
            jax.ShapeDtypeStruct((depth, 4, 16, row_wide), BF),
        ],
        grant_of=16,
    )
    row_full = row_full.reshape(width, row_wide)
    kv_at = 2 * NS
    state_full = row_full[:, :kv_at]
    small = small.reshape(depth, 4, -1)
    offsets = [sum(sizes[:i]) for i in range(6)]
    cut = [small[:, :, at : at + size] for at, size in zip(offsets, sizes)]
    seg_all = lax.dynamic_index_in_dim(cut[5], zi, 0, keepdims=False).astype(F32)
    segs = jnp.stack(
        [lax.dynamic_index_in_dim(seg_all, me ^ k, 0, keepdims=False) for k in (0, 2, 1, 3)]
    )
    first_full = cut[0].reshape(-1).astype(F32)
    second_full = cut[1].reshape(-1).astype(F32)
    eighth = filter_taps.shape[2]
    taps_all = jnp.transpose(
        cut[2].reshape(depth, 4, CONV + 1, heads_in, eighth), (2, 3, 0, 1, 4)
    ).reshape(CONV + 1, 4, chans)
    taps = lax.dynamic_index_in_dim(taps_all, me, 1, keepdims=False).astype(F32)
    staps = (
        jnp.transpose(cut[3].reshape(depth, 4, CONV + 1, -1), (2, 0, 1, 3))
        .reshape(CONV + 1, 2 * NS)
        .astype(F32)
    )
    gate_all = jnp.transpose(
        cut[4].reshape(depth, 4, heads_in, eighth), (2, 0, 1, 3)
    ).reshape(4, chans)
    gate_gain_mine = lax.dynamic_index_in_dim(gate_all, me, 0, keepdims=False).astype(F32)

    order = jnp.arange(group)
    live_all = (segs >= 0).astype(F32)
    same = (segs[:, :, None] == segs[:, None, :]) & (order[None, None, :] <= order[None, :, None])
    position = jnp.sum(same.astype(F32), axis=2) - 1.0
    half = HEAD // 2
    frequency = ROPE_BASE ** (-2.0 * jnp.arange(half).astype(F32) / HEAD)
    angle = position.reshape(count, 1) * frequency[None, :]
    cosine, sine = jnp.cos(angle), jnp.sin(angle)
    cosine = jnp.concatenate([cosine, cosine], axis=1)
    sine = jnp.concatenate([-sine, sine], axis=1)
    live_mine = lax.dynamic_slice_in_dim(
        (segments >= 0).astype(F32), ti * rows, rows
    )[:, None]
    seg_cols = jnp.broadcast_to(segs.reshape(count, 1), (count, HEAD))
    seg_rows = jnp.broadcast_to(segs[:, None, :], (4, 8, group))

    def halves(v):
        n = v.shape[0] // 2
        return v[:n], v[n:]

    my_log = lax.dynamic_slice_in_dim(decay_log, me * heads, heads)
    my_bias = lax.dynamic_slice_in_dim(step_bias, me * heads, heads)
    my_skip = lax.dynamic_slice_in_dim(skip_gain, me * heads, heads)
    head_rows = jnp.pad(
        jnp.repeat(jnp.stack([-jnp.exp(my_log), my_bias, my_skip]), HEAD, axis=1), ((0, 5), (0, 0))
    )
    lane_head = me * heads + jnp.arange(chans) // HEAD
    picker = (jnp.arange(128)[:, None] == lane_head[None, :]).astype(F32)
    first_lane = (jnp.arange(chans) % HEAD == 0)[:, None]
    slots = ((jnp.arange(128)[None, :] == lane_head[:, None]) & first_lane).astype(BF)
    taps_pad = jnp.pad(taps, ((0, 3), (0, 0)))
    staps_pad = jnp.pad(staps, ((0, 3), (0, 0)))
    gain_pad = jnp.pad(gate_gain_mine[None], ((0, 7), (0, 0)))

    resid = tokens.astype(F32)
    normed_input, scale_one = norm_rows(resid, first_full)
    normed_low = normed_input.astype(BF)
    normed = act_gather(normed_low, ti)
    then_plan = (False, False, True)
    then_keep, then_send = prepare(
        (gate_up[:, 0], gate_up[:, 1], down_weight), then_plan, xi
    )
    then_send = after(then_send, normed[0], row_x)
    then_mine = deal_out(then_keep, then_send, xi, ci)
    gu_w, down_w = z_gather(then_mine[:, : 2 * ffn]), z_gather(then_mine[:, 2 * ffn :])
    grad_out = cotangent.astype(F32)
    feed_low = after((live_mine * grad_out).astype(BF), then_mine)
    feed_grad = act_gather(feed_low, ti)
    row_out = times(normed, row_full)
    first_w = after(first_w, row_out)
    out_w, mix_w = first_w[:, :wide], first_w[:, wide:]
    mix_out = times(normed, mix_w)

    per_half = list(
        zip(mix_out, row_out, halves(seg_cols), halves(seg_rows), halves(cosine), halves(sine))
    )
    near_far, whole = [], (False,) * 4 + (True,) * 4 + (False,) * 2
    for m, r, sc, sr, co, si in per_half:
        near_far.append((m, r, sc, sr, taps_pad, staps_pad, picker, head_rows, co, si))
    ahead = [
        over_groups(
            functools.partial(mixer_forward, heads),
            2,
            group,
            common,
            whole,
            [
                jax.ShapeDtypeStruct((count // 2, chans), F32),
                jax.ShapeDtypeStruct((2, 8, group), F32),
                jax.ShapeDtypeStruct((count // 2, HEAD), BF),
            ],
        )
        for common in near_far
    ]
    squares = jnp.concatenate([ahead[0][1], ahead[1][1]])
    gate_scale = halves(lax.rsqrt(sum_group(squares) / total_chans + EPS))
    gate_normal = [
        a[0] * g[:, 0].reshape(count // 2, 1) for a, g in zip(ahead, gate_scale)
    ]

    out_w = after(out_w, feed_grad)
    branch = [
        jnp.concatenate([(n * gate_gain_mine).astype(BF), a[2]], axis=1)
        for n, a in zip(gate_normal, ahead)
    ]
    hidden = resid + live_mine * times_back([(branch, out_w)], ti)
    second, scale_two = norm_rows(hidden, second_full)

    second_all = act_gather(second.astype(BF), ti)
    gu_low, activation = [], []
    for second_half, feed_half in zip(second_all, feed_grad):
        gate_up_out = dot(second_half, gu_w)
        gate_part, up_part = gate_up_out[:, :ffn], gate_up_out[:, ffn:]
        act_grad = dot(feed_half, down_w)
        act = jax.nn.silu(gate_part)
        activation.append((act * up_part).astype(BF))
        gu_low.append(
            jnp.concatenate([act_grad * up_part * silu_slope(gate_part), act_grad * act], axis=1)
            .astype(BF)
        )
    down_sum = z_scatter(grads(feed_grad, activation))
    gu_sum = z_scatter(grads(second_all, gu_low))
    second_split = split_back([(gu_low, gu_w)], ti)
    second_grad = join_rows(*second_split)
    feed_split = split_back([(after(activation, second_split), down_w)], ti)
    hidden_part, second_gain_grad = norm_rows_back(hidden, second_full, scale_two, second_grad)
    hidden_grad = grad_out + hidden_part
    mix_grad = act_gather((live_mine * hidden_grad).astype(BF), ti)
    feed_split = after(feed_split, mix_grad[0])
    output = (hidden + live_mine * join_rows(*feed_split)).astype(BF)
    (down_weight_grad,) = deal_back(
        after(down_sum, mix_grad[0]), ("turned",), (ffn,), xi, ci
    )
    branch_grad = times(mix_grad, after(out_w, feed_split))
    out_term = grads(mix_grad, branch)
    out_sum = z_scatter(out_term)

    inner_sum = jnp.concatenate(
        [
            jnp.sum(b[:, :chans] * gate_gain_mine * n, axis=-1).reshape(2, 1, group)
            for b, n in zip(branch_grad, gate_normal)
        ]
    )
    inner_sum = sum_group(jnp.broadcast_to(inner_sum, (4, 8, group)))
    inner_sum = halves(after(inner_sum, out_term))
    inner_sum = (inner_sum[0], after(inner_sum[1], gu_sum))
    back = [
        over_groups(
            functools.partial(mixer_backward, heads, total_chans),
            2,
            group,
            common + (slots, branch_grad[i], ahead[i][0], gate_scale[i], gain_pad, inner_sum[i]),
            whole + (True, False, False, False, True, False),
            [
                jax.ShapeDtypeStruct((count // 2, 2 * chans + HEAD), BF),
                jax.ShapeDtypeStruct((count // 2, 3 * HEAD), BF),
                jax.ShapeDtypeStruct((count // 2, 2 * NS), F32),
                jax.ShapeDtypeStruct((2, 16, chans), F32),
                jax.ShapeDtypeStruct((2, 8, 2 * NS), F32),
            ],
        )
        for i, common in enumerate(near_far)
    ]
    mix_low, kv_low, state_raw_grad, small_rows, small_state = zip(*back)
    normed_late = after(normed, output, down_weight_grad)
    mix_term = grads(normed_late, mix_low)
    mix_sum = z_scatter(mix_term)

    small_rows = jnp.concatenate(small_rows)
    small_state = jnp.concatenate(small_state)
    state_taps_grad = jnp.sum(small_state, axis=0)[: CONV + 1]
    state_near = after(state_raw_grad[0], mix_term)
    state_split = split_rows(state_near, state_raw_grad[1], ti)
    summed_split = split_back(
        [(after(mix_low, state_split), mix_w), (kv_low, row_full[:, kv_at:])], ti
    )
    head_rows_sum = jnp.sum(after(small_rows, summed_split), axis=0)
    head_all = spread_xc(sum_z(head_rows_sum, depth), xi, ci).reshape(4, 16, chans)
    state_low = join_rows(*state_split).astype(BF)
    summed = join_rows(*summed_split)
    (gate_up_grad,) = deal_back(after(gu_sum, summed_split), ("two",), (ffn,), xi, ci)
    mixer_out_grad, attend_out_grad = deal_back(
        after(out_sum, summed_split), ("turned",) * 2, (chans, HEAD), xi, ci
    )
    state_low_all = act_gather(state_low, ti)
    normed_grad = summed + contract("tn,cn->tc", state_low, state_full)
    resid_part, first_gain_grad = norm_rows_back(resid, first_full, scale_one, normed_grad)
    tokens_grad = hidden_grad + resid_part

    mixer_in_grad, query_weight_grad = deal_back(
        mix_sum, ("two", ""), (chans, HEAD), xi, ci
    )
    kv_part = grads(normed, after(kv_low, summed_split)).reshape(depth, 2, 2, shard, 3 * HEAD)
    shape = jax.ShapeDtypeStruct((2, depth, shard, 3 * HEAD), BF)
    kv_keep, kv_send = simple(kv_first_kernel, (ci.reshape(1), kv_part), [shape, shape])
    kv_keep, kv_send = simple(
        kv_second_kernel,
        (xi.reshape(1), kv_keep, swap_c(kv_send)),
        [jax.ShapeDtypeStruct(shape.shape[1:], F32), jax.ShapeDtypeStruct(shape.shape[1:], BF)],
    )
    kv_sum = kv_keep + swap_x(kv_send).astype(F32)
    state_part = grads(normed, state_low_all).reshape(depth, 4, shard, 2 * NS)
    state_part = lax.dynamic_slice(
        state_part, (0, me, 0, ti * NS), (depth, 1, shard, NS)
    )[:, 0].astype(F32)
    row_part = jnp.concatenate([kv_sum, state_part], axis=2)
    row_sum = z_scatter_small(row_part, zi, depth)
    keys_values_grad = row_sum[:, : 2 * HEAD].reshape(shard, 2, HEAD)
    step_weight_grad = row_sum[:, 2 * HEAD : 2 * HEAD + heads_in]
    state_mine = row_sum[:, 3 * HEAD :]
    state_weight_grad = order_t(
        state_mine, swap_t(state_mine.astype(BF)).astype(F32), ti, axis=1
    )

    dp_at = zi * 4 + me
    parts = [second_gain_grad, state_taps_grad.reshape(-1), first_gain_grad]
    packed = sum_all(jnp.concatenate(parts).reshape(-1, 128), depth).reshape(-1)
    second_mine = lax.dynamic_slice_in_dim(packed, dp_at * shard, shard)
    first_mine = lax.dynamic_slice_in_dim(
        packed[packed.size - width :], dp_at * shard, shard
    )
    state_shard = state_taps.shape[1]
    state_taps_mine = lax.dynamic_slice_in_dim(
        packed[width : packed.size - width].reshape(CONV + 1, 2 * NS),
        dp_at * state_shard,
        state_shard,
        1,
    )
    by_head = jnp.transpose(
        head_all[:, :9].reshape(4, 9, heads, HEAD), (1, 0, 2, 3)
    ).reshape(9, heads_in, HEAD)
    taps_out = lax.dynamic_slice_in_dim(by_head[: CONV + 1], dp_at * eighth, eighth, 2)
    gate_out = lax.dynamic_slice_in_dim(by_head[5], dp_at * eighth, eighth, 1)
    return (
        output,
        tokens_grad,
        first_mine,
        mixer_in_grad,
        state_weight_grad,
        step_weight_grad,
        taps_out,
        state_taps_mine,
        by_head[7, :, 0],
        by_head[8, :, 0],
        jnp.sum(by_head[6], axis=1),
        gate_out,
        mixer_out_grad,
        query_weight_grad,
        keys_values_grad,
        attend_out_grad,
        second_mine,
        gate_up_grad,
        down_weight_grad,
    )


def solution(mesh):
    dp, tensor = mesh.shape["dp"], mesh.shape["tensor"]
    depth = dp // 4
    split = Mesh(mesh.devices.reshape(depth, 2, 2, tensor), ("z", "x", "c", "t"))
    D = ("z", "x", "c")
    T = "t"
    R = ("z", "x", "c", "t")
    weights = (
        P(D),
        P(D, None, T),
        P(D, None),
        P(D, T),
        P(None, T, D),
        P(None, D),
        P(T),
        P(T),
        P(T),
        P(T, D),
        P(T, D),
        P(D, T),
        P(D, None, T),
        P(T, D),
        P(D),
        P(D, None, T),
        P(T, D),
    )

    def run(*args):
        return on_device(depth, *args)

    return jax.shard_map(
        run,
        mesh=split,
        in_specs=(P(R, None), P(D), P(R, None)) + weights,
        out_specs=(P(R, None), P(R, None)) + weights,
        check_vma=False,
    )
```

time: 1020 us -> 636 us (0.62); the launches traced: 1000 us -> 628 us
  waiting for transfers between devices: 401 us -> 232 us
  starting transfers between devices: 222 us -> 99.8 us
  other arithmetic: 131 us -> 32.4 us
  local copies, waits for them, and re-layouts: 141 us -> 65.3 us
  Pallas kernels: 0 us -> 64.3 us
  matrix products: 98.7 us -> 118 us
  between operations: 5.16 us -> 16.9 us
    ppermute x54 -> x12, waiting for transfers between devices: 246 us -> 19.8 us  [the longest x1 9.64 us: z_gather_first(): lax.ppermute(v, 'z', [(0, 1), (1, 2), (2, 3)])]
    ppermute x54 -> x12, starting transfers between devices: 151 us -> 22.2 us  [the longest x2 5.04 us: sum_z(): return v + lax.ppermute(v, 'z', [(0, 2), (2, 0), (1, 3), (3, 1)])]
    ppermute x23 -> x22, waiting for transfers between devices: 31.2 us -> 106 us  [swap_x(): return lax.ppermute(v, 'x', [(0, 1), (1, 0)])]
    ppermute x14, waiting for transfers between devices: 103 us -> 34.5 us  [swap_t(): return lax.ppermute(v, 't', [(0, 1), (1, 0)])]
    pallas_call x0 -> x35, Pallas kernels: none -> 64.3 us  [the longest x4 29.2 us: over_groups(): pl.pallas_call(kernel, grid=(groups,), in_specs=specs, out_specs=[spec(o....]
    ppermute x9 -> x10, waiting for transfers between devices: 21.5 us -> 59.3 us  [swap_xt(): return lax.ppermute(v, ('x', 't'), [(0, 3), (1, 2), (2, 1), (3, 0)])]
    another operation x29 -> x10, other arithmetic: 40.8 us -> 3.5 us  [the longest x3 3.23 us: z_gather_rel(): jnp.stack([v, jnp.where(zi == 3, last, above), two, jnp.where(zi == 0, la...]
    dot_general x4 -> x10, matrix products: 16.4 us -> 43.8 us  [dot(): return jnp.dot(left, right, preferred_element_type=F32)]
  transfers between devices with their start and end apart: 123 -> 88, of which waited for: 48 -> 37; matrix products, arithmetic and copies ran while one was open for 32% -> 25% of each run, Pallas kernels for 0% -> 10%
where the time goes in v2:
time: 636 us; the launch traced here: 628 us
  waiting for transfers between devices  232 us (36%)
  matrix products  118 us (19%)
  starting transfers between devices  99.8 us (16%)
  local copies, waits for them, and re-layouts  65.3 us (10%)
  Pallas kernels  64.3 us (10%)
  other arithmetic  32.4 us (5%)
  between operations  16.9 us (3%)
    ppermute x22, waiting for transfers between devices, swap_x(): return lax.ppermute(v, 'x', [(0, 1), (1, 0)])  106 us
    dot_general x23, matrix products, contract(): return jnp.einsum(form, left, right, preferred_element_type=F32)  73.8 us
    ppermute x10, waiting for transfers between devices, swap_xt(): return lax.ppermute(v, ('x', 't'), [(0, 3), (1, 2), (2, 1), (3, 0)])  59.3 us
    dot_general x10, matrix products, dot(): return jnp.dot(left, right, preferred_element_type=F32)  43.8 us
    unnamed x316, local copies, waits for them, and re-layouts  39.1 us
    ppermute x14, waiting for transfers between devices, swap_t(): return lax.ppermute(v, 't', [(0, 1), (1, 0)])  34.5 us
    pallas_call x4, Pallas kernels, over_groups(): pl.pallas_call(kernel, grid=(groups,), in_specs=specs, out_specs=[spec(o....  29.2 us
    ppermute x23, starting transfers between devices, swap_c(): return lax.ppermute(v, 'c', [(0, 1), (1, 0)])  26.3 us
  transfers between devices with their start and end apart: 88, of which 37 were waited for; matrix products, arithmetic and copies ran while one was open for 25% of the time, Pallas kernels for 10%

profile of v2, /device:TPU:17, one launch (start us, length us, event | category | flops | bytes accessed | tf_op | source)
XLA Modules:
  0.0 628.3 jit_solution(14108250561585674734)
XLA Ops:
  7.3 2.8 fusion.94
  13.0 3.2 collective-permute-start.3
  16.2 3.0 collective-permute-start.2
  19.2 4.2 collective-permute-done
  23.4 9.6 %collective-permute-done.3 = bf16[144,896]{1,0:T(8,128)(2,1)S(1)} collective-permute-done((bf16[144,896]{1,0:T(8,128)(2,1)S(1)}, bf16[144,896]{1,0:T(8,128)(2,1)S(1)}, u32[]{:S(2)}, u32[]{:S(2)}) %collective-permute-start.3) | collective-permute-done | bytes 258080 | tf_op jit(solution)/shard_map/ppermute | solution.py:118
  35.9 6.0 collective-permute-done.1
  49.0 22.5 %collective-permute-done.4.x_ref = bf16[4,144,896]{2,1,0:T(8,128)(2,1)S(1)} collective-permute-done((bf16[4,144,896]{2,1,0:T(8,128)(2,1)}, bf16[4,144,896]{2,1,0:T(8,128)(2,1)S(1)}, u32[]{:S(2)}, u32[]{:S(2)}) %collective-permute-start.4) | collective-permute-done | bytes 1032224 | tf_op jit(solution)/shard_map/ppermute | solution.py:59
  72.9 3.3 fusion.93
  90.6 5.3 collective-permute-done.7.t_ref
  96.8 11.2 %collective-permute-done.9.xt_ref = bf16[128,2048]{1,0:T(8,128)(2,1)} collective-permute-done((bf16[128,2048]{1,0:T(8,128)(2,1)S(1)}, bf16[128,2048]{1,0:T(8,128)(2,1)}, u32[]{:S(2)}, u32[]{:S(2)}) %collective-permute-start.9) | collective-permute-done | bytes 524320 | tf_op jit(solution)/shard_map/ppermute | solution.py:67
  114.3 13.4 %collective-permute-done.16.got_ref = bf16[2,128,1536]{2,1,0:T(8,128)(2,1)S(1)} collective-permute-done((bf16[2,128,1536]{2,1,0:T(8,128)(2,1)}, bf16[2,128,1536]{2,1,0:T(8,128)(2,1)S(1)}, u32[]{:S(2)}, u32[]{:S(2)}) %collective-permute-start.16) | collective-permute-done | bytes 786464 | tf_op jit(solution)/shard_map/ppermute | solution.py:59
  137.3 3.6 fusion.105.row_ref
  142.4 6.1 collective-permute-done.18.t_ref
  149.4 11.2 %collective-permute-done.20.xt_ref = bf16[128,2048]{1,0:T(8,128)(2,1)} collective-permute-done((bf16[128,2048]{1,0:T(8,128)(2,1)}, bf16[128,2048]{1,0:T(8,128)(2,1)}, u32[]{:S(2)}, u32[]{:S(2)}) %collective-permute-start.20) | collective-permute-done | bytes 524320 | tf_op jit(solution)/shard_map/ppermute | solution.py:67
  160.6 3.2 shard_map.349
  165.0 5.2 fusion.106.row_ref
  170.2 4.5 fusion.6.mix_ref
  174.9 5.0 shard_map.344
  181.8 4.3 fusion.4.mix_ref
  186.3 5.0 shard_map.345
  205.5 2.5 collective-permute-done.22.got_ref
  215.6 9.9 %reduce-scatter.7.cloned.1.call-start = ((), (), s32[]{:S(2)}) async-start(), calls=%async_computation.8 | async-start | bytes 2621440 | tf_op jit(solution)/shard_map/reduce_scatter | solution.py:110
  225.5 11.1 %collective-permute-done.24 = bf16[128,2048]{1,0:T(8,128)(2,1)} collective-permute-done((bf16[128,2048]{1,0:T(8,128)(2,1)}, bf16[128,2048]{1,0:T(8,128)(2,1)}, u32[]{:S(2)}, u32[]{:S(2)}) %collective-permute-start.24) | collective-permute-done | bytes 524320 | tf_op jit(solution)/shard_map/ppermute | solution.py:59
  242.6 10.4 %collective-permute-done.26.t_ref = bf16[128,2048]{1,0:T(8,128)(2,1)S(1)} collective-permute-done((bf16[128,2048]{1,0:T(8,128)(2,1)S(1)}, bf16[128,2048]{1,0:T(8,128)(2,1)S(1)}, u32[]{:S(2)}, u32[]{:S(2)}) %collective-permute-start.26) | collective-permute-done | bytes 524320 | tf_op jit(solution)/shard_map/ppermute | solution.py:63
  253.8 11.3 %collective-permute-done.28.xt_ref = bf16[128,2048]{1,0:T(8,128)(2,1)S(1)} collective-permute-done((bf16[128,2048]{1,0:T(8,128)(2,1)S(1)}, bf16[128,2048]{1,0:T(8,128)(2,1)S(1)}, u32[]{:S(2)}, u32[]{:S(2)}) %collective-permute-start.28) | collective-permute-done | bytes 524320 | tf_op jit(solution)/shard_map/ppermute | solution.py:67
  268.1 6.5 %fusion.107 = f32[512,1024]{1,0:T(8,128)} fusion(bf16[512,2048]{1,0:T(8,128)(2,1)} %shard_map.351, bf16[2048,1024]{1,0:T(8,128)(2,1)} %all-gather.6.cloned.1.call-done), kind=kOutput, calls=%fused_computation.232 | convolution fusion | flops 2147483648 | bytes 8388608 | tf_op jit(solution)/shard_map/dot_general | solution.py:26
  274.6 5.3 all-gather.8.cloned.1.call-done
  279.9 5.5 multiply_convert_fusion.4
  285.4 4.2 fusion.108
  289.6 4.2 multiply_convert_fusion.2
  293.8 3.1 fusion.112
  296.9 4.2 add_convert_fusion.4
  301.2 4.3 fusion.33
  305.5 5.9 add_convert_fusion
  311.9 5.1 convolution_convert_fusion
  325.3 11.4 %collective-permute-done.34 = bf16[128,2048]{1,0:T(8,128)(2,1)S(1)} collective-permute-done((bf16[128,2048]{1,0:T(8,128)(2,1)S(1)}, bf16[128,2048]{1,0:T(8,128)(2,1)S(1)}, u32[]{:S(2)}, u32[]{:S(2)}) %collective-permute-start.34) | collective-permute-done | bytes 524320 | tf_op jit(solution)/shard_map/ppermute | solution.py:67
  336.7 11.2 %collective-permute-done.33 = bf16[128,2048]{1,0:T(8,128)(2,1)S(1)} collective-permute-done((bf16[128,2048]{1,0:T(8,128)(2,1)S(1)}, bf16[128,2048]{1,0:T(8,128)(2,1)S(1)}, u32[]{:S(2)}, u32[]{:S(2)}) %collective-permute-start.33) | collective-permute-done | bytes 524320 | tf_op jit(solution)/shard_map/ppermute | solution.py:59
  355.7 7.6 %collective-permute-done.35.t_ref = bf16[128,2048]{1,0:T(8,128)(2,1)S(1)} collective-permute-done((bf16[128,2048]{1,0:T(8,128)(2,1)S(1)}, bf16[128,2048]{1,0:T(8,128)(2,1)S(1)}, u32[]{:S(2)}, u32[]{:S(2)}) %collective-permute-start.35) | collective-permute-done | bytes 524320 | tf_op jit(solution)/shard_map/ppermute | solution.py:63
  364.3 11.5 %collective-permute-done.37.xt_ref = bf16[128,2048]{1,0:T(8,128)(2,1)S(1)} collective-permute-done((bf16[128,2048]{1,0:T(8,128)(2,1)S(1)}, bf16[128,2048]{1,0:T(8,128)(2,1)S(1)}, u32[]{:S(2)}, u32[]{:S(2)}) %collective-permute-start.37) | collective-permute-done | bytes 524320 | tf_op jit(solution)/shard_map/ppermute | solution.py:67
  387.4 2.7 add_convert_fusion.5
  390.4 3.6 fusion.111.grad_ref
  404.2 23.3 %collective-permute-done.45.got_ref = bf16[2,128,512]{2,1,0:T(8,128)(2,1)S(1)} collective-permute-done((bf16[2,128,512]{2,1,0:T(8,128)(2,1)S(1)}, bf16[2,128,512]{2,1,0:T(8,128)(2,1)S(1)}, u32[]{:S(2)}, u32[]{:S(2)}) %collective-permute-start.45) | collective-permute-done | bytes 262176 | tf_op jit(solution)/shard_map/ppermute | solution.py:59
  429.9 3.2 add_convert_fusion.7
  435.5 9.5 %shard_map.355 = (bf16[512,896]{1,0:T(8,128)(2,1)S(1)}, bf16[512,384]{1,0:T(8,128)(2,1)S(1)}, f32[512,512]{1,0:T(8,128)S(1)}, f32[2,16,384]{2,1,0:T(8,128)S(1)}, f32[2,8,512]{2,1,0:T(8,128)S(1)}) custom-call(f32[512,896]{1,0:T(8,128)S(1)} %copy-done.10, f32[512,896]{1,0:T(8,128)S(1)} %copy-done.4, f32[512,128]{1,0:T(8,128)S(1)} %copy-done.29, ...), custom_call_target="tpu_custom_call" | custom-call | tf_op jit(solution)/shard_map/pallas_call | solution.py:404
  457.1 9.7 %shard_map.356 = (bf16[512,896]{1,0:T(8,128)(2,1)S(1)}, bf16[512,384]{1,0:T(8,128)(2,1)S(1)}, f32[512,512]{1,0:T(8,128)S(1)}, f32[2,16,384]{2,1,0:T(8,128)S(1)}, f32[2,8,512]{2,1,0:T(8,128)S(1)}) custom-call(f32[512,896]{1,0:T(8,128)S(1)} %copy-done.8, f32[512,896]{1,0:T(8,128)S(1)} %copy-done.6, f32[512,128]{1,0:T(8,128)S(1)} %copy-done.27, ...), custom_call_target="tpu_custom_call" | custom-call | tf_op jit(solution)/shard_map/pallas_call | solution.py:404
  468.5 4.1 fusion.113
  472.7 4.5 add_convert_fusion.1
  482.3 5.4 fusion
  487.8 4.0 add_convert_fusion.3
  495.3 2.5 collective-permute-done.64.t_ref
  498.7 2.7 collective-permute-done.66.xt_ref
  502.7 4.7 fusion.2
  507.4 2.7 convolution_add_fusion.total_ref
  510.1 2.9 fusion.115
  513.0 3.0 add_convert_fusion.2
  516.0 2.8 shard_map.361
  527.2 3.3 collective-permute-start.74
  530.4 3.0 fusion.114
  542.3 8.3 %collective-permute-done.75 = f32[16,384]{1,0:T(8,128)S(1)} collective-permute-done((f32[16,384]{1,0:T(8,128)S(1)}, f32[16,384]{1,0:T(8,128)S(1)}, u32[]{:S(2)}, u32[]{:S(2)}) %collective-permute-start.75) | collective-permute-done | bytes 24608 | tf_op jit(solution)/shard_map/ppermute | solution.py:59
  554.8 4.0 fusion.25
  564.2 8.2 %collective-permute-done.56 = f32[52,128]{1,0:T(8,128)S(1)} collective-permute-done((f32[52,128]{1,0:T(8,128)S(1)}, f32[52,128]{1,0:T(8,128)S(1)}, u32[]{:S(2)}, u32[]{:S(2)}) %collective-permute-start.56) | collective-permute-done | bytes 26656 | tf_op jit(solution)/shard_map/ppermute | solution.py:59
  592.0 4.7 collective-permute-start.69
  604.8 3.0 shard_map.373
  607.8 3.1 collective-permute-done.60.got_ref
  (656 shorter events, 214.8 us)
Async XLA Ops:
  7.2 163.0 %all-gather.4.cloned.1.call-start = ((), (), s32[]{:S(2)}) async-start(), calls=%async_computation.4 | async-start | bytes 7208960 | tf_op jit(solution)/shard_map/all_gather | solution.py:106
  10.6 22.4 %collective-permute-start.10 = (bf16[2,128,1408]{2,1,0:T(8,128)(2,1)S(1)}, bf16[2,128,1408]{2,1,0:T(8,128)(2,1)S(1)}, u32[]{:S(2)}, u32[]{:S(2)}) collective-permute-start(bf16[2,128,1408]{2,1,0:T(8,128)(2,1)S(1)} %get-tuple-element.118), channel_id=1, source_target_pairs={{0,4},{4,0},{1,5},{5,1},{2,6},{6,2},{3,7},{7,3},{8,12},{12,8},{9,1... | collective-permute-start | bytes 2162696 | tf_op jit(solution)/shard_map/ppermute | solution.py:59
  12.8 10.6 %collective-permute-start = (bf16[144,896]{1,0:T(8,128)(2,1)S(1)}, bf16[144,896]{1,0:T(8,128)(2,1)}, u32[]{:S(2)}, u32[]{:S(2)}) collective-permute-start(bf16[144,896]{1,0:T(8,128)(2,1)S(1)} %fusion.56), channel_id=1, source_target_pairs={{0,16},{8,24},{16,0},{24,8},{1,17},{9,25},{17,1},{25,9},{2,18},{10... | collective-permute-start | bytes 774152 | tf_op jit(solution)/shard_map/ppermute | solution.py:117
  13.0 20.1 %collective-permute-start.3 = (bf16[144,896]{1,0:T(8,128)(2,1)S(1)}, bf16[144,896]{1,0:T(8,128)(2,1)S(1)}, u32[]{:S(2)}, u32[]{:S(2)}) collective-permute-start(bf16[144,896]{1,0:T(8,128)(2,1)S(1)} %fusion.56), channel_id=1, source_target_pairs={{0,8},{8,16},{16,24},{1,9},{9,17},{17,25},{2,10},{10,18},{18,26},{... | collective-permute-start | bytes 774152 | tf_op jit(solution)/shard_map/ppermute | solution.py:118
  16.2 16.9 %collective-permute-start.2 = (bf16[144,896]{1,0:T(8,128)(2,1)S(1)}, bf16[144,896]{1,0:T(8,128)(2,1)S(1)}, u32[]{:S(2)}, u32[]{:S(2)}) collective-permute-start(bf16[144,896]{1,0:T(8,128)(2,1)S(1)} %fusion.56), channel_id=1, source_target_pairs={{8,0},{16,8},{24,16},{9,1},{17,9},{25,17},{10,2},{18,10},{26,18},{... | collective-permute-start | bytes 774152 | tf_op jit(solution)/shard_map/ppermute | solution.py:119
  33.9 11.2 %collective-permute-start.11 = (bf16[2,128,1408]{2,1,0:T(8,128)(2,1)S(1)}, bf16[2,128,1408]{2,1,0:T(8,128)(2,1)S(1)}, u32[]{:S(2)}, u32[]{:S(2)}) collective-permute-start(bf16[2,128,1408]{2,1,0:T(8,128)(2,1)S(1)} %get-tuple-element.120), channel_id=1, source_target_pairs={{0,2},{2,0},{1,3},{3,1},{4,6},{6,4},{5,7},{7,5},{8,10},{10,8},{9,1... | collective-permute-start | bytes 2162696 | tf_op jit(solution)/shard_map/ppermute | solution.py:55
  46.9 221.2 %all-gather.6.cloned.1.call-start = ((), (), s32[]{:S(2)}) async-start(), calls=%async_computation.5 | async-start | bytes 5242880 | tf_op jit(solution)/shard_map/all_gather | solution.py:106
  47.4 24.0 %collective-permute-start.4 = (bf16[4,144,896]{2,1,0:T(8,128)(2,1)}, bf16[4,144,896]{2,1,0:T(8,128)(2,1)S(1)}, u32[]{:S(2)}, u32[]{:S(2)}) collective-permute-start(bf16[4,144,896]{2,1,0:T(8,128)(2,1)} %pad_maximum_fusion.2.own_ref), channel_id=1, source_target_pairs={{0,4},{4,0},{1,5},{5,1},{2,6},{6,2},{3,7},{7,3},{8,12},{12,8},{9,1... | collective-permute-start | bytes 3096584 | tf_op jit(solution)/shard_map/ppermute | solution.py:59
  48.0 29.8 %collective-permute-start.5 = (bf16[4,144,896]{2,1,0:T(8,128)(2,1)}, bf16[4,144,896]{2,1,0:T(8,128)(2,1)S(1)}, u32[]{:S(2)}, u32[]{:S(2)}) collective-permute-start(bf16[4,144,896]{2,1,0:T(8,128)(2,1)} %pad_maximum_fusion.2.own_ref), channel_id=1, source_target_pairs={{0,2},{2,0},{1,3},{3,1},{4,6},{6,4},{5,7},{7,5},{8,10},{10,8},{9,1... | collective-permute-start | bytes 3096584 | tf_op jit(solution)/shard_map/ppermute | solution.py:55
  82.2 13.7 %collective-permute-start.7 = (bf16[128,2048]{1,0:T(8,128)(2,1)S(1)}, bf16[128,2048]{1,0:T(8,128)(2,1)S(1)}, u32[]{:S(2)}, u32[]{:S(2)}) collective-permute-start(bf16[128,2048]{1,0:T(8,128)(2,1)S(1)} %fusion.20.own_ref), channel_id=1, source_target_pairs={{0,1},{1,0},{2,3},{3,2},{4,5},{5,4},{6,7},{7,6},{8,9},{9,8},{10,11... | collective-permute-start | bytes 1572872 | tf_op jit(solution)/shard_map/ppermute | solution.py:63
  83.5 13.3 %collective-permute-start.8 = (bf16[128,2048]{1,0:T(8,128)(2,1)S(1)}, bf16[128,2048]{1,0:T(8,128)(2,1)}, u32[]{:S(2)}, u32[]{:S(2)}) collective-permute-start(bf16[128,2048]{1,0:T(8,128)(2,1)S(1)} %fusion.20.own_ref), channel_id=1, source_target_pairs={{0,4},{4,0},{1,5},{5,1},{2,6},{6,2},{3,7},{7,3},{8,12},{12,8},{9,1... | collective-permute-start | bytes 1572872 | tf_op jit(solution)/shard_map/ppermute | solution.py:59
  83.7 24.3 %collective-permute-start.9 = (bf16[128,2048]{1,0:T(8,128)(2,1)S(1)}, bf16[128,2048]{1,0:T(8,128)(2,1)}, u32[]{:S(2)}, u32[]{:S(2)}) collective-permute-start(bf16[128,2048]{1,0:T(8,128)(2,1)S(1)} %fusion.20.own_ref), channel_id=1, source_target_pairs={{0,5},{1,4},{4,1},{5,0},{2,7},{3,6},{6,3},{7,2},{8,13},{9,12},{12,... | collective-permute-start | bytes 1572872 | tf_op jit(solution)/shard_map/ppermute | solution.py:67
  109.4 18.3 %collective-permute-start.16 = (bf16[2,128,1536]{2,1,0:T(8,128)(2,1)}, bf16[2,128,1536]{2,1,0:T(8,128)(2,1)S(1)}, u32[]{:S(2)}, u32[]{:S(2)}) collective-permute-start(bf16[2,128,1536]{2,1,0:T(8,128)(2,1)} %get-tuple-element.130), channel_id=1, source_target_pairs={{0,4},{4,0},{1,5},{5,1},{2,6},{6,2},{3,7},{7,3},{8,12},{12,8},{9,1... | collective-permute-start | bytes 2359304 | tf_op jit(solution)/shard_map/ppermute | solution.py:59
  109.9 55.1 %collective-permute-start.12 = (bf16[512,2048]{1,0:T(8,128)(2,1)S(1)}, bf16[512,2048]{1,0:T(8,128)(2,1)}, u32[]{:S(2)}, u32[]{:S(2)}) collective-permute-start(bf16[512,2048]{1,0:T(8,128)(2,1)S(1)} %shard_map.340), channel_id=1, source_target_pairs={{0,2},{2,0},{1,3},{3,1},{4,6},{6,4},{5,7},{7,5},{8,10},{10,8},{9,1... | collective-permute-start | bytes 6291464 | tf_op jit(solution)/shard_map/ppermute | solution.py:55
  134.6 13.9 %collective-permute-start.18 = (bf16[128,2048]{1,0:T(8,128)(2,1)}, bf16[128,2048]{1,0:T(8,128)(2,1)}, u32[]{:S(2)}, u32[]{:S(2)}) collective-permute-start(bf16[128,2048]{1,0:T(8,128)(2,1)} %fusion.19.own_ref), channel_id=1, source_target_pairs={{0,1},{1,0},{2,3},{3,2},{4,5},{5,4},{6,7},{7,6},{8,9},{9,8},{10,11... | collective-permute-start | bytes 1572872 | tf_op jit(solution)/shard_map/ppermute | solution.py:63
  135.9 13.5 %collective-permute-start.19 = (bf16[128,2048]{1,0:T(8,128)(2,1)}, bf16[128,2048]{1,0:T(8,128)(2,1)}, u32[]{:S(2)}, u32[]{:S(2)}) collective-permute-start(bf16[128,2048]{1,0:T(8,128)(2,1)} %fusion.19.own_ref), channel_id=1, source_target_pairs={{0,4},{4,0},{1,5},{5,1},{2,6},{6,2},{3,7},{7,3},{8,12},{12,8},{9,1... | collective-permute-start | bytes 1572872 | tf_op jit(solution)/shard_map/ppermute | solution.py:59
  136.2 24.4 %collective-permute-start.20 = (bf16[128,2048]{1,0:T(8,128)(2,1)}, bf16[128,2048]{1,0:T(8,128)(2,1)}, u32[]{:S(2)}, u32[]{:S(2)}) collective-permute-start(bf16[128,2048]{1,0:T(8,128)(2,1)} %fusion.19.own_ref), channel_id=1, source_target_pairs={{0,5},{1,4},{4,1},{5,0},{2,7},{3,6},{6,3},{7,2},{8,13},{9,12},{12,... | collective-permute-start | bytes 1572872 | tf_op jit(solution)/shard_map/ppermute | solution.py:67
  142.0 137.8 %all-gather.8.cloned.1.call-start = ((), (), s32[]{:S(2)}) async-start(), calls=%async_computation.6 | async-start | bytes 2621440 | tf_op jit(solution)/shard_map/all_gather | solution.py:106
  163.8 36.3 %collective-permute-start.21 = (bf16[512,2048]{1,0:T(8,128)(2,1)}, bf16[512,2048]{1,0:T(8,128)(2,1)}, u32[]{:S(2)}, u32[]{:S(2)}) collective-permute-start(bf16[512,2048]{1,0:T(8,128)(2,1)} %shard_map.349), channel_id=1, source_target_pairs={{0,2},{2,0},{1,3},{3,1},{4,6},{6,4},{5,7},{7,5},{8,10},{10,8},{9,1... | collective-permute-start | bytes 6291464 | tf_op jit(solution)/shard_map/ppermute | solution.py:55
  211.1 14.5 %collective-permute-start.25 = (bf16[128,2048]{1,0:T(8,128)(2,1)}, bf16[128,2048]{1,0:T(8,128)(2,1)}, u32[]{:S(2)}, u32[]{:S(2)}) collective-permute-start(bf16[128,2048]{1,0:T(8,128)(2,1)} %get-tuple-element.140), channel_id=1, source_target_pairs={{0,5},{1,4},{4,1},{5,0},{2,7},{3,6},{6,3},{7,2},{8,13},{9,12},{12,... | collective-permute-start | bytes 1572872 | tf_op jit(solution)/shard_map/ppermute | solution.py:67
  212.2 24.3 %collective-permute-start.24 = (bf16[128,2048]{1,0:T(8,128)(2,1)}, bf16[128,2048]{1,0:T(8,128)(2,1)}, u32[]{:S(2)}, u32[]{:S(2)}) collective-permute-start(bf16[128,2048]{1,0:T(8,128)(2,1)} %get-tuple-element.139), channel_id=1, source_target_pairs={{0,4},{4,0},{1,5},{5,1},{2,6},{6,2},{3,7},{7,3},{8,12},{12,8},{9,1... | collective-permute-start | bytes 1572872 | tf_op jit(solution)/shard_map/ppermute | solution.py:59
  213.3 24.0 %collective-permute-start.23 = (bf16[128,2048]{1,0:T(8,128)(2,1)}, bf16[128,2048]{1,0:T(8,128)(2,1)}, u32[]{:S(2)}, u32[]{:S(2)}) collective-permute-start(bf16[128,2048]{1,0:T(8,128)(2,1)} %get-tuple-element.138), channel_id=1, source_target_pairs={{0,1},{1,0},{2,3},{3,2},{4,5},{5,4},{6,7},{7,6},{8,9},{9,8},{10,11... | collective-permute-start | bytes 1572872 | tf_op jit(solution)/shard_map/ppermute | solution.py:63
  215.6 183.7 %reduce-scatter.7.cloned.1.call-start = ((), (), s32[]{:S(2)}) async-start(), calls=%async_computation.8 | async-start | bytes 2621440 | tf_op jit(solution)/shard_map/reduce_scatter | solution.py:110
  239.8 13.1 %collective-permute-start.26 = (bf16[128,2048]{1,0:T(8,128)(2,1)S(1)}, bf16[128,2048]{1,0:T(8,128)(2,1)S(1)}, u32[]{:S(2)}, u32[]{:S(2)}) collective-permute-start(bf16[128,2048]{1,0:T(8,128)(2,1)S(1)} %multiply_convert_fusion.7.own_ref), channel_id=1, source_target_pairs={{0,1},{1,0},{2,3},{3,2},{4,5},{5,4},{6,7},{7,6},{8,9},{9,8},{10,11... | collective-permute-start | bytes 1572872 | tf_op jit(solution)/shard_map/ppermute | solution.py:63
  241.0 12.8 %collective-permute-start.27 = (bf16[128,2048]{1,0:T(8,128)(2,1)S(1)}, bf16[128,2048]{1,0:T(8,128)(2,1)S(1)}, u32[]{:S(2)}, u32[]{:S(2)}) collective-permute-start(bf16[128,2048]{1,0:T(8,128)(2,1)S(1)} %multiply_convert_fusion.7.own_ref), channel_id=1, source_target_pairs={{0,4},{4,0},{1,5},{5,1},{2,6},{6,2},{3,7},{7,3},{8,12},{12,8},{9,1... | collective-permute-start | bytes 1572872 | tf_op jit(solution)/shard_map/ppermute | solution.py:59
  241.4 23.7 %collective-permute-start.28 = (bf16[128,2048]{1,0:T(8,128)(2,1)S(1)}, bf16[128,2048]{1,0:T(8,128)(2,1)S(1)}, u32[]{:S(2)}, u32[]{:S(2)}) collective-permute-start(bf16[128,2048]{1,0:T(8,128)(2,1)S(1)} %multiply_convert_fusion.7.own_ref), channel_id=1, source_target_pairs={{0,5},{1,4},{4,1},{5,0},{2,7},{3,6},{6,3},{7,2},{8,13},{9,12},{12,... | collective-permute-start | bytes 1572872 | tf_op jit(solution)/shard_map/ppermute | solution.py:67
  266.6 18.8 %collective-permute-start.29 = (bf16[512,2048]{1,0:T(8,128)(2,1)}, bf16[512,2048]{1,0:T(8,128)(2,1)}, u32[]{:S(2)}, u32[]{:S(2)}) collective-permute-start(bf16[512,2048]{1,0:T(8,128)(2,1)} %shard_map.351), channel_id=1, source_target_pairs={{0,2},{2,0},{1,3},{3,1},{4,6},{6,4},{5,7},{7,5},{8,10},{10,8},{9,1... | collective-permute-start | bytes 6291464 | tf_op jit(solution)/shard_map/ppermute | solution.py:55
  301.1 149.1 %reduce-scatter.5.cloned.1.call-start = ((), (), s32[]{:S(2)}) async-start(), calls=%async_computation.7 | async-start | bytes 5242880 | tf_op jit(solution)/shard_map/reduce_scatter | solution.py:110
  311.5 227.5 %reduce-scatter.11.cloned.1.call-start = ((), (), s32[]{:S(2)}) async-start(), calls=%async_computation.10 | async-start | bytes 2621440 | tf_op jit(solution)/shard_map/reduce_scatter | solution.py:110
  322.6 14.1 %collective-permute-start.34 = (bf16[128,2048]{1,0:T(8,128)(2,1)S(1)}, bf16[128,2048]{1,0:T(8,128)(2,1)S(1)}, u32[]{:S(2)}, u32[]{:S(2)}) collective-permute-start(bf16[128,2048]{1,0:T(8,128)(2,1)S(1)} %get-tuple-element.144), channel_id=1, source_target_pairs={{0,5},{1,4},{4,1},{5,0},{2,7},{3,6},{6,3},{7,2},{8,13},{9,12},{12,... | collective-permute-start | bytes 1572872 | tf_op jit(solution)/shard_map/ppermute | solution.py:67
  324.8 23.2 %collective-permute-start.33 = (bf16[128,2048]{1,0:T(8,128)(2,1)S(1)}, bf16[128,2048]{1,0:T(8,128)(2,1)S(1)}, u32[]{:S(2)}, u32[]{:S(2)}) collective-permute-start(bf16[128,2048]{1,0:T(8,128)(2,1)S(1)} %get-tuple-element.143), channel_id=1, source_target_pairs={{0,4},{4,0},{1,5},{5,1},{2,6},{6,2},{3,7},{7,3},{8,12},{12,8},{9,1... | collective-permute-start | bytes 1572872 | tf_op jit(solution)/shard_map/ppermute | solution.py:59
  325.0 23.6 %collective-permute-start.32 = (bf16[128,2048]{1,0:T(8,128)(2,1)S(1)}, bf16[128,2048]{1,0:T(8,128)(2,1)S(1)}, u32[]{:S(2)}, u32[]{:S(2)}) collective-permute-start(bf16[128,2048]{1,0:T(8,128)(2,1)S(1)} %get-tuple-element.142), channel_id=1, source_target_pairs={{0,1},{1,0},{2,3},{3,2},{4,5},{5,4},{6,7},{7,6},{8,9},{9,8},{10,11... | collective-permute-start | bytes 1572872 | tf_op jit(solution)/shard_map/ppermute | solution.py:63
  350.2 13.1 %collective-permute-start.35 = (bf16[128,2048]{1,0:T(8,128)(2,1)S(1)}, bf16[128,2048]{1,0:T(8,128)(2,1)S(1)}, u32[]{:S(2)}, u32[]{:S(2)}) collective-permute-start(bf16[128,2048]{1,0:T(8,128)(2,1)S(1)} %multiply_convert_fusion.own_ref), channel_id=1, source_target_pairs={{0,1},{1,0},{2,3},{3,2},{4,5},{5,4},{6,7},{7,6},{8,9},{9,8},{10,11... | collective-permute-start | bytes 1572872 | tf_op jit(solution)/shard_map/ppermute | solution.py:63
  351.5 12.8 %collective-permute-start.36 = (bf16[128,2048]{1,0:T(8,128)(2,1)S(1)}, bf16[128,2048]{1,0:T(8,128)(2,1)S(1)}, u32[]{:S(2)}, u32[]{:S(2)}) collective-permute-start(bf16[128,2048]{1,0:T(8,128)(2,1)S(1)} %multiply_convert_fusion.own_ref), channel_id=1, source_target_pairs={{0,4},{4,0},{1,5},{5,1},{2,6},{6,2},{3,7},{7,3},{8,12},{12,8},{9,1... | collective-permute-start | bytes 1572872 | tf_op jit(solution)/shard_map/ppermute | solution.py:59
  352.7 23.1 %collective-permute-start.37 = (bf16[128,2048]{1,0:T(8,128)(2,1)S(1)}, bf16[128,2048]{1,0:T(8,128)(2,1)S(1)}, u32[]{:S(2)}, u32[]{:S(2)}) collective-permute-start(bf16[128,2048]{1,0:T(8,128)(2,1)S(1)} %multiply_convert_fusion.own_ref), channel_id=1, source_target_pairs={{0,5},{1,4},{4,1},{5,0},{2,7},{3,6},{6,3},{7,2},{8,13},{9,12},{12,... | collective-permute-start | bytes 1572872 | tf_op jit(solution)/shard_map/ppermute | solution.py:67
  354.5 24.8 %collective-permute-start.31 = (bf16[512,2048]{1,0:T(8,128)(2,1)S(1)}, bf16[512,2048]{1,0:T(8,128)(2,1)S(1)}, u32[]{:S(2)}, u32[]{:S(2)}) collective-permute-start(bf16[512,2048]{1,0:T(8,128)(2,1)S(1)} %convolution_convert_fusion.1), channel_id=1, source_target_pairs={{0,2},{2,0},{1,3},{3,1},{4,6},{6,4},{5,7},{7,5},{8,10},{10,8},{9,1... | collective-permute-start | bytes 6291464 | tf_op jit(solution)/shard_map/ppermute | solution.py:55
  375.9 10.1 %collective-permute-start.41 = (bf16[512,2048]{1,0:T(8,128)(2,1)S(1)}, bf16[512,2048]{1,0:T(8,128)(2,1)S(1)}, u32[]{:S(2)}, u32[]{:S(2)}) collective-permute-start(bf16[512,2048]{1,0:T(8,128)(2,1)S(1)} %shard_map.354), channel_id=1, source_target_pairs={{0,2},{2,0},{1,3},{3,1},{4,6},{6,4},{5,7},{7,5},{8,10},{10,8},{9,1... | collective-permute-start | bytes 6291464 | tf_op jit(solution)/shard_map/ppermute | solution.py:55
  390.2 208.5 %reduce-scatter.9.cloned.1.call-start = ((), (), s32[]{:S(2)}) async-start(), calls=%async_computation.9 | async-start | bytes 4587520 | tf_op jit(solution)/shard_map/reduce_scatter | solution.py:110
  396.6 33.3 %collective-permute-start.40 = (bf16[128,2048]{1,0:T(8,128)(2,1)}, bf16[128,2048]{1,0:T(8,128)(2,1)}, u32[]{:S(2)}, u32[]{:S(2)}) collective-permute-start(bf16[128,2048]{1,0:T(8,128)(2,1)} %copy-done.80), channel_id=1, source_target_pairs={{0,5},{1,4},{4,1},{5,0},{2,7},{3,6},{6,3},{7,2},{8,13},{9,12},{12,... | collective-permute-start | bytes 1572872 | tf_op jit(solution)/shard_map/ppermute | solution.py:67
  398.6 31.3 %collective-permute-start.39 = (bf16[128,2048]{1,0:T(8,128)(2,1)}, bf16[128,2048]{1,0:T(8,128)(2,1)}, u32[]{:S(2)}, u32[]{:S(2)}) collective-permute-start(bf16[128,2048]{1,0:T(8,128)(2,1)} %copy-done.79), channel_id=1, source_target_pairs={{0,4},{4,0},{1,5},{5,1},{2,6},{6,2},{3,7},{7,3},{8,12},{12,8},{9,1... | collective-permute-start | bytes 1572872 | tf_op jit(solution)/shard_map/ppermute | solution.py:59
  398.8 31.1 %collective-permute-start.38 = (bf16[128,2048]{1,0:T(8,128)(2,1)}, bf16[128,2048]{1,0:T(8,128)(2,1)}, u32[]{:S(2)}, u32[]{:S(2)}) collective-permute-start(bf16[128,2048]{1,0:T(8,128)(2,1)} %copy-done.78), channel_id=1, source_target_pairs={{0,1},{1,0},{2,3},{3,2},{4,5},{5,4},{6,7},{7,6},{8,9},{9,8},{10,11... | collective-permute-start | bytes 1572872 | tf_op jit(solution)/shard_map/ppermute | solution.py:63
  400.5 27.0 %collective-permute-start.45 = (bf16[2,128,512]{2,1,0:T(8,128)(2,1)S(1)}, bf16[2,128,512]{2,1,0:T(8,128)(2,1)S(1)}, u32[]{:S(2)}, u32[]{:S(2)}) collective-permute-start(bf16[2,128,512]{2,1,0:T(8,128)(2,1)S(1)} %get-tuple-element.163), channel_id=1, source_target_pairs={{0,4},{4,0},{1,5},{5,1},{2,6},{6,2},{3,7},{7,3},{8,12},{12,8},{9,1... | collective-permute-start | bytes 786440 | tf_op jit(solution)/shard_map/ppermute | solution.py:59
  403.2 26.1 %collective-permute-start.43 = (f32[4,8,256]{2,1,0:T(8,128)S(1)}, f32[4,8,256]{2,1,0:T(8,128)S(1)}, u32[]{:S(2)}, u32[]{:S(2)}) collective-permute-start(f32[4,8,256]{2,1,0:T(8,128)S(1)} %maximum_add_fusion.2), channel_id=1, source_target_pairs={{0,4},{4,0},{1,5},{5,1},{2,6},{6,2},{3,7},{7,3},{8,12},{12,8},{9,1... | collective-permute-start | bytes 98312 | tf_op jit(solution)/shard_map/ppermute | solution.py:59
  467.9 9.4 %collective-permute-start.47 = (bf16[512,512]{1,0:T(8,128)(2,1)}, bf16[512,512]{1,0:T(8,128)(2,1)}, u32[]{:S(2)}, u32[]{:S(2)}) collective-permute-start(bf16[512,512]{1,0:T(8,128)(2,1)} %convert_element_type.277), channel_id=1, source_target_pairs={{0,2},{2,0},{1,3},{3,1},{4,6},{6,4},{5,7},{7,5},{8,10},{10,8},{9,1... | collective-permute-start | bytes 1572872 | tf_op jit(solution)/shard_map/ppermute | solution.py:55
  479.6 12.9 %collective-permute-start.54 = (bf16[128,512]{1,0:T(8,128)(2,1)S(1)}, bf16[128,512]{1,0:T(8,128)(2,1)S(1)}, u32[]{:S(2)}, u32[]{:S(2)}) collective-permute-start(bf16[128,512]{1,0:T(8,128)(2,1)S(1)} %get-tuple-element.173), channel_id=1, source_target_pairs={{0,5},{1,4},{4,1},{5,0},{2,7},{3,6},{6,3},{7,2},{8,13},{9,12},{12,... | collective-permute-start | bytes 393224 | tf_op jit(solution)/shard_map/ppermute | solution.py:67
  481.5 11.0 %collective-permute-start.53 = (bf16[128,512]{1,0:T(8,128)(2,1)S(1)}, bf16[128,512]{1,0:T(8,128)(2,1)S(1)}, u32[]{:S(2)}, u32[]{:S(2)}) collective-permute-start(bf16[128,512]{1,0:T(8,128)(2,1)S(1)} %get-tuple-element.172), channel_id=1, source_target_pairs={{0,4},{4,0},{1,5},{5,1},{2,6},{6,2},{3,7},{7,3},{8,12},{12,8},{9,1... | collective-permute-start | bytes 393224 | tf_op jit(solution)/shard_map/ppermute | solution.py:59
  481.7 10.8 %collective-permute-start.52 = (bf16[128,512]{1,0:T(8,128)(2,1)S(1)}, bf16[128,512]{1,0:T(8,128)(2,1)S(1)}, u32[]{:S(2)}, u32[]{:S(2)}) collective-permute-start(bf16[128,512]{1,0:T(8,128)(2,1)S(1)} %get-tuple-element.171), channel_id=1, source_target_pairs={{0,1},{1,0},{2,3},{3,2},{4,5},{5,4},{6,7},{7,6},{8,9},{9,8},{10,11... | collective-permute-start | bytes 393224 | tf_op jit(solution)/shard_map/ppermute | solution.py:63
  491.8 24.2 %collective-permute-start.48 = (bf16[512,2048]{1,0:T(8,128)(2,1)}, bf16[512,2048]{1,0:T(8,128)(2,1)}, u32[]{:S(2)}, u32[]{:S(2)}) collective-permute-start(bf16[512,2048]{1,0:T(8,128)(2,1)} %add_convert_fusion.3), channel_id=1, source_target_pairs={{0,2},{2,0},{1,3},{3,1},{4,6},{6,4},{5,7},{7,5},{8,10},{10,8},{9,1... | collective-permute-start | bytes 6291464 | tf_op jit(solution)/shard_map/ppermute | solution.py:55
  524.5 29.9 %collective-permute-start.51 = (bf16[128,2048]{1,0:T(8,128)(2,1)}, bf16[128,2048]{1,0:T(8,128)(2,1)}, u32[]{:S(2)}, u32[]{:S(2)}) collective-permute-start(bf16[128,2048]{1,0:T(8,128)(2,1)} %copy-done.83), channel_id=1, source_target_pairs={{0,5},{1,4},{4,1},{5,0},{2,7},{3,6},{6,3},{7,2},{8,13},{9,12},{12,... | collective-permute-start | bytes 1572872 | tf_op jit(solution)/shard_map/ppermute | solution.py:67
  526.5 28.2 %collective-permute-start.50 = (bf16[128,2048]{1,0:T(8,128)(2,1)}, bf16[128,2048]{1,0:T(8,128)(2,1)}, u32[]{:S(2)}, u32[]{:S(2)}) collective-permute-start(bf16[128,2048]{1,0:T(8,128)(2,1)} %copy-done.82), channel_id=1, source_target_pairs={{0,4},{4,0},{1,5},{5,1},{2,6},{6,2},{3,7},{7,3},{8,12},{12,8},{9,1... | collective-permute-start | bytes 1572872 | tf_op jit(solution)/shard_map/ppermute | solution.py:59
  526.8 28.0 %collective-permute-start.49 = (bf16[128,2048]{1,0:T(8,128)(2,1)}, bf16[128,2048]{1,0:T(8,128)(2,1)}, u32[]{:S(2)}, u32[]{:S(2)}) collective-permute-start(bf16[128,2048]{1,0:T(8,128)(2,1)} %copy-done.81), channel_id=1, source_target_pairs={{0,1},{1,0},{2,3},{3,2},{4,5},{5,4},{6,7},{7,6},{8,9},{9,8},{10,11... | collective-permute-start | bytes 1572872 | tf_op jit(solution)/shard_map/ppermute | solution.py:63
  533.4 17.2 %collective-permute-start.75 = (f32[16,384]{1,0:T(8,128)S(1)}, f32[16,384]{1,0:T(8,128)S(1)}, u32[]{:S(2)}, u32[]{:S(2)}) collective-permute-start(f32[16,384]{1,0:T(8,128)S(1)} %add.399), channel_id=1, source_target_pairs={{0,4},{4,0},{1,5},{5,1},{2,6},{6,2},{3,7},{7,3},{8,12},{12,8},{9,1... | collective-permute-start | bytes 73736 | tf_op jit(solution)/shard_map/ppermute | solution.py:59
  538.0 24.6 %collective-permute-start.62 = (bf16[2,4,128,384]{3,2,1,0:T(8,128)(2,1)}, bf16[2,4,128,384]{3,2,1,0:T(8,128)(2,1)}, u32[]{:S(2)}, u32[]{:S(2)}) collective-permute-start(bf16[2,4,128,384]{3,2,1,0:T(8,128)(2,1)} %get-tuple-element.192), channel_id=1, source_target_pairs={{0,2},{2,0},{1,3},{3,1},{4,6},{6,4},{5,7},{7,5},{8,10},{10,8},{9,1... | collective-permute-start | bytes 2359304 | tf_op jit(solution)/shard_map/ppermute | solution.py:55
  552.8 22.9 %collective-permute-start.77 = (bf16[2,128,512]{2,1,0:T(8,128)(2,1)}, bf16[2,128,512]{2,1,0:T(8,128)(2,1)}, u32[]{:S(2)}, u32[]{:S(2)}) collective-permute-start(bf16[2,128,512]{2,1,0:T(8,128)(2,1)} %get-tuple-element.200), channel_id=1, source_target_pairs={{0,4},{4,0},{1,5},{5,1},{2,6},{6,2},{3,7},{7,3},{8,12},{12,8},{9,1... | collective-permute-start | bytes 786440 | tf_op jit(solution)/shard_map/ppermute | solution.py:59
  554.4 25.6 %collective-permute-start.79 = (bf16[2,128,1024]{2,1,0:T(8,128)(2,1)}, bf16[2,128,1024]{2,1,0:T(8,128)(2,1)}, u32[]{:S(2)}, u32[]{:S(2)}) collective-permute-start(bf16[2,128,1024]{2,1,0:T(8,128)(2,1)} %get-tuple-element.208), channel_id=1, source_target_pairs={{0,4},{4,0},{1,5},{5,1},{2,6},{6,2},{3,7},{7,3},{8,12},{12,8},{9,1... | collective-permute-start | bytes 1572872 | tf_op jit(solution)/shard_map/ppermute | solution.py:59
  560.7 11.8 %collective-permute-start.56 = (f32[52,128]{1,0:T(8,128)S(1)}, f32[52,128]{1,0:T(8,128)S(1)}, u32[]{:S(2)}, u32[]{:S(2)}) collective-permute-start(f32[52,128]{1,0:T(8,128)S(1)} %fusion.88), channel_id=1, source_target_pairs={{0,4},{4,0},{1,5},{5,1},{2,6},{6,2},{3,7},{7,3},{8,12},{12,8},{9,1... | collective-permute-start | bytes 79880 | tf_op jit(solution)/shard_map/ppermute | solution.py:59
  563.9 20.7 %collective-permute-start.63 = (bf16[4,128,384]{2,1,0:T(8,128)(2,1)S(1)}, bf16[4,128,384]{2,1,0:T(8,128)(2,1)S(1)}, u32[]{:S(2)}, u32[]{:S(2)}) collective-permute-start(bf16[4,128,384]{2,1,0:T(8,128)(2,1)S(1)} %get-tuple-element.194), channel_id=1, source_target_pairs={{0,4},{4,0},{1,5},{5,1},{2,6},{6,2},{3,7},{7,3},{8,12},{12,8},{9,1... | collective-permute-start | bytes 1179656 | tf_op jit(solution)/shard_map/ppermute | solution.py:59
  576.7 13.6 %collective-permute-start.78 = (bf16[2,128,512]{2,1,0:T(8,128)(2,1)S(1)}, bf16[2,128,512]{2,1,0:T(8,128)(2,1)S(1)}, u32[]{:S(2)}, u32[]{:S(2)}) collective-permute-start(bf16[2,128,512]{2,1,0:T(8,128)(2,1)S(1)} %get-tuple-element.202), channel_id=1, source_target_pairs={{0,2},{2,0},{1,3},{3,1},{4,6},{6,4},{5,7},{7,5},{8,10},{10,8},{9,1... | collective-permute-start | bytes 786440 | tf_op jit(solution)/shard_map/ppermute | solution.py:55
  582.3 22.4 %collective-permute-start.80 = (bf16[2,128,1024]{2,1,0:T(8,128)(2,1)S(1)}, bf16[2,128,1024]{2,1,0:T(8,128)(2,1)}, u32[]{:S(2)}, u32[]{:S(2)}) collective-permute-start(bf16[2,128,1024]{2,1,0:T(8,128)(2,1)S(1)} %get-tuple-element.210), channel_id=1, source_target_pairs={{0,2},{2,0},{1,3},{3,1},{4,6},{6,4},{5,7},{7,5},{8,10},{10,8},{9,1... | collective-permute-start | bytes 1572872 | tf_op jit(solution)/shard_map/ppermute | solution.py:55
  587.3 13.8 %collective-permute-start.70 = (bf16[128,640]{1,0:T(8,128)(2,1)}, bf16[128,640]{1,0:T(8,128)(2,1)}, u32[]{:S(2)}, u32[]{:S(2)}) collective-permute-start(bf16[128,640]{1,0:T(8,128)(2,1)} %get-tuple-element.295), channel_id=1, source_target_pairs={{24,16},{0,8},{25,17},{1,9},{26,18},{2,10},{27,19},{3,11},{28,20},... | collective-permute-start | bytes 491528 | tf_op jit(solution)/shard_map/ppermute | solution.py:139
  592.0 21.0 %collective-permute-start.69 = (bf16[128,640]{1,0:T(8,128)(2,1)}, bf16[128,640]{1,0:T(8,128)(2,1)S(1)}, u32[]{:S(2)}, u32[]{:S(2)}) collective-permute-start(bf16[128,640]{1,0:T(8,128)(2,1)} %get-tuple-element.297), channel_id=1, source_target_pairs={{0,8},{8,16},{16,24},{1,9},{9,17},{17,25},{2,10},{10,18},{18,26},{... | collective-permute-start | bytes 491528 | tf_op jit(solution)/shard_map/ppermute | solution.py:141
  596.7 16.4 %collective-permute-start.68 = (bf16[128,640]{1,0:T(8,128)(2,1)}, bf16[128,640]{1,0:T(8,128)(2,1)}, u32[]{:S(2)}, u32[]{:S(2)}) collective-permute-start(bf16[128,640]{1,0:T(8,128)(2,1)} %get-tuple-element.296), channel_id=1, source_target_pairs={{8,0},{16,8},{24,16},{9,1},{17,9},{25,17},{10,2},{18,10},{26,18},{... | collective-permute-start | bytes 491528 | tf_op jit(solution)/shard_map/ppermute | solution.py:140
  599.9 11.0 %collective-permute-start.60 = (bf16[2,128,896]{2,1,0:T(8,128)(2,1)S(1)}, bf16[2,128,896]{2,1,0:T(8,128)(2,1)S(1)}, u32[]{:S(2)}, u32[]{:S(2)}) collective-permute-start(bf16[2,128,896]{2,1,0:T(8,128)(2,1)S(1)} %get-tuple-element.185), channel_id=1, source_target_pairs={{0,4},{4,0},{1,5},{5,1},{2,6},{6,2},{3,7},{7,3},{8,12},{12,8},{9,1... | collective-permute-start | bytes 1376264 | tf_op jit(solution)/shard_map/ppermute | solution.py:59
  602.9 10.1 %collective-permute-start.71 = (bf16[128,640]{1,0:T(8,128)(2,1)}, bf16[128,640]{1,0:T(8,128)(2,1)}, u32[]{:S(2)}, u32[]{:S(2)}) collective-permute-start(bf16[128,640]{1,0:T(8,128)(2,1)} %fusion.43), channel_id=1, source_target_pairs={{0,16},{8,24},{16,0},{24,8},{1,17},{9,25},{17,1},{25,9},{2,18},{10... | collective-permute-start | bytes 491528 | tf_op jit(solution)/shard_map/ppermute | solution.py:143
  (177 other events, 1189.7 us)
Sparse Core Ops, SparseCore 0:
  47.0 105.7 all-gather.3
  154.4 79.3 all-gather.5
  235.3 44.5 all-gather.7
  301.2 43.3 reduce-scatter.6
  346.8 77.1 reduce-scatter.4
  426.2 43.1 reduce-scatter.10
  477.4 69.3 reduce-scatter.8

commit v3 on v2

--- a/solution.py
+++ b/solution.py
@@ -90,15 +90,18 @@
     )
 
 
-def act_gather(v, ti):
+def act_gather(v, ti, *earlier):
     rows, n = v.shape
+    got = (swap_t(v), swap_x(v), swap_xt(v))
+    if earlier:
+        v = after(v, *earlier)
     near = pl.pallas_call(
         place_pair,
         in_specs=[SMEM] + [VMEM] * 4,
         out_specs=VMEM,
         out_shape=jax.ShapeDtypeStruct((4 * rows, n), v.dtype),
         compiler_params=grant(8),
-    )(ti.reshape(1), v, swap_t(v), swap_x(v), swap_xt(v))
+    )(ti.reshape(1), v, *got)
     return near, swap_c(near)
 
 
@@ -128,41 +131,26 @@
     return jnp.stack([v, jnp.where(zi == 3, last, above), two, jnp.where(zi == 0, last, below)])
 
 
-def z_scatter_small(parts, zi, depth):
-    if depth != 4:
-        return lax.psum_scatter(parts.astype(BF), "z", scatter_dimension=0, tiled=False).astype(F32)
-
-    def part(k):
-        return lax.dynamic_index_in_dim(parts, (zi + k) % 4, 0, keepdims=False)
-
-    one, two, three = part(1).astype(BF), part(2), part(3).astype(BF)
-    corner = lax.ppermute(jnp.where(zi == 3, one, three), "z", [(3, 2), (0, 1)])
-    down = lax.ppermute(three, "z", [(1, 0), (2, 1), (3, 2)])
-    up = lax.ppermute(one, "z", [(0, 1), (1, 2), (2, 3)])
-    mid = (two + corner.astype(F32)).astype(BF)
-    far = lax.ppermute(mid, "z", [(0, 2), (1, 3), (2, 0), (3, 1)])
-    return part(0) + down.astype(F32) + up.astype(F32) + far.astype(F32)
-
-
 def sum_z(v, depth):
     if depth != 4:
         return lax.psum(v, "z")
-    v = v + lax.ppermute(v, "z", [(0, 1), (1, 0), (2, 3), (3, 2)])
-    return v + lax.ppermute(v, "z", [(0, 2), (2, 0), (1, 3), (3, 1)])
-
-
-def sum_all(v, depth):
+    one = lax.ppermute(v, "z", [(0, 1), (1, 0), (2, 3), (3, 2)])
+    two = lax.ppermute(v, "z", [(0, 2), (2, 0), (1, 3), (3, 1)])
+    three = lax.ppermute(v, "z", [(0, 3), (3, 0), (1, 2), (2, 1)])
+    return (v + one) + (two + three)
+
+
+def sum_all(v, depth, *earlier):
     v = v + swap_c(v)
-    v = v + swap_x(v)
-    v = v + swap_t(v)
+    v = (v + swap_t(v)) + (swap_x(v) + swap_xt(v))
+    v = after(v, *earlier)
     return sum_z(v, depth)
 
 
 def sum_group(v):
     v = v + jnp.roll(swap_c(v), 2, axis=0)
-    got = swap_x(v)
-    v = v + jnp.stack([got[1], got[0], got[3], got[2]])
-    return v + swap_t(v)
+    far = swap_x(v) + swap_xt(v)
+    return (v + swap_t(v)) + jnp.stack([far[1], far[0], far[3], far[2]])
 
 
 HIGH = lax.Precision.HIGHEST
@@ -285,7 +273,7 @@
 
 def mixer_backward(heads, total_chans, mix_ref, row_ref, seg_ref, seg_row_ref, taps_ref, staps_ref,
                    pick_ref, head_ref, cos_ref, sin_ref, slot_ref, grad_ref, gated_ref, scale_ref,
-                   gain_ref, sum_ref, mix_low_ref, kv_low_ref, state_ref, small_ref, staps_out_ref):
+                   gain_ref, sum_ref, mix_low_ref, row_low_ref, small_ref, staps_out_ref):
     rows = mix_ref.shape[0]
     chans = heads * HEAD
     seg_col, seg_row = seg_ref[...], seg_row_ref[0]
@@ -363,7 +351,7 @@
     state_grad, stap_grads = filter_rows_back(
         state_raw, staps, masks, act_grad * (ssig * (1.0 + spre * (1.0 - ssig)))
     )
-    state_ref[...] = state_grad
+    row_low_ref[:, : 2 * NS] = state_grad.astype(BF)
     staps_out_ref[0] = jnp.zeros(staps_out_ref.shape[1:], F32)
     for i, v in enumerate(stap_grads):
         staps_out_ref[0, i : i + 1] = v
@@ -384,9 +372,10 @@
     query_grad = mm(scores_low, keys) * root
     keys_grad = mm_lt(scores_low, query) * root
     mix_low_ref[:, 2 * chans :] = rope(query_grad, cosine, -sine).astype(BF)
-    kv_low_ref[:, :HEAD] = rope(keys_grad, cosine, -sine).astype(BF)
-    kv_low_ref[:, HEAD : 2 * HEAD] = values_grad.astype(BF)
-    kv_low_ref[:, 2 * HEAD :] = mm(step_pre_grad.astype(BF), slot_ref[...]).astype(BF)
+    at = 2 * NS
+    row_low_ref[:, at : at + HEAD] = rope(keys_grad, cosine, -sine).astype(BF)
+    row_low_ref[:, at + HEAD : at + 2 * HEAD] = values_grad.astype(BF)
+    row_low_ref[:, at + 2 * HEAD :] = mm(step_pre_grad.astype(BF), slot_ref[...]).astype(BF)
 
 
 def over_groups(kernel, groups, rows, args, whole, outs):
@@ -468,8 +457,10 @@
     )(ti.reshape(1), keep, got)
 
 
-def join_rows(mine, to_t, to_x, to_xt):
+def join_rows(mine, to_t, to_x, to_xt, earlier=()):
     got = (swap_t(to_t), swap_x(to_x), swap_xt(to_xt))
+    if earlier:
+        mine = after(mine, *earlier)
     return mine + got[0].astype(F32) + got[1].astype(F32) + got[2].astype(F32)
 
 
@@ -551,9 +542,14 @@
     )
 
 
-def start_kernel(xi_ref, blocks_ref, keep_ref, send_ref):
-    keep_ref[...] = blocks_ref[xi_ref[0]]
-    send_ref[...] = blocks_ref[1 - xi_ref[0]]
+def start_kernel(xi_ref, *refs):
+    keep_ref, send_ref = refs[-2:]
+    x, at = xi_ref[0], 0
+    for ref in refs[:-2]:
+        n = ref.shape[-1]
+        keep_ref[:, :, at : at + n] = ref[x]
+        send_ref[:, :, at : at + n] = ref[1 - x]
+        at += n
 
 
 def finish_kernel(plan, at_ref, keep_ref, got_ref, *outs):
@@ -577,23 +573,33 @@
                 at += n
 
 
-def deal_back(summed, plan, widths, xi, ci):
-    shard = summed.shape[0] // 4
-    blocks = summed.reshape(2, 2, shard, -1)
-    shape = jax.ShapeDtypeStruct(blocks.shape[1:], BF)
-    keep, send = simple(start_kernel, (xi.reshape(1), blocks), [shape, shape])
-    keep, got = middle(keep, send, xi, ci)
+def deal_start(summed, xi):
+    shard = summed[0].shape[0] // 4
+    blocks = [v.reshape(2, 2, shard, -1) for v in summed]
+    shape = jax.ShapeDtypeStruct((2, shard, sum(v.shape[-1] for v in blocks)), BF)
+    return simple(start_kernel, (xi.reshape(1), *blocks), [shape, shape])
+
+
+def deal_middle(keep, send, ci):
+    shape = jax.ShapeDtypeStruct(keep.shape, BF)
+    return simple(middle_kernel, (ci.reshape(1), keep, swap_x(send)), [shape, shape])
+
+
+def deal_finish(keep, send, plan, widths, xi, ci):
+    shard = keep.shape[1]
     shapes = {"turned": lambda n: (4 * n, shard), "two": lambda n: (shard, 2, 4 * n)}
     outs = [
         jax.ShapeDtypeStruct(shapes.get(k, lambda n: (shard, 4 * n))(n), F32)
         for n, k in zip(widths, plan)
     ]
     return simple(
-        functools.partial(finish_kernel, plan), (jnp.stack([xi, ci]), keep, got), outs
-    )
-
-
-def kv_first_kernel(ci_ref, part_ref, keep_ref, send_ref):
+        functools.partial(finish_kernel, plan),
+        (jnp.stack([xi, ci]), keep, swap_c(send)),
+        outs,
+    )
+
+
+def row_first_kernel(ci_ref, part_ref, keep_ref, send_ref):
     c = ci_ref[0]
     for k in range(part_ref.shape[0]):
         for x in range(2):
@@ -601,7 +607,7 @@
             send_ref[x, k] = part_ref[k, x, 1 - c]
 
 
-def kv_second_kernel(xi_ref, keep_ref, got_ref, keep_out, send_out):
+def row_second_kernel(xi_ref, keep_ref, got_ref, keep_out, send_out):
     x = xi_ref[0]
     keep_out[...] = keep_ref[x].astype(F32) + got_ref[x].astype(F32)
     send_out[...] = (keep_ref[1 - x].astype(F32) + got_ref[1 - x].astype(F32)).astype(BF)
@@ -666,7 +672,6 @@
     wide = chans + HEAD
 
     row_z = z_gather_rel(row_own, row_got, zi, depth)
-    first_mine = after(first_mine, row_z)
     first_w = z_gather(first_mine)
     row_x = swap_x(row_z)
     row_full, small = simple(
@@ -749,14 +754,14 @@
     )
     then_send = after(then_send, normed[0], row_x)
     then_mine = deal_out(then_keep, then_send, xi, ci)
-    gu_w, down_w = z_gather(then_mine[:, : 2 * ffn]), z_gather(then_mine[:, 2 * ffn :])
+    then_w = z_gather(then_mine)
     grad_out = cotangent.astype(F32)
     feed_low = after((live_mine * grad_out).astype(BF), then_mine)
-    feed_grad = act_gather(feed_low, ti)
     row_out = times(normed, row_full)
     first_w = after(first_w, row_out)
     out_w, mix_w = first_w[:, :wide], first_w[:, wide:]
     mix_out = times(normed, mix_w)
+    feed_grad = act_gather(feed_low, ti, *mix_out)
 
     per_half = list(
         zip(mix_out, row_out, halves(seg_cols), halves(seg_rows), halves(cosine), halves(sine))
@@ -794,31 +799,34 @@
     second, scale_two = norm_rows(hidden, second_full)
 
     second_all = act_gather(second.astype(BF), ti)
-    gu_low, activation = [], []
-    for second_half, feed_half in zip(second_all, feed_grad):
-        gate_up_out = dot(second_half, gu_w)
-        gate_part, up_part = gate_up_out[:, :ffn], gate_up_out[:, ffn:]
+    gu_w, down_w = then_w[:, : 2 * ffn], then_w[:, 2 * ffn :]
+    gate_up_out = times(second_all, gu_w)
+    activation = [(jax.nn.silu(v[:, :ffn]) * v[:, ffn:]).astype(BF) for v in gate_up_out]
+    down_term = grads(feed_grad, activation)
+    down_w = after(down_w, down_term)
+    gu_low = []
+    for v, feed_half in zip(gate_up_out, feed_grad):
+        gate_part, up_part = v[:, :ffn], v[:, ffn:]
         act_grad = dot(feed_half, down_w)
-        act = jax.nn.silu(gate_part)
-        activation.append((act * up_part).astype(BF))
         gu_low.append(
-            jnp.concatenate([act_grad * up_part * silu_slope(gate_part), act_grad * act], axis=1)
-            .astype(BF)
+            jnp.concatenate(
+                [
+                    act_grad * up_part * silu_slope(gate_part),
+                    act_grad * jax.nn.silu(gate_part),
+                ],
+                axis=1,
+            ).astype(BF)
         )
-    down_sum = z_scatter(grads(feed_grad, activation))
+    down_sum = z_scatter(down_term)
     gu_sum = z_scatter(grads(second_all, gu_low))
     second_split = split_back([(gu_low, gu_w)], ti)
     second_grad = join_rows(*second_split)
     feed_split = split_back([(after(activation, second_split), down_w)], ti)
     hidden_part, second_gain_grad = norm_rows_back(hidden, second_full, scale_two, second_grad)
     hidden_grad = grad_out + hidden_part
-    mix_grad = act_gather((live_mine * hidden_grad).astype(BF), ti)
-    feed_split = after(feed_split, mix_grad[0])
-    output = (hidden + live_mine * join_rows(*feed_split)).astype(BF)
-    (down_weight_grad,) = deal_back(
-        after(down_sum, mix_grad[0]), ("turned",), (ffn,), xi, ci
-    )
-    branch_grad = times(mix_grad, after(out_w, feed_split))
+    mix_low_rows = after((live_mine * hidden_grad).astype(BF), feed_split, down_sum)
+    mix_grad = act_gather(mix_low_rows, ti)
+    branch_grad = times(mix_grad, out_w)
     out_term = grads(mix_grad, branch)
     out_sum = z_scatter(out_term)
 
@@ -829,7 +837,10 @@
         ]
     )
     inner_sum = sum_group(jnp.broadcast_to(inner_sum, (4, 8, group)))
-    inner_sum = halves(after(inner_sum, out_term))
+    inner_sum = after(inner_sum, out_term)
+    feed_split = after(feed_split, inner_sum)
+    output = (hidden + live_mine * join_rows(*feed_split)).astype(BF)
+    inner_sum = halves(inner_sum)
     inner_sum = (inner_sum[0], after(inner_sum[1], gu_sum))
     back = [
         over_groups(
@@ -840,68 +851,72 @@
             whole + (True, False, False, False, True, False),
             [
                 jax.ShapeDtypeStruct((count // 2, 2 * chans + HEAD), BF),
-                jax.ShapeDtypeStruct((count // 2, 3 * HEAD), BF),
-                jax.ShapeDtypeStruct((count // 2, 2 * NS), F32),
+                jax.ShapeDtypeStruct((count // 2, row_wide), BF),
                 jax.ShapeDtypeStruct((2, 16, chans), F32),
                 jax.ShapeDtypeStruct((2, 8, 2 * NS), F32),
             ],
         )
         for i, common in enumerate(near_far)
     ]
-    mix_low, kv_low, state_raw_grad, small_rows, small_state = zip(*back)
-    normed_late = after(normed, output, down_weight_grad)
-    mix_term = grads(normed_late, mix_low)
+    mix_low, row_low, small_rows, small_state = zip(*back)
+    then_parts = deal_start(after((down_sum, gu_sum), output), xi)
+    mix_term = grads(after(normed, then_parts), mix_low)
+    then_parts = deal_middle(*then_parts, ci)
     mix_sum = z_scatter(mix_term)
 
     small_rows = jnp.concatenate(small_rows)
     small_state = jnp.concatenate(small_state)
     state_taps_grad = jnp.sum(small_state, axis=0)[: CONV + 1]
-    state_near = after(state_raw_grad[0], mix_term)
-    state_split = split_rows(state_near, state_raw_grad[1], ti)
     summed_split = split_back(
-        [(after(mix_low, state_split), mix_w), (kv_low, row_full[:, kv_at:])], ti
-    )
-    head_rows_sum = jnp.sum(after(small_rows, summed_split), axis=0)
-    head_all = spread_xc(sum_z(head_rows_sum, depth), xi, ci).reshape(4, 16, chans)
-    state_low = join_rows(*state_split).astype(BF)
-    summed = join_rows(*summed_split)
-    (gate_up_grad,) = deal_back(after(gu_sum, summed_split), ("two",), (ffn,), xi, ci)
-    mixer_out_grad, attend_out_grad = deal_back(
-        after(out_sum, summed_split), ("turned",) * 2, (chans, HEAD), xi, ci
-    )
-    state_low_all = act_gather(state_low, ti)
-    normed_grad = summed + contract("tn,cn->tc", state_low, state_full)
+        [(after(mix_low, mix_term, then_parts), mix_w), (row_low, row_full)], ti
+    )
+    row_part = grads(normed, after(row_low, summed_split)).reshape(depth, 2, 2, shard, row_wide)
+    shape = jax.ShapeDtypeStruct((2, depth, shard, row_wide), BF)
+    keep, send = simple(row_first_kernel, (ci.reshape(1), row_part), [shape, shape], grant_of=16)
+    keep, send = simple(
+        row_second_kernel,
+        (xi.reshape(1), keep, swap_c(send)),
+        [jax.ShapeDtypeStruct(shape.shape[1:], F32), jax.ShapeDtypeStruct(shape.shape[1:], BF)],
+        grant_of=16,
+    )
+    row_x = swap_x(send)
+    down_weight_grad, gate_up_grad = deal_finish(
+        *then_parts, ("turned", "two"), (ffn, ffn), xi, ci
+    )
+    ready = (send, down_weight_grad, gate_up_grad)
+    normed_grad = join_rows(*summed_split, earlier=ready)
+    out_parts = deal_middle(*deal_start((after(out_sum, normed_grad),), xi), ci)
+    mixer_out_grad, attend_out_grad = deal_finish(
+        *out_parts, ("turned",) * 2, (chans, HEAD), xi, ci
+    )
+    row_sum_xc = after(keep, normed_grad) + row_x.astype(F32)
+    row_sum = z_scatter(row_sum_xc.astype(BF).reshape(depth * shard, row_wide))
     resid_part, first_gain_grad = norm_rows_back(resid, first_full, scale_one, normed_grad)
     tokens_grad = hidden_grad + resid_part
 
-    mixer_in_grad, query_weight_grad = deal_back(
-        mix_sum, ("two", ""), (chans, HEAD), xi, ci
-    )
-    kv_part = grads(normed, after(kv_low, summed_split)).reshape(depth, 2, 2, shard, 3 * HEAD)
-    shape = jax.ShapeDtypeStruct((2, depth, shard, 3 * HEAD), BF)
-    kv_keep, kv_send = simple(kv_first_kernel, (ci.reshape(1), kv_part), [shape, shape])
-    kv_keep, kv_send = simple(
-        kv_second_kernel,
-        (xi.reshape(1), kv_keep, swap_c(kv_send)),
-        [jax.ShapeDtypeStruct(shape.shape[1:], F32), jax.ShapeDtypeStruct(shape.shape[1:], BF)],
-    )
-    kv_sum = kv_keep + swap_x(kv_send).astype(F32)
-    state_part = grads(normed, state_low_all).reshape(depth, 4, shard, 2 * NS)
-    state_part = lax.dynamic_slice(
-        state_part, (0, me, 0, ti * NS), (depth, 1, shard, NS)
-    )[:, 0].astype(F32)
-    row_part = jnp.concatenate([kv_sum, state_part], axis=2)
-    row_sum = z_scatter_small(row_part, zi, depth)
-    keys_values_grad = row_sum[:, : 2 * HEAD].reshape(shard, 2, HEAD)
-    step_weight_grad = row_sum[:, 2 * HEAD : 2 * HEAD + heads_in]
-    state_mine = row_sum[:, 3 * HEAD :]
-    state_weight_grad = order_t(
-        state_mine, swap_t(state_mine.astype(BF)).astype(F32), ti, axis=1
-    )
+    mix_parts = deal_middle(*deal_start((mix_sum,), xi), ci)
+    mixer_in_grad, query_weight_grad = deal_finish(
+        *mix_parts, ("two", ""), (chans, HEAD), xi, ci
+    )
+    state_sum = row_sum[:, :kv_at]
+    state_weight_grad = state_sum.astype(F32) + swap_t(state_sum).astype(F32)
+    row_sum = row_sum.astype(F32)
+    keys_values_grad = row_sum[:, kv_at : kv_at + 2 * HEAD].reshape(shard, 2, HEAD)
+    step_weight_grad = row_sum[:, kv_at + 2 * HEAD : kv_at + 2 * HEAD + heads_in]
 
     dp_at = zi * 4 + me
+    head_sum = (small_rows[0] + small_rows[1] + small_rows[2] + small_rows[3])[:9]
+    slots_of = jnp.arange(8)[:, None, None] == ti * 4 + me
+    head_part = jnp.where(slots_of, head_sum[None], 0.0)
     parts = [second_gain_grad, state_taps_grad.reshape(-1), first_gain_grad]
-    packed = sum_all(jnp.concatenate(parts).reshape(-1, 128), depth).reshape(-1)
+    packed = jnp.concatenate(
+        [head_part.reshape(-1, 128), jnp.concatenate(parts).reshape(-1, 128)]
+    )
+    packed = sum_all(packed, depth, row_sum_xc)
+    head_all = lax.dynamic_slice_in_dim(
+        packed[: head_part.size // 128], ti * (head_part.size // 256), head_part.size // 256
+    )
+    packed = packed[head_part.size // 128 :].reshape(-1)
     second_mine = lax.dynamic_slice_in_dim(packed, dp_at * shard, shard)
     first_mine = lax.dynamic_slice_in_dim(
         packed[packed.size - width :], dp_at * shard, shard
@@ -914,7 +929,7 @@
         1,
     )
     by_head = jnp.transpose(
-        head_all[:, :9].reshape(4, 9, heads, HEAD), (1, 0, 2, 3)
+        head_all.reshape(4, 9, heads, HEAD), (1, 0, 2, 3)
     ).reshape(9, heads_in, HEAD)
     taps_out = lax.dynamic_slice_in_dim(by_head[: CONV + 1], dp_at * eighth, eighth, 2)
     gate_out = lax.dynamic_slice_in_dim(by_head[5], dp_at * eighth, eighth, 1)

time: 636 us -> 602 us (0.947)
  starting transfers between devices: 99.8 us -> 66.4 us
  waiting for transfers between devices: 232 us -> 248 us
  other arithmetic: 32.4 us -> 23 us
  matrix products: 118 us -> 109 us
  local copies, waits for them, and re-layouts: 65.3 us -> 73 us
  Pallas kernels: 64.3 us -> 56.9 us
    unnamed x316 -> x320, local copies, waits for them, and re-layouts: 39.1 us -> 54.8 us
    ppermute x8 -> x3, waiting for transfers between devices: 0.02 us -> 14.8 us  [the longest x1 13.5 us: sum_z(): three = lax.ppermute(v, 'z', [(0, 3), (3, 0), (1, 2), (2, 1)])]
    ppermute x22 -> x18, waiting for transfers between devices: 106 us -> 94 us  [swap_x(): return lax.ppermute(v, 'x', [(0, 1), (1, 0)])]
    ppermute x8 -> x3, starting transfers between devices: 14.5 us -> 3.98 us  [the longest x1 2.8 us: sum_z(): two = lax.ppermute(v, 'z', [(0, 2), (2, 0), (1, 3), (3, 1)])]
    reduce_scatter x4, starting transfers between devices: 10.6 us -> 1.42 us  [z_scatter(): return lax.psum_scatter(v, 'z', scatter_dimension=0, tiled=True)]
    dot_general x23 -> x20, matrix products: 73.8 us -> 65.4 us  [contract(): return jnp.einsum(form, left, right, preferred_element_type=F32)]
    ppermute x23 -> x19, starting transfers between devices: 26.3 us -> 19.2 us  [swap_c(): return lax.ppermute(v, 'c', [(0, 1), (1, 0)])]
    ppermute x10 -> x11, waiting for transfers between devices: 59.3 us -> 66.1 us  [swap_xt(): return lax.ppermute(v, ('x', 't'), [(0, 3), (1, 2), (2, 1), (3, 0)])]
  transfers between devices with their start and end apart: 88 -> 74, of which waited for: 37 -> 42; matrix products, arithmetic and copies ran while one was open for 25% -> 24% of each run, Pallas kernels for 10% -> 9%
where the time goes in v3:
time: 602 us; the launch traced here: 592 us
  waiting for transfers between devices  248 us (41%)
  matrix products  109 us (18%)
  local copies, waits for them, and re-layouts  73 us (12%)
  starting transfers between devices  66.4 us (11%)
  Pallas kernels  56.9 us (9%)
  other arithmetic  23 us (4%)
  between operations  16.7 us (3%)
    ppermute x18, waiting for transfers between devices, swap_x(): return lax.ppermute(v, 'x', [(0, 1), (1, 0)])  94 us
    ppermute x11, waiting for transfers between devices, swap_xt(): return lax.ppermute(v, ('x', 't'), [(0, 3), (1, 2), (2, 1), (3, 0)])  66.1 us
    dot_general x20, matrix products, contract(): return jnp.einsum(form, left, right, preferred_element_type=F32)  65.4 us
    unnamed x320, local copies, waits for them, and re-layouts  54.8 us
    dot_general x10, matrix products, dot(): return jnp.dot(left, right, preferred_element_type=F32)  43.1 us
    ppermute x12, waiting for transfers between devices, swap_t(): return lax.ppermute(v, 't', [(0, 1), (1, 0)])  38.2 us
    pallas_call x4, Pallas kernels, over_groups(): pl.pallas_call(kernel, grid=(groups,), in_specs=specs, out_specs=[spec(o....  29.3 us
    ppermute x19, starting transfers between devices, swap_c(): return lax.ppermute(v, 'c', [(0, 1), (1, 0)])  19.2 us
  transfers between devices with their start and end apart: 74, of which 42 were waited for; matrix products, arithmetic and copies ran while one was open for 24% of the time, Pallas kernels for 9%

profile of v3, /device:TPU:17, one launch (start us, length us, event | category | flops | bytes accessed | tf_op | source)
XLA Modules:
  0.0 592.3 jit_solution(17688397135230830231)
XLA Ops:
  7.3 2.8 fusion.80
  13.0 3.2 collective-permute-start.3
  16.2 3.0 collective-permute-start.2
  19.2 4.2 collective-permute-done
  23.4 9.6 %collective-permute-done.3 = bf16[144,896]{1,0:T(8,128)(2,1)S(1)} collective-permute-done((bf16[144,896]{1,0:T(8,128)(2,1)S(1)}, bf16[144,896]{1,0:T(8,128)(2,1)S(1)}, u32[]{:S(2)}, u32[]{:S(2)}) %collective-permute-start.3) | collective-permute-done | bytes 258080 | tf_op jit(solution)/shard_map/ppermute | solution.py:121
  39.0 5.6 collective-permute-done.1
  47.7 21.8 %collective-permute-done.4.x_ref = bf16[4,144,896]{2,1,0:T(8,128)(2,1)S(1)} collective-permute-done((bf16[4,144,896]{2,1,0:T(8,128)(2,1)S(1)}, bf16[4,144,896]{2,1,0:T(8,128)(2,1)S(1)}, u32[]{:S(2)}, u32[]{:S(2)}) %collective-permute-start.4) | collective-permute-done | bytes 1032224 | tf_op jit(solution)/shard_map/ppermute | solution.py:59
  83.6 7.2 %collective-permute-done.7.t_ref = bf16[128,2048]{1,0:T(8,128)(2,1)S(1)} collective-permute-done((bf16[128,2048]{1,0:T(8,128)(2,1)S(1)}, bf16[128,2048]{1,0:T(8,128)(2,1)S(1)}, u32[]{:S(2)}, u32[]{:S(2)}) %collective-permute-start.7) | collective-permute-done | bytes 524320 | tf_op jit(solution)/shard_map/ppermute | solution.py:63
  91.7 11.2 %collective-permute-done.9.xt_ref = bf16[128,2048]{1,0:T(8,128)(2,1)} collective-permute-done((bf16[128,2048]{1,0:T(8,128)(2,1)S(1)}, bf16[128,2048]{1,0:T(8,128)(2,1)}, u32[]{:S(2)}, u32[]{:S(2)}) %collective-permute-start.9) | collective-permute-done | bytes 524320 | tf_op jit(solution)/shard_map/ppermute | solution.py:67
  102.9 2.6 shard_map.340
  108.9 17.9 %collective-permute-done.17.got_ref = bf16[2,128,1536]{2,1,0:T(8,128)(2,1)S(1)} collective-permute-done((bf16[2,128,1536]{2,1,0:T(8,128)(2,1)}, bf16[2,128,1536]{2,1,0:T(8,128)(2,1)S(1)}, u32[]{:S(2)}, u32[]{:S(2)}) %collective-permute-start.17) | collective-permute-done | bytes 786464 | tf_op jit(solution)/shard_map/ppermute | solution.py:59
  127.7 3.1 multiply_sine_fusion
  130.8 6.2 %fusion.92.row_ref = f32[512,896]{1,0:T(8,128)} fusion(bf16[512,2048]{1,0:T(8,128)(2,1)} %shard_map.340, bf16[2048,896]{1,0:T(8,128)(2,1)} %bitcast.139), kind=kOutput, calls=%fused_computation.212 | convolution fusion | flops 1879048192 | bytes 7602176 | tf_op jit(solution)/shard_map/dot_general | solution.py:26
  142.0 6.3 %fusion.93.row_ref = f32[512,896]{1,0:T(8,128)} fusion(bf16[512,2048]{1,0:T(8,128)(2,1)} %collective-permute-done.12, bf16[2048,896]{1,0:T(8,128)(2,1)} %bitcast.140), kind=kOutput, calls=%fused_computation.213 | convolution fusion | flops 1879048192 | bytes 7602176 | tf_op jit(solution)/shard_map/dot_general | solution.py:26
  148.3 5.3 fusion.13.mix_ref
  153.7 4.8 fusion.11.mix_ref
  160.1 4.4 collective-permute-done.21.xt_ref
  170.3 5.0 shard_map.344
  176.2 5.0 shard_map.345
  191.4 3.0 collective-permute-done.14
  199.3 2.5 collective-permute-done.23.got_ref
  205.7 11.5 %collective-permute-done.26 = bf16[128,2048]{1,0:T(8,128)(2,1)S(1)} collective-permute-done((bf16[128,2048]{1,0:T(8,128)(2,1)S(1)}, bf16[128,2048]{1,0:T(8,128)(2,1)S(1)}, u32[]{:S(2)}, u32[]{:S(2)}) %collective-permute-start.26) | collective-permute-done | bytes 524320 | tf_op jit(solution)/shard_map/ppermute | solution.py:67
  217.2 10.1 %collective-permute-done.25 = bf16[128,2048]{1,0:T(8,128)(2,1)S(1)} collective-permute-done((bf16[128,2048]{1,0:T(8,128)(2,1)S(1)}, bf16[128,2048]{1,0:T(8,128)(2,1)S(1)}, u32[]{:S(2)}, u32[]{:S(2)}) %collective-permute-start.25) | collective-permute-done | bytes 524320 | tf_op jit(solution)/shard_map/ppermute | solution.py:59
  230.3 2.3 collective-permute-start.29
  232.6 10.6 %collective-permute-done.27.t_ref = bf16[128,2048]{1,0:T(8,128)(2,1)S(1)} collective-permute-done((bf16[128,2048]{1,0:T(8,128)(2,1)S(1)}, bf16[128,2048]{1,0:T(8,128)(2,1)S(1)}, u32[]{:S(2)}, u32[]{:S(2)}) %collective-permute-start.27) | collective-permute-done | bytes 524320 | tf_op jit(solution)/shard_map/ppermute | solution.py:63
  243.2 12.0 %collective-permute-done.29.xt_ref = bf16[128,2048]{1,0:T(8,128)(2,1)S(1)} collective-permute-done((bf16[128,2048]{1,0:T(8,128)(2,1)S(1)}, bf16[128,2048]{1,0:T(8,128)(2,1)S(1)}, u32[]{:S(2)}, u32[]{:S(2)}) %collective-permute-start.29) | collective-permute-done | bytes 524320 | tf_op jit(solution)/shard_map/ppermute | solution.py:67
  258.2 5.3 fusion.5
  263.8 4.5 fusion.3
  270.8 2.9 fusion.94
  273.7 2.8 add_convert_fusion.5
  279.0 3.9 multiply_convert_fusion.2
  283.0 4.4 fusion.33
  290.0 6.2 %add_convert_fusion = bf16[2048,1024]{1,0:T(8,128)(2,1)} fusion(f32[2048,1024]{1,0:T(8,128)S(1)} %fusion.33, bf16[512,2048]{1,0:T(8,128)(2,1)} %shard_map.351, bf16[512,512]{1,0:T(8,128)(2,1)S(1)} %get-tuple-element.311, bf16[512,512]{1,0:T(8,128)(2,1)S(1)} %get-tuple-element.310), kind=kOutput, calls=%fused_computation | convolution fusion | flops 2153775104 | bytes 15728640 | tf_op jit(solution)/shard_map/tc,tk->ck/dot_general | solution.py:30
  296.8 5.0 convolution_convert_fusion
  301.8 4.6 fusion.1.total_ref
  314.0 10.5 %collective-permute-done.35 = bf16[128,2048]{1,0:T(8,128)(2,1)S(1)} collective-permute-done((bf16[128,2048]{1,0:T(8,128)(2,1)S(1)}, bf16[128,2048]{1,0:T(8,128)(2,1)S(1)}, u32[]{:S(2)}, u32[]{:S(2)}) %collective-permute-start.35) | collective-permute-done | bytes 524320 | tf_op jit(solution)/shard_map/ppermute | solution.py:67
  324.5 10.2 %collective-permute-done.34 = bf16[128,2048]{1,0:T(8,128)(2,1)S(1)} collective-permute-done((bf16[128,2048]{1,0:T(8,128)(2,1)S(1)}, bf16[128,2048]{1,0:T(8,128)(2,1)S(1)}, u32[]{:S(2)}, u32[]{:S(2)}) %collective-permute-start.34) | collective-permute-done | bytes 524320 | tf_op jit(solution)/shard_map/ppermute | solution.py:59
  344.4 10.6 %collective-permute-done.36.t_ref = bf16[128,2048]{1,0:T(8,128)(2,1)S(1)} collective-permute-done((bf16[128,2048]{1,0:T(8,128)(2,1)S(1)}, bf16[128,2048]{1,0:T(8,128)(2,1)S(1)}, u32[]{:S(2)}, u32[]{:S(2)}) %collective-permute-start.36) | collective-permute-done | bytes 524320 | tf_op jit(solution)/shard_map/ppermute | solution.py:63
  355.1 11.9 %collective-permute-done.38.xt_ref = bf16[128,2048]{1,0:T(8,128)(2,1)S(1)} collective-permute-done((bf16[128,2048]{1,0:T(8,128)(2,1)S(1)}, bf16[128,2048]{1,0:T(8,128)(2,1)S(1)}, u32[]{:S(2)}, u32[]{:S(2)}) %collective-permute-start.38) | collective-permute-done | bytes 524320 | tf_op jit(solution)/shard_map/ppermute | solution.py:67
  375.2 2.7 add_convert_fusion.4
  379.5 3.0 fusion.97.grad_ref
  399.7 9.5 %shard_map.355 = (bf16[512,896]{1,0:T(8,128)(2,1)S(1)}, bf16[512,896]{1,0:T(8,128)(2,1)S(1)}, f32[2,16,384]{2,1,0:T(8,128)S(1)}, f32[2,8,512]{2,1,0:T(8,128)S(1)}) custom-call(f32[512,896]{1,0:T(8,128)S(1)} %copy-done.7, f32[512,896]{1,0:T(8,128)S(1)} %copy-done.5, f32[512,128]{1,0:T(8,128)S(1)} %copy-done.25, ...), custom_call_target="tpu_custom_call" | custom-call | tf_op jit(solution)/shard_map/pallas_call | solution.py:393
  425.2 9.7 %shard_map.356 = (bf16[512,896]{1,0:T(8,128)(2,1)S(1)}, bf16[512,896]{1,0:T(8,128)(2,1)S(1)}, f32[2,16,384]{2,1,0:T(8,128)S(1)}, f32[2,8,512]{2,1,0:T(8,128)S(1)}) custom-call(f32[512,896]{1,0:T(8,128)S(1)} %copy-done.3, f32[512,896]{1,0:T(8,128)S(1)} %copy-done.1, f32[512,128]{1,0:T(8,128)S(1)} %copy-done.23, ...), custom_call_target="tpu_custom_call" | custom-call | tf_op jit(solution)/shard_map/pallas_call | solution.py:393
  435.0 4.7 fusion.98
  439.7 5.8 add_convert_fusion.2
  449.7 4.5 fusion.7
  454.3 2.4 add_convert_fusion.3
  457.5 2.4 fusion.9
  459.8 2.4 convolution_add_fusion.total_ref
  466.0 4.0 fusion.99
  470.0 4.0 add_convert_fusion.1
  483.2 3.4 shard_map.362
  492.5 10.4 %collective-permute-done.52 = bf16[128,2048]{1,0:T(8,128)(2,1)} collective-permute-done((bf16[128,2048]{1,0:T(8,128)(2,1)}, bf16[128,2048]{1,0:T(8,128)(2,1)}, u32[]{:S(2)}, u32[]{:S(2)}) %collective-permute-start.52) | collective-permute-done | bytes 524320 | tf_op jit(solution)/shard_map/ppermute | solution.py:59
  504.0 3.3 fusion.25
  513.2 14.9 %collective-permute-done.65.got_ref = bf16[2,128,512]{2,1,0:T(8,128)(2,1)S(1)} collective-permute-done((bf16[2,128,512]{2,1,0:T(8,128)(2,1)S(1)}, bf16[2,128,512]{2,1,0:T(8,128)(2,1)S(1)}, u32[]{:S(2)}, u32[]{:S(2)}) %collective-permute-start.65) | collective-permute-done | bytes 262176 | tf_op jit(solution)/shard_map/ppermute | solution.py:59
  531.0 3.8 collective-permute-done.57
  534.9 2.3 convert_add_fusion
  537.2 2.8 collective-permute-start.60
  541.3 3.6 fusion.24
  547.8 13.5 %collective-permute-done.61 = f32[268,128]{1,0:T(8,128)S(1)} collective-permute-done((f32[268,128]{1,0:T(8,128)S(1)}, f32[268,128]{1,0:T(8,128)S(1)}, u32[]{:S(2)}, u32[]{:S(2)}) %collective-permute-start.61) | collective-permute-done | bytes 137248 | tf_op jit(solution)/shard_map/ppermute | solution.py:139
  563.1 5.7 reduce-scatter.16.cloned.1.call-done
  570.0 3.5 collective-permute-done.62.got_ref
  573.7 2.4 collective-permute-start.63
  582.8 2.2 shard_map.365
  (616 shorter events, 184.6 us)
Async XLA Ops:
  7.2 141.1 %all-gather.3.cloned.1.call-start = ((), (), s32[]{:S(2)}) async-start(), calls=%async_computation.5 | async-start | bytes 7208960 | tf_op jit(solution)/shard_map/all_gather | solution.py:109
  10.6 22.4 %collective-permute-start.10 = (bf16[2,128,1408]{2,1,0:T(8,128)(2,1)S(1)}, bf16[2,128,1408]{2,1,0:T(8,128)(2,1)S(1)}, u32[]{:S(2)}, u32[]{:S(2)}) collective-permute-start(bf16[2,128,1408]{2,1,0:T(8,128)(2,1)S(1)} %get-tuple-element.112), channel_id=1, source_target_pairs={{0,4},{4,0},{1,5},{5,1},{2,6},{6,2},{3,7},{7,3},{8,12},{12,8},{9,1... | collective-permute-start | bytes 2162696 | tf_op jit(solution)/shard_map/ppermute | solution.py:59
  12.8 10.6 %collective-permute-start = (bf16[144,896]{1,0:T(8,128)(2,1)S(1)}, bf16[144,896]{1,0:T(8,128)(2,1)}, u32[]{:S(2)}, u32[]{:S(2)}) collective-permute-start(bf16[144,896]{1,0:T(8,128)(2,1)S(1)} %fusion.42), channel_id=1, source_target_pairs={{0,16},{8,24},{16,0},{24,8},{1,17},{9,25},{17,1},{25,9},{2,18},{10... | collective-permute-start | bytes 774152 | tf_op jit(solution)/shard_map/ppermute | solution.py:120
  13.0 20.1 %collective-permute-start.3 = (bf16[144,896]{1,0:T(8,128)(2,1)S(1)}, bf16[144,896]{1,0:T(8,128)(2,1)S(1)}, u32[]{:S(2)}, u32[]{:S(2)}) collective-permute-start(bf16[144,896]{1,0:T(8,128)(2,1)S(1)} %fusion.42), channel_id=1, source_target_pairs={{0,8},{8,16},{16,24},{1,9},{9,17},{17,25},{2,10},{10,18},{18,26},{... | collective-permute-start | bytes 774152 | tf_op jit(solution)/shard_map/ppermute | solution.py:121
  16.2 16.9 %collective-permute-start.2 = (bf16[144,896]{1,0:T(8,128)(2,1)S(1)}, bf16[144,896]{1,0:T(8,128)(2,1)S(1)}, u32[]{:S(2)}, u32[]{:S(2)}) collective-permute-start(bf16[144,896]{1,0:T(8,128)(2,1)S(1)} %fusion.42), channel_id=1, source_target_pairs={{8,0},{16,8},{24,16},{9,1},{17,9},{25,17},{10,2},{18,10},{26,18},{... | collective-permute-start | bytes 774152 | tf_op jit(solution)/shard_map/ppermute | solution.py:122
  37.3 220.8 %all-gather.5.cloned.1.call-start = ((), (), s32[]{:S(2)}) async-start(), calls=%async_computation.6 | async-start | bytes 7864320 | tf_op jit(solution)/shard_map/all_gather | solution.py:109
  37.4 7.3 %collective-permute-start.1 = (bf16[144,896]{1,0:T(8,128)(2,1)}, bf16[144,896]{1,0:T(8,128)(2,1)S(1)}, u32[]{:S(2)}, u32[]{:S(2)}) collective-permute-start(bf16[144,896]{1,0:T(8,128)(2,1)} %collective-permute-done), channel_id=1, source_target_pairs={{16,24},{8,0},{17,25},{9,1},{18,26},{10,2},{19,27},{11,3},{20,28},... | collective-permute-start | bytes 774152 | tf_op jit(solution)/shard_map/ppermute | solution.py:130
  45.9 23.7 %collective-permute-start.4 = (bf16[4,144,896]{2,1,0:T(8,128)(2,1)S(1)}, bf16[4,144,896]{2,1,0:T(8,128)(2,1)S(1)}, u32[]{:S(2)}, u32[]{:S(2)}) collective-permute-start(bf16[4,144,896]{2,1,0:T(8,128)(2,1)S(1)} %pad_maximum_fusion.2.own_ref), channel_id=1, source_target_pairs={{0,4},{4,0},{1,5},{5,1},{2,6},{6,2},{3,7},{7,3},{8,12},{12,8},{9,1... | collective-permute-start | bytes 3096584 | tf_op jit(solution)/shard_map/ppermute | solution.py:59
  46.6 26.8 %collective-permute-start.5 = (bf16[4,144,896]{2,1,0:T(8,128)(2,1)S(1)}, bf16[4,144,896]{2,1,0:T(8,128)(2,1)S(1)}, u32[]{:S(2)}, u32[]{:S(2)}) collective-permute-start(bf16[4,144,896]{2,1,0:T(8,128)(2,1)S(1)} %pad_maximum_fusion.2.own_ref), channel_id=1, source_target_pairs={{0,2},{2,0},{1,3},{3,1},{4,6},{6,4},{5,7},{7,5},{8,10},{10,8},{9,1... | collective-permute-start | bytes 3096584 | tf_op jit(solution)/shard_map/ppermute | solution.py:55
  77.6 13.1 %collective-permute-start.7 = (bf16[128,2048]{1,0:T(8,128)(2,1)S(1)}, bf16[128,2048]{1,0:T(8,128)(2,1)S(1)}, u32[]{:S(2)}, u32[]{:S(2)}) collective-permute-start(bf16[128,2048]{1,0:T(8,128)(2,1)S(1)} %fusion.20.own_ref), channel_id=1, source_target_pairs={{0,1},{1,0},{2,3},{3,2},{4,5},{5,4},{6,7},{7,6},{8,9},{9,8},{10,11... | collective-permute-start | bytes 1572872 | tf_op jit(solution)/shard_map/ppermute | solution.py:63
  78.8 12.9 %collective-permute-start.8 = (bf16[128,2048]{1,0:T(8,128)(2,1)S(1)}, bf16[128,2048]{1,0:T(8,128)(2,1)S(1)}, u32[]{:S(2)}, u32[]{:S(2)}) collective-permute-start(bf16[128,2048]{1,0:T(8,128)(2,1)S(1)} %fusion.20.own_ref), channel_id=1, source_target_pairs={{0,4},{4,0},{1,5},{5,1},{2,6},{6,2},{3,7},{7,3},{8,12},{12,8},{9,1... | collective-permute-start | bytes 1572872 | tf_op jit(solution)/shard_map/ppermute | solution.py:59
  79.1 23.9 %collective-permute-start.9 = (bf16[128,2048]{1,0:T(8,128)(2,1)S(1)}, bf16[128,2048]{1,0:T(8,128)(2,1)}, u32[]{:S(2)}, u32[]{:S(2)}) collective-permute-start(bf16[128,2048]{1,0:T(8,128)(2,1)S(1)} %fusion.20.own_ref), channel_id=1, source_target_pairs={{0,5},{1,4},{4,1},{5,0},{2,7},{3,6},{6,3},{7,2},{8,13},{9,12},{12,... | collective-permute-start | bytes 1572872 | tf_op jit(solution)/shard_map/ppermute | solution.py:67
  105.5 36.4 %collective-permute-start.12 = (bf16[512,2048]{1,0:T(8,128)(2,1)}, bf16[512,2048]{1,0:T(8,128)(2,1)}, u32[]{:S(2)}, u32[]{:S(2)}) collective-permute-start(bf16[512,2048]{1,0:T(8,128)(2,1)} %shard_map.340), channel_id=1, source_target_pairs={{0,2},{2,0},{1,3},{3,1},{4,6},{6,4},{5,7},{7,5},{8,10},{10,8},{9,1... | collective-permute-start | bytes 6291464 | tf_op jit(solution)/shard_map/ppermute | solution.py:55
  107.3 19.5 %collective-permute-start.17 = (bf16[2,128,1536]{2,1,0:T(8,128)(2,1)}, bf16[2,128,1536]{2,1,0:T(8,128)(2,1)S(1)}, u32[]{:S(2)}, u32[]{:S(2)}) collective-permute-start(bf16[2,128,1536]{2,1,0:T(8,128)(2,1)} %get-tuple-element.123), channel_id=1, source_target_pairs={{0,4},{4,0},{1,5},{5,1},{2,6},{6,2},{3,7},{7,3},{8,12},{12,8},{9,1... | collective-permute-start | bytes 2359304 | tf_op jit(solution)/shard_map/ppermute | solution.py:59
  126.9 10.1 %collective-permute-start.18 = (bf16[2,128,1536]{2,1,0:T(8,128)(2,1)S(1)}, bf16[2,128,1536]{2,1,0:T(8,128)(2,1)S(1)}, u32[]{:S(2)}, u32[]{:S(2)}) collective-permute-start(bf16[2,128,1536]{2,1,0:T(8,128)(2,1)S(1)} %get-tuple-element.125), channel_id=1, source_target_pairs={{0,2},{2,0},{1,3},{3,1},{4,6},{6,4},{5,7},{7,5},{8,10},{10,8},{9,1... | collective-permute-start | bytes 2359304 | tf_op jit(solution)/shard_map/ppermute | solution.py:55
  138.8 19.7 %collective-permute-start.19 = (bf16[128,2048]{1,0:T(8,128)(2,1)S(1)}, bf16[128,2048]{1,0:T(8,128)(2,1)S(1)}, u32[]{:S(2)}, u32[]{:S(2)}) collective-permute-start(bf16[128,2048]{1,0:T(8,128)(2,1)S(1)} %fusion.19.own_ref), channel_id=1, source_target_pairs={{0,1},{1,0},{2,3},{3,2},{4,5},{5,4},{6,7},{7,6},{8,9},{9,8},{10,11... | collective-permute-start | bytes 1572872 | tf_op jit(solution)/shard_map/ppermute | solution.py:63
  140.0 19.3 %collective-permute-start.20 = (bf16[128,2048]{1,0:T(8,128)(2,1)S(1)}, bf16[128,2048]{1,0:T(8,128)(2,1)S(1)}, u32[]{:S(2)}, u32[]{:S(2)}) collective-permute-start(bf16[128,2048]{1,0:T(8,128)(2,1)S(1)} %fusion.19.own_ref), channel_id=1, source_target_pairs={{0,4},{4,0},{1,5},{5,1},{2,6},{6,2},{3,7},{7,3},{8,12},{12,8},{9,1... | collective-permute-start | bytes 1572872 | tf_op jit(solution)/shard_map/ppermute | solution.py:59
  140.3 24.3 %collective-permute-start.21 = (bf16[128,2048]{1,0:T(8,128)(2,1)S(1)}, bf16[128,2048]{1,0:T(8,128)(2,1)S(1)}, u32[]{:S(2)}, u32[]{:S(2)}) collective-permute-start(bf16[128,2048]{1,0:T(8,128)(2,1)S(1)} %fusion.19.own_ref), channel_id=1, source_target_pairs={{0,5},{1,4},{4,1},{5,0},{2,7},{3,6},{6,3},{7,2},{8,13},{9,12},{12,... | collective-permute-start | bytes 1572872 | tf_op jit(solution)/shard_map/ppermute | solution.py:67
  141.5 200.3 %reduce-scatter.8.cloned.1.call-start = ((), (), s32[]{:S(2)}) async-start(), calls=%async_computation.7 | async-start | bytes 2621440 | tf_op jit(solution)/shard_map/reduce_scatter | solution.py:113
  168.6 26.0 %collective-permute-start.22 = (bf16[512,2048]{1,0:T(8,128)(2,1)S(1)}, bf16[512,2048]{1,0:T(8,128)(2,1)}, u32[]{:S(2)}, u32[]{:S(2)}) collective-permute-start(bf16[512,2048]{1,0:T(8,128)(2,1)S(1)} %shard_map.349), channel_id=1, source_target_pairs={{0,2},{2,0},{1,3},{3,1},{4,6},{6,4},{5,7},{7,5},{8,10},{10,8},{9,1... | collective-permute-start | bytes 6291464 | tf_op jit(solution)/shard_map/ppermute | solution.py:55
  186.8 4.6 collective-permute-start.15
  196.3 5.5 collective-permute-start.23
  203.0 14.2 %collective-permute-start.26 = (bf16[128,2048]{1,0:T(8,128)(2,1)S(1)}, bf16[128,2048]{1,0:T(8,128)(2,1)S(1)}, u32[]{:S(2)}, u32[]{:S(2)}) collective-permute-start(bf16[128,2048]{1,0:T(8,128)(2,1)S(1)} %get-tuple-element.134), channel_id=1, source_target_pairs={{0,5},{1,4},{4,1},{5,0},{2,7},{3,6},{6,3},{7,2},{8,13},{9,12},{12,... | collective-permute-start | bytes 1572872 | tf_op jit(solution)/shard_map/ppermute | solution.py:67
  203.2 24.2 %collective-permute-start.25 = (bf16[128,2048]{1,0:T(8,128)(2,1)S(1)}, bf16[128,2048]{1,0:T(8,128)(2,1)S(1)}, u32[]{:S(2)}, u32[]{:S(2)}) collective-permute-start(bf16[128,2048]{1,0:T(8,128)(2,1)S(1)} %get-tuple-element.133), channel_id=1, source_target_pairs={{0,4},{4,0},{1,5},{5,1},{2,6},{6,2},{3,7},{7,3},{8,12},{12,8},{9,1... | collective-permute-start | bytes 1572872 | tf_op jit(solution)/shard_map/ppermute | solution.py:59
  204.4 24.7 %collective-permute-start.24 = (bf16[128,2048]{1,0:T(8,128)(2,1)S(1)}, bf16[128,2048]{1,0:T(8,128)(2,1)S(1)}, u32[]{:S(2)}, u32[]{:S(2)}) collective-permute-start(bf16[128,2048]{1,0:T(8,128)(2,1)S(1)} %get-tuple-element.132), channel_id=1, source_target_pairs={{0,1},{1,0},{2,3},{3,2},{4,5},{5,4},{6,7},{7,6},{8,9},{9,8},{10,11... | collective-permute-start | bytes 1572872 | tf_op jit(solution)/shard_map/ppermute | solution.py:63
  229.9 13.3 %collective-permute-start.27 = (bf16[128,2048]{1,0:T(8,128)(2,1)S(1)}, bf16[128,2048]{1,0:T(8,128)(2,1)S(1)}, u32[]{:S(2)}, u32[]{:S(2)}) collective-permute-start(bf16[128,2048]{1,0:T(8,128)(2,1)S(1)} %multiply_convert_fusion.7.own_ref), channel_id=1, source_target_pairs={{0,1},{1,0},{2,3},{3,2},{4,5},{5,4},{6,7},{7,6},{8,9},{9,8},{10,11... | collective-permute-start | bytes 1572872 | tf_op jit(solution)/shard_map/ppermute | solution.py:63
  230.1 13.0 %collective-permute-start.28 = (bf16[128,2048]{1,0:T(8,128)(2,1)S(1)}, bf16[128,2048]{1,0:T(8,128)(2,1)S(1)}, u32[]{:S(2)}, u32[]{:S(2)}) collective-permute-start(bf16[128,2048]{1,0:T(8,128)(2,1)S(1)} %multiply_convert_fusion.7.own_ref), channel_id=1, source_target_pairs={{0,4},{4,0},{1,5},{5,1},{2,6},{6,2},{3,7},{7,3},{8,12},{12,8},{9,1... | collective-permute-start | bytes 1572872 | tf_op jit(solution)/shard_map/ppermute | solution.py:59
  230.3 24.9 %collective-permute-start.29 = (bf16[128,2048]{1,0:T(8,128)(2,1)S(1)}, bf16[128,2048]{1,0:T(8,128)(2,1)S(1)}, u32[]{:S(2)}, u32[]{:S(2)}) collective-permute-start(bf16[128,2048]{1,0:T(8,128)(2,1)S(1)} %multiply_convert_fusion.7.own_ref), channel_id=1, source_target_pairs={{0,5},{1,4},{4,1},{5,0},{2,7},{3,6},{6,3},{7,2},{8,13},{9,12},{12,... | collective-permute-start | bytes 1572872 | tf_op jit(solution)/shard_map/ppermute | solution.py:67
  256.6 7.2 %collective-permute-start.30 = (bf16[512,2048]{1,0:T(8,128)(2,1)}, bf16[512,2048]{1,0:T(8,128)(2,1)}, u32[]{:S(2)}, u32[]{:S(2)}) collective-permute-start(bf16[512,2048]{1,0:T(8,128)(2,1)} %shard_map.351), channel_id=1, source_target_pairs={{0,2},{2,0},{1,3},{3,1},{4,6},{6,4},{5,7},{7,5},{8,10},{10,8},{9,1... | collective-permute-start | bytes 6291464 | tf_op jit(solution)/shard_map/ppermute | solution.py:55
  276.5 140.7 %reduce-scatter.10.cloned.1.call-start = ((), (), s32[]{:S(2)}) async-start(), calls=%async_computation.8 | async-start | bytes 5242880 | tf_op jit(solution)/shard_map/reduce_scatter | solution.py:113
  296.3 211.5 %reduce-scatter.14.cloned.1.call-start = ((), (), s32[]{:S(2)}) async-start(), calls=%async_computation.10 | async-start | bytes 2621440 | tf_op jit(solution)/shard_map/reduce_scatter | solution.py:113
  301.7 4.7 collective-permute-start.31
  309.5 28.2 %collective-permute-start.32 = (bf16[512,2048]{1,0:T(8,128)(2,1)S(1)}, bf16[512,2048]{1,0:T(8,128)(2,1)S(1)}, u32[]{:S(2)}, u32[]{:S(2)}) collective-permute-start(bf16[512,2048]{1,0:T(8,128)(2,1)S(1)} %convolution_convert_fusion.1), channel_id=1, source_target_pairs={{0,2},{2,0},{1,3},{3,1},{4,6},{6,4},{5,7},{7,5},{8,10},{10,8},{9,1... | collective-permute-start | bytes 6291464 | tf_op jit(solution)/shard_map/ppermute | solution.py:55
  310.0 14.4 %collective-permute-start.35 = (bf16[128,2048]{1,0:T(8,128)(2,1)S(1)}, bf16[128,2048]{1,0:T(8,128)(2,1)S(1)}, u32[]{:S(2)}, u32[]{:S(2)}) collective-permute-start(bf16[128,2048]{1,0:T(8,128)(2,1)S(1)} %get-tuple-element.139), channel_id=1, source_target_pairs={{0,5},{1,4},{4,1},{5,0},{2,7},{3,6},{6,3},{7,2},{8,13},{9,12},{12,... | collective-permute-start | bytes 1572872 | tf_op jit(solution)/shard_map/ppermute | solution.py:67
  311.4 23.3 %collective-permute-start.34 = (bf16[128,2048]{1,0:T(8,128)(2,1)S(1)}, bf16[128,2048]{1,0:T(8,128)(2,1)S(1)}, u32[]{:S(2)}, u32[]{:S(2)}) collective-permute-start(bf16[128,2048]{1,0:T(8,128)(2,1)S(1)} %get-tuple-element.138), channel_id=1, source_target_pairs={{0,4},{4,0},{1,5},{5,1},{2,6},{6,2},{3,7},{7,3},{8,12},{12,8},{9,1... | collective-permute-start | bytes 1572872 | tf_op jit(solution)/shard_map/ppermute | solution.py:59
  311.7 24.5 %collective-permute-start.33 = (bf16[128,2048]{1,0:T(8,128)(2,1)S(1)}, bf16[128,2048]{1,0:T(8,128)(2,1)S(1)}, u32[]{:S(2)}, u32[]{:S(2)}) collective-permute-start(bf16[128,2048]{1,0:T(8,128)(2,1)S(1)} %get-tuple-element.137), channel_id=1, source_target_pairs={{0,1},{1,0},{2,3},{3,2},{4,5},{5,4},{6,7},{7,6},{8,9},{9,8},{10,11... | collective-permute-start | bytes 1572872 | tf_op jit(solution)/shard_map/ppermute | solution.py:63
  341.7 13.2 %collective-permute-start.36 = (bf16[128,2048]{1,0:T(8,128)(2,1)S(1)}, bf16[128,2048]{1,0:T(8,128)(2,1)S(1)}, u32[]{:S(2)}, u32[]{:S(2)}) collective-permute-start(bf16[128,2048]{1,0:T(8,128)(2,1)S(1)} %multiply_convert_fusion.own_ref), channel_id=1, source_target_pairs={{0,1},{1,0},{2,3},{3,2},{4,5},{5,4},{6,7},{7,6},{8,9},{9,8},{10,11... | collective-permute-start | bytes 1572872 | tf_op jit(solution)/shard_map/ppermute | solution.py:63
  342.2 12.9 %collective-permute-start.37 = (bf16[128,2048]{1,0:T(8,128)(2,1)S(1)}, bf16[128,2048]{1,0:T(8,128)(2,1)S(1)}, u32[]{:S(2)}, u32[]{:S(2)}) collective-permute-start(bf16[128,2048]{1,0:T(8,128)(2,1)S(1)} %multiply_convert_fusion.own_ref), channel_id=1, source_target_pairs={{0,4},{4,0},{1,5},{5,1},{2,6},{6,2},{3,7},{7,3},{8,12},{12,8},{9,1... | collective-permute-start | bytes 1572872 | tf_op jit(solution)/shard_map/ppermute | solution.py:59
  343.4 23.6 %collective-permute-start.38 = (bf16[128,2048]{1,0:T(8,128)(2,1)S(1)}, bf16[128,2048]{1,0:T(8,128)(2,1)S(1)}, u32[]{:S(2)}, u32[]{:S(2)}) collective-permute-start(bf16[128,2048]{1,0:T(8,128)(2,1)S(1)} %multiply_convert_fusion.own_ref), channel_id=1, source_target_pairs={{0,5},{1,4},{4,1},{5,0},{2,7},{3,6},{6,3},{7,2},{8,13},{9,12},{12,... | collective-permute-start | bytes 1572872 | tf_op jit(solution)/shard_map/ppermute | solution.py:67
  367.1 5.4 collective-permute-start.39
  377.9 183.7 %reduce-scatter.12.cloned.1.call-start = ((), (), s32[]{:S(2)}) async-start(), calls=%async_computation.9 | async-start | bytes 4587520 | tf_op jit(solution)/shard_map/reduce_scatter | solution.py:113
  389.7 22.6 %collective-permute-start.46 = (bf16[128,2048]{1,0:T(8,128)(2,1)}, bf16[128,2048]{1,0:T(8,128)(2,1)S(1)}, u32[]{:S(2)}, u32[]{:S(2)}) collective-permute-start(bf16[128,2048]{1,0:T(8,128)(2,1)} %copy-done.80), channel_id=1, source_target_pairs={{0,5},{1,4},{4,1},{5,0},{2,7},{3,6},{6,3},{7,2},{8,13},{9,12},{12,... | collective-permute-start | bytes 1572872 | tf_op jit(solution)/shard_map/ppermute | solution.py:67
  391.0 23.3 %collective-permute-start.45 = (bf16[128,2048]{1,0:T(8,128)(2,1)}, bf16[128,2048]{1,0:T(8,128)(2,1)S(1)}, u32[]{:S(2)}, u32[]{:S(2)}) collective-permute-start(bf16[128,2048]{1,0:T(8,128)(2,1)} %copy-done.79), channel_id=1, source_target_pairs={{0,4},{4,0},{1,5},{5,1},{2,6},{6,2},{3,7},{7,3},{8,12},{12,8},{9,1... | collective-permute-start | bytes 1572872 | tf_op jit(solution)/shard_map/ppermute | solution.py:59
  392.2 23.9 %collective-permute-start.44 = (bf16[128,2048]{1,0:T(8,128)(2,1)}, bf16[128,2048]{1,0:T(8,128)(2,1)S(1)}, u32[]{:S(2)}, u32[]{:S(2)}) collective-permute-start(bf16[128,2048]{1,0:T(8,128)(2,1)} %copy-done.78), channel_id=1, source_target_pairs={{0,1},{1,0},{2,3},{3,2},{4,5},{5,4},{6,7},{7,6},{8,9},{9,8},{10,11... | collective-permute-start | bytes 1572872 | tf_op jit(solution)/shard_map/ppermute | solution.py:63
  421.6 24.1 %collective-permute-start.47 = (bf16[2,128,1536]{2,1,0:T(8,128)(2,1)}, bf16[2,128,1536]{2,1,0:T(8,128)(2,1)}, u32[]{:S(2)}, u32[]{:S(2)}) collective-permute-start(bf16[2,128,1536]{2,1,0:T(8,128)(2,1)} %get-tuple-element.158), channel_id=1, source_target_pairs={{0,4},{4,0},{1,5},{5,1},{2,6},{6,2},{3,7},{7,3},{8,12},{12,8},{9,1... | collective-permute-start | bytes 2359304 | tf_op jit(solution)/shard_map/ppermute | solution.py:59
  445.6 123.2 %reduce-scatter.16.cloned.1.call-start = ((), (), s32[]{:S(2)}) async-start(), calls=%async_computation.11 | async-start | bytes 1146880
  456.7 5.6 collective-permute-start.48
  477.0 9.7 %collective-permute-start.49 = (bf16[2,4,128,896]{3,2,1,0:T(8,128)(2,1)}, bf16[2,4,128,896]{3,2,1,0:T(8,128)(2,1)S(1)}, u32[]{:S(2)}, u32[]{:S(2)}) collective-permute-start(bf16[2,4,128,896]{3,2,1,0:T(8,128)(2,1)} %get-tuple-element.174), channel_id=1, source_target_pairs={{0,2},{2,0},{1,3},{3,1},{4,6},{6,4},{5,7},{7,5},{8,10},{10,8},{9,1... | collective-permute-start | bytes 5505032 | tf_op jit(solution)/shard_map/ppermute | solution.py:55
  477.0 5.1 collective-permute-start.50
  477.6 14.9 %collective-permute-start.53 = (bf16[128,2048]{1,0:T(8,128)(2,1)}, bf16[128,2048]{1,0:T(8,128)(2,1)}, u32[]{:S(2)}, u32[]{:S(2)}) collective-permute-start(bf16[128,2048]{1,0:T(8,128)(2,1)} %copy-done.83), channel_id=1, source_target_pairs={{0,5},{1,4},{4,1},{5,0},{2,7},{3,6},{6,3},{7,2},{8,13},{9,12},{12,... | collective-permute-start | bytes 1572872 | tf_op jit(solution)/shard_map/ppermute | solution.py:67
  478.9 23.9 %collective-permute-start.52 = (bf16[128,2048]{1,0:T(8,128)(2,1)}, bf16[128,2048]{1,0:T(8,128)(2,1)}, u32[]{:S(2)}, u32[]{:S(2)}) collective-permute-start(bf16[128,2048]{1,0:T(8,128)(2,1)} %copy-done.82), channel_id=1, source_target_pairs={{0,4},{4,0},{1,5},{5,1},{2,6},{6,2},{3,7},{7,3},{8,12},{12,8},{9,1... | collective-permute-start | bytes 1572872 | tf_op jit(solution)/shard_map/ppermute | solution.py:59
  479.2 24.8 %collective-permute-start.51 = (bf16[128,2048]{1,0:T(8,128)(2,1)}, bf16[128,2048]{1,0:T(8,128)(2,1)}, u32[]{:S(2)}, u32[]{:S(2)}) collective-permute-start(bf16[128,2048]{1,0:T(8,128)(2,1)} %copy-done.81), channel_id=1, source_target_pairs={{0,1},{1,0},{2,3},{3,2},{4,5},{5,4},{6,7},{7,6},{8,9},{9,8},{10,11... | collective-permute-start | bytes 1572872 | tf_op jit(solution)/shard_map/ppermute | solution.py:63
  492.3 42.6 %collective-permute-start.58 = (bf16[4,128,896]{2,1,0:T(8,128)(2,1)}, bf16[4,128,896]{2,1,0:T(8,128)(2,1)}, u32[]{:S(2)}, u32[]{:S(2)}) collective-permute-start(bf16[4,128,896]{2,1,0:T(8,128)(2,1)} %get-tuple-element.175), channel_id=1, source_target_pairs={{0,4},{4,0},{1,5},{5,1},{2,6},{6,2},{3,7},{7,3},{8,12},{12,8},{9,1... | collective-permute-start | bytes 2752520 | tf_op jit(solution)/shard_map/ppermute | solution.py:59
  508.9 19.1 %collective-permute-start.65 = (bf16[2,128,512]{2,1,0:T(8,128)(2,1)S(1)}, bf16[2,128,512]{2,1,0:T(8,128)(2,1)S(1)}, u32[]{:S(2)}, u32[]{:S(2)}) collective-permute-start(bf16[2,128,512]{2,1,0:T(8,128)(2,1)S(1)} %get-tuple-element.193), channel_id=1, source_target_pairs={{0,4},{4,0},{1,5},{5,1},{2,6},{6,2},{3,7},{7,3},{8,12},{12,8},{9,1... | collective-permute-start | bytes 786440 | tf_op jit(solution)/shard_map/ppermute | solution.py:59
  509.8 21.2 %collective-permute-start.56 = (f32[268,128]{1,0:T(8,128)S(1)}, f32[268,128]{1,0:T(8,128)S(1)}, u32[]{:S(2)}, u32[]{:S(2)}) collective-permute-start(f32[268,128]{1,0:T(8,128)S(1)} %fusion.76), channel_id=1, source_target_pairs={{0,4},{4,0},{1,5},{5,1},{2,6},{6,2},{3,7},{7,3},{8,12},{12,8},{9,1... | collective-permute-start | bytes 411656 | tf_op jit(solution)/shard_map/ppermute | solution.py:59
  510.5 24.3 %collective-permute-start.57 = (f32[268,128]{1,0:T(8,128)S(1)}, f32[268,128]{1,0:T(8,128)S(1)}, u32[]{:S(2)}, u32[]{:S(2)}) collective-permute-start(f32[268,128]{1,0:T(8,128)S(1)} %fusion.76), channel_id=1, source_target_pairs={{0,5},{1,4},{4,1},{5,0},{2,7},{3,6},{6,3},{7,2},{8,13},{9,12},{12,... | collective-permute-start | bytes 411656 | tf_op jit(solution)/shard_map/ppermute | solution.py:67
  511.7 23.1 %collective-permute-start.55 = (f32[268,128]{1,0:T(8,128)S(1)}, f32[268,128]{1,0:T(8,128)S(1)}, u32[]{:S(2)}, u32[]{:S(2)}) collective-permute-start(f32[268,128]{1,0:T(8,128)S(1)} %fusion.76), channel_id=1, source_target_pairs={{0,1},{1,0},{2,3},{3,2},{4,5},{5,4},{6,7},{7,6},{8,9},{9,8},{10,11... | collective-permute-start | bytes 411656 | tf_op jit(solution)/shard_map/ppermute | solution.py:63
  528.1 16.8 %collective-permute-start.66 = (bf16[2,128,512]{2,1,0:T(8,128)(2,1)S(1)}, bf16[2,128,512]{2,1,0:T(8,128)(2,1)S(1)}, u32[]{:S(2)}, u32[]{:S(2)}) collective-permute-start(bf16[2,128,512]{2,1,0:T(8,128)(2,1)S(1)} %get-tuple-element.195), channel_id=1, source_target_pairs={{0,2},{2,0},{1,3},{3,1},{4,6},{6,4},{5,7},{7,5},{8,10},{10,8},{9,1... | collective-permute-start | bytes 786440 | tf_op jit(solution)/shard_map/ppermute | solution.py:55
  537.2 10.6 %collective-permute-start.60 = (f32[268,128]{1,0:T(8,128)S(1)}, f32[268,128]{1,0:T(8,128)S(1)}, u32[]{:S(2)}, u32[]{:S(2)}) collective-permute-start(f32[268,128]{1,0:T(8,128)S(1)} %add_add_fusion.1), channel_id=1, source_target_pairs={{0,16},{16,0},{8,24},{24,8},{1,17},{17,1},{9,25},{25,9},{2,18},{18... | collective-permute-start | bytes 411656 | tf_op jit(solution)/shard_map/ppermute | solution.py:138
  540.0 21.3 %collective-permute-start.61 = (f32[268,128]{1,0:T(8,128)S(1)}, f32[268,128]{1,0:T(8,128)S(1)}, u32[]{:S(2)}, u32[]{:S(2)}) collective-permute-start(f32[268,128]{1,0:T(8,128)S(1)} %add_add_fusion.1), channel_id=1, source_target_pairs={{0,24},{24,0},{8,16},{16,8},{1,25},{25,1},{9,17},{17,9},{2,26},{26... | collective-permute-start | bytes 411656 | tf_op jit(solution)/shard_map/ppermute | solution.py:139
  540.0 21.3 %collective-permute-start.59 = (f32[268,128]{1,0:T(8,128)S(1)}, f32[268,128]{1,0:T(8,128)S(1)}, u32[]{:S(2)}, u32[]{:S(2)}) collective-permute-start(f32[268,128]{1,0:T(8,128)S(1)} %add_add_fusion.1), channel_id=1, source_target_pairs={{0,8},{8,0},{16,24},{24,16},{1,9},{9,1},{17,25},{25,17},{2,10},{10... | collective-permute-start | bytes 411656 | tf_op jit(solution)/shard_map/ppermute | solution.py:137
  562.9 10.7 %collective-permute-start.62 = (bf16[2,128,896]{2,1,0:T(8,128)(2,1)S(1)}, bf16[2,128,896]{2,1,0:T(8,128)(2,1)S(1)}, u32[]{:S(2)}, u32[]{:S(2)}) collective-permute-start(bf16[2,128,896]{2,1,0:T(8,128)(2,1)S(1)} %get-tuple-element.187), channel_id=1, source_target_pairs={{0,4},{4,0},{1,5},{5,1},{2,6},{6,2},{3,7},{7,3},{8,12},{12,8},{9,1... | collective-permute-start | bytes 1376264 | tf_op jit(solution)/shard_map/ppermute | solution.py:59
  569.9 12.0 %collective-permute-start.64 = (bf16[128,512]{0,1:T(8,128)(2,1)S(1)}, bf16[128,512]{0,1:T(8,128)(2,1)S(1)}, u32[]{:S(2)}, u32[]{:S(2)}) collective-permute-start(bf16[128,512]{0,1:T(8,128)(2,1)S(1)} %slice.332), channel_id=1, source_target_pairs={{0,1},{1,0},{2,3},{3,2},{4,5},{5,4},{6,7},{7,6},{8,9},{9,8},{10,11... | collective-permute-start | bytes 393224 | tf_op jit(solution)/shard_map/ppermute | solution.py:63
  573.7 9.1 %collective-permute-start.63 = (bf16[2,128,896]{2,1,0:T(8,128)(2,1)S(1)}, bf16[2,128,896]{2,1,0:T(8,128)(2,1)S(1)}, u32[]{:S(2)}, u32[]{:S(2)}) collective-permute-start(bf16[2,128,896]{2,1,0:T(8,128)(2,1)S(1)} %get-tuple-element.189), channel_id=1, source_target_pairs={{0,2},{2,0},{1,3},{3,1},{4,6},{6,4},{5,7},{7,5},{8,10},{10,8},{9,1... | collective-permute-start | bytes 1376264 | tf_op jit(solution)/shard_map/ppermute | solution.py:55
  (164 other events, 1071.8 us)
Sparse Core Ops, SparseCore 0:
  37.4 103.7 all-gather.2
  143.4 113.5 all-gather.4
  276.6 42.6 reduce-scatter.7
  321.6 77.2 reduce-scatter.9
  401.0 43.1 reduce-scatter.13
  446.5 68.9 reduce-scatter.11
  541.4 27.3 reduce-scatter.15

commit v4 on v3

--- a/solution.py
+++ b/solution.py
@@ -142,8 +142,8 @@
 
 def sum_all(v, depth, *earlier):
     v = v + swap_c(v)
-    v = (v + swap_t(v)) + (swap_x(v) + swap_xt(v))
-    v = after(v, *earlier)
+    got = (swap_t(v), swap_x(v), swap_xt(v))
+    v = (after(v, *earlier) + got[0]) + (got[1] + got[2])
     return sum_z(v, depth)
 
 
@@ -885,12 +885,14 @@
     )
     ready = (send, down_weight_grad, gate_up_grad)
     normed_grad = join_rows(*summed_split, earlier=ready)
-    out_parts = deal_middle(*deal_start((after(out_sum, normed_grad),), xi), ci)
+    row_sum_xc = after(keep, normed_grad) + row_x.astype(F32)
+    row_sum_xc = row_sum_xc.astype(BF)
+    row_sum = z_scatter(row_sum_xc.reshape(depth * shard, row_wide))
+    out_keep, out_send = deal_start((after(out_sum, normed_grad),), xi)
+    out_parts = deal_middle(out_keep, after(out_send, row_sum_xc), ci)
     mixer_out_grad, attend_out_grad = deal_finish(
         *out_parts, ("turned",) * 2, (chans, HEAD), xi, ci
     )
-    row_sum_xc = after(keep, normed_grad) + row_x.astype(F32)
-    row_sum = z_scatter(row_sum_xc.astype(BF).reshape(depth * shard, row_wide))
     resid_part, first_gain_grad = norm_rows_back(resid, first_full, scale_one, normed_grad)
     tokens_grad = hidden_grad + resid_part
 

time: 602 us -> 595 us (0.988)
    unnamed x320 -> x318, local copies, waits for them, and re-layouts: 54.8 us -> 49.1 us
  transfers between devices with their start and end apart: 74 -> 74, of which waited for: 42 -> 44; matrix products, arithmetic and copies ran while one was open for 24% -> 24% of each run, Pallas kernels for 9% -> 9%
where the time goes in v4:
time: 595 us; the launch traced here: 586 us
  waiting for transfers between devices  248 us (42%)
  matrix products  108 us (18%)
  local copies, waits for them, and re-layouts  67.4 us (11%)
  starting transfers between devices  66.8 us (11%)
  Pallas kernels  57.4 us (10%)
  other arithmetic  20.9 us (4%)
  between operations  16.8 us (3%)
    ppermute x18, waiting for transfers between devices, swap_x(): return lax.ppermute(v, 'x', [(0, 1), (1, 0)])  91.2 us
    ppermute x11, waiting for transfers between devices, swap_xt(): return lax.ppermute(v, ('x', 't'), [(0, 3), (1, 2), (2, 1), (3, 0)])  69.5 us
    dot_general x20, matrix products, contract(): return jnp.einsum(form, left, right, preferred_element_type=F32)  65.4 us
    unnamed x318, local copies, waits for them, and re-layouts  49.1 us
    dot_general x10, matrix products, dot(): return jnp.dot(left, right, preferred_element_type=F32)  43.1 us
    ppermute x12, waiting for transfers between devices, swap_t(): return lax.ppermute(v, 't', [(0, 1), (1, 0)])  38.2 us
    pallas_call x4, Pallas kernels, over_groups(): pl.pallas_call(kernel, grid=(groups,), in_specs=specs, out_specs=[spec(o....  29.3 us
    ppermute x19, starting transfers between devices, swap_c(): return lax.ppermute(v, 'c', [(0, 1), (1, 0)])  20.1 us
  transfers between devices with their start and end apart: 74, of which 44 were waited for; matrix products, arithmetic and copies ran while one was open for 24% of the time, Pallas kernels for 9%

profile of v4, /device:TPU:17, one launch (start us, length us, event | category | flops | bytes accessed | tf_op | source)
XLA Modules:
  0.0 585.5 jit_solution(6591032372416145812)
XLA Ops:
  7.3 2.8 fusion.80
  13.0 3.2 collective-permute-start.3
  16.2 3.0 collective-permute-start.2
  19.2 4.2 collective-permute-done
  23.4 9.6 %collective-permute-done.3 = bf16[144,896]{1,0:T(8,128)(2,1)S(1)} collective-permute-done((bf16[144,896]{1,0:T(8,128)(2,1)S(1)}, bf16[144,896]{1,0:T(8,128)(2,1)S(1)}, u32[]{:S(2)}, u32[]{:S(2)}) %collective-permute-start.3) | collective-permute-done | bytes 258080 | tf_op jit(solution)/shard_map/ppermute | solution.py:121
  39.0 5.6 collective-permute-done.1
  47.7 21.8 %collective-permute-done.4.x_ref = bf16[4,144,896]{2,1,0:T(8,128)(2,1)S(1)} collective-permute-done((bf16[4,144,896]{2,1,0:T(8,128)(2,1)S(1)}, bf16[4,144,896]{2,1,0:T(8,128)(2,1)S(1)}, u32[]{:S(2)}, u32[]{:S(2)}) %collective-permute-start.4) | collective-permute-done | bytes 1032224 | tf_op jit(solution)/shard_map/ppermute | solution.py:59
  83.6 7.2 %collective-permute-done.7.t_ref = bf16[128,2048]{1,0:T(8,128)(2,1)S(1)} collective-permute-done((bf16[128,2048]{1,0:T(8,128)(2,1)S(1)}, bf16[128,2048]{1,0:T(8,128)(2,1)S(1)}, u32[]{:S(2)}, u32[]{:S(2)}) %collective-permute-start.7) | collective-permute-done | bytes 524320 | tf_op jit(solution)/shard_map/ppermute | solution.py:63
  91.8 11.2 %collective-permute-done.9.xt_ref = bf16[128,2048]{1,0:T(8,128)(2,1)} collective-permute-done((bf16[128,2048]{1,0:T(8,128)(2,1)S(1)}, bf16[128,2048]{1,0:T(8,128)(2,1)}, u32[]{:S(2)}, u32[]{:S(2)}) %collective-permute-start.9) | collective-permute-done | bytes 524320 | tf_op jit(solution)/shard_map/ppermute | solution.py:67
  102.9 2.6 shard_map.340
  108.9 17.9 %collective-permute-done.17.got_ref = bf16[2,128,1536]{2,1,0:T(8,128)(2,1)S(1)} collective-permute-done((bf16[2,128,1536]{2,1,0:T(8,128)(2,1)}, bf16[2,128,1536]{2,1,0:T(8,128)(2,1)S(1)}, u32[]{:S(2)}, u32[]{:S(2)}) %collective-permute-start.17) | collective-permute-done | bytes 786464 | tf_op jit(solution)/shard_map/ppermute | solution.py:59
  127.7 3.1 multiply_sine_fusion
  130.8 6.2 %fusion.92.row_ref = f32[512,896]{1,0:T(8,128)} fusion(bf16[512,2048]{1,0:T(8,128)(2,1)} %shard_map.340, bf16[2048,896]{1,0:T(8,128)(2,1)} %bitcast.139), kind=kOutput, calls=%fused_computation.212 | convolution fusion | flops 1879048192 | bytes 7602176 | tf_op jit(solution)/shard_map/dot_general | solution.py:26
  142.0 6.3 %fusion.93.row_ref = f32[512,896]{1,0:T(8,128)} fusion(bf16[512,2048]{1,0:T(8,128)(2,1)} %collective-permute-done.12, bf16[2048,896]{1,0:T(8,128)(2,1)} %bitcast.140), kind=kOutput, calls=%fused_computation.213 | convolution fusion | flops 1879048192 | bytes 7602176 | tf_op jit(solution)/shard_map/dot_general | solution.py:26
  148.3 5.3 fusion.13.mix_ref
  153.7 4.8 fusion.11.mix_ref
  160.1 4.4 collective-permute-done.21.xt_ref
  170.3 5.0 shard_map.344
  176.2 5.0 shard_map.345
  191.3 3.0 collective-permute-done.14
  199.3 2.5 collective-permute-done.23.got_ref
  205.7 11.5 %collective-permute-done.26 = bf16[128,2048]{1,0:T(8,128)(2,1)S(1)} collective-permute-done((bf16[128,2048]{1,0:T(8,128)(2,1)S(1)}, bf16[128,2048]{1,0:T(8,128)(2,1)S(1)}, u32[]{:S(2)}, u32[]{:S(2)}) %collective-permute-start.26) | collective-permute-done | bytes 524320 | tf_op jit(solution)/shard_map/ppermute | solution.py:67
  217.2 10.1 %collective-permute-done.25 = bf16[128,2048]{1,0:T(8,128)(2,1)S(1)} collective-permute-done((bf16[128,2048]{1,0:T(8,128)(2,1)S(1)}, bf16[128,2048]{1,0:T(8,128)(2,1)S(1)}, u32[]{:S(2)}, u32[]{:S(2)}) %collective-permute-start.25) | collective-permute-done | bytes 524320 | tf_op jit(solution)/shard_map/ppermute | solution.py:59
  230.2 2.3 collective-permute-start.29
  232.6 10.6 %collective-permute-done.27.t_ref = bf16[128,2048]{1,0:T(8,128)(2,1)S(1)} collective-permute-done((bf16[128,2048]{1,0:T(8,128)(2,1)S(1)}, bf16[128,2048]{1,0:T(8,128)(2,1)S(1)}, u32[]{:S(2)}, u32[]{:S(2)}) %collective-permute-start.27) | collective-permute-done | bytes 524320 | tf_op jit(solution)/shard_map/ppermute | solution.py:63
  243.1 12.0 %collective-permute-done.29.xt_ref = bf16[128,2048]{1,0:T(8,128)(2,1)S(1)} collective-permute-done((bf16[128,2048]{1,0:T(8,128)(2,1)S(1)}, bf16[128,2048]{1,0:T(8,128)(2,1)S(1)}, u32[]{:S(2)}, u32[]{:S(2)}) %collective-permute-start.29) | collective-permute-done | bytes 524320 | tf_op jit(solution)/shard_map/ppermute | solution.py:67
  258.1 5.3 fusion.5
  263.8 4.5 fusion.3
  270.7 2.9 fusion.94
  273.6 2.8 add_convert_fusion.5
  279.0 3.9 multiply_convert_fusion.2
  282.9 4.4 fusion.33
  290.0 6.2 %add_convert_fusion = bf16[2048,1024]{1,0:T(8,128)(2,1)} fusion(f32[2048,1024]{1,0:T(8,128)S(1)} %fusion.33, bf16[512,2048]{1,0:T(8,128)(2,1)} %shard_map.351, bf16[512,512]{1,0:T(8,128)(2,1)S(1)} %get-tuple-element.313, bf16[512,512]{1,0:T(8,128)(2,1)S(1)} %get-tuple-element.312), kind=kOutput, calls=%fused_computation | convolution fusion | flops 2153775104 | bytes 15728640 | tf_op jit(solution)/shard_map/tc,tk->ck/dot_general | solution.py:30
  296.7 5.0 convolution_convert_fusion
  301.8 4.6 fusion.1.total_ref
  313.9 10.5 %collective-permute-done.35 = bf16[128,2048]{1,0:T(8,128)(2,1)S(1)} collective-permute-done((bf16[128,2048]{1,0:T(8,128)(2,1)S(1)}, bf16[128,2048]{1,0:T(8,128)(2,1)S(1)}, u32[]{:S(2)}, u32[]{:S(2)}) %collective-permute-start.35) | collective-permute-done | bytes 524320 | tf_op jit(solution)/shard_map/ppermute | solution.py:67
  324.4 10.2 %collective-permute-done.34 = bf16[128,2048]{1,0:T(8,128)(2,1)S(1)} collective-permute-done((bf16[128,2048]{1,0:T(8,128)(2,1)S(1)}, bf16[128,2048]{1,0:T(8,128)(2,1)S(1)}, u32[]{:S(2)}, u32[]{:S(2)}) %collective-permute-start.34) | collective-permute-done | bytes 524320 | tf_op jit(solution)/shard_map/ppermute | solution.py:59
  344.3 10.6 %collective-permute-done.36.t_ref = bf16[128,2048]{1,0:T(8,128)(2,1)S(1)} collective-permute-done((bf16[128,2048]{1,0:T(8,128)(2,1)S(1)}, bf16[128,2048]{1,0:T(8,128)(2,1)S(1)}, u32[]{:S(2)}, u32[]{:S(2)}) %collective-permute-start.36) | collective-permute-done | bytes 524320 | tf_op jit(solution)/shard_map/ppermute | solution.py:63
  355.0 11.9 %collective-permute-done.38.xt_ref = bf16[128,2048]{1,0:T(8,128)(2,1)S(1)} collective-permute-done((bf16[128,2048]{1,0:T(8,128)(2,1)S(1)}, bf16[128,2048]{1,0:T(8,128)(2,1)S(1)}, u32[]{:S(2)}, u32[]{:S(2)}) %collective-permute-start.38) | collective-permute-done | bytes 524320 | tf_op jit(solution)/shard_map/ppermute | solution.py:67
  375.1 2.7 add_convert_fusion.4
  379.4 3.0 fusion.97.grad_ref
  399.8 9.5 %shard_map.355 = (bf16[512,896]{1,0:T(8,128)(2,1)S(1)}, bf16[512,896]{1,0:T(8,128)(2,1)S(1)}, f32[2,16,384]{2,1,0:T(8,128)S(1)}, f32[2,8,512]{2,1,0:T(8,128)S(1)}) custom-call(f32[512,896]{1,0:T(8,128)S(1)} %copy-done.7, f32[512,896]{1,0:T(8,128)S(1)} %copy-done.5, f32[512,128]{1,0:T(8,128)S(1)} %copy-done.25, ...), custom_call_target="tpu_custom_call" | custom-call | tf_op jit(solution)/shard_map/pallas_call | solution.py:393
  425.2 9.7 %shard_map.356 = (bf16[512,896]{1,0:T(8,128)(2,1)S(1)}, bf16[512,896]{1,0:T(8,128)(2,1)S(1)}, f32[2,16,384]{2,1,0:T(8,128)S(1)}, f32[2,8,512]{2,1,0:T(8,128)S(1)}) custom-call(f32[512,896]{1,0:T(8,128)S(1)} %copy-done.3, f32[512,896]{1,0:T(8,128)S(1)} %copy-done.1, f32[512,128]{1,0:T(8,128)S(1)} %copy-done.23, ...), custom_call_target="tpu_custom_call" | custom-call | tf_op jit(solution)/shard_map/pallas_call | solution.py:393
  435.0 4.7 fusion.98
  439.7 5.8 add_convert_fusion.2
  449.7 4.6 fusion.7
  454.3 2.4 add_convert_fusion.3
  457.4 2.4 fusion.9
  459.8 2.4 convolution_add_fusion.total_ref
  465.9 4.0 fusion.99
  469.9 4.0 add_convert_fusion.1
  481.9 3.4 shard_map.362
  487.7 3.3 collective-permute-done.53
  491.0 10.4 %collective-permute-done.52 = bf16[128,2048]{1,0:T(8,128)(2,1)} collective-permute-done((bf16[128,2048]{1,0:T(8,128)(2,1)}, bf16[128,2048]{1,0:T(8,128)(2,1)}, u32[]{:S(2)}, u32[]{:S(2)}) %collective-permute-start.52) | collective-permute-done | bytes 524320 | tf_op jit(solution)/shard_map/ppermute | solution.py:59
  502.6 2.7 fusion.25
  509.7 11.3 %collective-permute-done.55 = bf16[4,128,896]{2,1,0:T(8,128)(2,1)S(1)} collective-permute-done((bf16[4,128,896]{2,1,0:T(8,128)(2,1)S(1)}, bf16[4,128,896]{2,1,0:T(8,128)(2,1)S(1)}, u32[]{:S(2)}, u32[]{:S(2)}) %collective-permute-start.55) | collective-permute-done | bytes 917536 | tf_op jit(solution)/shard_map/ppermute | solution.py:59
  524.0 3.8 collective-permute-done.58
  527.8 2.8 collective-permute-start.60
  532.0 2.8 fusion.24
  535.9 2.5 collective-permute-done.60
  538.5 13.5 %collective-permute-done.61 = f32[268,128]{1,0:T(8,128)} collective-permute-done((f32[268,128]{1,0:T(8,128)S(1)}, f32[268,128]{1,0:T(8,128)}, u32[]{:S(2)}, u32[]{:S(2)}) %collective-permute-start.61) | collective-permute-done | bytes 137248 | tf_op jit(solution)/shard_map/ppermute | solution.py:139
  556.7 2.7 reduce-scatter.16.cloned.1.call-done
  560.7 4.0 collective-permute-done.62.got_ref
  564.8 2.8 collective-permute-start.63
  (614 shorter events, 183.6 us)
Async XLA Ops:
  7.2 141.1 %all-gather.3.cloned.1.call-start = ((), (), s32[]{:S(2)}) async-start(), calls=%async_computation.5 | async-start | bytes 7208960 | tf_op jit(solution)/shard_map/all_gather | solution.py:109
  10.6 22.4 %collective-permute-start.10 = (bf16[2,128,1408]{2,1,0:T(8,128)(2,1)S(1)}, bf16[2,128,1408]{2,1,0:T(8,128)(2,1)S(1)}, u32[]{:S(2)}, u32[]{:S(2)}) collective-permute-start(bf16[2,128,1408]{2,1,0:T(8,128)(2,1)S(1)} %get-tuple-element.113), channel_id=1, source_target_pairs={{0,4},{4,0},{1,5},{5,1},{2,6},{6,2},{3,7},{7,3},{8,12},{12,8},{9,1... | collective-permute-start | bytes 2162696 | tf_op jit(solution)/shard_map/ppermute | solution.py:59
  12.8 10.6 %collective-permute-start = (bf16[144,896]{1,0:T(8,128)(2,1)S(1)}, bf16[144,896]{1,0:T(8,128)(2,1)}, u32[]{:S(2)}, u32[]{:S(2)}) collective-permute-start(bf16[144,896]{1,0:T(8,128)(2,1)S(1)} %fusion.42), channel_id=1, source_target_pairs={{0,16},{8,24},{16,0},{24,8},{1,17},{9,25},{17,1},{25,9},{2,18},{10... | collective-permute-start | bytes 774152 | tf_op jit(solution)/shard_map/ppermute | solution.py:120
  13.0 20.1 %collective-permute-start.3 = (bf16[144,896]{1,0:T(8,128)(2,1)S(1)}, bf16[144,896]{1,0:T(8,128)(2,1)S(1)}, u32[]{:S(2)}, u32[]{:S(2)}) collective-permute-start(bf16[144,896]{1,0:T(8,128)(2,1)S(1)} %fusion.42), channel_id=1, source_target_pairs={{0,8},{8,16},{16,24},{1,9},{9,17},{17,25},{2,10},{10,18},{18,26},{... | collective-permute-start | bytes 774152 | tf_op jit(solution)/shard_map/ppermute | solution.py:121
  16.2 16.9 %collective-permute-start.2 = (bf16[144,896]{1,0:T(8,128)(2,1)S(1)}, bf16[144,896]{1,0:T(8,128)(2,1)S(1)}, u32[]{:S(2)}, u32[]{:S(2)}) collective-permute-start(bf16[144,896]{1,0:T(8,128)(2,1)S(1)} %fusion.42), channel_id=1, source_target_pairs={{8,0},{16,8},{24,16},{9,1},{17,9},{25,17},{10,2},{18,10},{26,18},{... | collective-permute-start | bytes 774152 | tf_op jit(solution)/shard_map/ppermute | solution.py:122
  37.3 220.8 %all-gather.5.cloned.1.call-start = ((), (), s32[]{:S(2)}) async-start(), calls=%async_computation.6 | async-start | bytes 7864320 | tf_op jit(solution)/shard_map/all_gather | solution.py:109
  37.4 7.3 %collective-permute-start.1 = (bf16[144,896]{1,0:T(8,128)(2,1)}, bf16[144,896]{1,0:T(8,128)(2,1)S(1)}, u32[]{:S(2)}, u32[]{:S(2)}) collective-permute-start(bf16[144,896]{1,0:T(8,128)(2,1)} %collective-permute-done), channel_id=1, source_target_pairs={{16,24},{8,0},{17,25},{9,1},{18,26},{10,2},{19,27},{11,3},{20,28},... | collective-permute-start | bytes 774152 | tf_op jit(solution)/shard_map/ppermute | solution.py:130
  45.9 23.7 %collective-permute-start.4 = (bf16[4,144,896]{2,1,0:T(8,128)(2,1)S(1)}, bf16[4,144,896]{2,1,0:T(8,128)(2,1)S(1)}, u32[]{:S(2)}, u32[]{:S(2)}) collective-permute-start(bf16[4,144,896]{2,1,0:T(8,128)(2,1)S(1)} %pad_maximum_fusion.2.own_ref), channel_id=1, source_target_pairs={{0,4},{4,0},{1,5},{5,1},{2,6},{6,2},{3,7},{7,3},{8,12},{12,8},{9,1... | collective-permute-start | bytes 3096584 | tf_op jit(solution)/shard_map/ppermute | solution.py:59
  46.6 26.8 %collective-permute-start.5 = (bf16[4,144,896]{2,1,0:T(8,128)(2,1)S(1)}, bf16[4,144,896]{2,1,0:T(8,128)(2,1)S(1)}, u32[]{:S(2)}, u32[]{:S(2)}) collective-permute-start(bf16[4,144,896]{2,1,0:T(8,128)(2,1)S(1)} %pad_maximum_fusion.2.own_ref), channel_id=1, source_target_pairs={{0,2},{2,0},{1,3},{3,1},{4,6},{6,4},{5,7},{7,5},{8,10},{10,8},{9,1... | collective-permute-start | bytes 3096584 | tf_op jit(solution)/shard_map/ppermute | solution.py:55
  77.6 13.1 %collective-permute-start.7 = (bf16[128,2048]{1,0:T(8,128)(2,1)S(1)}, bf16[128,2048]{1,0:T(8,128)(2,1)S(1)}, u32[]{:S(2)}, u32[]{:S(2)}) collective-permute-start(bf16[128,2048]{1,0:T(8,128)(2,1)S(1)} %fusion.20.own_ref), channel_id=1, source_target_pairs={{0,1},{1,0},{2,3},{3,2},{4,5},{5,4},{6,7},{7,6},{8,9},{9,8},{10,11... | collective-permute-start | bytes 1572872 | tf_op jit(solution)/shard_map/ppermute | solution.py:63
  78.8 12.9 %collective-permute-start.8 = (bf16[128,2048]{1,0:T(8,128)(2,1)S(1)}, bf16[128,2048]{1,0:T(8,128)(2,1)S(1)}, u32[]{:S(2)}, u32[]{:S(2)}) collective-permute-start(bf16[128,2048]{1,0:T(8,128)(2,1)S(1)} %fusion.20.own_ref), channel_id=1, source_target_pairs={{0,4},{4,0},{1,5},{5,1},{2,6},{6,2},{3,7},{7,3},{8,12},{12,8},{9,1... | collective-permute-start | bytes 1572872 | tf_op jit(solution)/shard_map/ppermute | solution.py:59
  79.1 23.9 %collective-permute-start.9 = (bf16[128,2048]{1,0:T(8,128)(2,1)S(1)}, bf16[128,2048]{1,0:T(8,128)(2,1)}, u32[]{:S(2)}, u32[]{:S(2)}) collective-permute-start(bf16[128,2048]{1,0:T(8,128)(2,1)S(1)} %fusion.20.own_ref), channel_id=1, source_target_pairs={{0,5},{1,4},{4,1},{5,0},{2,7},{3,6},{6,3},{7,2},{8,13},{9,12},{12,... | collective-permute-start | bytes 1572872 | tf_op jit(solution)/shard_map/ppermute | solution.py:67
  105.5 36.5 %collective-permute-start.12 = (bf16[512,2048]{1,0:T(8,128)(2,1)}, bf16[512,2048]{1,0:T(8,128)(2,1)}, u32[]{:S(2)}, u32[]{:S(2)}) collective-permute-start(bf16[512,2048]{1,0:T(8,128)(2,1)} %shard_map.340), channel_id=1, source_target_pairs={{0,2},{2,0},{1,3},{3,1},{4,6},{6,4},{5,7},{7,5},{8,10},{10,8},{9,1... | collective-permute-start | bytes 6291464 | tf_op jit(solution)/shard_map/ppermute | solution.py:55
  107.3 19.5 %collective-permute-start.17 = (bf16[2,128,1536]{2,1,0:T(8,128)(2,1)}, bf16[2,128,1536]{2,1,0:T(8,128)(2,1)S(1)}, u32[]{:S(2)}, u32[]{:S(2)}) collective-permute-start(bf16[2,128,1536]{2,1,0:T(8,128)(2,1)} %get-tuple-element.124), channel_id=1, source_target_pairs={{0,4},{4,0},{1,5},{5,1},{2,6},{6,2},{3,7},{7,3},{8,12},{12,8},{9,1... | collective-permute-start | bytes 2359304 | tf_op jit(solution)/shard_map/ppermute | solution.py:59
  126.9 10.1 %collective-permute-start.18 = (bf16[2,128,1536]{2,1,0:T(8,128)(2,1)S(1)}, bf16[2,128,1536]{2,1,0:T(8,128)(2,1)S(1)}, u32[]{:S(2)}, u32[]{:S(2)}) collective-permute-start(bf16[2,128,1536]{2,1,0:T(8,128)(2,1)S(1)} %get-tuple-element.126), channel_id=1, source_target_pairs={{0,2},{2,0},{1,3},{3,1},{4,6},{6,4},{5,7},{7,5},{8,10},{10,8},{9,1... | collective-permute-start | bytes 2359304 | tf_op jit(solution)/shard_map/ppermute | solution.py:55
  138.8 19.7 %collective-permute-start.19 = (bf16[128,2048]{1,0:T(8,128)(2,1)S(1)}, bf16[128,2048]{1,0:T(8,128)(2,1)S(1)}, u32[]{:S(2)}, u32[]{:S(2)}) collective-permute-start(bf16[128,2048]{1,0:T(8,128)(2,1)S(1)} %fusion.19.own_ref), channel_id=1, source_target_pairs={{0,1},{1,0},{2,3},{3,2},{4,5},{5,4},{6,7},{7,6},{8,9},{9,8},{10,11... | collective-permute-start | bytes 1572872 | tf_op jit(solution)/shard_map/ppermute | solution.py:63
  140.0 19.3 %collective-permute-start.20 = (bf16[128,2048]{1,0:T(8,128)(2,1)S(1)}, bf16[128,2048]{1,0:T(8,128)(2,1)S(1)}, u32[]{:S(2)}, u32[]{:S(2)}) collective-permute-start(bf16[128,2048]{1,0:T(8,128)(2,1)S(1)} %fusion.19.own_ref), channel_id=1, source_target_pairs={{0,4},{4,0},{1,5},{5,1},{2,6},{6,2},{3,7},{7,3},{8,12},{12,8},{9,1... | collective-permute-start | bytes 1572872 | tf_op jit(solution)/shard_map/ppermute | solution.py:59
  140.3 24.3 %collective-permute-start.21 = (bf16[128,2048]{1,0:T(8,128)(2,1)S(1)}, bf16[128,2048]{1,0:T(8,128)(2,1)S(1)}, u32[]{:S(2)}, u32[]{:S(2)}) collective-permute-start(bf16[128,2048]{1,0:T(8,128)(2,1)S(1)} %fusion.19.own_ref), channel_id=1, source_target_pairs={{0,5},{1,4},{4,1},{5,0},{2,7},{3,6},{6,3},{7,2},{8,13},{9,12},{12,... | collective-permute-start | bytes 1572872 | tf_op jit(solution)/shard_map/ppermute | solution.py:67
  141.5 200.2 %reduce-scatter.8.cloned.1.call-start = ((), (), s32[]{:S(2)}) async-start(), calls=%async_computation.7 | async-start | bytes 2621440 | tf_op jit(solution)/shard_map/reduce_scatter | solution.py:113
  168.6 26.0 %collective-permute-start.22 = (bf16[512,2048]{1,0:T(8,128)(2,1)S(1)}, bf16[512,2048]{1,0:T(8,128)(2,1)}, u32[]{:S(2)}, u32[]{:S(2)}) collective-permute-start(bf16[512,2048]{1,0:T(8,128)(2,1)S(1)} %shard_map.349), channel_id=1, source_target_pairs={{0,2},{2,0},{1,3},{3,1},{4,6},{6,4},{5,7},{7,5},{8,10},{10,8},{9,1... | collective-permute-start | bytes 6291464 | tf_op jit(solution)/shard_map/ppermute | solution.py:55
  186.7 4.6 collective-permute-start.15
  196.3 5.5 collective-permute-start.23
  203.0 14.2 %collective-permute-start.26 = (bf16[128,2048]{1,0:T(8,128)(2,1)S(1)}, bf16[128,2048]{1,0:T(8,128)(2,1)S(1)}, u32[]{:S(2)}, u32[]{:S(2)}) collective-permute-start(bf16[128,2048]{1,0:T(8,128)(2,1)S(1)} %get-tuple-element.135), channel_id=1, source_target_pairs={{0,5},{1,4},{4,1},{5,0},{2,7},{3,6},{6,3},{7,2},{8,13},{9,12},{12,... | collective-permute-start | bytes 1572872 | tf_op jit(solution)/shard_map/ppermute | solution.py:67
  203.2 24.1 %collective-permute-start.25 = (bf16[128,2048]{1,0:T(8,128)(2,1)S(1)}, bf16[128,2048]{1,0:T(8,128)(2,1)S(1)}, u32[]{:S(2)}, u32[]{:S(2)}) collective-permute-start(bf16[128,2048]{1,0:T(8,128)(2,1)S(1)} %get-tuple-element.134), channel_id=1, source_target_pairs={{0,4},{4,0},{1,5},{5,1},{2,6},{6,2},{3,7},{7,3},{8,12},{12,8},{9,1... | collective-permute-start | bytes 1572872 | tf_op jit(solution)/shard_map/ppermute | solution.py:59
  204.4 24.7 %collective-permute-start.24 = (bf16[128,2048]{1,0:T(8,128)(2,1)S(1)}, bf16[128,2048]{1,0:T(8,128)(2,1)S(1)}, u32[]{:S(2)}, u32[]{:S(2)}) collective-permute-start(bf16[128,2048]{1,0:T(8,128)(2,1)S(1)} %get-tuple-element.133), channel_id=1, source_target_pairs={{0,1},{1,0},{2,3},{3,2},{4,5},{5,4},{6,7},{7,6},{8,9},{9,8},{10,11... | collective-permute-start | bytes 1572872 | tf_op jit(solution)/shard_map/ppermute | solution.py:63
  229.8 13.3 %collective-permute-start.27 = (bf16[128,2048]{1,0:T(8,128)(2,1)S(1)}, bf16[128,2048]{1,0:T(8,128)(2,1)S(1)}, u32[]{:S(2)}, u32[]{:S(2)}) collective-permute-start(bf16[128,2048]{1,0:T(8,128)(2,1)S(1)} %multiply_convert_fusion.7.own_ref), channel_id=1, source_target_pairs={{0,1},{1,0},{2,3},{3,2},{4,5},{5,4},{6,7},{7,6},{8,9},{9,8},{10,11... | collective-permute-start | bytes 1572872 | tf_op jit(solution)/shard_map/ppermute | solution.py:63
  230.1 13.1 %collective-permute-start.28 = (bf16[128,2048]{1,0:T(8,128)(2,1)S(1)}, bf16[128,2048]{1,0:T(8,128)(2,1)S(1)}, u32[]{:S(2)}, u32[]{:S(2)}) collective-permute-start(bf16[128,2048]{1,0:T(8,128)(2,1)S(1)} %multiply_convert_fusion.7.own_ref), channel_id=1, source_target_pairs={{0,4},{4,0},{1,5},{5,1},{2,6},{6,2},{3,7},{7,3},{8,12},{12,8},{9,1... | collective-permute-start | bytes 1572872 | tf_op jit(solution)/shard_map/ppermute | solution.py:59
  230.2 24.9 %collective-permute-start.29 = (bf16[128,2048]{1,0:T(8,128)(2,1)S(1)}, bf16[128,2048]{1,0:T(8,128)(2,1)S(1)}, u32[]{:S(2)}, u32[]{:S(2)}) collective-permute-start(bf16[128,2048]{1,0:T(8,128)(2,1)S(1)} %multiply_convert_fusion.7.own_ref), channel_id=1, source_target_pairs={{0,5},{1,4},{4,1},{5,0},{2,7},{3,6},{6,3},{7,2},{8,13},{9,12},{12,... | collective-permute-start | bytes 1572872 | tf_op jit(solution)/shard_map/ppermute | solution.py:67
  256.6 7.2 %collective-permute-start.30 = (bf16[512,2048]{1,0:T(8,128)(2,1)}, bf16[512,2048]{1,0:T(8,128)(2,1)}, u32[]{:S(2)}, u32[]{:S(2)}) collective-permute-start(bf16[512,2048]{1,0:T(8,128)(2,1)} %shard_map.351), channel_id=1, source_target_pairs={{0,2},{2,0},{1,3},{3,1},{4,6},{6,4},{5,7},{7,5},{8,10},{10,8},{9,1... | collective-permute-start | bytes 6291464 | tf_op jit(solution)/shard_map/ppermute | solution.py:55
  276.5 140.8 %reduce-scatter.10.cloned.1.call-start = ((), (), s32[]{:S(2)}) async-start(), calls=%async_computation.8 | async-start | bytes 5242880 | tf_op jit(solution)/shard_map/reduce_scatter | solution.py:113
  296.2 238.6 %reduce-scatter.14.cloned.1.call-start = ((), (), s32[]{:S(2)}) async-start(), calls=%async_computation.10 | async-start | bytes 2621440 | tf_op jit(solution)/shard_map/reduce_scatter | solution.py:113
  301.7 4.7 collective-permute-start.31
  309.4 28.2 %collective-permute-start.32 = (bf16[512,2048]{1,0:T(8,128)(2,1)S(1)}, bf16[512,2048]{1,0:T(8,128)(2,1)S(1)}, u32[]{:S(2)}, u32[]{:S(2)}) collective-permute-start(bf16[512,2048]{1,0:T(8,128)(2,1)S(1)} %convolution_convert_fusion.1), channel_id=1, source_target_pairs={{0,2},{2,0},{1,3},{3,1},{4,6},{6,4},{5,7},{7,5},{8,10},{10,8},{9,1... | collective-permute-start | bytes 6291464 | tf_op jit(solution)/shard_map/ppermute | solution.py:55
  310.0 14.4 %collective-permute-start.35 = (bf16[128,2048]{1,0:T(8,128)(2,1)S(1)}, bf16[128,2048]{1,0:T(8,128)(2,1)S(1)}, u32[]{:S(2)}, u32[]{:S(2)}) collective-permute-start(bf16[128,2048]{1,0:T(8,128)(2,1)S(1)} %get-tuple-element.140), channel_id=1, source_target_pairs={{0,5},{1,4},{4,1},{5,0},{2,7},{3,6},{6,3},{7,2},{8,13},{9,12},{12,... | collective-permute-start | bytes 1572872 | tf_op jit(solution)/shard_map/ppermute | solution.py:67
  311.3 23.3 %collective-permute-start.34 = (bf16[128,2048]{1,0:T(8,128)(2,1)S(1)}, bf16[128,2048]{1,0:T(8,128)(2,1)S(1)}, u32[]{:S(2)}, u32[]{:S(2)}) collective-permute-start(bf16[128,2048]{1,0:T(8,128)(2,1)S(1)} %get-tuple-element.139), channel_id=1, source_target_pairs={{0,4},{4,0},{1,5},{5,1},{2,6},{6,2},{3,7},{7,3},{8,12},{12,8},{9,1... | collective-permute-start | bytes 1572872 | tf_op jit(solution)/shard_map/ppermute | solution.py:59
  311.6 24.4 %collective-permute-start.33 = (bf16[128,2048]{1,0:T(8,128)(2,1)S(1)}, bf16[128,2048]{1,0:T(8,128)(2,1)S(1)}, u32[]{:S(2)}, u32[]{:S(2)}) collective-permute-start(bf16[128,2048]{1,0:T(8,128)(2,1)S(1)} %get-tuple-element.138), channel_id=1, source_target_pairs={{0,1},{1,0},{2,3},{3,2},{4,5},{5,4},{6,7},{7,6},{8,9},{9,8},{10,11... | collective-permute-start | bytes 1572872 | tf_op jit(solution)/shard_map/ppermute | solution.py:63
  341.7 13.2 %collective-permute-start.36 = (bf16[128,2048]{1,0:T(8,128)(2,1)S(1)}, bf16[128,2048]{1,0:T(8,128)(2,1)S(1)}, u32[]{:S(2)}, u32[]{:S(2)}) collective-permute-start(bf16[128,2048]{1,0:T(8,128)(2,1)S(1)} %multiply_convert_fusion.own_ref), channel_id=1, source_target_pairs={{0,1},{1,0},{2,3},{3,2},{4,5},{5,4},{6,7},{7,6},{8,9},{9,8},{10,11... | collective-permute-start | bytes 1572872 | tf_op jit(solution)/shard_map/ppermute | solution.py:63
  342.1 12.9 %collective-permute-start.37 = (bf16[128,2048]{1,0:T(8,128)(2,1)S(1)}, bf16[128,2048]{1,0:T(8,128)(2,1)S(1)}, u32[]{:S(2)}, u32[]{:S(2)}) collective-permute-start(bf16[128,2048]{1,0:T(8,128)(2,1)S(1)} %multiply_convert_fusion.own_ref), channel_id=1, source_target_pairs={{0,4},{4,0},{1,5},{5,1},{2,6},{6,2},{3,7},{7,3},{8,12},{12,8},{9,1... | collective-permute-start | bytes 1572872 | tf_op jit(solution)/shard_map/ppermute | solution.py:59
  343.3 23.6 %collective-permute-start.38 = (bf16[128,2048]{1,0:T(8,128)(2,1)S(1)}, bf16[128,2048]{1,0:T(8,128)(2,1)S(1)}, u32[]{:S(2)}, u32[]{:S(2)}) collective-permute-start(bf16[128,2048]{1,0:T(8,128)(2,1)S(1)} %multiply_convert_fusion.own_ref), channel_id=1, source_target_pairs={{0,5},{1,4},{4,1},{5,0},{2,7},{3,6},{6,3},{7,2},{8,13},{9,12},{12,... | collective-permute-start | bytes 1572872 | tf_op jit(solution)/shard_map/ppermute | solution.py:67
  367.1 5.4 collective-permute-start.39
  377.9 175.3 %reduce-scatter.12.cloned.1.call-start = ((), (), s32[]{:S(2)}) async-start(), calls=%async_computation.9 | async-start | bytes 4587520 | tf_op jit(solution)/shard_map/reduce_scatter | solution.py:113
  389.7 22.7 %collective-permute-start.46 = (bf16[128,2048]{1,0:T(8,128)(2,1)}, bf16[128,2048]{1,0:T(8,128)(2,1)S(1)}, u32[]{:S(2)}, u32[]{:S(2)}) collective-permute-start(bf16[128,2048]{1,0:T(8,128)(2,1)} %copy-done.76), channel_id=1, source_target_pairs={{0,5},{1,4},{4,1},{5,0},{2,7},{3,6},{6,3},{7,2},{8,13},{9,12},{12,... | collective-permute-start | bytes 1572872 | tf_op jit(solution)/shard_map/ppermute | solution.py:67
  391.0 23.3 %collective-permute-start.45 = (bf16[128,2048]{1,0:T(8,128)(2,1)}, bf16[128,2048]{1,0:T(8,128)(2,1)S(1)}, u32[]{:S(2)}, u32[]{:S(2)}) collective-permute-start(bf16[128,2048]{1,0:T(8,128)(2,1)} %copy-done.75), channel_id=1, source_target_pairs={{0,4},{4,0},{1,5},{5,1},{2,6},{6,2},{3,7},{7,3},{8,12},{12,8},{9,1... | collective-permute-start | bytes 1572872 | tf_op jit(solution)/shard_map/ppermute | solution.py:59
  392.1 23.9 %collective-permute-start.44 = (bf16[128,2048]{1,0:T(8,128)(2,1)}, bf16[128,2048]{1,0:T(8,128)(2,1)S(1)}, u32[]{:S(2)}, u32[]{:S(2)}) collective-permute-start(bf16[128,2048]{1,0:T(8,128)(2,1)} %copy-done.74), channel_id=1, source_target_pairs={{0,1},{1,0},{2,3},{3,2},{4,5},{5,4},{6,7},{7,6},{8,9},{9,8},{10,11... | collective-permute-start | bytes 1572872 | tf_op jit(solution)/shard_map/ppermute | solution.py:63
  421.6 24.0 %collective-permute-start.47 = (bf16[2,128,1536]{2,1,0:T(8,128)(2,1)}, bf16[2,128,1536]{2,1,0:T(8,128)(2,1)}, u32[]{:S(2)}, u32[]{:S(2)}) collective-permute-start(bf16[2,128,1536]{2,1,0:T(8,128)(2,1)} %get-tuple-element.159), channel_id=1, source_target_pairs={{0,4},{4,0},{1,5},{5,1},{2,6},{6,2},{3,7},{7,3},{8,12},{12,8},{9,1... | collective-permute-start | bytes 2359304 | tf_op jit(solution)/shard_map/ppermute | solution.py:59
  445.6 113.8 %reduce-scatter.16.cloned.1.call-start = ((), (), s32[]{:S(2)}) async-start(), calls=%async_computation.11 | async-start | bytes 1146880
  456.7 5.6 collective-permute-start.48
  475.5 9.8 %collective-permute-start.49 = (bf16[2,4,128,896]{3,2,1,0:T(8,128)(2,1)}, bf16[2,4,128,896]{3,2,1,0:T(8,128)(2,1)}, u32[]{:S(2)}, u32[]{:S(2)}) collective-permute-start(bf16[2,4,128,896]{3,2,1,0:T(8,128)(2,1)} %get-tuple-element.175), channel_id=1, source_target_pairs={{0,2},{2,0},{1,3},{3,1},{4,6},{6,4},{5,7},{7,5},{8,10},{10,8},{9,1... | collective-permute-start | bytes 5505032 | tf_op jit(solution)/shard_map/ppermute | solution.py:55
  475.6 5.2 collective-permute-start.50
  476.2 14.8 %collective-permute-start.53 = (bf16[128,2048]{1,0:T(8,128)(2,1)}, bf16[128,2048]{1,0:T(8,128)(2,1)}, u32[]{:S(2)}, u32[]{:S(2)}) collective-permute-start(bf16[128,2048]{1,0:T(8,128)(2,1)} %copy-done.79), channel_id=1, source_target_pairs={{0,5},{1,4},{4,1},{5,0},{2,7},{3,6},{6,3},{7,2},{8,13},{9,12},{12,... | collective-permute-start | bytes 1572872 | tf_op jit(solution)/shard_map/ppermute | solution.py:67
  477.5 23.9 %collective-permute-start.52 = (bf16[128,2048]{1,0:T(8,128)(2,1)}, bf16[128,2048]{1,0:T(8,128)(2,1)}, u32[]{:S(2)}, u32[]{:S(2)}) collective-permute-start(bf16[128,2048]{1,0:T(8,128)(2,1)} %copy-done.78), channel_id=1, source_target_pairs={{0,4},{4,0},{1,5},{5,1},{2,6},{6,2},{3,7},{7,3},{8,12},{12,8},{9,1... | collective-permute-start | bytes 1572872 | tf_op jit(solution)/shard_map/ppermute | solution.py:59
  477.8 24.8 %collective-permute-start.51 = (bf16[128,2048]{1,0:T(8,128)(2,1)}, bf16[128,2048]{1,0:T(8,128)(2,1)}, u32[]{:S(2)}, u32[]{:S(2)}) collective-permute-start(bf16[128,2048]{1,0:T(8,128)(2,1)} %copy-done.77), channel_id=1, source_target_pairs={{0,1},{1,0},{2,3},{3,2},{4,5},{5,4},{6,7},{7,6},{8,9},{9,8},{10,11... | collective-permute-start | bytes 1572872 | tf_op jit(solution)/shard_map/ppermute | solution.py:63
  487.3 33.7 %collective-permute-start.55 = (bf16[4,128,896]{2,1,0:T(8,128)(2,1)S(1)}, bf16[4,128,896]{2,1,0:T(8,128)(2,1)S(1)}, u32[]{:S(2)}, u32[]{:S(2)}) collective-permute-start(bf16[4,128,896]{2,1,0:T(8,128)(2,1)S(1)} %get-tuple-element.176), channel_id=1, source_target_pairs={{0,4},{4,0},{1,5},{5,1},{2,6},{6,2},{3,7},{7,3},{8,12},{12,8},{9,1... | collective-permute-start | bytes 2752520 | tf_op jit(solution)/shard_map/ppermute | solution.py:59
  507.0 17.0 %collective-permute-start.57 = (f32[268,128]{1,0:T(8,128)S(1)}, f32[268,128]{1,0:T(8,128)S(1)}, u32[]{:S(2)}, u32[]{:S(2)}) collective-permute-start(f32[268,128]{1,0:T(8,128)S(1)} %fusion.76), channel_id=1, source_target_pairs={{0,4},{4,0},{1,5},{5,1},{2,6},{6,2},{3,7},{7,3},{8,12},{12,8},{9,1... | collective-permute-start | bytes 411656 | tf_op jit(solution)/shard_map/ppermute | solution.py:59
  507.8 19.9 %collective-permute-start.58 = (f32[268,128]{1,0:T(8,128)S(1)}, f32[268,128]{1,0:T(8,128)S(1)}, u32[]{:S(2)}, u32[]{:S(2)}) collective-permute-start(f32[268,128]{1,0:T(8,128)S(1)} %fusion.76), channel_id=1, source_target_pairs={{0,5},{1,4},{4,1},{5,0},{2,7},{3,6},{6,3},{7,2},{8,13},{9,12},{12,... | collective-permute-start | bytes 411656 | tf_op jit(solution)/shard_map/ppermute | solution.py:67
  509.0 18.8 %collective-permute-start.56 = (f32[268,128]{1,0:T(8,128)S(1)}, f32[268,128]{1,0:T(8,128)S(1)}, u32[]{:S(2)}, u32[]{:S(2)}) collective-permute-start(f32[268,128]{1,0:T(8,128)S(1)} %fusion.76), channel_id=1, source_target_pairs={{0,1},{1,0},{2,3},{3,2},{4,5},{5,4},{6,7},{7,6},{8,9},{9,8},{10,11... | collective-permute-start | bytes 411656 | tf_op jit(solution)/shard_map/ppermute | solution.py:63
  527.8 10.6 %collective-permute-start.60 = (f32[268,128]{1,0:T(8,128)S(1)}, f32[268,128]{1,0:T(8,128)}, u32[]{:S(2)}, u32[]{:S(2)}) collective-permute-start(f32[268,128]{1,0:T(8,128)S(1)} %add_add_fusion.1), channel_id=1, source_target_pairs={{0,16},{16,0},{8,24},{24,8},{1,17},{17,1},{9,25},{25,9},{2,18},{18... | collective-permute-start | bytes 411656 | tf_op jit(solution)/shard_map/ppermute | solution.py:138
  530.6 21.3 %collective-permute-start.61 = (f32[268,128]{1,0:T(8,128)S(1)}, f32[268,128]{1,0:T(8,128)}, u32[]{:S(2)}, u32[]{:S(2)}) collective-permute-start(f32[268,128]{1,0:T(8,128)S(1)} %add_add_fusion.1), channel_id=1, source_target_pairs={{0,24},{24,0},{8,16},{16,8},{1,25},{25,1},{9,17},{17,9},{2,26},{26... | collective-permute-start | bytes 411656 | tf_op jit(solution)/shard_map/ppermute | solution.py:139
  530.6 21.3 %collective-permute-start.59 = (f32[268,128]{1,0:T(8,128)S(1)}, f32[268,128]{1,0:T(8,128)}, u32[]{:S(2)}, u32[]{:S(2)}) collective-permute-start(f32[268,128]{1,0:T(8,128)S(1)} %add_add_fusion.1), channel_id=1, source_target_pairs={{0,8},{8,0},{16,24},{24,16},{1,9},{9,1},{17,25},{25,17},{2,10},{10... | collective-permute-start | bytes 411656 | tf_op jit(solution)/shard_map/ppermute | solution.py:137
  535.9 18.9 %collective-permute-start.65 = (bf16[2,128,512]{2,1,0:T(8,128)(2,1)S(1)}, bf16[2,128,512]{2,1,0:T(8,128)(2,1)S(1)}, u32[]{:S(2)}, u32[]{:S(2)}) collective-permute-start(bf16[2,128,512]{2,1,0:T(8,128)(2,1)S(1)} %get-tuple-element.195), channel_id=1, source_target_pairs={{0,4},{4,0},{1,5},{5,1},{2,6},{6,2},{3,7},{7,3},{8,12},{12,8},{9,1... | collective-permute-start | bytes 786440 | tf_op jit(solution)/shard_map/ppermute | solution.py:59
  554.4 10.3 %collective-permute-start.62 = (bf16[2,128,896]{2,1,0:T(8,128)(2,1)S(1)}, bf16[2,128,896]{2,1,0:T(8,128)(2,1)S(1)}, u32[]{:S(2)}, u32[]{:S(2)}) collective-permute-start(bf16[2,128,896]{2,1,0:T(8,128)(2,1)S(1)} %get-tuple-element.188), channel_id=1, source_target_pairs={{0,4},{4,0},{1,5},{5,1},{2,6},{6,2},{3,7},{7,3},{8,12},{12,8},{9,1... | collective-permute-start | bytes 1376264 | tf_op jit(solution)/shard_map/ppermute | solution.py:59
  554.8 17.2 %collective-permute-start.66 = (bf16[2,128,512]{2,1,0:T(8,128)(2,1)S(1)}, bf16[2,128,512]{2,1,0:T(8,128)(2,1)S(1)}, u32[]{:S(2)}, u32[]{:S(2)}) collective-permute-start(bf16[2,128,512]{2,1,0:T(8,128)(2,1)S(1)} %get-tuple-element.197), channel_id=1, source_target_pairs={{0,2},{2,0},{1,3},{3,1},{4,6},{6,4},{5,7},{7,5},{8,10},{10,8},{9,1... | collective-permute-start | bytes 786440 | tf_op jit(solution)/shard_map/ppermute | solution.py:55
  560.6 14.6 %collective-permute-start.64 = (bf16[128,512]{0,1:T(8,128)(2,1)S(1)}, bf16[128,512]{0,1:T(8,128)(2,1)S(1)}, u32[]{:S(2)}, u32[]{:S(2)}) collective-permute-start(bf16[128,512]{0,1:T(8,128)(2,1)S(1)} %slice.332), channel_id=1, source_target_pairs={{0,1},{1,0},{2,3},{3,2},{4,5},{5,4},{6,7},{7,6},{8,9},{9,8},{10,11... | collective-permute-start | bytes 393224 | tf_op jit(solution)/shard_map/ppermute | solution.py:63
  564.8 11.2 %collective-permute-start.63 = (bf16[2,128,896]{2,1,0:T(8,128)(2,1)S(1)}, bf16[2,128,896]{2,1,0:T(8,128)(2,1)S(1)}, u32[]{:S(2)}, u32[]{:S(2)}) collective-permute-start(bf16[2,128,896]{2,1,0:T(8,128)(2,1)S(1)} %get-tuple-element.190), channel_id=1, source_target_pairs={{0,2},{2,0},{1,3},{3,1},{4,6},{6,4},{5,7},{7,5},{8,10},{10,8},{9,1... | collective-permute-start | bytes 1376264 | tf_op jit(solution)/shard_map/ppermute | solution.py:55
  (163 other events, 1167.9 us)
Sparse Core Ops, SparseCore 0:
  37.4 103.7 all-gather.2
  143.4 113.5 all-gather.4
  276.6 42.6 reduce-scatter.7
  321.5 77.1 reduce-scatter.9
  400.9 43.1 reduce-scatter.13
  446.4 69.1 reduce-scatter.11
  532.1 27.3 reduce-scatter.15

commit v5 on v4

--- a/solution.py
+++ b/solution.py
@@ -900,6 +900,7 @@
     mixer_in_grad, query_weight_grad = deal_finish(
         *mix_parts, ("two", ""), (chans, HEAD), xi, ci
     )
+    row_sum = after(row_sum, mixer_in_grad)
     state_sum = row_sum[:, :kv_at]
     state_weight_grad = state_sum.astype(F32) + swap_t(state_sum).astype(F32)
     row_sum = row_sum.astype(F32)

time: 595 us -> 590 us (level)
  the two profiles are of different devices: /device:TPU:17 before, /device:TPU:0 now
where the time goes in v5:
time: 590 us; the launch traced here: 581 us
  waiting for transfers between devices  243 us (41%)
  matrix products  110 us (19%)
  local copies, waits for them, and re-layouts  68.8 us (12%)
  starting transfers between devices  64.1 us (11%)
  Pallas kernels  57.5 us (10%)
  other arithmetic  20.9 us (4%)
  between operations  17 us (3%)
    ppermute x18, waiting for transfers between devices, swap_x(): return lax.ppermute(v, 'x', [(0, 1), (1, 0)])  94.2 us
    ppermute x11, waiting for transfers between devices, swap_xt(): return lax.ppermute(v, ('x', 't'), [(0, 3), (1, 2), (2, 1), (3, 0)])  69 us
    dot_general x20, matrix products, contract(): return jnp.einsum(form, left, right, preferred_element_type=F32)  66 us
    unnamed x321, local copies, waits for them, and re-layouts  49.3 us
    dot_general x10, matrix products, dot(): return jnp.dot(left, right, preferred_element_type=F32)  43.7 us
    ppermute x12, waiting for transfers between devices, swap_t(): return lax.ppermute(v, 't', [(0, 1), (1, 0)])  35.1 us
    pallas_call x4, Pallas kernels, over_groups(): pl.pallas_call(kernel, grid=(groups,), in_specs=specs, out_specs=[spec(o....  29.2 us
    pallas_call x18, Pallas kernels, simple(): pl.pallas_call(kernel, in_specs=[SMEM] * scalars + [VMEM] * (len(args) -...  19.3 us
  transfers between devices with their start and end apart: 74, of which 43 were waited for; matrix products, arithmetic and copies ran while one was open for 24% of the time, Pallas kernels for 10%

profile of v5, /device:TPU:0, one launch (start us, length us, event | category | flops | bytes accessed | tf_op | source)
XLA Modules:
  0.0 580.7 jit_solution(14283250090341744130)
XLA Ops:
  7.3 2.8 fusion.80
  10.6 3.0 collective-permute-start.10
  14.6 2.7 collective-permute-start
  17.2 3.5 collective-permute-start.3
  22.0 8.0 %collective-permute-done = bf16[144,896]{1,0:T(8,128)(2,1)} collective-permute-done((bf16[144,896]{1,0:T(8,128)(2,1)S(1)}, bf16[144,896]{1,0:T(8,128)(2,1)}, u32[]{:S(2)}, u32[]{:S(2)}) %collective-permute-start) | collective-permute-done | bytes 258080 | tf_op jit(solution)/shard_map/ppermute | solution.py:120
  30.0 4.1 collective-permute-done.2
  40.0 8.8 %collective-permute-done.1 = bf16[144,896]{1,0:T(8,128)(2,1)S(1)} collective-permute-done((bf16[144,896]{1,0:T(8,128)(2,1)}, bf16[144,896]{1,0:T(8,128)(2,1)S(1)}, u32[]{:S(2)}, u32[]{:S(2)}) %collective-permute-start.1) | collective-permute-done | bytes 258080 | tf_op jit(solution)/shard_map/ppermute | solution.py:130
  51.0 23.2 %collective-permute-done.4.x_ref = bf16[4,144,896]{2,1,0:T(8,128)(2,1)S(1)} collective-permute-done((bf16[4,144,896]{2,1,0:T(8,128)(2,1)S(1)}, bf16[4,144,896]{2,1,0:T(8,128)(2,1)S(1)}, u32[]{:S(2)}, u32[]{:S(2)}) %collective-permute-start.4) | collective-permute-done | bytes 1032224 | tf_op jit(solution)/shard_map/ppermute | solution.py:59
  87.3 7.2 %collective-permute-done.7.t_ref = bf16[128,2048]{1,0:T(8,128)(2,1)S(1)} collective-permute-done((bf16[128,2048]{1,0:T(8,128)(2,1)S(1)}, bf16[128,2048]{1,0:T(8,128)(2,1)S(1)}, u32[]{:S(2)}, u32[]{:S(2)}) %collective-permute-start.7) | collective-permute-done | bytes 524320 | tf_op jit(solution)/shard_map/ppermute | solution.py:63
  94.4 2.4 collective-permute-done.8.x_ref
  96.8 10.2 %collective-permute-done.9.xt_ref = bf16[128,2048]{1,0:T(8,128)(2,1)} collective-permute-done((bf16[128,2048]{1,0:T(8,128)(2,1)S(1)}, bf16[128,2048]{1,0:T(8,128)(2,1)}, u32[]{:S(2)}, u32[]{:S(2)}) %collective-permute-start.9) | collective-permute-done | bytes 524320 | tf_op jit(solution)/shard_map/ppermute | solution.py:67
  107.0 2.6 shard_map.340
  111.7 18.3 %collective-permute-done.17.got_ref = bf16[2,128,1536]{2,1,0:T(8,128)(2,1)S(1)} collective-permute-done((bf16[2,128,1536]{2,1,0:T(8,128)(2,1)}, bf16[2,128,1536]{2,1,0:T(8,128)(2,1)S(1)}, u32[]{:S(2)}, u32[]{:S(2)}) %collective-permute-start.17) | collective-permute-done | bytes 786464 | tf_op jit(solution)/shard_map/ppermute | solution.py:59
  130.2 3.2 multiply_sine_fusion
  133.3 6.2 %fusion.92.row_ref = f32[512,896]{1,0:T(8,128)} fusion(bf16[512,2048]{1,0:T(8,128)(2,1)} %shard_map.340, bf16[2048,896]{1,0:T(8,128)(2,1)} %bitcast.139), kind=kOutput, calls=%fused_computation.212 | convolution fusion | flops 1879048192 | bytes 7602176 | tf_op jit(solution)/shard_map/dot_general | solution.py:26
  145.4 6.3 %fusion.93.row_ref = f32[512,896]{1,0:T(8,128)} fusion(bf16[512,2048]{1,0:T(8,128)(2,1)} %collective-permute-done.12, bf16[2048,896]{1,0:T(8,128)(2,1)} %bitcast.140), kind=kOutput, calls=%fused_computation.213 | convolution fusion | flops 1879048192 | bytes 7602176 | tf_op jit(solution)/shard_map/dot_general | solution.py:26
  151.7 5.8 %fusion.13.mix_ref = f32[512,896]{1,0:T(8,128)S(1)} fusion(bf16[512,2048]{1,0:T(8,128)(2,1)} %shard_map.340, bf16[2048,1408]{1,0:T(8,128)(2,1)} %all-gather.3.cloned.1.call-done), kind=kOutput, calls=%fused_computation.23 | convolution fusion | flops 1879048192 | bytes 7602176 | tf_op jit(solution)/shard_map/dot_general | solution.py:26
  157.5 4.6 fusion.11.mix_ref
  163.8 4.2 collective-permute-done.21.xt_ref
  173.8 5.0 shard_map.344
  179.7 5.0 shard_map.345
  190.1 2.4 collective-permute-start.16
  195.6 3.4 collective-permute-done.14
  202.3 2.8 collective-permute-done.23.got_ref
  209.9 12.2 %collective-permute-done.26 = bf16[128,2048]{1,0:T(8,128)(2,1)S(1)} collective-permute-done((bf16[128,2048]{1,0:T(8,128)(2,1)S(1)}, bf16[128,2048]{1,0:T(8,128)(2,1)S(1)}, u32[]{:S(2)}, u32[]{:S(2)}) %collective-permute-start.26) | collective-permute-done | bytes 524320 | tf_op jit(solution)/shard_map/ppermute | solution.py:67
  222.1 9.5 %collective-permute-done.25 = bf16[128,2048]{1,0:T(8,128)(2,1)S(1)} collective-permute-done((bf16[128,2048]{1,0:T(8,128)(2,1)S(1)}, bf16[128,2048]{1,0:T(8,128)(2,1)S(1)}, u32[]{:S(2)}, u32[]{:S(2)}) %collective-permute-start.25) | collective-permute-done | bytes 524320 | tf_op jit(solution)/shard_map/ppermute | solution.py:59
  236.8 10.5 %collective-permute-done.27.t_ref = bf16[128,2048]{1,0:T(8,128)(2,1)S(1)} collective-permute-done((bf16[128,2048]{1,0:T(8,128)(2,1)S(1)}, bf16[128,2048]{1,0:T(8,128)(2,1)S(1)}, u32[]{:S(2)}, u32[]{:S(2)}) %collective-permute-start.27) | collective-permute-done | bytes 524320 | tf_op jit(solution)/shard_map/ppermute | solution.py:63
  248.8 10.9 %collective-permute-done.29.xt_ref = bf16[128,2048]{1,0:T(8,128)(2,1)S(1)} collective-permute-done((bf16[128,2048]{1,0:T(8,128)(2,1)S(1)}, bf16[128,2048]{1,0:T(8,128)(2,1)S(1)}, u32[]{:S(2)}, u32[]{:S(2)}) %collective-permute-start.29) | collective-permute-done | bytes 524320 | tf_op jit(solution)/shard_map/ppermute | solution.py:67
  261.1 5.3 fusion.5
  266.8 4.5 fusion.3
  273.8 2.9 fusion.94
  276.7 2.8 add_convert_fusion.5
  282.0 4.2 multiply_convert_fusion.2
  286.2 4.4 fusion.33
  293.2 6.2 %add_convert_fusion = bf16[2048,1024]{1,0:T(8,128)(2,1)} fusion(f32[2048,1024]{1,0:T(8,128)S(1)} %fusion.33, bf16[512,2048]{1,0:T(8,128)(2,1)} %shard_map.351, bf16[512,512]{1,0:T(8,128)(2,1)S(1)} %get-tuple-element.315, bf16[512,512]{1,0:T(8,128)(2,1)S(1)} %get-tuple-element.314), kind=kOutput, calls=%fused_computation | convolution fusion | flops 2153775104 | bytes 15728640 | tf_op jit(solution)/shard_map/tc,tk->ck/dot_general | solution.py:30
  300.0 5.0 convolution_convert_fusion
  305.5 4.6 fusion.1.total_ref
  318.0 10.8 %collective-permute-done.35 = bf16[128,2048]{1,0:T(8,128)(2,1)S(1)} collective-permute-done((bf16[128,2048]{1,0:T(8,128)(2,1)S(1)}, bf16[128,2048]{1,0:T(8,128)(2,1)S(1)}, u32[]{:S(2)}, u32[]{:S(2)}) %collective-permute-start.35) | collective-permute-done | bytes 524320 | tf_op jit(solution)/shard_map/ppermute | solution.py:67
  328.9 9.6 %collective-permute-done.34 = bf16[128,2048]{1,0:T(8,128)(2,1)S(1)} collective-permute-done((bf16[128,2048]{1,0:T(8,128)(2,1)S(1)}, bf16[128,2048]{1,0:T(8,128)(2,1)S(1)}, u32[]{:S(2)}, u32[]{:S(2)}) %collective-permute-start.34) | collective-permute-done | bytes 524320 | tf_op jit(solution)/shard_map/ppermute | solution.py:59
  348.2 10.5 %collective-permute-done.36.t_ref = bf16[128,2048]{1,0:T(8,128)(2,1)S(1)} collective-permute-done((bf16[128,2048]{1,0:T(8,128)(2,1)S(1)}, bf16[128,2048]{1,0:T(8,128)(2,1)S(1)}, u32[]{:S(2)}, u32[]{:S(2)}) %collective-permute-start.36) | collective-permute-done | bytes 524320 | tf_op jit(solution)/shard_map/ppermute | solution.py:63
  360.1 10.9 %collective-permute-done.38.xt_ref = bf16[128,2048]{1,0:T(8,128)(2,1)S(1)} collective-permute-done((bf16[128,2048]{1,0:T(8,128)(2,1)S(1)}, bf16[128,2048]{1,0:T(8,128)(2,1)S(1)}, u32[]{:S(2)}, u32[]{:S(2)}) %collective-permute-start.38) | collective-permute-done | bytes 524320 | tf_op jit(solution)/shard_map/ppermute | solution.py:67
  378.1 2.7 add_convert_fusion.4
  382.4 3.1 fusion.97.grad_ref
  405.1 9.5 %shard_map.355 = (bf16[512,896]{1,0:T(8,128)(2,1)S(1)}, bf16[512,896]{1,0:T(8,128)(2,1)S(1)}, f32[2,16,384]{2,1,0:T(8,128)S(1)}, f32[2,8,512]{2,1,0:T(8,128)S(1)}) custom-call(f32[512,896]{1,0:T(8,128)S(1)} %copy-done.7, f32[512,896]{1,0:T(8,128)S(1)} %copy-done.5, f32[512,128]{1,0:T(8,128)S(1)} %copy-done.25, ...), custom_call_target="tpu_custom_call" | custom-call | tf_op jit(solution)/shard_map/pallas_call | solution.py:393
  428.3 9.7 %shard_map.356 = (bf16[512,896]{1,0:T(8,128)(2,1)S(1)}, bf16[512,896]{1,0:T(8,128)(2,1)S(1)}, f32[2,16,384]{2,1,0:T(8,128)S(1)}, f32[2,8,512]{2,1,0:T(8,128)S(1)}) custom-call(f32[512,896]{1,0:T(8,128)S(1)} %copy-done.3, f32[512,896]{1,0:T(8,128)S(1)} %copy-done.1, f32[512,128]{1,0:T(8,128)S(1)} %copy-done.23, ...), custom_call_target="tpu_custom_call" | custom-call | tf_op jit(solution)/shard_map/pallas_call | solution.py:393
  438.1 4.7 fusion.98
  442.8 5.9 %add_convert_fusion.2 = bf16[2048,896]{1,0:T(8,128)(2,1)} fusion(f32[2048,896]{1,0:T(8,128)S(1)} %fusion.98, bf16[512,2048]{1,0:T(8,128)(2,1)} %shard_map.340, bf16[512,896]{1,0:T(8,128)(2,1)S(1)} %copy-done.68), kind=kOutput, calls=%fused_computation.2 | convolution fusion | flops 1882718208 | bytes 14024704 | tf_op jit(solution)/shard_map/tc,tk->ck/dot_general | solution.py:30
  452.8 5.2 fusion.7
  458.1 2.4 add_convert_fusion.3
  460.6 2.4 fusion.9
  463.0 2.4 convolution_add_fusion.total_ref
  469.1 4.0 fusion.99
  473.1 4.0 add_convert_fusion.1
  485.2 3.4 shard_map.362
  490.6 4.7 collective-permute-done.53
  495.4 9.7 %collective-permute-done.52 = bf16[128,2048]{1,0:T(8,128)(2,1)} collective-permute-done((bf16[128,2048]{1,0:T(8,128)(2,1)}, bf16[128,2048]{1,0:T(8,128)(2,1)}, u32[]{:S(2)}, u32[]{:S(2)}) %collective-permute-start.52) | collective-permute-done | bytes 524320 | tf_op jit(solution)/shard_map/ppermute | solution.py:59
  506.1 2.8 fusion.25
  514.0 10.6 %collective-permute-done.55 = bf16[4,128,896]{2,1,0:T(8,128)(2,1)S(1)} collective-permute-done((bf16[4,128,896]{2,1,0:T(8,128)(2,1)S(1)}, bf16[4,128,896]{2,1,0:T(8,128)(2,1)S(1)}, u32[]{:S(2)}, u32[]{:S(2)}) %collective-permute-start.55) | collective-permute-done | bytes 917536 | tf_op jit(solution)/shard_map/ppermute | solution.py:59
  527.6 4.1 collective-permute-done.58
  533.0 2.3 collective-permute-start.59
  535.4 2.8 fusion.24
  542.7 8.2 %collective-permute-done.59 = f32[268,128]{1,0:T(8,128)} collective-permute-done((f32[268,128]{1,0:T(8,128)S(1)}, f32[268,128]{1,0:T(8,128)}, u32[]{:S(2)}, u32[]{:S(2)}) %collective-permute-start.59) | collective-permute-done | bytes 137248 | tf_op jit(solution)/shard_map/ppermute | solution.py:137
  552.1 4.1 collective-permute-done.62.got_ref
  557.3 3.1 reduce-scatter.16.cloned.1.call-done
  (618 shorter events, 181.6 us)
Async XLA Ops:
  7.2 144.5 %all-gather.3.cloned.1.call-start = ((), (), s32[]{:S(2)}) async-start(), calls=%async_computation.5 | async-start | bytes 7208960 | tf_op jit(solution)/shard_map/all_gather | solution.py:109
  10.6 23.5 %collective-permute-start.10 = (bf16[2,128,1408]{2,1,0:T(8,128)(2,1)S(1)}, bf16[2,128,1408]{2,1,0:T(8,128)(2,1)S(1)}, u32[]{:S(2)}, u32[]{:S(2)}) collective-permute-start(bf16[2,128,1408]{2,1,0:T(8,128)(2,1)S(1)} %get-tuple-element.114), channel_id=1, source_target_pairs={{0,4},{4,0},{1,5},{5,1},{2,6},{6,2},{3,7},{7,3},{8,12},{12,8},{9,1... | collective-permute-start | bytes 2162696 | tf_op jit(solution)/shard_map/ppermute | solution.py:59
  14.6 15.5 %collective-permute-start = (bf16[144,896]{1,0:T(8,128)(2,1)S(1)}, bf16[144,896]{1,0:T(8,128)(2,1)}, u32[]{:S(2)}, u32[]{:S(2)}) collective-permute-start(bf16[144,896]{1,0:T(8,128)(2,1)S(1)} %fusion.42), channel_id=1, source_target_pairs={{0,16},{8,24},{16,0},{24,8},{1,17},{9,25},{17,1},{25,9},{2,18},{10... | collective-permute-start | bytes 774152 | tf_op jit(solution)/shard_map/ppermute | solution.py:120
  17.2 12.8 %collective-permute-start.3 = (bf16[144,896]{1,0:T(8,128)(2,1)S(1)}, bf16[144,896]{1,0:T(8,128)(2,1)S(1)}, u32[]{:S(2)}, u32[]{:S(2)}) collective-permute-start(bf16[144,896]{1,0:T(8,128)(2,1)S(1)} %fusion.42), channel_id=1, source_target_pairs={{0,8},{8,16},{16,24},{1,9},{9,17},{17,25},{2,10},{10,18},{18,26},{... | collective-permute-start | bytes 774152 | tf_op jit(solution)/shard_map/ppermute | solution.py:121
  20.7 13.4 %collective-permute-start.2 = (bf16[144,896]{1,0:T(8,128)(2,1)S(1)}, bf16[144,896]{1,0:T(8,128)(2,1)S(1)}, u32[]{:S(2)}, u32[]{:S(2)}) collective-permute-start(bf16[144,896]{1,0:T(8,128)(2,1)S(1)} %fusion.42), channel_id=1, source_target_pairs={{8,0},{16,8},{24,16},{9,1},{17,9},{25,17},{10,2},{18,10},{26,18},{... | collective-permute-start | bytes 774152 | tf_op jit(solution)/shard_map/ppermute | solution.py:122
  38.3 222.9 %all-gather.5.cloned.1.call-start = ((), (), s32[]{:S(2)}) async-start(), calls=%async_computation.6 | async-start | bytes 7864320 | tf_op jit(solution)/shard_map/all_gather | solution.py:109
  38.3 10.5 %collective-permute-start.1 = (bf16[144,896]{1,0:T(8,128)(2,1)}, bf16[144,896]{1,0:T(8,128)(2,1)S(1)}, u32[]{:S(2)}, u32[]{:S(2)}) collective-permute-start(bf16[144,896]{1,0:T(8,128)(2,1)} %collective-permute-done), channel_id=1, source_target_pairs={{16,24},{8,0},{17,25},{9,1},{18,26},{10,2},{19,27},{11,3},{20,28},... | collective-permute-start | bytes 774152 | tf_op jit(solution)/shard_map/ppermute | solution.py:130
  50.0 24.1 %collective-permute-start.4 = (bf16[4,144,896]{2,1,0:T(8,128)(2,1)S(1)}, bf16[4,144,896]{2,1,0:T(8,128)(2,1)S(1)}, u32[]{:S(2)}, u32[]{:S(2)}) collective-permute-start(bf16[4,144,896]{2,1,0:T(8,128)(2,1)S(1)} %pad_maximum_fusion.2.own_ref), channel_id=1, source_target_pairs={{0,4},{4,0},{1,5},{5,1},{2,6},{6,2},{3,7},{7,3},{8,12},{12,8},{9,1... | collective-permute-start | bytes 3096584 | tf_op jit(solution)/shard_map/ppermute | solution.py:59
  50.9 25.4 %collective-permute-start.5 = (bf16[4,144,896]{2,1,0:T(8,128)(2,1)S(1)}, bf16[4,144,896]{2,1,0:T(8,128)(2,1)S(1)}, u32[]{:S(2)}, u32[]{:S(2)}) collective-permute-start(bf16[4,144,896]{2,1,0:T(8,128)(2,1)S(1)} %pad_maximum_fusion.2.own_ref), channel_id=1, source_target_pairs={{0,2},{2,0},{1,3},{3,1},{4,6},{6,4},{5,7},{7,5},{8,10},{10,8},{9,1... | collective-permute-start | bytes 3096584 | tf_op jit(solution)/shard_map/ppermute | solution.py:55
  80.5 14.0 %collective-permute-start.7 = (bf16[128,2048]{1,0:T(8,128)(2,1)S(1)}, bf16[128,2048]{1,0:T(8,128)(2,1)S(1)}, u32[]{:S(2)}, u32[]{:S(2)}) collective-permute-start(bf16[128,2048]{1,0:T(8,128)(2,1)S(1)} %fusion.20.own_ref), channel_id=1, source_target_pairs={{0,1},{1,0},{2,3},{3,2},{4,5},{5,4},{6,7},{7,6},{8,9},{9,8},{10,11... | collective-permute-start | bytes 1572872 | tf_op jit(solution)/shard_map/ppermute | solution.py:63
  82.0 14.8 %collective-permute-start.8 = (bf16[128,2048]{1,0:T(8,128)(2,1)S(1)}, bf16[128,2048]{1,0:T(8,128)(2,1)S(1)}, u32[]{:S(2)}, u32[]{:S(2)}) collective-permute-start(bf16[128,2048]{1,0:T(8,128)(2,1)S(1)} %fusion.20.own_ref), channel_id=1, source_target_pairs={{0,4},{4,0},{1,5},{5,1},{2,6},{6,2},{3,7},{7,3},{8,12},{12,8},{9,1... | collective-permute-start | bytes 1572872 | tf_op jit(solution)/shard_map/ppermute | solution.py:59
  82.5 24.4 %collective-permute-start.9 = (bf16[128,2048]{1,0:T(8,128)(2,1)S(1)}, bf16[128,2048]{1,0:T(8,128)(2,1)}, u32[]{:S(2)}, u32[]{:S(2)}) collective-permute-start(bf16[128,2048]{1,0:T(8,128)(2,1)S(1)} %fusion.20.own_ref), channel_id=1, source_target_pairs={{0,5},{1,4},{4,1},{5,0},{2,7},{3,6},{6,3},{7,2},{8,13},{9,12},{12,... | collective-permute-start | bytes 1572872 | tf_op jit(solution)/shard_map/ppermute | solution.py:67
  109.6 35.8 %collective-permute-start.12 = (bf16[512,2048]{1,0:T(8,128)(2,1)}, bf16[512,2048]{1,0:T(8,128)(2,1)}, u32[]{:S(2)}, u32[]{:S(2)}) collective-permute-start(bf16[512,2048]{1,0:T(8,128)(2,1)} %shard_map.340), channel_id=1, source_target_pairs={{0,2},{2,0},{1,3},{3,1},{4,6},{6,4},{5,7},{7,5},{8,10},{10,8},{9,1... | collective-permute-start | bytes 6291464 | tf_op jit(solution)/shard_map/ppermute | solution.py:55
  109.8 20.2 %collective-permute-start.17 = (bf16[2,128,1536]{2,1,0:T(8,128)(2,1)}, bf16[2,128,1536]{2,1,0:T(8,128)(2,1)S(1)}, u32[]{:S(2)}, u32[]{:S(2)}) collective-permute-start(bf16[2,128,1536]{2,1,0:T(8,128)(2,1)} %get-tuple-element.125), channel_id=1, source_target_pairs={{0,4},{4,0},{1,5},{5,1},{2,6},{6,2},{3,7},{7,3},{8,12},{12,8},{9,1... | collective-permute-start | bytes 2359304 | tf_op jit(solution)/shard_map/ppermute | solution.py:59
  130.1 9.5 %collective-permute-start.18 = (bf16[2,128,1536]{2,1,0:T(8,128)(2,1)S(1)}, bf16[2,128,1536]{2,1,0:T(8,128)(2,1)S(1)}, u32[]{:S(2)}, u32[]{:S(2)}) collective-permute-start(bf16[2,128,1536]{2,1,0:T(8,128)(2,1)S(1)} %get-tuple-element.127), channel_id=1, source_target_pairs={{0,2},{2,0},{1,3},{3,1},{4,6},{6,4},{5,7},{7,5},{8,10},{10,8},{9,1... | collective-permute-start | bytes 2359304 | tf_op jit(solution)/shard_map/ppermute | solution.py:55
  141.3 20.8 %collective-permute-start.19 = (bf16[128,2048]{1,0:T(8,128)(2,1)S(1)}, bf16[128,2048]{1,0:T(8,128)(2,1)S(1)}, u32[]{:S(2)}, u32[]{:S(2)}) collective-permute-start(bf16[128,2048]{1,0:T(8,128)(2,1)S(1)} %fusion.19.own_ref), channel_id=1, source_target_pairs={{0,1},{1,0},{2,3},{3,2},{4,5},{5,4},{6,7},{7,6},{8,9},{9,8},{10,11... | collective-permute-start | bytes 1572872 | tf_op jit(solution)/shard_map/ppermute | solution.py:63
  142.9 20.2 %collective-permute-start.20 = (bf16[128,2048]{1,0:T(8,128)(2,1)S(1)}, bf16[128,2048]{1,0:T(8,128)(2,1)S(1)}, u32[]{:S(2)}, u32[]{:S(2)}) collective-permute-start(bf16[128,2048]{1,0:T(8,128)(2,1)S(1)} %fusion.19.own_ref), channel_id=1, source_target_pairs={{0,4},{4,0},{1,5},{5,1},{2,6},{6,2},{3,7},{7,3},{8,12},{12,8},{9,1... | collective-permute-start | bytes 1572872 | tf_op jit(solution)/shard_map/ppermute | solution.py:59
  143.4 24.7 %collective-permute-start.21 = (bf16[128,2048]{1,0:T(8,128)(2,1)S(1)}, bf16[128,2048]{1,0:T(8,128)(2,1)S(1)}, u32[]{:S(2)}, u32[]{:S(2)}) collective-permute-start(bf16[128,2048]{1,0:T(8,128)(2,1)S(1)} %fusion.19.own_ref), channel_id=1, source_target_pairs={{0,5},{1,4},{4,1},{5,0},{2,7},{3,6},{6,3},{7,2},{8,13},{9,12},{12,... | collective-permute-start | bytes 1572872 | tf_op jit(solution)/shard_map/ppermute | solution.py:67
  144.9 199.8 %reduce-scatter.8.cloned.1.call-start = ((), (), s32[]{:S(2)}) async-start(), calls=%async_computation.7 | async-start | bytes 2621440 | tf_op jit(solution)/shard_map/reduce_scatter | solution.py:113
  172.2 27.1 %collective-permute-start.22 = (bf16[512,2048]{1,0:T(8,128)(2,1)S(1)}, bf16[512,2048]{1,0:T(8,128)(2,1)}, u32[]{:S(2)}, u32[]{:S(2)}) collective-permute-start(bf16[512,2048]{1,0:T(8,128)(2,1)S(1)} %shard_map.349), channel_id=1, source_target_pairs={{0,2},{2,0},{1,3},{3,1},{4,6},{6,4},{5,7},{7,5},{8,10},{10,8},{9,1... | collective-permute-start | bytes 6291464 | tf_op jit(solution)/shard_map/ppermute | solution.py:55
  189.6 6.0 %collective-permute-start.15 = (f32[4,8,256]{2,1,0:T(8,128)S(1)}, f32[4,8,256]{2,1,0:T(8,128)S(1)}, u32[]{:S(2)}, u32[]{:S(2)}) collective-permute-start(f32[4,8,256]{2,1,0:T(8,128)S(1)} %maximum_add_fusion), channel_id=1, source_target_pairs={{0,4},{4,0},{1,5},{5,1},{2,6},{6,2},{3,7},{7,3},{8,12},{12,8},{9,1... | collective-permute-start | bytes 98312 | tf_op jit(solution)/shard_map/ppermute | solution.py:59
  190.1 5.4 collective-permute-start.16
  206.4 15.8 %collective-permute-start.26 = (bf16[128,2048]{1,0:T(8,128)(2,1)S(1)}, bf16[128,2048]{1,0:T(8,128)(2,1)S(1)}, u32[]{:S(2)}, u32[]{:S(2)}) collective-permute-start(bf16[128,2048]{1,0:T(8,128)(2,1)S(1)} %get-tuple-element.136), channel_id=1, source_target_pairs={{0,5},{1,4},{4,1},{5,0},{2,7},{3,6},{6,3},{7,2},{8,13},{9,12},{12,... | collective-permute-start | bytes 1572872 | tf_op jit(solution)/shard_map/ppermute | solution.py:67
  206.9 24.7 %collective-permute-start.25 = (bf16[128,2048]{1,0:T(8,128)(2,1)S(1)}, bf16[128,2048]{1,0:T(8,128)(2,1)S(1)}, u32[]{:S(2)}, u32[]{:S(2)}) collective-permute-start(bf16[128,2048]{1,0:T(8,128)(2,1)S(1)} %get-tuple-element.135), channel_id=1, source_target_pairs={{0,4},{4,0},{1,5},{5,1},{2,6},{6,2},{3,7},{7,3},{8,12},{12,8},{9,1... | collective-permute-start | bytes 1572872 | tf_op jit(solution)/shard_map/ppermute | solution.py:59
  208.4 24.1 %collective-permute-start.24 = (bf16[128,2048]{1,0:T(8,128)(2,1)S(1)}, bf16[128,2048]{1,0:T(8,128)(2,1)S(1)}, u32[]{:S(2)}, u32[]{:S(2)}) collective-permute-start(bf16[128,2048]{1,0:T(8,128)(2,1)S(1)} %get-tuple-element.134), channel_id=1, source_target_pairs={{0,1},{1,0},{2,3},{3,2},{4,5},{5,4},{6,7},{7,6},{8,9},{9,8},{10,11... | collective-permute-start | bytes 1572872 | tf_op jit(solution)/shard_map/ppermute | solution.py:63
  233.2 14.0 %collective-permute-start.27 = (bf16[128,2048]{1,0:T(8,128)(2,1)S(1)}, bf16[128,2048]{1,0:T(8,128)(2,1)S(1)}, u32[]{:S(2)}, u32[]{:S(2)}) collective-permute-start(bf16[128,2048]{1,0:T(8,128)(2,1)S(1)} %multiply_convert_fusion.7.own_ref), channel_id=1, source_target_pairs={{0,1},{1,0},{2,3},{3,2},{4,5},{5,4},{6,7},{7,6},{8,9},{9,8},{10,11... | collective-permute-start | bytes 1572872 | tf_op jit(solution)/shard_map/ppermute | solution.py:63
  233.9 14.8 %collective-permute-start.28 = (bf16[128,2048]{1,0:T(8,128)(2,1)S(1)}, bf16[128,2048]{1,0:T(8,128)(2,1)S(1)}, u32[]{:S(2)}, u32[]{:S(2)}) collective-permute-start(bf16[128,2048]{1,0:T(8,128)(2,1)S(1)} %multiply_convert_fusion.7.own_ref), channel_id=1, source_target_pairs={{0,4},{4,0},{1,5},{5,1},{2,6},{6,2},{3,7},{7,3},{8,12},{12,8},{9,1... | collective-permute-start | bytes 1572872 | tf_op jit(solution)/shard_map/ppermute | solution.py:59
  234.5 25.2 %collective-permute-start.29 = (bf16[128,2048]{1,0:T(8,128)(2,1)S(1)}, bf16[128,2048]{1,0:T(8,128)(2,1)S(1)}, u32[]{:S(2)}, u32[]{:S(2)}) collective-permute-start(bf16[128,2048]{1,0:T(8,128)(2,1)S(1)} %multiply_convert_fusion.7.own_ref), channel_id=1, source_target_pairs={{0,5},{1,4},{4,1},{5,0},{2,7},{3,6},{6,3},{7,2},{8,13},{9,12},{12,... | collective-permute-start | bytes 1572872 | tf_op jit(solution)/shard_map/ppermute | solution.py:67
  261.1 5.7 collective-permute-start.30
  279.5 140.7 %reduce-scatter.10.cloned.1.call-start = ((), (), s32[]{:S(2)}) async-start(), calls=%async_computation.8 | async-start | bytes 5242880 | tf_op jit(solution)/shard_map/reduce_scatter | solution.py:113
  299.5 238.7 %reduce-scatter.14.cloned.1.call-start = ((), (), s32[]{:S(2)}) async-start(), calls=%async_computation.10 | async-start | bytes 2621440 | tf_op jit(solution)/shard_map/reduce_scatter | solution.py:113
  305.0 5.1 collective-permute-start.31
  313.1 27.6 %collective-permute-start.32 = (bf16[512,2048]{1,0:T(8,128)(2,1)S(1)}, bf16[512,2048]{1,0:T(8,128)(2,1)S(1)}, u32[]{:S(2)}, u32[]{:S(2)}) collective-permute-start(bf16[512,2048]{1,0:T(8,128)(2,1)S(1)} %convolution_convert_fusion.1), channel_id=1, source_target_pairs={{0,2},{2,0},{1,3},{3,1},{4,6},{6,4},{5,7},{7,5},{8,10},{10,8},{9,1... | collective-permute-start | bytes 6291464 | tf_op jit(solution)/shard_map/ppermute | solution.py:55
  313.2 15.7 %collective-permute-start.35 = (bf16[128,2048]{1,0:T(8,128)(2,1)S(1)}, bf16[128,2048]{1,0:T(8,128)(2,1)S(1)}, u32[]{:S(2)}, u32[]{:S(2)}) collective-permute-start(bf16[128,2048]{1,0:T(8,128)(2,1)S(1)} %get-tuple-element.141), channel_id=1, source_target_pairs={{0,5},{1,4},{4,1},{5,0},{2,7},{3,6},{6,3},{7,2},{8,13},{9,12},{12,... | collective-permute-start | bytes 1572872 | tf_op jit(solution)/shard_map/ppermute | solution.py:67
  314.6 23.9 %collective-permute-start.34 = (bf16[128,2048]{1,0:T(8,128)(2,1)S(1)}, bf16[128,2048]{1,0:T(8,128)(2,1)S(1)}, u32[]{:S(2)}, u32[]{:S(2)}) collective-permute-start(bf16[128,2048]{1,0:T(8,128)(2,1)S(1)} %get-tuple-element.140), channel_id=1, source_target_pairs={{0,4},{4,0},{1,5},{5,1},{2,6},{6,2},{3,7},{7,3},{8,12},{12,8},{9,1... | collective-permute-start | bytes 1572872 | tf_op jit(solution)/shard_map/ppermute | solution.py:59
  315.2 24.4 %collective-permute-start.33 = (bf16[128,2048]{1,0:T(8,128)(2,1)S(1)}, bf16[128,2048]{1,0:T(8,128)(2,1)S(1)}, u32[]{:S(2)}, u32[]{:S(2)}) collective-permute-start(bf16[128,2048]{1,0:T(8,128)(2,1)S(1)} %get-tuple-element.139), channel_id=1, source_target_pairs={{0,1},{1,0},{2,3},{3,2},{4,5},{5,4},{6,7},{7,6},{8,9},{9,8},{10,11... | collective-permute-start | bytes 1572872 | tf_op jit(solution)/shard_map/ppermute | solution.py:63
  344.7 14.0 %collective-permute-start.36 = (bf16[128,2048]{1,0:T(8,128)(2,1)S(1)}, bf16[128,2048]{1,0:T(8,128)(2,1)S(1)}, u32[]{:S(2)}, u32[]{:S(2)}) collective-permute-start(bf16[128,2048]{1,0:T(8,128)(2,1)S(1)} %multiply_convert_fusion.own_ref), channel_id=1, source_target_pairs={{0,1},{1,0},{2,3},{3,2},{4,5},{5,4},{6,7},{7,6},{8,9},{9,8},{10,11... | collective-permute-start | bytes 1572872 | tf_op jit(solution)/shard_map/ppermute | solution.py:63
  345.3 14.8 %collective-permute-start.37 = (bf16[128,2048]{1,0:T(8,128)(2,1)S(1)}, bf16[128,2048]{1,0:T(8,128)(2,1)S(1)}, u32[]{:S(2)}, u32[]{:S(2)}) collective-permute-start(bf16[128,2048]{1,0:T(8,128)(2,1)S(1)} %multiply_convert_fusion.own_ref), channel_id=1, source_target_pairs={{0,4},{4,0},{1,5},{5,1},{2,6},{6,2},{3,7},{7,3},{8,12},{12,8},{9,1... | collective-permute-start | bytes 1572872 | tf_op jit(solution)/shard_map/ppermute | solution.py:59
  346.3 24.7 %collective-permute-start.38 = (bf16[128,2048]{1,0:T(8,128)(2,1)S(1)}, bf16[128,2048]{1,0:T(8,128)(2,1)S(1)}, u32[]{:S(2)}, u32[]{:S(2)}) collective-permute-start(bf16[128,2048]{1,0:T(8,128)(2,1)S(1)} %multiply_convert_fusion.own_ref), channel_id=1, source_target_pairs={{0,5},{1,4},{4,1},{5,0},{2,7},{3,6},{6,3},{7,2},{8,13},{9,12},{12,... | collective-permute-start | bytes 1572872 | tf_op jit(solution)/shard_map/ppermute | solution.py:67
  380.8 158.6 %reduce-scatter.12.cloned.1.call-start = ((), (), s32[]{:S(2)}) async-start(), calls=%async_computation.9 | async-start | bytes 4587520 | tf_op jit(solution)/shard_map/reduce_scatter | solution.py:113
  388.2 4.8 collective-permute-start.43
  393.5 24.2 %collective-permute-start.46 = (bf16[128,2048]{1,0:T(8,128)(2,1)}, bf16[128,2048]{1,0:T(8,128)(2,1)S(1)}, u32[]{:S(2)}, u32[]{:S(2)}) collective-permute-start(bf16[128,2048]{1,0:T(8,128)(2,1)} %copy-done.76), channel_id=1, source_target_pairs={{0,5},{1,4},{4,1},{5,0},{2,7},{3,6},{6,3},{7,2},{8,13},{9,12},{12,... | collective-permute-start | bytes 1572872 | tf_op jit(solution)/shard_map/ppermute | solution.py:67
  395.1 23.9 %collective-permute-start.45 = (bf16[128,2048]{1,0:T(8,128)(2,1)}, bf16[128,2048]{1,0:T(8,128)(2,1)S(1)}, u32[]{:S(2)}, u32[]{:S(2)}) collective-permute-start(bf16[128,2048]{1,0:T(8,128)(2,1)} %copy-done.75), channel_id=1, source_target_pairs={{0,4},{4,0},{1,5},{5,1},{2,6},{6,2},{3,7},{7,3},{8,12},{12,8},{9,1... | collective-permute-start | bytes 1572872 | tf_op jit(solution)/shard_map/ppermute | solution.py:59
  396.8 22.1 %collective-permute-start.44 = (bf16[128,2048]{1,0:T(8,128)(2,1)}, bf16[128,2048]{1,0:T(8,128)(2,1)S(1)}, u32[]{:S(2)}, u32[]{:S(2)}) collective-permute-start(bf16[128,2048]{1,0:T(8,128)(2,1)} %copy-done.74), channel_id=1, source_target_pairs={{0,1},{1,0},{2,3},{3,2},{4,5},{5,4},{6,7},{7,6},{8,9},{9,8},{10,11... | collective-permute-start | bytes 1572872 | tf_op jit(solution)/shard_map/ppermute | solution.py:63
  424.5 24.3 %collective-permute-start.47 = (bf16[2,128,1536]{2,1,0:T(8,128)(2,1)}, bf16[2,128,1536]{2,1,0:T(8,128)(2,1)}, u32[]{:S(2)}, u32[]{:S(2)}) collective-permute-start(bf16[2,128,1536]{2,1,0:T(8,128)(2,1)} %get-tuple-element.160), channel_id=1, source_target_pairs={{0,4},{4,0},{1,5},{5,1},{2,6},{6,2},{3,7},{7,3},{8,12},{12,8},{9,1... | collective-permute-start | bytes 2359304 | tf_op jit(solution)/shard_map/ppermute | solution.py:59
  448.7 111.8 %reduce-scatter.16.cloned.1.call-start = ((), (), s32[]{:S(2)}) async-start(), calls=%async_computation.11 | async-start | bytes 1146880
  460.5 4.9 collective-permute-start.48
  478.7 9.9 %collective-permute-start.49 = (bf16[2,4,128,896]{3,2,1,0:T(8,128)(2,1)}, bf16[2,4,128,896]{3,2,1,0:T(8,128)(2,1)}, u32[]{:S(2)}, u32[]{:S(2)}) collective-permute-start(bf16[2,4,128,896]{3,2,1,0:T(8,128)(2,1)} %get-tuple-element.176), channel_id=1, source_target_pairs={{0,2},{2,0},{1,3},{3,1},{4,6},{6,4},{5,7},{7,5},{8,10},{10,8},{9,1... | collective-permute-start | bytes 5505032 | tf_op jit(solution)/shard_map/ppermute | solution.py:55
  479.2 4.8 collective-permute-start.50
  479.3 16.0 %collective-permute-start.53 = (bf16[128,2048]{1,0:T(8,128)(2,1)}, bf16[128,2048]{1,0:T(8,128)(2,1)}, u32[]{:S(2)}, u32[]{:S(2)}) collective-permute-start(bf16[128,2048]{1,0:T(8,128)(2,1)} %copy-done.79), channel_id=1, source_target_pairs={{0,5},{1,4},{4,1},{5,0},{2,7},{3,6},{6,3},{7,2},{8,13},{9,12},{12,... | collective-permute-start | bytes 1572872 | tf_op jit(solution)/shard_map/ppermute | solution.py:67
  480.3 24.8 %collective-permute-start.52 = (bf16[128,2048]{1,0:T(8,128)(2,1)}, bf16[128,2048]{1,0:T(8,128)(2,1)}, u32[]{:S(2)}, u32[]{:S(2)}) collective-permute-start(bf16[128,2048]{1,0:T(8,128)(2,1)} %copy-done.78), channel_id=1, source_target_pairs={{0,4},{4,0},{1,5},{5,1},{2,6},{6,2},{3,7},{7,3},{8,12},{12,8},{9,1... | collective-permute-start | bytes 1572872 | tf_op jit(solution)/shard_map/ppermute | solution.py:59
  480.8 25.3 %collective-permute-start.51 = (bf16[128,2048]{1,0:T(8,128)(2,1)}, bf16[128,2048]{1,0:T(8,128)(2,1)}, u32[]{:S(2)}, u32[]{:S(2)}) collective-permute-start(bf16[128,2048]{1,0:T(8,128)(2,1)} %copy-done.77), channel_id=1, source_target_pairs={{0,1},{1,0},{2,3},{3,2},{4,5},{5,4},{6,7},{7,6},{8,9},{9,8},{10,11... | collective-permute-start | bytes 1572872 | tf_op jit(solution)/shard_map/ppermute | solution.py:63
  490.6 34.1 %collective-permute-start.55 = (bf16[4,128,896]{2,1,0:T(8,128)(2,1)S(1)}, bf16[4,128,896]{2,1,0:T(8,128)(2,1)S(1)}, u32[]{:S(2)}, u32[]{:S(2)}) collective-permute-start(bf16[4,128,896]{2,1,0:T(8,128)(2,1)S(1)} %get-tuple-element.177), channel_id=1, source_target_pairs={{0,4},{4,0},{1,5},{5,1},{2,6},{6,2},{3,7},{7,3},{8,12},{12,8},{9,1... | collective-permute-start | bytes 2752520 | tf_op jit(solution)/shard_map/ppermute | solution.py:59
  510.5 17.1 %collective-permute-start.57 = (f32[268,128]{1,0:T(8,128)S(1)}, f32[268,128]{1,0:T(8,128)S(1)}, u32[]{:S(2)}, u32[]{:S(2)}) collective-permute-start(f32[268,128]{1,0:T(8,128)S(1)} %fusion.76), channel_id=1, source_target_pairs={{0,4},{4,0},{1,5},{5,1},{2,6},{6,2},{3,7},{7,3},{8,12},{12,8},{9,1... | collective-permute-start | bytes 411656 | tf_op jit(solution)/shard_map/ppermute | solution.py:59
  511.0 20.7 %collective-permute-start.58 = (f32[268,128]{1,0:T(8,128)S(1)}, f32[268,128]{1,0:T(8,128)S(1)}, u32[]{:S(2)}, u32[]{:S(2)}) collective-permute-start(f32[268,128]{1,0:T(8,128)S(1)} %fusion.76), channel_id=1, source_target_pairs={{0,5},{1,4},{4,1},{5,0},{2,7},{3,6},{6,3},{7,2},{8,13},{9,12},{12,... | collective-permute-start | bytes 411656 | tf_op jit(solution)/shard_map/ppermute | solution.py:67
  513.0 18.7 %collective-permute-start.56 = (f32[268,128]{1,0:T(8,128)S(1)}, f32[268,128]{1,0:T(8,128)S(1)}, u32[]{:S(2)}, u32[]{:S(2)}) collective-permute-start(f32[268,128]{1,0:T(8,128)S(1)} %fusion.76), channel_id=1, source_target_pairs={{0,1},{1,0},{2,3},{3,2},{4,5},{5,4},{6,7},{7,6},{8,9},{9,8},{10,11... | collective-permute-start | bytes 411656 | tf_op jit(solution)/shard_map/ppermute | solution.py:63
  531.7 11.0 %collective-permute-start.60 = (f32[268,128]{1,0:T(8,128)S(1)}, f32[268,128]{1,0:T(8,128)}, u32[]{:S(2)}, u32[]{:S(2)}) collective-permute-start(f32[268,128]{1,0:T(8,128)S(1)} %add_add_fusion.1), channel_id=1, source_target_pairs={{0,16},{16,0},{8,24},{24,8},{1,17},{17,1},{9,25},{25,9},{2,18},{18... | collective-permute-start | bytes 411656 | tf_op jit(solution)/shard_map/ppermute | solution.py:138
  531.8 10.9 %collective-permute-start.61 = (f32[268,128]{1,0:T(8,128)S(1)}, f32[268,128]{1,0:T(8,128)}, u32[]{:S(2)}, u32[]{:S(2)}) collective-permute-start(f32[268,128]{1,0:T(8,128)S(1)} %add_add_fusion.1), channel_id=1, source_target_pairs={{0,24},{24,0},{8,16},{16,8},{1,25},{25,1},{9,17},{17,9},{2,26},{26... | collective-permute-start | bytes 411656 | tf_op jit(solution)/shard_map/ppermute | solution.py:139
  533.0 18.0 %collective-permute-start.59 = (f32[268,128]{1,0:T(8,128)S(1)}, f32[268,128]{1,0:T(8,128)}, u32[]{:S(2)}, u32[]{:S(2)}) collective-permute-start(f32[268,128]{1,0:T(8,128)S(1)} %add_add_fusion.1), channel_id=1, source_target_pairs={{0,8},{8,0},{16,24},{24,16},{1,9},{9,1},{17,25},{25,17},{2,10},{10... | collective-permute-start | bytes 411656 | tf_op jit(solution)/shard_map/ppermute | solution.py:137
  539.3 17.3 %collective-permute-start.65 = (bf16[2,128,512]{2,1,0:T(8,128)(2,1)S(1)}, bf16[2,128,512]{2,1,0:T(8,128)(2,1)S(1)}, u32[]{:S(2)}, u32[]{:S(2)}) collective-permute-start(bf16[2,128,512]{2,1,0:T(8,128)(2,1)S(1)} %get-tuple-element.197), channel_id=1, source_target_pairs={{0,4},{4,0},{1,5},{5,1},{2,6},{6,2},{3,7},{7,3},{8,12},{12,8},{9,1... | collective-permute-start | bytes 786440 | tf_op jit(solution)/shard_map/ppermute | solution.py:59
  540.7 15.6 %collective-permute-start.62 = (bf16[2,128,896]{2,1,0:T(8,128)(2,1)S(1)}, bf16[2,128,896]{2,1,0:T(8,128)(2,1)S(1)}, u32[]{:S(2)}, u32[]{:S(2)}) collective-permute-start(bf16[2,128,896]{2,1,0:T(8,128)(2,1)S(1)} %get-tuple-element.189), channel_id=1, source_target_pairs={{0,4},{4,0},{1,5},{5,1},{2,6},{6,2},{3,7},{7,3},{8,12},{12,8},{9,1... | collective-permute-start | bytes 1376264 | tf_op jit(solution)/shard_map/ppermute | solution.py:59
  556.3 5.3 collective-permute-start.63
  556.7 12.8 %collective-permute-start.66 = (bf16[2,128,512]{2,1,0:T(8,128)(2,1)S(1)}, bf16[2,128,512]{2,1,0:T(8,128)(2,1)S(1)}, u32[]{:S(2)}, u32[]{:S(2)}) collective-permute-start(bf16[2,128,512]{2,1,0:T(8,128)(2,1)S(1)} %get-tuple-element.199), channel_id=1, source_target_pairs={{0,2},{2,0},{1,3},{3,1},{4,6},{6,4},{5,7},{7,5},{8,10},{10,8},{9,1... | collective-permute-start | bytes 786440 | tf_op jit(solution)/shard_map/ppermute | solution.py:55
  563.8 8.8 %collective-permute-start.64 = (bf16[128,512]{0,1:T(8,128)(2,1)S(1)}, bf16[128,512]{0,1:T(8,128)(2,1)S(1)}, u32[]{:S(2)}, u32[]{:S(2)}) collective-permute-start(bf16[128,512]{0,1:T(8,128)(2,1)S(1)} %slice.279), channel_id=1, source_target_pairs={{0,1},{1,0},{2,3},{3,2},{4,5},{5,4},{6,7},{7,6},{8,9},{9,8},{10,11... | collective-permute-start | bytes 393224 | tf_op jit(solution)/shard_map/ppermute | solution.py:63
  (165 other events, 1468.3 us)
Sparse Core Ops, SparseCore 0:
  38.4 106.2 all-gather.2
  146.8 113.6 all-gather.4
  279.6 41.9 reduce-scatter.7
  323.9 76.0 reduce-scatter.9
  402.2 44.3 reduce-scatter.13
  448.8 67.7 reduce-scatter.11
  535.4 24.9 reduce-scatter.15
